TPU v7x, 32 devices: a whole 2x2x4 slice. The times are simulated.
32 devices in a mesh: groups: 2 (over y), tiles: 4 (over z), chan: 2 (over x), rep: 2 (over core).
Axes of the slice: x: 2, y: 2, z: 4, core: 2. Of those that a mesh axis runs over, the one named last changes fastest.
Arguments:
- fields: bfloat16 [4, 12, 128, 256], P(('groups', 'rep'), 'tiles'), parts along dimension 0, may hold values from -6 to 6
- tile_rows: int32 [4, 3], replicated, may hold values from -1 to 5, as said below
- weights: bfloat16 [9, 128, 128], P(None, 'chan'), may hold values from -0.1875 to 0.1875
- bias: float32 [128], P('chan'), may hold values from -3 to 3
- cotangent: bfloat16 [4, 12, 128, 256], P(('groups', 'rep'), 'tiles', 'chan'), parts along dimension 0, may hold values from -6 to 6
Outputs:
- result: bfloat16 [4, 12, 128, 256], P(('groups', 'rep'), 'tiles', 'chan'), parts along dimension 0
- grad_fields: bfloat16 [4, 12, 128, 256], P(('groups', 'rep'), 'tiles', 'chan'), parts along dimension 0
- grad_weights: float32 [18, 128, 128], P('groups', 'chan'), parts along dimension 0
- grad_bias: float32 [256], P(('groups', 'chan')), parts along dimension 0
There are 2 independent parts, one for each index of `groups`. A program takes and returns all parts, laid end to end along the dimension named above; an argument that names none is the same for every part. Nothing has to cross between parts.
Inputs may be any that keep to these rules, and one draw needn't show every extreme that they name: tile_rows[d, k] is the tile row of the tile in slot k of tile column d, or -1 for an empty slot; the rows of one column are distinct, every column holds one tile or more, and some column holds 3.
All inputs are finite; a program needn't handle non-finite values.
Results may differ from a plain program's by a relative error of at most 0.005.
Values may be sent and summed in bfloat16 or wider, within the bound.
No kernel may reach another device: no remote copies, remote signals or barrier semaphores. Data moves between devices by JAX's collectives and lax.ppermute only.
A program may use at most 64 MiB of HBM per device.

v0:
```python
import math

import jax
import jax.numpy as jnp
from jax import lax
from jax.sharding import PartitionSpec as P

C = 128
TS = 16
SLOTS = 3


def extended(array, sides, width):
    for axis, dim in sides:
        devices, length = (lax.axis_size(axis), array.shape[dim])
        up = [(i, (i + 1) % devices) for i in range(devices)]
        down = [(j, i) for i, j in up]
        last = lax.slice_in_dim(array, length - width, length, axis=dim)
        first = lax.slice_in_dim(array, 0, width, axis=dim)
        before = lax.ppermute(last, axis, up)
        after = lax.ppermute(first, axis, down)
        array = jnp.concatenate([before, array, after], axis=dim)
    return array


def swapped(block, axis, stride):
    count = lax.axis_size(axis)
    route = []
    for low in range(count):
        high = low | 1 << stride
        if high != low and high < count:
            route += [(low, high), (high, low)]
    return lax.ppermute(block, axis, route)


def match_rows(wanted, held_rows, occupied):
    matches = (
        (wanted[:, None] == held_rows[None, :]) & occupied[:, None] & (held_rows[None, :] >= 0)
    )
    return matches.astype(jnp.float32)


def select_rows(selector, values):
    return jnp.einsum(
        "kl,l...->k...", selector, values.astype(jnp.float32), precision=lax.Precision.HIGHEST
    )


def make_lookups(tile_rows):
    devices = lax.axis_size("tiles")
    position = lax.axis_index("tiles")
    own_rows = lax.dynamic_index_in_dim(tile_rows, position, 0, keepdims=False)
    left_rows = lax.dynamic_index_in_dim(
        tile_rows, (position + devices - 1) % devices, 0, keepdims=False
    )
    right_rows = lax.dynamic_index_in_dim(tile_rows, (position + 1) % devices, 0, keepdims=False)
    occupied = own_rows >= 0
    at_top = (own_rows == 2 * tile_rows.shape[1] - 1).astype(jnp.float32)
    return (
        match_rows(own_rows, left_rows, occupied),
        match_rows(own_rows, right_rows, occupied),
        match_rows(own_rows - 1, own_rows, occupied),
        match_rows(own_rows + 1, own_rows, occupied),
        at_top,
    )


def swap_edges(stacked):
    return extended(stacked, (("tiles", 0),), 1)


def fold_partner(top_row):
    devices = lax.axis_size("tiles")
    for bit_level in range(devices.bit_length() - 1):
        top_row = swapped(top_row, "tiles", bit_level)
    return top_row


def pad_tiles(values, lookups):
    west_match, east_match, below, above, at_top = lookups
    received = swap_edges(jnp.stack([values[..., 0], values[..., -1]]))
    west_pad = select_rows(west_match, received[0]).astype(jnp.bfloat16)
    east_pad = select_rows(east_match, received[3]).astype(jnp.bfloat16)
    widened = jnp.concatenate([west_pad[..., None], values, east_pad[..., None]], axis=-1)
    south_pad = select_rows(below, widened[:, :, -1, :])
    north_pad = select_rows(above, widened[:, :, 0, :])
    top_row = jnp.einsum(
        "l,lcw->cw",
        at_top,
        widened[:, :, -1, :].astype(jnp.float32),
        precision=lax.Precision.HIGHEST,
    ).astype(jnp.bfloat16)
    mirrored = jnp.flip(fold_partner(top_row), -1).astype(jnp.float32)
    north_pad = north_pad + at_top[:, None, None] * mirrored[None]
    return jnp.concatenate(
        [
            south_pad[:, :, None].astype(jnp.bfloat16),
            widened,
            north_pad[:, :, None].astype(jnp.bfloat16),
        ],
        axis=2,
    )


def pad_adjoint(pad_grads, lookups):
    west_match, east_match, below, above, at_top = lookups
    south_grads = pad_grads[:, :, 0, :]
    north_grads = pad_grads[:, :, -1, :]
    widened = pad_grads[:, :, 1:-1, :]
    top_row = jnp.einsum("k,kcw->cw", at_top, north_grads, precision=lax.Precision.HIGHEST)
    returned = fold_partner(jnp.flip(top_row, -1).astype(jnp.bfloat16)).astype(jnp.float32)
    upper_add = jnp.einsum("kl,kcw->lcw", below, south_grads, precision=lax.Precision.HIGHEST)
    upper_add = upper_add + at_top[:, None, None] * returned[None]
    lower_add = jnp.einsum("kl,kcw->lcw", above, north_grads, precision=lax.Precision.HIGHEST)
    widened = widened.at[:, :, -1, :].add(upper_add).at[:, :, 0, :].add(lower_add)
    rim_grads = jnp.stack([widened[..., 0], widened[..., -1]]).astype(jnp.bfloat16)
    received = swap_edges(rim_grads)
    interior = widened[..., 1:-1]
    interior = interior.at[..., 0].add(select_rows(west_match, received[0]))
    interior = interior.at[..., -1].add(select_rows(east_match, received[3]))
    return interior


def convolve(operand, kernel):
    return lax.conv_general_dilated(
        operand, kernel, (1, 1), "VALID", preferred_element_type=jnp.float32
    )


def on_device(fields, tile_rows, weights, bias, cotangent):
    own_width = weights.shape[1]
    lookups = make_lookups(tile_rows)
    occupied = (tile_rows[lax.axis_index("tiles")] >= 0)[:, None, None, None]
    inputs = jnp.where(occupied, fields[0].reshape(SLOTS, C, TS, TS), jnp.zeros((), jnp.bfloat16))
    padded = pad_tiles(inputs, lookups)
    kernel = weights.reshape(3, 3, own_width, C).transpose(2, 3, 0, 1)
    pre_act = convolve(padded, kernel) + bias[None, :, None, None]
    channel_start = lax.axis_index("chan") * own_width
    own_inputs = lax.dynamic_slice_in_dim(inputs, channel_start, own_width, 1)
    result = jnp.where(occupied, own_inputs.astype(jnp.float32) + jax.nn.gelu(pre_act), 0.0).astype(
        jnp.bfloat16
    )
    upstream = jnp.where(
        occupied, cotangent[0].reshape(SLOTS, own_width, TS, TS).astype(jnp.float32), 0.0
    )
    pullback = jax.vjp(jax.nn.gelu, pre_act)[1]
    slopes = pullback(upstream)[0].astype(jnp.bfloat16)
    flipped = jnp.flip(weights.reshape(3, 3, own_width, C), (0, 1)).transpose(3, 2, 0, 1)
    wide_slopes = jnp.pad(slopes, ((0, 0), (0, 0), (2, 2), (2, 2)))
    partial_grads = convolve(wide_slopes, flipped).reshape(SLOTS, C, (TS + 2) * (TS + 2))
    spread = lax.psum_scatter(partial_grads, "chan", scatter_dimension=1, tiled=True)
    pad_grads = spread.reshape(SLOTS, own_width, TS + 2, TS + 2)
    back = pad_adjoint(pad_grads, lookups)
    grad_fields = jnp.where(occupied, upstream + back, 0.0).astype(jnp.bfloat16)
    tap_grads = []
    for row_shift in range(3):
        for col_shift in range(3):
            window = padded[:, :, row_shift : row_shift + TS, col_shift : col_shift + TS]
            tap_grads.append(
                jnp.einsum("scjk,sojk->oc", window, slopes, preferred_element_type=jnp.float32)
            )
    local_weights = jnp.stack(tap_grads)
    local_bias = jnp.sum(slopes.astype(jnp.float32), axis=(0, 2, 3))
    total_weights, total_bias = lax.psum((local_weights, local_bias), ("tiles", "rep"))
    grad_scale = 1.0 / math.sqrt(
        lax.axis_size("rep") * fields.shape[0] * lax.axis_size("tiles") * SLOTS * TS * TS
    )
    result_out = result.reshape(1, SLOTS, own_width, TS * TS)
    grad_out = grad_fields.reshape(1, SLOTS, own_width, TS * TS)
    return (result_out, grad_out, total_weights * grad_scale, total_bias * grad_scale)


def solution(mesh):
    in_specs = (
        P(("groups", "rep"), "tiles", None, None),
        P(),
        P(None, "chan", None),
        P("chan"),
        P(("groups", "rep"), "tiles", "chan", None),
    )
    out_specs = (
        P(("groups", "rep"), "tiles", "chan", None),
        P(("groups", "rep"), "tiles", "chan", None),
        P("groups", "chan", None),
        P(("groups", "chan")),
    )
    return jax.shard_map(
        on_device, mesh=mesh, in_specs=in_specs, out_specs=out_specs, check_vma=False
    )
```

profile of v0, /device:TPU:0, one launch (start us, length us, event | category | flops | bytes accessed | tf_op | source)
XLA Modules:
  0.0 142.8 jit_solution(7366810916726707100)
XLA Ops:
  8.0 1.1 copy.181
  9.3 3.1 %collective-permute-start = (bf16[1,3,128,16]{2,1,3,0:T(4,128)(2,1)S(1)}, bf16[1,3,128,16]{2,1,3,0:T(4,128)(2,1)S(1)}, u32[]{:S(2)}, u32[]{:S(2)}) collective-permute-start(bf16[1,3,128,16]{2,1,3,0:T(4,128)(2,1)S(1)} %bitcast.277), channel_id=1, source_target_pairs={{0,4},{4,8},{8,12},{12,0},{1,5},{5,9},{9,13},{13,1},{2,6},{6,10},{... | collective-permute-start | bytes 36872 | tf_op jit(solution)/shard_map/ppermute | solution.py:20
  12.3 2.1 %collective-permute-start.1 = (bf16[1,3,128,16]{2,1,3,0:T(4,128)(2,1)S(1)}, bf16[1,3,128,16]{2,1,3,0:T(4,128)(2,1)S(1)}, u32[]{:S(2)}, u32[]{:S(2)}) collective-permute-start(bf16[1,3,128,16]{2,1,3,0:T(4,128)(2,1)S(1)} %bitcast.276), channel_id=1, source_target_pairs={{4,0},{8,4},{12,8},{0,12},{5,1},{9,5},{13,9},{1,13},{6,2},{10,6},{... | collective-permute-start | bytes 36872 | tf_op jit(solution)/shard_map/ppermute | solution.py:21
  17.1 1.5 %collective-permute-start.2 = (bf16[128,18]{0,1:T(8,128)(2,1)S(1)}, bf16[128,18]{0,1:T(8,128)(2,1)S(1)}, u32[]{:S(2)}, u32[]{:S(2)}) collective-permute-start(bf16[128,18]{0,1:T(8,128)(2,1)S(1)} %bitcast.280), channel_id=1, source_target_pairs={{0,4},{4,0},{8,12},{12,8},{1,5},{5,1},{9,13},{13,9},{2,6},{6,2},{1... | collective-permute-start | bytes 13832 | tf_op jit(solution)/shard_map/ppermute | solution.py:33
  18.9 1.9 %collective-permute-done.2 = bf16[128,18]{0,1:T(8,128)(2,1)S(1)} collective-permute-done((bf16[128,18]{0,1:T(8,128)(2,1)S(1)}, bf16[128,18]{0,1:T(8,128)(2,1)S(1)}, u32[]{:S(2)}, u32[]{:S(2)}) %collective-permute-start.2) | collective-permute-done | bytes 4640 | tf_op jit(solution)/shard_map/ppermute | solution.py:33
  20.8 2.5 %collective-permute-start.3 = (bf16[128,18]{0,1:T(8,128)(2,1)S(1)}, bf16[128,18]{0,1:T(8,128)(2,1)S(1)}, u32[]{:S(2)}, u32[]{:S(2)}) collective-permute-start(bf16[128,18]{0,1:T(8,128)(2,1)S(1)} %collective-permute-done.2), channel_id=1, source_target_pairs={{0,8},{8,0},{4,12},{12,4},{1,9},{9,1},{5,13},{13,5},{2,10},{10,2},... | collective-permute-start | bytes 13832 | tf_op jit(solution)/shard_map/ppermute | solution.py:33
  23.3 0.9 pad_maximum_fusion.1
  24.2 1.2 collective-permute-done.3
  26.8 0.9 add_multiply_fusion
  30.3 0.8 fusion.96
  33.3 1.2 copy.209
  34.6 13.6 %psum.15 = f32[64]{0:T(128)S(1)} all-reduce(f32[64]{0:T(128)S(1)} %get-tuple-element.68), channel_id=1, replica_groups=mesh['groups'=2,'tiles'=4,'chan'=2,'rep'=2] {'tiles','rep'}, use_global_device_ids=true, to_apply=%region_3.4 | all-reduce | flops 64 | bytes 512 | tf_op jit(solution)/shard_map/psum | solution.py:164
  51.3 19.3 %all-reduce.6.cloned.1.call-done = f32[3,128,324]{2,0,1:T(4,128)} async-done(((f32[3,128,324]{2,0,1:T(4,128)}), f32[3,128,324]{2,0,1:T(4,128)}) %all-reduce.6.cloned.1.call-update) | async-done | bytes 497680
  70.6 1.1 constant_dynamic-slice_fusion.3
  72.9 1.6 %collective-permute-start.4 = (bf16[64,18]{0,1:T(8,128)(2,1)S(1)}, bf16[64,18]{0,1:T(8,128)(2,1)S(1)}, u32[]{:S(2)}, u32[]{:S(2)}) collective-permute-start(bf16[64,18]{0,1:T(8,128)(2,1)S(1)} %rev.11), channel_id=1, source_target_pairs={{0,4},{4,0},{8,12},{12,8},{1,5},{5,1},{9,13},{13,9},{2,6},{6,2},{1... | collective-permute-start | bytes 6920 | tf_op jit(solution)/shard_map/ppermute | solution.py:33
  74.7 1.9 %collective-permute-done.4 = bf16[64,18]{0,1:T(8,128)(2,1)S(1)} collective-permute-done((bf16[64,18]{0,1:T(8,128)(2,1)S(1)}, bf16[64,18]{0,1:T(8,128)(2,1)S(1)}, u32[]{:S(2)}, u32[]{:S(2)}) %collective-permute-start.4) | collective-permute-done | bytes 2336 | tf_op jit(solution)/shard_map/ppermute | solution.py:33
  76.6 2.4 %collective-permute-start.5 = (bf16[64,18]{0,1:T(8,128)(2,1)S(1)}, bf16[64,18]{0,1:T(8,128)(2,1)S(1)}, u32[]{:S(2)}, u32[]{:S(2)}) collective-permute-start(bf16[64,18]{0,1:T(8,128)(2,1)S(1)} %collective-permute-done.4), channel_id=1, source_target_pairs={{0,8},{8,0},{4,12},{12,4},{1,9},{9,1},{5,13},{13,5},{2,10},{10,2},... | collective-permute-start | bytes 6920 | tf_op jit(solution)/shard_map/ppermute | solution.py:33
  79.3 1.8 %collective-permute-done.5 = bf16[64,18]{0,1:T(8,128)(2,1)S(1)} collective-permute-done((bf16[64,18]{0,1:T(8,128)(2,1)S(1)}, bf16[64,18]{0,1:T(8,128)(2,1)S(1)}, u32[]{:S(2)}, u32[]{:S(2)}) %collective-permute-start.5) | collective-permute-done | bytes 2336 | tf_op jit(solution)/shard_map/ppermute | solution.py:33
  81.4 1.5 %collective-permute-start.6 = (bf16[1,3,64,16]{2,1,3,0:T(4,128)(2,1)S(1)}, bf16[1,3,64,16]{2,1,3,0:T(4,128)(2,1)S(1)}, u32[]{:S(2)}, u32[]{:S(2)}) collective-permute-start(bf16[1,3,64,16]{2,1,3,0:T(4,128)(2,1)S(1)} %bitcast.278), channel_id=1, source_target_pairs={{0,4},{4,8},{8,12},{12,0},{1,5},{5,9},{9,13},{13,1},{2,6},{6,10},{... | collective-permute-start | bytes 18440 | tf_op jit(solution)/shard_map/ppermute | solution.py:20
  82.9 43.8 %all-reduce.4.cloned.1.call-done = f32[9,64,128]{2,1,0:T(8,128)} async-done(((f32[9,64,128]{2,1,0:T(8,128)}), f32[9,64,128]{2,1,0:T(8,128)}) %all-reduce.4.cloned.1.call-update) | async-done | bytes 294928 | tf_op jit(solution)/shard_map/psum | solution.py:164
  126.7 1.7 %broadcast_multiply_fusion = f32[9,64,128]{2,1,0:T(8,128)} fusion(f32[9,64,128]{2,1,0:T(8,128)} %all-reduce.4.cloned.1.call-done), kind=kLoop, calls=%fused_computation.78 | loop fusion | flops 73728 | bytes 589824 | tf_op jit(solution)/shard_map/mul | solution.py:170
  128.4 3.8 %collective-permute-start.7 = (bf16[1,3,64,16]{2,1,3,0:T(4,128)(2,1)S(1)}, bf16[1,3,64,16]{2,1,3,0:T(4,128)(2,1)S(1)}, u32[]{:S(2)}, u32[]{:S(2)}) collective-permute-start(bf16[1,3,64,16]{2,1,3,0:T(4,128)(2,1)S(1)} %bitcast.279), channel_id=1, source_target_pairs={{4,0},{8,4},{12,8},{0,12},{5,1},{9,5},{13,9},{1,13},{6,2},{10,6},{... | collective-permute-start | bytes 18440 | tf_op jit(solution)/shard_map/ppermute | solution.py:21
  132.4 1.3 collective-permute-done.7
  134.4 0.8 copy.241
  (122 shorter events, 15.7 us)
Async XLA Ops:
  7.2 19.7 %copy-start = (bf16[9,64,128]{2,1,0:T(8,128)(2,1)S(1)}, bf16[9,64,128]{2,1,0:T(8,128)(2,1)}, u32[]{:S(2)}) copy-start(bf16[9,64,128]{2,1,0:T(8,128)(2,1)} %param.15) | copy-start | bytes 442372
  7.2 7.6 %copy-start.8 = (u32[32]{0:T(128)S(1)}, u32[32]{0:T(128)}, u32[]{:S(2)}) copy-start(u32[32]{0:T(128)} %constant.189) | copy-start | bytes 388
  7.2 7.3 %copy-start.6 = (s32[4,3]{1,0:T(4,128)S(1)}, s32[4,3]{1,0:T(4,128)}, u32[]{:S(2)}) copy-start(s32[4,3]{1,0:T(4,128)} %param.14) | copy-start | bytes 148
  7.2 7.4 %copy-start.5 = (bf16[1,3,64,256]{3,2,1,0:T(8,128)(2,1)S(1)}, bf16[1,3,64,256]{3,2,1,0:T(8,128)(2,1)}, u32[]{:S(2)}) copy-start(bf16[1,3,64,256]{3,2,1,0:T(8,128)(2,1)} %param.17) | copy-start | bytes 294916
  7.2 63.4 %all-reduce.6.cloned.1.call-start = ((), (), s32[]{:S(2)}) async-start(), calls=%async_computation.1 | async-start | bytes 1572864
  9.3 6.8 %collective-permute-start = (bf16[1,3,128,16]{2,1,3,0:T(4,128)(2,1)S(1)}, bf16[1,3,128,16]{2,1,3,0:T(4,128)(2,1)S(1)}, u32[]{:S(2)}, u32[]{:S(2)}) collective-permute-start(bf16[1,3,128,16]{2,1,3,0:T(4,128)(2,1)S(1)} %bitcast.277), channel_id=1, source_target_pairs={{0,4},{4,8},{8,12},{12,0},{1,5},{5,9},{9,13},{13,1},{2,6},{6,10},{... | collective-permute-start | bytes 36872 | tf_op jit(solution)/shard_map/ppermute | solution.py:20
  12.3 3.9 %collective-permute-start.1 = (bf16[1,3,128,16]{2,1,3,0:T(4,128)(2,1)S(1)}, bf16[1,3,128,16]{2,1,3,0:T(4,128)(2,1)S(1)}, u32[]{:S(2)}, u32[]{:S(2)}) collective-permute-start(bf16[1,3,128,16]{2,1,3,0:T(4,128)(2,1)S(1)} %bitcast.276), channel_id=1, source_target_pairs={{4,0},{8,4},{12,8},{0,12},{5,1},{9,5},{13,9},{1,13},{6,2},{10,6},{... | collective-permute-start | bytes 36872 | tf_op jit(solution)/shard_map/ppermute | solution.py:21
  17.1 3.7 %collective-permute-start.2 = (bf16[128,18]{0,1:T(8,128)(2,1)S(1)}, bf16[128,18]{0,1:T(8,128)(2,1)S(1)}, u32[]{:S(2)}, u32[]{:S(2)}) collective-permute-start(bf16[128,18]{0,1:T(8,128)(2,1)S(1)} %bitcast.280), channel_id=1, source_target_pairs={{0,4},{4,0},{8,12},{12,8},{1,5},{5,1},{9,13},{13,9},{2,6},{6,2},{1... | collective-permute-start | bytes 13832 | tf_op jit(solution)/shard_map/ppermute | solution.py:33
  20.8 4.5 %collective-permute-start.3 = (bf16[128,18]{0,1:T(8,128)(2,1)S(1)}, bf16[128,18]{0,1:T(8,128)(2,1)S(1)}, u32[]{:S(2)}, u32[]{:S(2)}) collective-permute-start(bf16[128,18]{0,1:T(8,128)(2,1)S(1)} %collective-permute-done.2), channel_id=1, source_target_pairs={{0,8},{8,0},{4,12},{12,4},{1,9},{9,1},{5,13},{13,5},{2,10},{10,2},... | collective-permute-start | bytes 13832 | tf_op jit(solution)/shard_map/ppermute | solution.py:33
  26.2 0.7 copy-start.7
  26.2 0.7 copy-start.10
  31.2 0.7 copy-start.9
  33.3 14.9 %copy-start.4 = (bf16[3,128,16,16]{1,3,2,0:T(8,128)(2,1)S(1)}, bf16[3,128,16,16]{1,3,2,0:T(8,128)(2,1)}, u32[]{:S(2)}) copy-start(bf16[3,128,16,16]{1,3,2,0:T(8,128)(2,1)} %get-tuple-element.90) | copy-start | bytes 589828
  34.6 13.9 %copy-start.3 = (bf16[3,128,16,16]{1,3,2,0:T(8,128)(2,1)S(1)}, bf16[3,128,16,16]{1,3,2,0:T(8,128)(2,1)}, u32[]{:S(2)}) copy-start(bf16[3,128,16,16]{1,3,2,0:T(8,128)(2,1)} %get-tuple-element.80) | copy-start | bytes 589828
  34.6 92.1 %all-reduce.4.cloned.1.call-start = ((), (), s32[]{:S(2)}) async-start(), calls=%async_computation | async-start | bytes 589824 | tf_op jit(solution)/shard_map/psum | solution.py:164
  49.2 0.9 copy-start.2
  50.6 0.7 copy-start.1
  72.9 3.7 %collective-permute-start.4 = (bf16[64,18]{0,1:T(8,128)(2,1)S(1)}, bf16[64,18]{0,1:T(8,128)(2,1)S(1)}, u32[]{:S(2)}, u32[]{:S(2)}) collective-permute-start(bf16[64,18]{0,1:T(8,128)(2,1)S(1)} %rev.11), channel_id=1, source_target_pairs={{0,4},{4,0},{8,12},{12,8},{1,5},{5,1},{9,13},{13,9},{2,6},{6,2},{1... | collective-permute-start | bytes 6920 | tf_op jit(solution)/shard_map/ppermute | solution.py:33
  76.6 4.5 %collective-permute-start.5 = (bf16[64,18]{0,1:T(8,128)(2,1)S(1)}, bf16[64,18]{0,1:T(8,128)(2,1)S(1)}, u32[]{:S(2)}, u32[]{:S(2)}) collective-permute-start(bf16[64,18]{0,1:T(8,128)(2,1)S(1)} %collective-permute-done.4), channel_id=1, source_target_pairs={{0,8},{8,0},{4,12},{12,4},{1,9},{9,1},{5,13},{13,5},{2,10},{10,2},... | collective-permute-start | bytes 6920 | tf_op jit(solution)/shard_map/ppermute | solution.py:33
  81.4 50.9 %collective-permute-start.6 = (bf16[1,3,64,16]{2,1,3,0:T(4,128)(2,1)S(1)}, bf16[1,3,64,16]{2,1,3,0:T(4,128)(2,1)S(1)}, u32[]{:S(2)}, u32[]{:S(2)}) collective-permute-start(bf16[1,3,64,16]{2,1,3,0:T(4,128)(2,1)S(1)} %bitcast.278), channel_id=1, source_target_pairs={{0,4},{4,8},{8,12},{12,0},{1,5},{5,9},{9,13},{13,1},{2,6},{6,10},{... | collective-permute-start | bytes 18440 | tf_op jit(solution)/shard_map/ppermute | solution.py:20
  128.4 5.2 %collective-permute-start.7 = (bf16[1,3,64,16]{2,1,3,0:T(4,128)(2,1)S(1)}, bf16[1,3,64,16]{2,1,3,0:T(4,128)(2,1)S(1)}, u32[]{:S(2)}, u32[]{:S(2)}) collective-permute-start(bf16[1,3,64,16]{2,1,3,0:T(4,128)(2,1)S(1)} %bitcast.279), channel_id=1, source_target_pairs={{4,0},{8,4},{12,8},{0,12},{5,1},{9,5},{13,9},{1,13},{6,2},{10,6},{... | collective-permute-start | bytes 18440 | tf_op jit(solution)/shard_map/ppermute | solution.py:21
Sparse Core Ops, SparseCore 0:
  34.7 35.8 all-reduce.5
  73.7 52.9 all-reduce.3
where the time goes:
time: 143 us
  waiting for transfers between devices  71.3 us (50%)
  starting transfers between devices  18.5 us (13%)
  between operations  15.3 us (11%)
  blocking collectives  13.6 us (10%)
  local copies, waits for them, and re-layouts  11.8 us (8%)
  other arithmetic  6.23 us (4%)
  matrix products  5.93 us (4%)
    psum x1, waiting for transfers between devices, on_device(): lax.psum((local_weights, local_bias), ('tiles', 'rep'))  43.8 us
    unnamed x3, waiting for transfers between devices  19.3 us
    psum x1, blocking collectives, on_device(): lax.psum((local_weights, local_bias), ('tiles', 'rep'))  13.6 us
    ppermute x4, starting transfers between devices, swapped(): return lax.ppermute(block, axis, route)  7.93 us
    ppermute x4, waiting for transfers between devices, swapped(): return lax.ppermute(block, axis, route)  6.85 us
    unnamed x30, local copies, waits for them, and re-layouts  6.53 us
    ppermute x2, starting transfers between devices, extended(): after = lax.ppermute(first, axis, down)  5.9 us
    ppermute x2, starting transfers between devices, extended(): before = lax.ppermute(last, axis, up)  4.62 us
  transfers between devices with their start and end apart: 10, of which 8 were waited for; matrix products, arithmetic and copies ran while one was open for 6% of the time, Pallas kernels for 0%

commit v1 on v0

v1 whole, which is shorter than its diff:
```python
import math

import jax
import jax.numpy as jnp
from jax import lax
from jax.experimental import pallas as pl
from jax.experimental.pallas import tpu as pltpu
from jax.sharding import PartitionSpec as P

C = 128
TS = 16
SLOTS = 3
CELLS = TS * TS
FRAME = 384
EDGE = TS + 2
EAST = SLOTS * EDGE
FOLD = 2 * SLOTS * EDGE
F32 = jnp.float32
BF16 = jnp.bfloat16
GELU_C = math.sqrt(2.0 / math.pi)
GELU_K = 0.044715


def iota(shape, dim):
    return lax.broadcasted_iota(jnp.int32, shape, dim)


def halo_plans(count):
    if count == 4:
        return [
            (lambda d: (d + 1) % 4, ("west", "fold")),
            (lambda d: (d + 3) % 4, ("east", "fold")),
            (lambda d: (d + 2) % 4, ("corner_w", "corner_e")),
            (None, ("corner_w", "corner_e")),
        ]
    return [
        (lambda d: (d + 1) % count, ("west",)),
        (lambda d: (d + count - 1) % count, ("east",)),
        (lambda d: count - 1 - d, ("fold",)),
        (lambda d: (count - d) % count, ("corner_w",)),
        (lambda d: (2 * count - 2 - d) % count, ("corner_e",)),
    ]


def slot_of(rows, column, row):
    found = jnp.int32(-1)
    for k in range(SLOTS):
        found = jnp.where((rows[column, k] == row) & (row >= 0), k, found)
    return found


def halo_sources(rows, count, source, target, roles):
    lane = iota((8, 128), 1)
    top = 2 * SLOTS - 1
    src = jnp.full((8, 128), -1, jnp.int32)
    for role, base, near, here in (
        ("west", 0, TS - 1, (source + 1) % count),
        ("east", EAST, 0, (source + count - 1) % count),
    ):
        if role not in roles:
            continue
        for k in range(SLOTS):
            row = rows[target, k]
            row_here = jnp.where(target == here, row, -8)
            same = slot_of(rows, source, row_here)
            south = jnp.where(slot_of(rows, target, row_here - 1) >= 0, slot_of(rows, source, row_here - 1), -1)
            above = jnp.where(row_here >= 0, row_here + 1, -8)
            north = jnp.where(slot_of(rows, target, above) >= 0, slot_of(rows, source, above), -1)
            p = lane - (base + k * EDGE)
            mid = jnp.where(same >= 0, same * CELLS + near - TS, -CELLS * 8)
            src = jnp.where((p >= 1) & (p <= TS), jnp.maximum(mid + TS * p, -1), src)
            src = jnp.where(p == 0, jnp.where(south >= 0, south * CELLS + CELLS - TS + near, -1), src)
            src = jnp.where(p == TS + 1, jnp.where(north >= 0, north * CELLS + near, -1), src)
    mine = slot_of(rows, source, jnp.int32(top))
    theirs = slot_of(rows, target, jnp.int32(top))
    both = (mine >= 0) & (theirs >= 0)
    if "fold" in roles:
        ok = both & (target == count - 1 - source)
        c = lane - FOLD
        last = jnp.where(ok, mine * CELLS + CELLS - 1, -CELLS * 8)
        src = jnp.where((c >= 0) & (c < TS), jnp.maximum(last - c, -1), src)
    through = both & (slot_of(rows, count - 1 - target, jnp.int32(top)) >= 0)
    for role, base, near, here in (
        ("corner_w", 0, 0, (count - source) % count),
        ("corner_e", EAST, TS - 1, (2 * count - 2 - source) % count),
    ):
        if role not in roles:
            continue
        ok = through & (target == here)
        spot = jnp.where(ok, base + theirs * EDGE + TS + 1, -1)
        src = jnp.where(lane == spot, mine * CELLS + CELLS - TS + near, src)
    return src


def halo_map(rows, count, source, plan):
    route, roles = plan
    target = source if route is None else route(source)
    src = halo_sources(rows, count, source, target, roles)
    hits = iota((SLOTS * CELLS, 128), 0) == src[0:1, :]
    return jnp.where(hits, 1.0, 0.0).astype(BF16)


def dot(lhs, rhs, dims=((1,), (0,))):
    return lax.dot_general(lhs, rhs, (dims, ((), ())), preferred_element_type=F32)


def pack_kernel(rows, fields, weights, bias, cot, *outs, count):
    own = weights.shape[1]
    position = lax.axis_index("tiles")
    cells = jnp.concatenate([fields[0, k] for k in range(SLOTS)], axis=1)
    plans = halo_plans(count)
    for plan, out in zip(plans, outs[: len(plans)]):
        out[...] = dot(cells, halo_map(rows, count, position, plan)).astype(BF16)
    shared = outs[len(plans)]
    for t in range(9):
        shared[t * own : (t + 1) * own, :] = weights[t]
    at = 9 * own
    for k in range(SLOTS):
        for half in range(2):
            shared[at : at + own, :] = cot[0, k, :, half * 128 : half * 128 + 128]
            at += own
    line = jnp.concatenate([bias[...], jnp.zeros((1, 128 - own), F32)], axis=1)
    high = line.astype(BF16).astype(F32)
    middle = (line - high).astype(BF16).astype(F32)
    low = line - high - middle
    shared[at : at + 16, :] = jnp.concatenate([high, middle, low, jnp.zeros((13, 128), F32)], axis=0).astype(BF16)


def main_kernel(rows, fields, weights, bias, cot, *refs, count, n_halos, n_others, half_rows):
    halos = refs[:n_halos]
    others = refs[n_halos : n_halos + n_others]
    result, base, edges, keep, send, turned = refs[n_halos + n_others :]
    own = weights.shape[1]
    position = lax.axis_index("tiles")
    chan = lax.axis_index("chan")
    rep = lax.axis_index("rep")
    top = 2 * SLOTS - 1
    lane = iota((1, FRAME), 1)
    column = lane % TS
    lane128 = iota((1, 128), 1)

    row = [rows[position, k] for k in range(SLOTS)]
    full = [jnp.where(r >= 0, 1.0, 0.0).astype(F32) for r in row]
    at_top = [jnp.where(r == top, 1.0, 0.0).astype(F32) for r in row]
    above = [
        [jnp.where((row[k] >= 0) & (row[l] == row[k] + 1), 1.0, 0.0).astype(F32) for l in range(SLOTS)]
        for k in range(SLOTS)
    ]

    eye = iota((own, 128), 0) == iota((own, 128), 1)

    def column_of(line):
        return jnp.sum(jnp.where(eye, line, 0.0), axis=1, keepdims=True)

    parts = []
    line = jnp.concatenate([bias[...], jnp.zeros((1, 128 - own), F32)], axis=1)
    taps = [weights[t] for t in range(9)]
    cots = [cot[0, k].astype(F32) for k in range(SLOTS)]
    parts.append((taps, cots, column_of(line)))
    for ref in others:
        taps = [ref[t * own : (t + 1) * own, :] for t in range(9)]
        cots = []
        at = 9 * own
        for k in range(SLOTS):
            cots.append(jnp.concatenate([ref[at : at + own, :], ref[at + own : at + 2 * own, :]], axis=1).astype(F32))
            at += 2 * own
        pieces = ref[at : at + 16, :].astype(F32)
        parts.append((taps, cots, column_of(pieces[0:1] + pieces[1:2] + pieces[2:3])))
    kernels = [
        jnp.concatenate([jnp.concatenate(taps[3 * a : 3 * a + 3], axis=1) for a in range(3)], axis=0)
        for taps, _, _ in parts
    ]
    turned[...] = jnp.transpose(jnp.concatenate(kernels, axis=0).astype(F32)).astype(BF16)
    start = pl.multiple_of(chan * own, own)
    back_kernel = jnp.concatenate([turned[pl.ds(b * C + start, own), :] for b in range(3)], axis=0)

    halo = halos[0][...].astype(F32)
    for ref in halos[1:]:
        halo = halo + ref[...].astype(F32)
    p_at = iota((128, FRAME), 0)
    west_at = jnp.where(p_at == 0, FRAME - TS, TS * (p_at - 1))
    frame_lane = iota((128, FRAME), 1)
    spread_west = jnp.where((p_at < EDGE) & (frame_lane == west_at), 1.0, 0.0).astype(BF16)
    spread_east = jnp.where((p_at < EDGE) & (frame_lane == west_at + TS - 1), 1.0, 0.0).astype(BF16)

    tiles = [fields[0, k].astype(F32) * full[k] for k in range(SLOTS)]
    fold = pltpu.roll(halo, 128 - FOLD, 1)
    grads = jnp.zeros((3 * own, 3 * C), F32)
    slope_sum = jnp.zeros((own, CELLS), F32)
    edge_sum = jnp.zeros((own, 128), F32)
    pads = []
    for k in range(SLOTS):
        north = at_top[k] * fold
        south = jnp.zeros((C, 128), F32)
        for l in range(SLOTS):
            if l != k:
                north = north + above[k][l] * tiles[l][:, :128]
                south = south + above[l][k] * tiles[l][:, 128:]
        ends = jnp.where(lane128 < TS, north, jnp.where(lane128 >= 128 - TS, south, 0.0))
        centre = jnp.concatenate([tiles[k], ends], axis=1)
        west = dot(pltpu.roll(halo, (128 - k * EDGE) % 128, 1).astype(BF16), spread_west)
        east = dot(pltpu.roll(halo, (128 - EAST - k * EDGE) % 128, 1).astype(BF16), spread_east)
        left = jnp.where(column == 0, west, pltpu.roll(centre, 1, 1))
        right = jnp.where(column == TS - 1, east, pltpu.roll(centre, FRAME - 1, 1))
        window = jnp.concatenate([left, centre, right], axis=0).astype(BF16)
        frames = []
        for n, (taps, cots, bias_column) in enumerate(parts):
            sums = dot(kernels[n], window)
            pre = (
                pltpu.roll(sums[:own], TS, 1)[:, :CELLS]
                + sums[own : 2 * own, :CELLS]
                + pltpu.roll(sums[2 * own :], FRAME - TS, 1)[:, :CELLS]
                + bias_column
            )
            square = pre * pre
            tanh = jnp.tanh(GELU_C * (pre * (1.0 + GELU_K * square)))
            half = 0.5 * (1.0 + tanh)
            up = cots[k] * full[k]
            slope = half + 0.5 * pre * (1.0 - tanh * tanh) * (GELU_C * (1.0 + 3.0 * GELU_K * square))
            slopes = (up * slope).astype(BF16).astype(F32)
            if n == 0:
                own_in = fields[0, k, pl.ds(start, own), :].astype(F32)
                result[0, k] = (full[k] * (own_in + pre * half)).astype(BF16)
                slope_sum = slope_sum + slopes
            wide = jnp.concatenate([slopes, jnp.zeros((own, FRAME - CELLS), F32)], axis=1)
            frames.append(
                jnp.concatenate([pltpu.roll(wide, FRAME - TS, 1), wide, pltpu.roll(wide, TS, 1)], axis=0).astype(BF16)
            )
        grads = grads + dot(frames[0], window, ((1,), (1,)))
        spread = dot(back_kernel, jnp.concatenate(frames, axis=0))
        first, second, third = spread[:own], spread[own : 2 * own], spread[2 * own :]
        pad = (
            second
            + jnp.where(column < TS - 1, pltpu.roll(first, FRAME - 1, 1), 0.0)
            + jnp.where(column > 0, pltpu.roll(third, 1, 1), 0.0)
        )
        pads.append(pad)
        edge_sum = edge_sum + pltpu.roll(dot(first.astype(BF16), spread_west, ((1,), (1,))), k * EDGE, 1)
        edge_sum = edge_sum + pltpu.roll(dot(third.astype(BF16), spread_east, ((1,), (1,))), EAST + k * EDGE, 1)
        crest = jnp.where(lane128 < TS, pad[:, CELLS:], 0.0) * at_top[k]
        edge_sum = edge_sum + pltpu.roll(crest, FOLD, 1)
    edges[...] = edge_sum.astype(BF16)
    for k in range(SLOTS):
        first = pads[k][:, :128]
        second = pads[k][:, 128:CELLS]
        for l in range(SLOTS):
            if l != k:
                ends = pads[l][:, CELLS:]
                first = first + jnp.where(lane128 < TS, ends, 0.0) * above[l][k]
                second = second + jnp.where(lane128 >= 128 - TS, ends, 0.0) * above[k][l]
        base[k] = parts[0][1][k] * full[k] + jnp.concatenate([first, second], axis=1)
    blocks = [grads[a * own : (a + 1) * own, b * C : (b + 1) * C] for a in range(3) for b in range(3)]
    bias_line = jnp.sum(jnp.where(eye, jnp.sum(slope_sum, axis=1, keepdims=True), 0.0), axis=0, keepdims=True)
    blocks.append(bias_line)
    blocks.append(jnp.zeros((2 * half_rows - 9 * own - 1, 128), F32))
    sums = jnp.concatenate(blocks, axis=0)
    low, high = sums[:half_rows], sums[half_rows:]
    keep[...] = jnp.where(rep == 0, low, high)
    send[...] = jnp.where(rep == 0, high, low)


def finish_kernel(rows, base, *refs, count):
    out = refs[-1]
    position = lax.axis_index("tiles")
    total = None
    for plan, ref in zip(halo_plans(count), refs[:-1]):
        part = dot(ref[...], halo_map(rows, count, position, plan), ((1,), (1,)))
        total = part if total is None else total + part
    for k in range(SLOTS):
        out[0, k] = (base[k] + total[:, k * CELLS : (k + 1) * CELLS]).astype(BF16)


def gather_kernel(mine, theirs, weights_out, bias_out):
    rep = lax.axis_index("rep")
    own = weights_out.shape[1]
    low = jnp.where(rep == 0, mine[...], theirs[...])
    high = jnp.where(rep == 0, theirs[...], mine[...])
    sums = jnp.concatenate([low, high], axis=0)
    for t in range(9):
        weights_out[t] = sums[t * own : (t + 1) * own]
    bias_out[...] = sums[9 * own : 9 * own + 1, :own]


SMEM = pl.BlockSpec(memory_space=pltpu.SMEM)
VMEM = pl.BlockSpec(memory_space=pltpu.VMEM)


def call(kernel, n_in, outs, scratch=(), rows_first=True):
    return pl.pallas_call(
        kernel,
        in_specs=([SMEM] if rows_first else []) + [VMEM] * n_in,
        out_specs=[VMEM] * len(outs),
        out_shape=outs,
        scratch_shapes=list(scratch),
        compiler_params=pltpu.CompilerParams(vmem_limit_bytes=48 << 20),
    )


def struct(shape, dtype):
    return jax.ShapeDtypeStruct(shape, dtype)


def on_device(fields, tile_rows, weights, bias, cotangent):
    own = weights.shape[1]
    count = lax.axis_size("tiles")
    chans = lax.axis_size("chan")
    reps = lax.axis_size("rep")
    plans = halo_plans(count)
    shared_rows = 9 * own + 2 * SLOTS * own + 16
    half_rows = -(-(9 * own + 1) // 32) * 16
    bias_line = bias.reshape(1, own)

    packed = call(
        lambda *refs: pack_kernel(*refs, count=count),
        4,
        [struct((C, 128), BF16)] * len(plans) + [struct((shared_rows, 128), BF16)],
    )(tile_rows, fields, weights, bias_line, cotangent)
    halos = []
    for (route, _), message in zip(plans, packed):
        if route is None:
            halos.append(message)
        else:
            halos.append(lax.ppermute(message, "tiles", [(i, route(i)) for i in range(count)]))
    others = [
        lax.ppermute(packed[-1], "chan", [(i, (i + s) % chans) for i in range(chans)]) for s in range(1, chans)
    ]

    result, base, edges, keep, send = call(
        lambda *refs: main_kernel(
            *refs, count=count, n_halos=len(halos), n_others=len(others), half_rows=half_rows
        ),
        4 + len(halos) + len(others),
        [
            struct((1, SLOTS, own, CELLS), BF16),
            struct((SLOTS, own, CELLS), F32),
            struct((own, 128), BF16),
            struct((half_rows, 128), F32),
            struct((half_rows, 128), F32),
        ],
        [pltpu.VMEM((3 * C, 3 * C), BF16)],
    )(tile_rows, fields, weights, bias_line, cotangent, *halos, *others)

    returned = [
        edges if route is None else lax.ppermute(edges, "tiles", [(route(i), i) for i in range(count)])
        for route, _ in plans
    ]
    grad_fields = call(
        lambda *refs: finish_kernel(*refs, count=count),
        1 + len(returned),
        [struct((1, SLOTS, own, CELLS), BF16)],
    )(tile_rows, base, *returned)[0]

    sums = keep + lax.ppermute(send, "rep", [(0, 1), (1, 0)])
    stride = 1
    while stride < count:
        rounded = sums.astype(BF16)
        other = lax.ppermute(rounded, "tiles", [(i, i ^ stride) for i in range(count)])
        sums = rounded.astype(F32) + other.astype(F32)
        stride *= 2
    grad_scale = 1.0 / math.sqrt(reps * fields.shape[0] * count * SLOTS * CELLS)
    sums = sums * grad_scale
    grad_weights, grad_bias = call(
        gather_kernel,
        2,
        [struct((9, own, C), F32), struct((1, own), F32)],
        rows_first=False,
    )(sums, lax.ppermute(sums, "rep", [(0, 1), (1, 0)]))
    return (result, grad_fields, grad_weights, grad_bias.reshape(own))


def solution(mesh):
    in_specs = (
        P(("groups", "rep"), "tiles", None, None),
        P(),
        P(None, "chan", None),
        P("chan"),
        P(("groups", "rep"), "tiles", "chan", None),
    )
    out_specs = (
        P(("groups", "rep"), "tiles", "chan", None),
        P(("groups", "rep"), "tiles", "chan", None),
        P("groups", "chan", None),
        P(("groups", "chan")),
    )
    return jax.shard_map(
        on_device, mesh=mesh, in_specs=in_specs, out_specs=out_specs, check_vma=False
    )
```

time: 143 us -> 42.7 us (0.30)
  waiting for transfers between devices: 71.3 us -> 17.3 us
  between operations: 15.3 us -> 0.69 us
  blocking collectives: 13.6 us -> 0 us
  local copies, waits for them, and re-layouts: 11.8 us -> 4.06 us
  Pallas kernels: 0 us -> 7.66 us
  other arithmetic: 6.23 us -> 0.07 us
  matrix products: 5.93 us -> 0 us
  starting transfers between devices: 18.5 us -> 12.7 us
    psum x1 -> x0, waiting for transfers between devices: 43.8 us -> none  [on_device(): lax.psum((local_weights, local_bias), ('tiles', 'rep'))]
    unnamed x3 -> x0, waiting for transfers between devices: 19.3 us -> none
    psum x1 -> x0, blocking collectives: 13.6 us -> none  [on_device(): lax.psum((local_weights, local_bias), ('tiles', 'rep'))]
    ppermute x8 -> x11, waiting for transfers between devices: 8.2 us -> 17.3 us  [the longest x2 9.67 us: on_device(): lax.ppermute(rounded, 'tiles', [(i, i ^ stride) for i in range(count)])]
    pallas_call x0 -> x4, Pallas kernels: none -> 7.66 us  [the longest x1 4.14 us: on_device(): call(lambda *refs: main_kernel(*refs, count=count, n_halos=len(halos), n_...]
    ppermute x8 -> x11, starting transfers between devices: 18.4 us -> 12.7 us  [the longest x3 4.61 us: on_device(): lax.ppermute(message, 'tiles', [(i, route(i)) for i in range(count)])]
    dot_general x19 -> x0, matrix products: 4.24 us -> none  [the longest x9 2 us: on_device(): jnp.einsum('scjk,sojk->oc', window, slopes, preferred_element_type=jnp.fl...]
    unnamed x30 -> x10, local copies, waits for them, and re-layouts: 6.53 us -> 4.06 us
  transfers between devices with their start and end apart: 10 -> 11, of which waited for: 8 -> 8; matrix products, arithmetic and copies ran while one was open for 6% -> 0% of each run, Pallas kernels for 0% -> 4%
where the time goes in v1:
time: 42.7 us; the launch traced here: 42.4 us
  waiting for transfers between devices  17.3 us (41%)
  starting transfers between devices  12.7 us (30%)
  Pallas kernels  7.66 us (18%)
  local copies, waits for them, and re-layouts  4.06 us (10%)
  between operations  0.69 us (2%)
    ppermute x2, waiting for transfers between devices, on_device(): lax.ppermute(rounded, 'tiles', [(i, i ^ stride) for i in range(count)])  9.67 us
    ppermute x3, starting transfers between devices, on_device(): lax.ppermute(message, 'tiles', [(i, route(i)) for i in range(count)])  4.61 us
    pallas_call x1, Pallas kernels, on_device(): call(lambda *refs: main_kernel(*refs, count=count, n_halos=len(halos), n_...  4.14 us
    unnamed x10, local copies, waits for them, and re-layouts  4.06 us
    ppermute x3, waiting for transfers between devices, on_device(): lax.ppermute(message, 'tiles', [(i, route(i)) for i in range(count)])  4.02 us
    ppermute x3, starting transfers between devices, on_device(): lax.ppermute(edges, 'tiles', [(route(i), i) for i in range(count)])  4.01 us
    ppermute x1, starting transfers between devices, on_device(): lax.ppermute(packed[-1], 'chan', [(i, (i + s) % chans) for i in range(cha...  3 us
    ppermute x3, waiting for transfers between devices, on_device(): lax.ppermute(edges, 'tiles', [(route(i), i) for i in range(count)])  2.18 us
  transfers between devices with their start and end apart: 11, of which 8 were waited for; matrix products, arithmetic and copies ran while one was open for 0% of the time, Pallas kernels for 4%

profile of v1, /device:TPU:0, one launch (start us, length us, event | category | flops | bytes accessed | tf_op | source)
XLA Modules:
  0.0 42.4 jit_solution(654389730470814817)
XLA Ops:
  0.6 0.6 %copy-done.4 = f32[64]{0:T(128)S(1)} copy-done((f32[64]{0:T(128)S(1)}, f32[64]{0:T(128)}, u32[]{:S(2)}) %copy-start.4) | copy-done | bytes 280
  1.3 0.9 %copy-done = bf16[1,3,128,256]{3,2,1,0:T(8,128)(2,1)S(1)} copy-done((bf16[1,3,128,256]{3,2,1,0:T(8,128)(2,1)S(1)}, bf16[1,3,128,256]{3,2,1,0:T(8,128)(2,1)}, u32[]{:S(2)}) %copy-start) | copy-done | bytes 196632
  2.2 0.9 %copy-done.1 = bf16[9,64,128]{2,1,0:T(8,128)(2,1)S(1)} copy-done((bf16[9,64,128]{2,1,0:T(8,128)(2,1)S(1)}, bf16[9,64,128]{2,1,0:T(8,128)(2,1)}, u32[]{:S(2)}) %copy-start.1) | copy-done | bytes 147480
  3.1 0.9 %copy-done.2 = bf16[1,3,64,256]{3,2,1,0:T(8,128)(2,1)S(1)} copy-done((bf16[1,3,64,256]{3,2,1,0:T(8,128)(2,1)S(1)}, bf16[1,3,64,256]{3,2,1,0:T(8,128)(2,1)}, u32[]{:S(2)}) %copy-start.2) | copy-done | bytes 98328
  4.0 0.7 %copy-done.3 = s32[4,3]{1,0:T(4,128)S(1)} copy-done((s32[4,3]{1,0:T(4,128)S(1)}, s32[4,3]{1,0:T(4,128)}, u32[]{:S(2)}) %copy-start.3) | copy-done | bytes 72
  4.7 1.1 %shard_map.84 = (bf16[128,128]{1,0:T(8,128)(2,1)S(1)}, bf16[128,128]{1,0:T(8,128)(2,1)S(1)}, bf16[128,128]{1,0:T(8,128)(2,1)S(1)}, bf16[128,128]{1,0:T(8,128)(2,1)S(1)}, bf16[976,128]{1,0:T(8,128)(2,1)S(1)}) custom-call(s32[4,3]{1,0:T(4,128)S(1)} %copy-done.3, bf16[1,3,128,256]{3,2,1,0:T(8,128)(2,1)S(1)} %copy-done, bf16[9,64,128]{2,1,0:T(8,128)(2,1)S(1)} %copy-done.1, ...), custom_call_target="tpu_custom_call" | custom-call | tf_op jit(solution)/shard_map/pallas_call | solution.py:313
  5.8 3.0 %collective-permute-start.3 = (bf16[976,128]{1,0:T(8,128)(2,1)S(1)}, bf16[976,128]{1,0:T(8,128)(2,1)S(1)}, u32[]{:S(2)}, u32[]{:S(2)}) collective-permute-start(bf16[976,128]{1,0:T(8,128)(2,1)S(1)} %get-tuple-element.20), channel_id=1, source_target_pairs={{0,2},{2,0},{1,3},{3,1},{4,6},{6,4},{5,7},{7,5},{8,10},{10,8},{9,1... | collective-permute-start | bytes 749576 | tf_op jit(solution)/shard_map/ppermute | solution.py:325
  8.8 1.6 %collective-permute-start = (bf16[128,128]{1,0:T(8,128)(2,1)S(1)}, bf16[128,128]{1,0:T(8,128)(2,1)S(1)}, u32[]{:S(2)}, u32[]{:S(2)}) collective-permute-start(bf16[128,128]{1,0:T(8,128)(2,1)S(1)} %get-tuple-element.16), channel_id=1, source_target_pairs={{0,4},{4,8},{8,12},{12,0},{1,5},{5,9},{9,13},{13,1},{2,6},{6,10},{... | collective-permute-start | bytes 98312 | tf_op jit(solution)/shard_map/ppermute | solution.py:323
  10.3 2.2 %collective-permute-start.1 = (bf16[128,128]{1,0:T(8,128)(2,1)S(1)}, bf16[128,128]{1,0:T(8,128)(2,1)S(1)}, u32[]{:S(2)}, u32[]{:S(2)}) collective-permute-start(bf16[128,128]{1,0:T(8,128)(2,1)S(1)} %get-tuple-element.17), channel_id=1, source_target_pairs={{0,12},{4,0},{8,4},{12,8},{1,13},{5,1},{9,5},{13,9},{2,14},{6,2},{... | collective-permute-start | bytes 98312 | tf_op jit(solution)/shard_map/ppermute | solution.py:323
  12.6 0.8 %collective-permute-start.2 = (bf16[128,128]{1,0:T(8,128)(2,1)S(1)}, bf16[128,128]{1,0:T(8,128)(2,1)S(1)}, u32[]{:S(2)}, u32[]{:S(2)}) collective-permute-start(bf16[128,128]{1,0:T(8,128)(2,1)S(1)} %get-tuple-element.18), channel_id=1, source_target_pairs={{0,8},{4,12},{8,0},{12,4},{1,9},{5,13},{9,1},{13,5},{2,10},{6,14},... | collective-permute-start | bytes 98312 | tf_op jit(solution)/shard_map/ppermute | solution.py:323
  13.4 1.3 %collective-permute-done.refs_5_ = bf16[128,128]{1,0:T(8,128)(2,1)S(1)} collective-permute-done((bf16[128,128]{1,0:T(8,128)(2,1)S(1)}, bf16[128,128]{1,0:T(8,128)(2,1)S(1)}, u32[]{:S(2)}, u32[]{:S(2)}) %collective-permute-start) | collective-permute-done | bytes 32800 | tf_op jit(solution)/shard_map/ppermute | solution.py:323
  14.7 2.7 %collective-permute-done.2.refs_7_ = bf16[128,128]{1,0:T(8,128)(2,1)S(1)} collective-permute-done((bf16[128,128]{1,0:T(8,128)(2,1)S(1)}, bf16[128,128]{1,0:T(8,128)(2,1)S(1)}, u32[]{:S(2)}, u32[]{:S(2)}) %collective-permute-start.2) | collective-permute-done | bytes 32800 | tf_op jit(solution)/shard_map/ppermute | solution.py:323
  17.4 4.1 %shard_map.85 = (bf16[1,3,64,256]{3,2,1,0:T(8,128)(2,1)}, f32[3,64,256]{2,1,0:T(8,128)S(1)}, bf16[64,128]{1,0:T(8,128)(2,1)S(1)}, f32[304,128]{1,0:T(8,128)S(1)}, f32[304,128]{1,0:T(8,128)S(1)}) custom-call(s32[4,3]{1,0:T(4,128)S(1)} %copy-done.3, bf16[1,3,128,256]{3,2,1,0:T(8,128)(2,1)S(1)} %copy-done, bf16[9,64,128]{2,1,0:T(8,128)(2,1)S(1)} %copy-done.1, ...), custom_call_target="tpu_custom_call" | custom-call | tf_op jit(solution)/shard_map/pallas_call | solution.py:328
  21.6 1.4 %collective-permute-done.7 = f32[304,128]{1,0:T(8,128)S(1)} collective-permute-done((f32[304,128]{1,0:T(8,128)S(1)}, f32[304,128]{1,0:T(8,128)S(1)}, u32[]{:S(2)}, u32[]{:S(2)}) %collective-permute-start.7) | collective-permute-done | bytes 155680 | tf_op jit(solution)/shard_map/ppermute | solution.py:353
  23.0 4.4 %collective-permute-done.8 = bf16[304,128]{1,0:T(8,128)(2,1)S(1)} collective-permute-done((bf16[304,128]{1,0:T(8,128)(2,1)S(1)}, bf16[304,128]{1,0:T(8,128)(2,1)S(1)}, u32[]{:S(2)}, u32[]{:S(2)}) %collective-permute-start.8) | collective-permute-done | bytes 77856 | tf_op jit(solution)/shard_map/ppermute | solution.py:357
  27.5 0.9 %collective-permute-start.9 = (bf16[304,128]{1,0:T(8,128)(2,1)S(1)}, bf16[304,128]{1,0:T(8,128)(2,1)S(1)}, u32[]{:S(2)}, u32[]{:S(2)}) collective-permute-start(bf16[304,128]{1,0:T(8,128)(2,1)S(1)} %add_convert_fusion), channel_id=1, source_target_pairs={{0,8},{4,12},{8,0},{12,4},{1,9},{5,13},{9,1},{13,5},{2,10},{6,14},... | collective-permute-start | bytes 233480 | tf_op jit(solution)/shard_map/ppermute | solution.py:357
  28.4 5.3 %collective-permute-done.9 = bf16[304,128]{1,0:T(8,128)(2,1)S(1)} collective-permute-done((bf16[304,128]{1,0:T(8,128)(2,1)S(1)}, bf16[304,128]{1,0:T(8,128)(2,1)S(1)}, u32[]{:S(2)}, u32[]{:S(2)}) %collective-permute-start.9) | collective-permute-done | bytes 77856 | tf_op jit(solution)/shard_map/ppermute | solution.py:357
  34.0 2.3 %collective-permute-start.5 = (bf16[64,128]{1,0:T(8,128)(2,1)S(1)}, bf16[64,128]{1,0:T(8,128)(2,1)S(1)}, u32[]{:S(2)}, u32[]{:S(2)}) collective-permute-start(bf16[64,128]{1,0:T(8,128)(2,1)S(1)} %get-tuple-element.23.refs_5_), channel_id=1, source_target_pairs={{12,0},{0,4},{4,8},{8,12},{13,1},{1,5},{5,9},{9,13},{14,2},{2,6},{... | collective-permute-start | bytes 49160 | tf_op jit(solution)/shard_map/ppermute | solution.py:344
  36.2 1.6 %collective-permute-start.4 = (bf16[64,128]{1,0:T(8,128)(2,1)S(1)}, bf16[64,128]{1,0:T(8,128)(2,1)S(1)}, u32[]{:S(2)}, u32[]{:S(2)}) collective-permute-start(bf16[64,128]{1,0:T(8,128)(2,1)S(1)} %get-tuple-element.23.refs_5_), channel_id=1, source_target_pairs={{4,0},{8,4},{12,8},{0,12},{5,1},{9,5},{13,9},{1,13},{6,2},{10,6},{... | collective-permute-start | bytes 49160 | tf_op jit(solution)/shard_map/ppermute | solution.py:344
  37.8 0.7 %collective-permute-done.6.refs_4_ = bf16[64,128]{1,0:T(8,128)(2,1)S(1)} collective-permute-done((bf16[64,128]{1,0:T(8,128)(2,1)S(1)}, bf16[64,128]{1,0:T(8,128)(2,1)S(1)}, u32[]{:S(2)}, u32[]{:S(2)}) %collective-permute-start.6) | collective-permute-done | bytes 16416 | tf_op jit(solution)/shard_map/ppermute | solution.py:344
  38.5 1.1 %collective-permute-done.5.refs_3_ = bf16[64,128]{1,0:T(8,128)(2,1)S(1)} collective-permute-done((bf16[64,128]{1,0:T(8,128)(2,1)S(1)}, bf16[64,128]{1,0:T(8,128)(2,1)S(1)}, u32[]{:S(2)}, u32[]{:S(2)}) %collective-permute-start.5) | collective-permute-done | bytes 16416 | tf_op jit(solution)/shard_map/ppermute | solution.py:344
  39.6 0.4 collective-permute-done.4.refs_2_
  40.0 1.7 %shard_map.86 = bf16[1,3,64,256]{3,2,1,0:T(8,128)(2,1)} custom-call(s32[4,3]{1,0:T(4,128)S(1)} %copy-done.3, f32[3,64,256]{2,1,0:T(8,128)S(1)} %get-tuple-element.22.refs_1_, bf16[64,128]{1,0:T(8,128)(2,1)S(1)} %collective-permute-done.4.refs_2_, bf16[64,128]{1,0:T(8,128)(2,1)S(1)} %collective-permute-done.5.refs_3_, ...), custom_call_target="tpu_custom_call" | custom-call | tf_op jit(solution)/shard_map/pallas_call | solution.py:347
  41.7 0.7 %shard_map.87 = (f32[9,64,128]{2,1,0:T(8,128)}, f32[1,64]{1,0:T(1,128)}) custom-call(f32[304,128]{1,0:T(8,128)S(1)} %add_multiply_fusion.mine, f32[304,128]{1,0:T(8,128)S(1)} %collective-permute-done.10.theirs), custom_call_target="tpu_custom_call" | custom-call | tf_op jit(solution)/shard_map/pallas_call | solution.py:362
  (15 shorter events, 0.4 us)
Async XLA Ops:
  0.6 0.7 %copy-start.4 = (f32[64]{0:T(128)S(1)}, f32[64]{0:T(128)}, u32[]{:S(2)}) copy-start(f32[64]{0:T(128)} %param.8) | copy-start | bytes 772
  1.3 0.9 %copy-start = (bf16[1,3,128,256]{3,2,1,0:T(8,128)(2,1)S(1)}, bf16[1,3,128,256]{3,2,1,0:T(8,128)(2,1)}, u32[]{:S(2)}) copy-start(bf16[1,3,128,256]{3,2,1,0:T(8,128)(2,1)} %refs_1_.3) | copy-start | bytes 589828
  2.2 0.9 %copy-start.1 = (bf16[9,64,128]{2,1,0:T(8,128)(2,1)S(1)}, bf16[9,64,128]{2,1,0:T(8,128)(2,1)}, u32[]{:S(2)}) copy-start(bf16[9,64,128]{2,1,0:T(8,128)(2,1)} %refs_2_.3) | copy-start | bytes 442372
  3.1 0.9 %copy-start.2 = (bf16[1,3,64,256]{3,2,1,0:T(8,128)(2,1)S(1)}, bf16[1,3,64,256]{3,2,1,0:T(8,128)(2,1)}, u32[]{:S(2)}) copy-start(bf16[1,3,64,256]{3,2,1,0:T(8,128)(2,1)} %refs_4_.3) | copy-start | bytes 294916
  4.0 0.7 %copy-start.3 = (s32[4,3]{1,0:T(4,128)S(1)}, s32[4,3]{1,0:T(4,128)}, u32[]{:S(2)}) copy-start(s32[4,3]{1,0:T(4,128)} %refs_0_.5) | copy-start | bytes 148
  5.8 11.6 %collective-permute-start.3 = (bf16[976,128]{1,0:T(8,128)(2,1)S(1)}, bf16[976,128]{1,0:T(8,128)(2,1)S(1)}, u32[]{:S(2)}, u32[]{:S(2)}) collective-permute-start(bf16[976,128]{1,0:T(8,128)(2,1)S(1)} %get-tuple-element.20), channel_id=1, source_target_pairs={{0,2},{2,0},{1,3},{3,1},{4,6},{6,4},{5,7},{7,5},{8,10},{10,8},{9,1... | collective-permute-start | bytes 749576 | tf_op jit(solution)/shard_map/ppermute | solution.py:325
  8.8 6.0 %collective-permute-start = (bf16[128,128]{1,0:T(8,128)(2,1)S(1)}, bf16[128,128]{1,0:T(8,128)(2,1)S(1)}, u32[]{:S(2)}, u32[]{:S(2)}) collective-permute-start(bf16[128,128]{1,0:T(8,128)(2,1)S(1)} %get-tuple-element.16), channel_id=1, source_target_pairs={{0,4},{4,8},{8,12},{12,0},{1,5},{5,9},{9,13},{13,1},{2,6},{6,10},{... | collective-permute-start | bytes 98312 | tf_op jit(solution)/shard_map/ppermute | solution.py:323
  10.3 4.4 %collective-permute-start.1 = (bf16[128,128]{1,0:T(8,128)(2,1)S(1)}, bf16[128,128]{1,0:T(8,128)(2,1)S(1)}, u32[]{:S(2)}, u32[]{:S(2)}) collective-permute-start(bf16[128,128]{1,0:T(8,128)(2,1)S(1)} %get-tuple-element.17), channel_id=1, source_target_pairs={{0,12},{4,0},{8,4},{12,8},{1,13},{5,1},{9,5},{13,9},{2,14},{6,2},{... | collective-permute-start | bytes 98312 | tf_op jit(solution)/shard_map/ppermute | solution.py:323
  12.6 4.8 %collective-permute-start.2 = (bf16[128,128]{1,0:T(8,128)(2,1)S(1)}, bf16[128,128]{1,0:T(8,128)(2,1)S(1)}, u32[]{:S(2)}, u32[]{:S(2)}) collective-permute-start(bf16[128,128]{1,0:T(8,128)(2,1)S(1)} %get-tuple-element.18), channel_id=1, source_target_pairs={{0,8},{4,12},{8,0},{12,4},{1,9},{5,13},{9,1},{13,5},{2,10},{6,14},... | collective-permute-start | bytes 98312 | tf_op jit(solution)/shard_map/ppermute | solution.py:323
  21.6 1.4 %collective-permute-start.7 = (f32[304,128]{1,0:T(8,128)S(1)}, f32[304,128]{1,0:T(8,128)S(1)}, u32[]{:S(2)}, u32[]{:S(2)}) collective-permute-start(f32[304,128]{1,0:T(8,128)S(1)} %get-tuple-element.25), channel_id=1, source_target_pairs={{0,1},{1,0},{2,3},{3,2},{4,5},{5,4},{6,7},{7,6},{8,9},{9,8},{10,11... | collective-permute-start | bytes 466952 | tf_op jit(solution)/shard_map/ppermute | solution.py:353
  23.0 4.5 %collective-permute-start.8 = (bf16[304,128]{1,0:T(8,128)(2,1)S(1)}, bf16[304,128]{1,0:T(8,128)(2,1)S(1)}, u32[]{:S(2)}, u32[]{:S(2)}) collective-permute-start(bf16[304,128]{1,0:T(8,128)(2,1)S(1)} %add_convert_fusion.1), channel_id=1, source_target_pairs={{0,4},{4,0},{8,12},{12,8},{1,5},{5,1},{9,13},{13,9},{2,6},{6,2},{1... | collective-permute-start | bytes 233480 | tf_op jit(solution)/shard_map/ppermute | solution.py:357
  27.5 6.2 %collective-permute-start.9 = (bf16[304,128]{1,0:T(8,128)(2,1)S(1)}, bf16[304,128]{1,0:T(8,128)(2,1)S(1)}, u32[]{:S(2)}, u32[]{:S(2)}) collective-permute-start(bf16[304,128]{1,0:T(8,128)(2,1)S(1)} %add_convert_fusion), channel_id=1, source_target_pairs={{0,8},{4,12},{8,0},{12,4},{1,9},{5,13},{9,1},{13,5},{2,10},{6,14},... | collective-permute-start | bytes 233480 | tf_op jit(solution)/shard_map/ppermute | solution.py:357
  33.7 8.0 %collective-permute-start.10 = (f32[304,128]{1,0:T(8,128)S(1)}, f32[304,128]{1,0:T(8,128)S(1)}, u32[]{:S(2)}, u32[]{:S(2)}) collective-permute-start(f32[304,128]{1,0:T(8,128)S(1)} %add_multiply_fusion.mine), channel_id=1, source_target_pairs={{0,1},{1,0},{2,3},{3,2},{4,5},{5,4},{6,7},{7,6},{8,9},{9,8},{10,11... | collective-permute-start | bytes 466952 | tf_op jit(solution)/shard_map/ppermute | solution.py:367
  33.8 4.7 %collective-permute-start.6 = (bf16[64,128]{1,0:T(8,128)(2,1)S(1)}, bf16[64,128]{1,0:T(8,128)(2,1)S(1)}, u32[]{:S(2)}, u32[]{:S(2)}) collective-permute-start(bf16[64,128]{1,0:T(8,128)(2,1)S(1)} %get-tuple-element.23.refs_5_), channel_id=1, source_target_pairs={{8,0},{12,4},{0,8},{4,12},{9,1},{13,5},{1,9},{5,13},{10,2},{14,6},... | collective-permute-start | bytes 49160 | tf_op jit(solution)/shard_map/ppermute | solution.py:344
  34.0 5.6 %collective-permute-start.5 = (bf16[64,128]{1,0:T(8,128)(2,1)S(1)}, bf16[64,128]{1,0:T(8,128)(2,1)S(1)}, u32[]{:S(2)}, u32[]{:S(2)}) collective-permute-start(bf16[64,128]{1,0:T(8,128)(2,1)S(1)} %get-tuple-element.23.refs_5_), channel_id=1, source_target_pairs={{12,0},{0,4},{4,8},{8,12},{13,1},{1,5},{5,9},{9,13},{14,2},{2,6},{... | collective-permute-start | bytes 49160 | tf_op jit(solution)/shard_map/ppermute | solution.py:344
  36.2 3.7 %collective-permute-start.4 = (bf16[64,128]{1,0:T(8,128)(2,1)S(1)}, bf16[64,128]{1,0:T(8,128)(2,1)S(1)}, u32[]{:S(2)}, u32[]{:S(2)}) collective-permute-start(bf16[64,128]{1,0:T(8,128)(2,1)S(1)} %get-tuple-element.23.refs_5_), channel_id=1, source_target_pairs={{4,0},{8,4},{12,8},{0,12},{5,1},{9,5},{13,9},{1,13},{6,2},{10,6},{... | collective-permute-start | bytes 49160 | tf_op jit(solution)/shard_map/ppermute | solution.py:344

commit v2 on v1

v2 whole, which is shorter than its diff:
```python
import math

import jax
import jax.numpy as jnp
from jax import lax
from jax.experimental import pallas as pl
from jax.experimental.pallas import tpu as pltpu
from jax.sharding import PartitionSpec as P

C = 128
TS = 16
SLOTS = 3
CELLS = TS * TS
FRAME = 384
EDGE = TS + 2
EAST = SLOTS * EDGE
FOLD = 2 * SLOTS * EDGE
F32 = jnp.float32
BF16 = jnp.bfloat16
GELU_C = math.sqrt(2.0 / math.pi)
GELU_K = 0.044715


def iota(shape, dim):
    return lax.broadcasted_iota(jnp.int32, shape, dim)


def halo_plans(count):
    if count == 4:
        return [
            (lambda d: (d + 1) % 4, ("west", "fold")),
            (lambda d: (d + 3) % 4, ("east", "fold")),
            (lambda d: (d + 2) % 4, ("corner_w", "corner_e")),
            (None, ("corner_w", "corner_e")),
        ]
    return [
        (lambda d: (d + 1) % count, ("west",)),
        (lambda d: (d + count - 1) % count, ("east",)),
        (lambda d: count - 1 - d, ("fold",)),
        (lambda d: (count - d) % count, ("corner_w",)),
        (lambda d: (2 * count - 2 - d) % count, ("corner_e",)),
    ]


def slot_of(rows, column, row):
    found = jnp.int32(-1)
    for k in range(SLOTS):
        found = jnp.where((rows[column, k] == row) & (row >= 0), k, found)
    return found


def halo_sources(rows, count, source, target, roles):
    lane = iota((8, 128), 1)
    top = 2 * SLOTS - 1
    src = jnp.full((8, 128), -1, jnp.int32)
    for role, base, near, here in (
        ("west", 0, TS - 1, (source + 1) % count),
        ("east", EAST, 0, (source + count - 1) % count),
    ):
        if role not in roles:
            continue
        for k in range(SLOTS):
            row = rows[target, k]
            row_here = jnp.where(target == here, row, -8)
            same = slot_of(rows, source, row_here)
            south = jnp.where(slot_of(rows, target, row_here - 1) >= 0, slot_of(rows, source, row_here - 1), -1)
            above = jnp.where(row_here >= 0, row_here + 1, -8)
            north = jnp.where(slot_of(rows, target, above) >= 0, slot_of(rows, source, above), -1)
            p = lane - (base + k * EDGE)
            mid = jnp.where(same >= 0, same * CELLS + near - TS, -CELLS * 8)
            src = jnp.where((p >= 1) & (p <= TS), jnp.maximum(mid + TS * p, -1), src)
            src = jnp.where(p == 0, jnp.where(south >= 0, south * CELLS + CELLS - TS + near, -1), src)
            src = jnp.where(p == TS + 1, jnp.where(north >= 0, north * CELLS + near, -1), src)
    mine = slot_of(rows, source, jnp.int32(top))
    theirs = slot_of(rows, target, jnp.int32(top))
    both = (mine >= 0) & (theirs >= 0)
    if "fold" in roles:
        ok = both & (target == count - 1 - source)
        c = lane - FOLD
        last = jnp.where(ok, mine * CELLS + CELLS - 1, -CELLS * 8)
        src = jnp.where((c >= 0) & (c < TS), jnp.maximum(last - c, -1), src)
    through = both & (slot_of(rows, count - 1 - target, jnp.int32(top)) >= 0)
    for role, base, near, here in (
        ("corner_w", 0, 0, (count - source) % count),
        ("corner_e", EAST, TS - 1, (2 * count - 2 - source) % count),
    ):
        if role not in roles:
            continue
        ok = through & (target == here)
        spot = jnp.where(ok, base + theirs * EDGE + TS + 1, -1)
        src = jnp.where(lane == spot, mine * CELLS + CELLS - TS + near, src)
    return src


def halo_map(rows, count, source, plan):
    route, roles = plan
    target = source if route is None else route(source)
    src = halo_sources(rows, count, source, target, roles)
    hits = iota((SLOTS * CELLS, 128), 0) == src[0:1, :]
    return jnp.where(hits, 1.0, 0.0).astype(BF16)


def dot(lhs, rhs, dims=((1,), (0,))):
    return lax.dot_general(lhs, rhs, (dims, ((), ())), preferred_element_type=F32)


def message_views(ref, own):
    taps = [ref.at[t * own : (t + 1) * own] for t in range(9)]
    base = 9 * own
    halves = [
        [ref.at[base + (2 * k + h) * own : base + (2 * k + h + 1) * own] for h in range(2)] for k in range(SLOTS)
    ]
    at = base + 2 * SLOTS * own
    return taps, halves, ref.at[at : at + 16]


def pack_kernel(rows_hbm, fields_hbm, weights_hbm, bias_hbm, cot_hbm, *refs, count):
    n = len(halo_plans(count))
    rows_out, fields_out, shared = refs[:3]
    outs = refs[3 : 3 + n]
    maps = refs[3 + n : 3 + 2 * n]
    rows, bias, sem = refs[3 + 2 * n :]
    own = weights_hbm.shape[1]
    taps, halves, pieces = message_views(shared, own)
    get_rows = pltpu.make_async_copy(rows_hbm, rows, sem.at[0])
    get_rows.start()
    get_fields = pltpu.make_async_copy(fields_hbm.at[0], fields_out, sem.at[1])
    get_fields.start()
    get_bias = pltpu.make_async_copy(bias_hbm, bias, sem.at[2])
    get_bias.start()
    more = [pltpu.make_async_copy(weights_hbm.at[t], taps[t], sem.at[3 + t]) for t in range(9)]
    for k in range(SLOTS):
        for h in range(2):
            source = cot_hbm.at[0, k, :, h * 128 : h * 128 + 128]
            more.append(pltpu.make_async_copy(source, halves[k][h], sem.at[12 + 2 * k + h]))
    for copy in more:
        copy.start()
    get_rows.wait()
    position = lax.axis_index("tiles")
    plans = halo_plans(count)
    for plan, out in zip(plans, maps):
        out[...] = halo_map(rows, count, position, plan)
    put_rows = pltpu.make_async_copy(rows, rows_out, sem.at[0])
    put_rows.start()
    get_fields.wait()
    cells = jnp.concatenate([fields_out[k] for k in range(SLOTS)], axis=1)
    for out, hits in zip(outs, maps):
        out[...] = dot(cells, hits[...]).astype(BF16)
    get_bias.wait()
    line = jnp.concatenate([bias[...], jnp.zeros((1, 128 - own), F32)], axis=1)
    high = line.astype(BF16).astype(F32)
    middle = (line - high).astype(BF16).astype(F32)
    low = line - high - middle
    pieces[...] = jnp.concatenate([high, middle, low, jnp.zeros((13, 128), F32)], axis=0).astype(BF16)
    for copy in more:
        copy.wait()
    put_rows.wait()


def flag(condition):
    return jnp.where(condition, 1.0, 0.0).astype(F32)


def slot_flags(rows):
    position = lax.axis_index("tiles")
    row = [rows[position, k] for k in range(SLOTS)]
    full = [flag(r >= 0) for r in row]
    at_top = [flag(r == 2 * SLOTS - 1) for r in row]
    above = [[flag((row[k] >= 0) & (row[l] == row[k] + 1)) for l in range(SLOTS)] for k in range(SLOTS)]
    return full, at_top, above


def window_kernel(rows, fields, shared, windows, spreads, kernel):
    own = kernel.shape[0] // 3
    full, _, above = slot_flags(rows)
    column = iota((1, FRAME), 1) % TS
    lane128 = iota((1, 128), 1)
    tiles = [fields[k].astype(F32) * full[k] for k in range(SLOTS)]
    for k in range(SLOTS):
        north = jnp.zeros((C, 128), F32)
        south = jnp.zeros((C, 128), F32)
        for l in range(SLOTS):
            if l != k:
                north = north + above[k][l] * tiles[l][:, :128]
                south = south + above[l][k] * tiles[l][:, 128:]
        ends = jnp.where(lane128 < TS, north, jnp.where(lane128 >= 128 - TS, south, 0.0))
        centre = jnp.concatenate([tiles[k], ends], axis=1)
        windows[k, :C] = jnp.where(column == 0, 0.0, pltpu.roll(centre, 1, 1)).astype(BF16)
        windows[k, C : 2 * C] = centre.astype(BF16)
        windows[k, 2 * C :] = jnp.where(column == TS - 1, 0.0, pltpu.roll(centre, FRAME - 1, 1)).astype(BF16)
    p_at = iota((128, FRAME), 0)
    frame_lane = iota((128, FRAME), 1)
    for side in range(2):
        for k in range(SLOTS):
            p = p_at - (side * EAST + k * EDGE)
            spot = jnp.where(p == 0, FRAME - TS, TS * (p - 1)) + side * (TS - 1)
            hits = (p >= 0) & (p < EDGE) & (frame_lane == spot)
            spreads[side, k] = jnp.where(hits, 1.0, 0.0).astype(BF16)
    taps, _, _ = message_views(shared, own)
    for a in range(3):
        for b in range(3):
            kernel[a * own : (a + 1) * own, b * C : (b + 1) * C] = taps[3 * a + b][...]


def column_of(pieces, own):
    eye = iota((own, 128), 0) == iota((own, 128), 1)
    parts = pieces[...].astype(F32)
    line = parts[0:1] + parts[1:2] + parts[2:3]
    return jnp.sum(jnp.where(eye, line, 0.0), axis=1, keepdims=True)


def activation(kernel, window, bias_column, up):
    own = bias_column.shape[0]
    sums = dot(kernel, window)
    pre = (
        pltpu.roll(sums[:own], TS, 1)[:, :CELLS]
        + sums[own : 2 * own, :CELLS]
        + pltpu.roll(sums[2 * own :], FRAME - TS, 1)[:, :CELLS]
        + bias_column
    )
    square = pre * pre
    tanh = jnp.tanh(GELU_C * (pre * (1.0 + GELU_K * square)))
    half = 0.5 + 0.5 * tanh
    slope = half + (0.5 * pre) * (1.0 - tanh * tanh) * (GELU_C + (3.0 * GELU_C * GELU_K) * square)
    return pre * half, (up * slope).astype(BF16).astype(F32)


def frame_of(slopes):
    own = slopes.shape[0]
    wide = jnp.concatenate([slopes, jnp.zeros((own, FRAME - CELLS), F32)], axis=1)
    return jnp.concatenate([pltpu.roll(wide, FRAME - TS, 1), wide, pltpu.roll(wide, TS, 1)], axis=0).astype(BF16)


def upstream_of(halves, k, full):
    return jnp.concatenate([halves[k][0][...], halves[k][1][...]], axis=1).astype(F32) * full[k]


def forward_kernel(rows, fields, shared, kernel, spreads, windows, *refs, n_halos, half_rows):
    halos = refs[:n_halos]
    full_windows, frames, result, keep, send = refs[n_halos:]
    own = kernel.shape[0] // 3
    full, at_top, _ = slot_flags(rows)
    start = pl.multiple_of(lax.axis_index("chan") * own, own)
    rep = lax.axis_index("rep")
    lane128 = iota((1, 128), 1)
    _, halves, pieces = message_views(shared, own)
    bias_column = column_of(pieces, own)
    halo = halos[0][...].astype(F32)
    for ref in halos[1:]:
        halo = halo + ref[...].astype(F32)
    turned = pltpu.roll(halo, 128 - FOLD, 1)
    fold = jnp.where(lane128 < TS, turned, 0.0)
    fold_left = jnp.where((lane128 > 0) & (lane128 < TS), pltpu.roll(turned, 1, 1), 0.0)
    fold_right = jnp.where(lane128 < TS - 1, pltpu.roll(turned, 127, 1), 0.0)
    halo = halo.astype(BF16)
    grads = jnp.zeros((3 * own, 3 * C), F32)
    slope_sum = jnp.zeros((own, CELLS), F32)
    for k in range(SLOTS):
        west = dot(halo, spreads[0, k])
        east = dot(halo, spreads[1, k])
        rest = jnp.zeros((C, CELLS), F32)
        left = windows[k, :C] + (west + jnp.concatenate([rest, at_top[k] * fold_left], axis=1)).astype(BF16)
        right = windows[k, 2 * C :] + (east + jnp.concatenate([rest, at_top[k] * fold_right], axis=1)).astype(BF16)
        centre = windows[k, C : 2 * C] + jnp.concatenate([rest, at_top[k] * fold], axis=1).astype(BF16)
        window = jnp.concatenate([left, centre, right], axis=0)
        full_windows[k] = window
        up = upstream_of(halves, k, full)
        gelu, slopes = activation(kernel[...], window, bias_column, up)
        result[k] = (full[k] * (fields[k, pl.ds(start, own), :].astype(F32) + gelu)).astype(BF16)
        slope_sum = slope_sum + slopes
        frame = frame_of(slopes)
        frames[k] = frame
        grads = grads + dot(frame, window, ((1,), (1,)))
    blocks = [grads[a * own : (a + 1) * own, b * C : (b + 1) * C] for a in range(3) for b in range(3)]
    eye = iota((own, 128), 0) == iota((own, 128), 1)
    bias_line = jnp.sum(jnp.where(eye, jnp.sum(slope_sum, axis=1, keepdims=True), 0.0), axis=0, keepdims=True)
    blocks.append(bias_line)
    blocks.append(jnp.zeros((2 * half_rows - 9 * own - 1, 128), F32))
    sums = jnp.concatenate(blocks, axis=0)
    low, high = sums[:half_rows], sums[half_rows:]
    keep[...] = jnp.where(rep == 0, low, high)
    send[...] = jnp.where(rep == 0, high, low)


def backward_kernel(rows, shared, kernel, spreads, windows, frames, result, *refs, n_others):
    others = refs[:n_others]
    base, edges, result_out, turned, sem = refs[n_others:]
    own = kernel.shape[0] // 3
    put = pltpu.make_async_copy(result, result_out.at[0], sem)
    put.start()
    full, at_top, above = slot_flags(rows)
    start = pl.multiple_of(lax.axis_index("chan") * own, own)
    column = iota((1, FRAME), 1) % TS
    lane128 = iota((1, 128), 1)
    kernels = [kernel[...]]
    columns, ups = [], []
    for ref in others:
        taps, halves, pieces = message_views(ref, own)
        kernels.append(
            jnp.concatenate(
                [jnp.concatenate([taps[3 * a + b][...] for b in range(3)], axis=1) for a in range(3)], axis=0
            )
        )
        columns.append(column_of(pieces, own))
        ups.append(halves)
    turned[...] = jnp.transpose(jnp.concatenate(kernels, axis=0).astype(F32)).astype(BF16)
    back_kernel = jnp.concatenate([turned[pl.ds(b * C + start, own), :] for b in range(3)], axis=0)
    edge_sum = jnp.zeros((own, 128), F32)
    pads = []
    for k in range(SLOTS):
        stack = [frames[k]]
        for other_kernel, bias_column, halves in zip(kernels[1:], columns, ups):
            _, slopes = activation(other_kernel, windows[k], bias_column, upstream_of(halves, k, full))
            stack.append(frame_of(slopes))
        spread = dot(back_kernel, jnp.concatenate(stack, axis=0))
        first, second, third = spread[:own], spread[own : 2 * own], spread[2 * own :]
        pad = (
            second
            + jnp.where(column < TS - 1, pltpu.roll(first, FRAME - 1, 1), 0.0)
            + jnp.where(column > 0, pltpu.roll(third, 1, 1), 0.0)
        )
        pads.append(pad)
        edge_sum = edge_sum + dot(first.astype(BF16), spreads[0, k], ((1,), (1,)))
        edge_sum = edge_sum + dot(third.astype(BF16), spreads[1, k], ((1,), (1,)))
        crest = jnp.where(lane128 < TS, pad[:, CELLS:], 0.0) * at_top[k]
        edge_sum = edge_sum + pltpu.roll(crest, FOLD, 1)
    edges[...] = edge_sum.astype(BF16)
    _, halves, _ = message_views(shared, own)
    for k in range(SLOTS):
        first = pads[k][:, :128]
        second = pads[k][:, 128:CELLS]
        for l in range(SLOTS):
            if l != k:
                ends = pads[l][:, CELLS:]
                first = first + jnp.where(lane128 < TS, ends, 0.0) * above[l][k]
                second = second + jnp.where(lane128 >= 128 - TS, ends, 0.0) * above[k][l]
        base[k] = upstream_of(halves, k, full) + jnp.concatenate([first, second], axis=1)
    put.wait()


def finish_kernel(base, *refs):
    out = refs[-1]
    n = len(refs) // 2
    total = None
    for received, hits in zip(refs[:n], refs[n:]):
        part = dot(received[...], hits[...], ((1,), (1,)))
        total = part if total is None else total + part
    for k in range(SLOTS):
        out[0, k] = (base[k] + total[:, k * CELLS : (k + 1) * CELLS]).astype(BF16)


def gather_kernel(mine, theirs, weights_out, bias_out):
    rep = lax.axis_index("rep")
    own = weights_out.shape[1]
    low = jnp.where(rep == 0, mine[...], theirs[...])
    high = jnp.where(rep == 0, theirs[...], mine[...])
    sums = jnp.concatenate([low, high], axis=0)
    for t in range(9):
        weights_out[t] = sums[t * own : (t + 1) * own]
    bias_out[...] = sums[9 * own : 9 * own + 1, :own]


SMEM = pl.BlockSpec(memory_space=pltpu.SMEM)
VMEM = pl.BlockSpec(memory_space=pltpu.VMEM)
HBM = pl.BlockSpec(memory_space=pltpu.HBM)


def call(kernel, specs, outs, scratch=(), out_specs=None, cost=None):
    return pl.pallas_call(
        kernel,
        in_specs=specs,
        out_specs=out_specs or [VMEM] * len(outs),
        out_shape=outs,
        scratch_shapes=list(scratch),
        cost_estimate=cost,
        compiler_params=pltpu.CompilerParams(vmem_limit_bytes=40 << 20),
    )


def struct(shape, dtype):
    return jax.ShapeDtypeStruct(shape, dtype)


def on_device(fields, tile_rows, weights, bias, cotangent):
    own = weights.shape[1]
    count = lax.axis_size("tiles")
    chans = lax.axis_size("chan")
    reps = lax.axis_size("rep")
    plans = halo_plans(count)
    n = len(plans)
    shared_rows = 9 * own + 2 * SLOTS * own + 16
    half_rows = -(-(9 * own + 1) // 32) * 16
    swap = [(0, 1), (1, 0)]

    rows, tiles, shared, *packed = call(
        lambda *refs: pack_kernel(*refs, count=count),
        [HBM] * 5,
        [struct(tile_rows.shape, jnp.int32), struct((SLOTS, C, CELLS), BF16), struct((shared_rows, 128), BF16)]
        + [struct((C, 128), BF16)] * n
        + [struct((SLOTS * CELLS, 128), BF16)] * n,
        [
            pltpu.SMEM(tile_rows.shape, jnp.int32),
            pltpu.VMEM((1, own), F32),
            pltpu.SemaphoreType.DMA((12 + 2 * SLOTS,)),
        ],
    )(*(pltpu.with_memory_space_constraint(x, pltpu.HBM) for x in (tile_rows, fields, weights, bias.reshape(1, own), cotangent)))
    messages, maps = packed[:n], packed[n:]
    halos = []
    for (route, _), message in zip(plans, messages):
        if route is None:
            halos.append(message)
        else:
            halos.append(lax.ppermute(message, "tiles", [(i, route(i)) for i in range(count)]))
    others = [lax.ppermute(shared, "chan", [(i, (i + s) % chans) for i in range(chans)]) for s in range(1, chans)]

    windows, spreads, kernel = call(
        window_kernel,
        [SMEM, VMEM, VMEM],
        [
            struct((SLOTS, 3 * C, FRAME), BF16),
            struct((2, SLOTS, 128, FRAME), BF16),
            struct((3 * own, 3 * C), BF16),
        ],
    )(rows, tiles, shared)

    windows, frames, result, keep, send = call(
        lambda *refs: forward_kernel(*refs, n_halos=n, half_rows=half_rows),
        [SMEM] + [VMEM] * (5 + n),
        [
            struct((SLOTS, 3 * C, FRAME), BF16),
            struct((SLOTS, 3 * own, FRAME), BF16),
            struct((SLOTS, own, CELLS), BF16),
            struct((half_rows, 128), F32),
            struct((half_rows, 128), F32),
        ],
    )(rows, tiles, shared, kernel, spreads, windows, *halos)

    send, others = lax.optimization_barrier((send, others))
    sums = keep + lax.ppermute(send, "rep", swap)
    rounded = sums.astype(BF16)
    frames, rounded = lax.optimization_barrier((frames, rounded))

    base, edges, result = call(
        lambda *refs: backward_kernel(*refs, n_others=len(others)),
        [SMEM] + [VMEM] * (6 + len(others)),
        [
            struct((SLOTS, own, CELLS), F32),
            struct((own, 128), BF16),
            struct((1, SLOTS, own, CELLS), BF16),
        ],
        [pltpu.VMEM((3 * C, 3 * own * chans), BF16), pltpu.SemaphoreType.DMA],
        out_specs=[VMEM, VMEM, HBM],
    )(rows, shared, kernel, spreads, windows, frames, result, *others)

    stride = 1
    while stride < count:
        other = lax.ppermute(rounded, "tiles", [(i, i ^ stride) for i in range(count)])
        sums = rounded.astype(F32) + other.astype(F32)
        rounded = sums.astype(BF16)
        if stride == 1:
            rounded, edges = lax.optimization_barrier((rounded, edges))
        stride *= 2
    grad_scale = 1.0 / math.sqrt(reps * fields.shape[0] * count * SLOTS * CELLS)
    sums = sums * grad_scale
    returned = [
        edges if route is None else lax.ppermute(edges, "tiles", [(route(i), i) for i in range(count)])
        for route, _ in plans
    ]
    sums, returned = lax.optimization_barrier((sums, returned))
    grad_fields = call(
        finish_kernel,
        [VMEM] * (1 + 2 * n),
        [struct((1, SLOTS, own, CELLS), BF16)],
    )(base, *returned, *maps)[0]
    grad_weights, grad_bias = call(
        gather_kernel,
        [VMEM, VMEM],
        [struct((9, own, C), F32), struct((1, own), F32)],
    )(sums, lax.ppermute(sums, "rep", swap))
    return (result, grad_fields, grad_weights, grad_bias.reshape(own))


def solution(mesh):
    in_specs = (
        P(("groups", "rep"), "tiles", None, None),
        P(),
        P(None, "chan", None),
        P("chan"),
        P(("groups", "rep"), "tiles", "chan", None),
    )
    out_specs = (
        P(("groups", "rep"), "tiles", "chan", None),
        P(("groups", "rep"), "tiles", "chan", None),
        P("groups", "chan", None),
        P(("groups", "chan")),
    )
    return jax.shard_map(
        on_device, mesh=mesh, in_specs=in_specs, out_specs=out_specs, check_vma=False
    )
```

time: 42.7 us -> 33.7 us (0.79)
  waiting for transfers between devices: 17.3 us -> 9.7 us
  local copies, waits for them, and re-layouts: 4.06 us -> 0 us
  Pallas kernels: 7.66 us -> 10.2 us
    ppermute x2, waiting for transfers between devices: 9.67 us -> 2.64 us  [on_device(): lax.ppermute(rounded, 'tiles', [(i, i ^ stride) for i in range(count)])]
    unnamed x10 -> x0, local copies, waits for them, and re-layouts: 4.06 us -> none
    pallas_call x4 -> x6, Pallas kernels: 7.66 us -> 10.2 us  [the longest x1 3.31 us: on_device(): call(lambda *refs: backward_kernel(*refs, n_others=len(others)), [SMEM] +...]
    ppermute x3, waiting for transfers between devices: 4.02 us -> 3.04 us  [on_device(): lax.ppermute(message, 'tiles', [(i, route(i)) for i in range(count)])]
    ppermute x2, starting transfers between devices: 1 us -> 1.66 us  [on_device(): lax.ppermute(rounded, 'tiles', [(i, i ^ stride) for i in range(count)])]
    ppermute x3, starting transfers between devices: 4.01 us -> 3.43 us  [on_device(): lax.ppermute(edges, 'tiles', [(route(i), i) for i in range(count)])]
  transfers between devices with their start and end apart: 11 -> 11, of which waited for: 8 -> 7; matrix products, arithmetic and copies ran while one was open for 0% -> 0% of each run, Pallas kernels for 4% -> 23%
where the time goes in v2:
time: 33.7 us; the launch traced here: 33.5 us
  starting transfers between devices  12.8 us (38%)
  Pallas kernels  10.2 us (30%)
  waiting for transfers between devices  9.7 us (29%)
  between operations  0.71 us (2%)
    ppermute x3, starting transfers between devices, on_device(): lax.ppermute(message, 'tiles', [(i, route(i)) for i in range(count)])  4.61 us
    ppermute x3, starting transfers between devices, on_device(): lax.ppermute(edges, 'tiles', [(route(i), i) for i in range(count)])  3.43 us
    pallas_call x1, Pallas kernels, on_device(): call(lambda *refs: backward_kernel(*refs, n_others=len(others)), [SMEM] +...  3.31 us
    ppermute x3, waiting for transfers between devices, on_device(): lax.ppermute(message, 'tiles', [(i, route(i)) for i in range(count)])  3.04 us
    ppermute x1, starting transfers between devices, on_device(): lax.ppermute(shared, 'chan', [(i, (i + s) % chans) for i in range(chans)])  3 us
    ppermute x2, waiting for transfers between devices, on_device(): lax.ppermute(rounded, 'tiles', [(i, i ^ stride) for i in range(count)])  2.64 us
    pallas_call x1, Pallas kernels, on_device(): call(lambda *refs: forward_kernel(*refs, n_halos=n, half_rows=half_rows),...  2.53 us
    ppermute x3, waiting for transfers between devices, on_device(): lax.ppermute(edges, 'tiles', [(route(i), i) for i in range(count)])  2.3 us
  transfers between devices with their start and end apart: 11, of which 7 were waited for; matrix products, arithmetic and copies ran while one was open for 0% of the time, Pallas kernels for 23%

profile of v2, /device:TPU:0, one launch (start us, length us, event | category | flops | bytes accessed | tf_op | source)
XLA Modules:
  0.0 33.5 jit_solution(7570193271122842061)
XLA Ops:
  0.6 1.7 %shard_map.84 = (s32[4,3]{1,0:T(4,128)S(1)}, bf16[3,128,256]{2,1,0:T(8,128)(2,1)S(1)}, bf16[976,128]{1,0:T(8,128)(2,1)S(1)}, bf16[128,128]{1,0:T(8,128)(2,1)S(1)...) custom-call(s32[4,3]{1,0:T(4,128)} %refs_0_.1, ...), custom_call_target="tpu_custom_call" | custom-call | tf_op jit(solution)/shard_map/pallas_call | solution.py:395
  2.3 3.0 %collective-permute-start.3 = (bf16[976,128]{1,0:T(8,128)(2,1)S(1)}, bf16[976,128]{1,0:T(8,128)(2,1)S(1)}, u32[]{:S(2)}, u32[]{:S(2)}) collective-permute-start(bf16[976,128]{1,0:T(8,128)(2,1)S(1)} %get-tuple-element.40.shared.refs_2_.refs_1_), channel_id=1, source_target_pairs={{0,2},{2,0},{1,3},{3,1},{4,6},{6,4},{5,7},{7,5},{8,10},{10,8},{9,1... | collective-permute-start | bytes 749576 | tf_op jit(solution)/shard_map/ppermute | solution.py:414
  5.3 1.6 %collective-permute-start = (bf16[128,128]{1,0:T(8,128)(2,1)S(1)}, bf16[128,128]{1,0:T(8,128)(2,1)S(1)}, u32[]{:S(2)}, u32[]{:S(2)}) collective-permute-start(bf16[128,128]{1,0:T(8,128)(2,1)S(1)} %get-tuple-element.45), channel_id=1, source_target_pairs={{0,4},{4,8},{8,12},{12,0},{1,5},{5,9},{9,13},{13,1},{2,6},{6,10},{... | collective-permute-start | bytes 98312 | tf_op jit(solution)/shard_map/ppermute | solution.py:413
  6.9 2.2 %collective-permute-start.1 = (bf16[128,128]{1,0:T(8,128)(2,1)S(1)}, bf16[128,128]{1,0:T(8,128)(2,1)S(1)}, u32[]{:S(2)}, u32[]{:S(2)}) collective-permute-start(bf16[128,128]{1,0:T(8,128)(2,1)S(1)} %get-tuple-element.46), channel_id=1, source_target_pairs={{0,12},{4,0},{8,4},{12,8},{1,13},{5,1},{9,5},{13,9},{2,14},{6,2},{... | collective-permute-start | bytes 98312 | tf_op jit(solution)/shard_map/ppermute | solution.py:413
  9.1 0.8 %collective-permute-start.2 = (bf16[128,128]{1,0:T(8,128)(2,1)S(1)}, bf16[128,128]{1,0:T(8,128)(2,1)S(1)}, u32[]{:S(2)}, u32[]{:S(2)}) collective-permute-start(bf16[128,128]{1,0:T(8,128)(2,1)S(1)} %get-tuple-element.47), channel_id=1, source_target_pairs={{0,8},{4,12},{8,0},{12,4},{1,9},{5,13},{9,1},{13,5},{2,10},{6,14},... | collective-permute-start | bytes 98312 | tf_op jit(solution)/shard_map/ppermute | solution.py:413
  9.9 1.0 %shard_map.85 = (bf16[3,384,384]{2,1,0:T(8,128)(2,1)S(1)}, bf16[2,3,128,384]{3,2,1,0:T(8,128)(2,1)S(1)}, bf16[192,384]{1,0:T(8,128)(2,1)S(1)}) custom-call(s32[4,3]{1,0:T(4,128)S(1)} %get-tuple-element.39.rows.refs_0_, bf16[3,128,256]{2,1,0:T(8,128)(2,1)S(1)} %get-tuple-element.41.fields.refs_1_, bf16[976,128]{1,0:T(8,128)(2,1)S(1)} %get-tuple-element.40.shared.refs_2_.refs_1_), custom_call_target="tpu_custom_call" | custom-call | tf_op jit(solution)/shard_map/pallas_call | solution.py:416
  10.9 0.4 %collective-permute-done.refs_6_ = bf16[128,128]{1,0:T(8,128)(2,1)S(1)} collective-permute-done((bf16[128,128]{1,0:T(8,128)(2,1)S(1)}, bf16[128,128]{1,0:T(8,128)(2,1)S(1)}, u32[]{:S(2)}, u32[]{:S(2)}) %collective-permute-start) | collective-permute-done | bytes 32800 | tf_op jit(solution)/shard_map/ppermute | solution.py:413
  11.2 0.0 collective-permute-done.1.refs_7_
  11.3 2.7 %collective-permute-done.2.refs_8_ = bf16[128,128]{1,0:T(8,128)(2,1)S(1)} collective-permute-done((bf16[128,128]{1,0:T(8,128)(2,1)S(1)}, bf16[128,128]{1,0:T(8,128)(2,1)S(1)}, u32[]{:S(2)}, u32[]{:S(2)}) %collective-permute-start.2) | collective-permute-done | bytes 32800 | tf_op jit(solution)/shard_map/ppermute | solution.py:413
  13.9 2.5 %shard_map.86 = (bf16[3,384,384]{2,1,0:T(8,128)(2,1)S(1)}, bf16[3,192,384]{2,1,0:T(8,128)(2,1)S(1)}, bf16[3,64,256]{2,1,0:T(8,128)(2,1)S(1)}, f32[304,128]{1,0:T(8,128)S(1)}, f32[304,128]{1,0:T(8,128)S(1)}) custom-call(s32[4,3]{1,0:T(4,128)S(1)} %get-tuple-element.39.rows.refs_0_, bf16[3,128,256]{2,1,0:T(8,128)(2,1)S(1)} %get-tuple-element.41.fields.refs_1_, ...), custom_call_target="tpu_custom_call" | custom-call | tf_op jit(solution)/shard_map/pallas_call | solution.py:426
  16.5 0.1 collective-permute-start.4
  16.6 1.4 %collective-permute-done.4 = f32[304,128]{1,0:T(8,128)S(1)} collective-permute-done((f32[304,128]{1,0:T(8,128)S(1)}, f32[304,128]{1,0:T(8,128)S(1)}, u32[]{:S(2)}, u32[]{:S(2)}) %collective-permute-start.4) | collective-permute-done | bytes 155680 | tf_op jit(solution)/shard_map/ppermute | solution.py:439
  17.9 0.1 collective-permute-start.5
  18.0 3.3 %shard_map.87 = (f32[3,64,256]{2,1,0:T(8,128)S(1)}, bf16[64,128]{1,0:T(8,128)(2,1)S(1)}, bf16[1,3,64,256]{3,2,1,0:T(8,128)(2,1)}) custom-call(s32[4,3]{1,0:T(4,128)S(1)} %get-tuple-element.39.rows.refs_0_, bf16[976,128]{1,0:T(8,128)(2,1)S(1)} %get-tuple-element.40.shared.refs_2_.refs_1_, bf16[192,384]{1,0:T(8,128)(2,1)S(1)} %get-tuple-element.42.refs_3_.refs_2_, ...), custom_call_target="tpu_custom_call" | custom-call | tf_op jit(solution)/shard_map/pallas_call | solution.py:443
  21.3 1.1 %collective-permute-done.5 = bf16[304,128]{1,0:T(8,128)(2,1)S(1)} collective-permute-done((bf16[304,128]{1,0:T(8,128)(2,1)S(1)}, bf16[304,128]{1,0:T(8,128)(2,1)S(1)}, u32[]{:S(2)}, u32[]{:S(2)}) %collective-permute-start.5) | collective-permute-done | bytes 77856 | tf_op jit(solution)/shard_map/ppermute | solution.py:457
  22.4 1.6 %collective-permute-start.6 = (bf16[304,128]{1,0:T(8,128)(2,1)S(1)}, bf16[304,128]{1,0:T(8,128)(2,1)S(1)}, u32[]{:S(2)}, u32[]{:S(2)}) collective-permute-start(bf16[304,128]{1,0:T(8,128)(2,1)S(1)} %add_convert_fusion), channel_id=1, source_target_pairs={{0,8},{4,12},{8,0},{12,4},{1,9},{5,13},{9,1},{13,5},{2,10},{6,14},... | collective-permute-start | bytes 233480 | tf_op jit(solution)/shard_map/ppermute | solution.py:457
  24.0 1.8 %collective-permute-start.7 = (bf16[64,128]{1,0:T(8,128)(2,1)S(1)}, bf16[64,128]{1,0:T(8,128)(2,1)S(1)}, u32[]{:S(2)}, u32[]{:S(2)}) collective-permute-start(bf16[64,128]{1,0:T(8,128)(2,1)S(1)} %get-tuple-element.66.refs_3_), channel_id=1, source_target_pairs={{4,0},{8,4},{12,8},{0,12},{5,1},{9,5},{13,9},{1,13},{6,2},{10,6},{... | collective-permute-start | bytes 49160 | tf_op jit(solution)/shard_map/ppermute | solution.py:466
  25.8 0.2 collective-permute-start.8
  26.1 1.4 %collective-permute-start.9 = (bf16[64,128]{1,0:T(8,128)(2,1)S(1)}, bf16[64,128]{1,0:T(8,128)(2,1)S(1)}, u32[]{:S(2)}, u32[]{:S(2)}) collective-permute-start(bf16[64,128]{1,0:T(8,128)(2,1)S(1)} %get-tuple-element.66.refs_3_), channel_id=1, source_target_pairs={{8,0},{12,4},{0,8},{4,12},{9,1},{13,5},{1,9},{5,13},{10,2},{14,6},... | collective-permute-start | bytes 49160 | tf_op jit(solution)/shard_map/ppermute | solution.py:466
  27.5 1.6 %collective-permute-done.6 = bf16[304,128]{1,0:T(8,128)(2,1)S(1)} collective-permute-done((bf16[304,128]{1,0:T(8,128)(2,1)S(1)}, bf16[304,128]{1,0:T(8,128)(2,1)S(1)}, u32[]{:S(2)}, u32[]{:S(2)}) %collective-permute-start.6) | collective-permute-done | bytes 77856 | tf_op jit(solution)/shard_map/ppermute | solution.py:457
  29.1 2.3 %collective-permute-done.8.refs_1_ = bf16[64,128]{1,0:T(8,128)(2,1)S(1)} collective-permute-done((bf16[64,128]{1,0:T(8,128)(2,1)S(1)}, bf16[64,128]{1,0:T(8,128)(2,1)S(1)}, u32[]{:S(2)}, u32[]{:S(2)}) %collective-permute-start.8) | collective-permute-done | bytes 16416 | tf_op jit(solution)/shard_map/ppermute | solution.py:466
  31.4 1.0 %shard_map.88 = bf16[1,3,64,256]{3,2,1,0:T(8,128)(2,1)} custom-call(f32[3,64,256]{2,1,0:T(8,128)S(1)} %get-tuple-element.58.base, bf16[64,128]{1,0:T(8,128)(2,1)S(1)} %collective-permute-done.7.refs_0_, bf16[64,128]{1,0:T(8,128)(2,1)S(1)} %collective-permute-done.8.refs_1_, bf16[64,128]{1,0:T(8,128)(2,1)S(1)} %collective-permute-done.9.refs_2_, ...), custom_call_target="tpu_custom_call" | custom-call | tf_op jit(solution)/shard_map/pallas_call | solution.py:470
  32.4 0.3 %collective-permute-done.10.theirs = f32[304,128]{1,0:T(8,128)S(1)} collective-permute-done((f32[304,128]{1,0:T(8,128)S(1)}, f32[304,128]{1,0:T(8,128)S(1)}, u32[]{:S(2)}, u32[]{:S(2)}) %collective-permute-start.10) | collective-permute-done | bytes 155680 | tf_op jit(solution)/shard_map/ppermute | solution.py:479
  32.7 0.7 %shard_map.89 = (f32[9,64,128]{2,1,0:T(8,128)}, f32[1,64]{1,0:T(1,128)}) custom-call(f32[304,128]{1,0:T(8,128)S(1)} %add_multiply_fusion.mine, f32[304,128]{1,0:T(8,128)S(1)} %collective-permute-done.10.theirs), custom_call_target="tpu_custom_call" | custom-call | tf_op jit(solution)/shard_map/pallas_call | solution.py:475
  (7 shorter events, 0.1 us)
Async XLA Ops:
  2.3 14.2 %collective-permute-start.3 = (bf16[976,128]{1,0:T(8,128)(2,1)S(1)}, bf16[976,128]{1,0:T(8,128)(2,1)S(1)}, u32[]{:S(2)}, u32[]{:S(2)}) collective-permute-start(bf16[976,128]{1,0:T(8,128)(2,1)S(1)} %get-tuple-element.40.shared.refs_2_.refs_1_), channel_id=1, source_target_pairs={{0,2},{2,0},{1,3},{3,1},{4,6},{6,4},{5,7},{7,5},{8,10},{10,8},{9,1... | collective-permute-start | bytes 749576 | tf_op jit(solution)/shard_map/ppermute | solution.py:414
  5.3 6.0 %collective-permute-start = (bf16[128,128]{1,0:T(8,128)(2,1)S(1)}, bf16[128,128]{1,0:T(8,128)(2,1)S(1)}, u32[]{:S(2)}, u32[]{:S(2)}) collective-permute-start(bf16[128,128]{1,0:T(8,128)(2,1)S(1)} %get-tuple-element.45), channel_id=1, source_target_pairs={{0,4},{4,8},{8,12},{12,0},{1,5},{5,9},{9,13},{13,1},{2,6},{6,10},{... | collective-permute-start | bytes 98312 | tf_op jit(solution)/shard_map/ppermute | solution.py:413
  6.9 4.4 %collective-permute-start.1 = (bf16[128,128]{1,0:T(8,128)(2,1)S(1)}, bf16[128,128]{1,0:T(8,128)(2,1)S(1)}, u32[]{:S(2)}, u32[]{:S(2)}) collective-permute-start(bf16[128,128]{1,0:T(8,128)(2,1)S(1)} %get-tuple-element.46), channel_id=1, source_target_pairs={{0,12},{4,0},{8,4},{12,8},{1,13},{5,1},{9,5},{13,9},{2,14},{6,2},{... | collective-permute-start | bytes 98312 | tf_op jit(solution)/shard_map/ppermute | solution.py:413
  9.1 4.8 %collective-permute-start.2 = (bf16[128,128]{1,0:T(8,128)(2,1)S(1)}, bf16[128,128]{1,0:T(8,128)(2,1)S(1)}, u32[]{:S(2)}, u32[]{:S(2)}) collective-permute-start(bf16[128,128]{1,0:T(8,128)(2,1)S(1)} %get-tuple-element.47), channel_id=1, source_target_pairs={{0,8},{4,12},{8,0},{12,4},{1,9},{5,13},{9,1},{13,5},{2,10},{6,14},... | collective-permute-start | bytes 98312 | tf_op jit(solution)/shard_map/ppermute | solution.py:413
  16.5 1.4 %collective-permute-start.4 = (f32[304,128]{1,0:T(8,128)S(1)}, f32[304,128]{1,0:T(8,128)S(1)}, u32[]{:S(2)}, u32[]{:S(2)}) collective-permute-start(f32[304,128]{1,0:T(8,128)S(1)} %get-tuple-element.53), channel_id=1, source_target_pairs={{0,1},{1,0},{2,3},{3,2},{4,5},{5,4},{6,7},{7,6},{8,9},{9,8},{10,11... | collective-permute-start | bytes 466952 | tf_op jit(solution)/shard_map/ppermute | solution.py:439
  17.9 4.5 %collective-permute-start.5 = (bf16[304,128]{1,0:T(8,128)(2,1)S(1)}, bf16[304,128]{1,0:T(8,128)(2,1)S(1)}, u32[]{:S(2)}, u32[]{:S(2)}) collective-permute-start(bf16[304,128]{1,0:T(8,128)(2,1)S(1)} %add_convert_fusion.1), channel_id=1, source_target_pairs={{0,4},{4,0},{8,12},{12,8},{1,5},{5,1},{9,13},{13,9},{2,6},{6,2},{1... | collective-permute-start | bytes 233480 | tf_op jit(solution)/shard_map/ppermute | solution.py:457
  22.4 6.6 %collective-permute-start.6 = (bf16[304,128]{1,0:T(8,128)(2,1)S(1)}, bf16[304,128]{1,0:T(8,128)(2,1)S(1)}, u32[]{:S(2)}, u32[]{:S(2)}) collective-permute-start(bf16[304,128]{1,0:T(8,128)(2,1)S(1)} %add_convert_fusion), channel_id=1, source_target_pairs={{0,8},{4,12},{8,0},{12,4},{1,9},{5,13},{9,1},{13,5},{2,10},{6,14},... | collective-permute-start | bytes 233480 | tf_op jit(solution)/shard_map/ppermute | solution.py:457
  24.0 5.0 %collective-permute-start.7 = (bf16[64,128]{1,0:T(8,128)(2,1)S(1)}, bf16[64,128]{1,0:T(8,128)(2,1)S(1)}, u32[]{:S(2)}, u32[]{:S(2)}) collective-permute-start(bf16[64,128]{1,0:T(8,128)(2,1)S(1)} %get-tuple-element.66.refs_3_), channel_id=1, source_target_pairs={{4,0},{8,4},{12,8},{0,12},{5,1},{9,5},{13,9},{1,13},{6,2},{10,6},{... | collective-permute-start | bytes 49160 | tf_op jit(solution)/shard_map/ppermute | solution.py:466
  25.8 5.5 %collective-permute-start.8 = (bf16[64,128]{1,0:T(8,128)(2,1)S(1)}, bf16[64,128]{1,0:T(8,128)(2,1)S(1)}, u32[]{:S(2)}, u32[]{:S(2)}) collective-permute-start(bf16[64,128]{1,0:T(8,128)(2,1)S(1)} %get-tuple-element.66.refs_3_), channel_id=1, source_target_pairs={{12,0},{0,4},{4,8},{8,12},{13,1},{1,5},{5,9},{9,13},{14,2},{2,6},{... | collective-permute-start | bytes 49160 | tf_op jit(solution)/shard_map/ppermute | solution.py:466
  26.1 5.3 %collective-permute-start.9 = (bf16[64,128]{1,0:T(8,128)(2,1)S(1)}, bf16[64,128]{1,0:T(8,128)(2,1)S(1)}, u32[]{:S(2)}, u32[]{:S(2)}) collective-permute-start(bf16[64,128]{1,0:T(8,128)(2,1)S(1)} %get-tuple-element.66.refs_3_), channel_id=1, source_target_pairs={{8,0},{12,4},{0,8},{4,12},{9,1},{13,5},{1,9},{5,13},{10,2},{14,6},... | collective-permute-start | bytes 49160 | tf_op jit(solution)/shard_map/ppermute | solution.py:466
  31.4 1.4 %collective-permute-start.10 = (f32[304,128]{1,0:T(8,128)S(1)}, f32[304,128]{1,0:T(8,128)S(1)}, u32[]{:S(2)}, u32[]{:S(2)}) collective-permute-start(f32[304,128]{1,0:T(8,128)S(1)} %add_multiply_fusion.mine), channel_id=1, source_target_pairs={{0,1},{1,0},{2,3},{3,2},{4,5},{5,4},{6,7},{7,6},{8,9},{9,8},{10,11... | collective-permute-start | bytes 466952 | tf_op jit(solution)/shard_map/ppermute | solution.py:479

commit v3 on v2

--- a/solution.py
+++ b/solution.py
@@ -28,67 +28,71 @@
 def halo_plans(count):
     if count == 4:
         return [
-            (lambda d: (d + 1) % 4, ("west", "fold")),
-            (lambda d: (d + 3) % 4, ("east", "fold")),
-            (lambda d: (d + 2) % 4, ("corner_w", "corner_e")),
-            (None, ("corner_w", "corner_e")),
+            (lambda d: 3 - d, ("side", "fold")),
+            (lambda d: d ^ 2, ("corner",)),
+            (lambda d: d ^ 1, ("side",)),
+            (None, ("corner",)),
         ]
     return [
         (lambda d: (d + 1) % count, ("west",)),
         (lambda d: (d + count - 1) % count, ("east",)),
         (lambda d: count - 1 - d, ("fold",)),
-        (lambda d: (count - d) % count, ("corner_w",)),
-        (lambda d: (2 * count - 2 - d) % count, ("corner_e",)),
+        (lambda d: (count - d) % count, ("corner_west",)),
+        (lambda d: (2 * count - 2 - d) % count, ("corner_east",)),
     ]
 
 
-def slot_of(rows, column, row):
-    found = jnp.int32(-1)
-    for k in range(SLOTS):
-        found = jnp.where((rows[column, k] == row) & (row >= 0), k, found)
-    return found
+def sum_routes(count):
+    if count == 4:
+        return [lambda d: d ^ 1, lambda d: 3 - d]
+    return [lambda d, s=1 << i: d ^ s for i in range(count.bit_length() - 1)]
 
 
 def halo_sources(rows, count, source, target, roles):
     lane = iota((8, 128), 1)
     top = 2 * SLOTS - 1
+    east = (lane >= EAST) & (lane < FOLD)
+    at = lane - jnp.where(east, EAST, 0)
+    k = jnp.where(at >= EDGE, 1, 0) + jnp.where(at >= 2 * EDGE, 1, 0)
+    p = at - EDGE * k
+    rim = lane < FOLD
+    row = jnp.where(k == 0, rows[target, 0], jnp.where(k == 1, rows[target, 1], rows[target, 2]))
+    row = jnp.where(rim, row, -1)
     src = jnp.full((8, 128), -1, jnp.int32)
-    for role, base, near, here in (
-        ("west", 0, TS - 1, (source + 1) % count),
-        ("east", EAST, 0, (source + count - 1) % count),
-    ):
-        if role not in roles:
-            continue
-        for k in range(SLOTS):
-            row = rows[target, k]
-            row_here = jnp.where(target == here, row, -8)
-            same = slot_of(rows, source, row_here)
-            south = jnp.where(slot_of(rows, target, row_here - 1) >= 0, slot_of(rows, source, row_here - 1), -1)
-            above = jnp.where(row_here >= 0, row_here + 1, -8)
-            north = jnp.where(slot_of(rows, target, above) >= 0, slot_of(rows, source, above), -1)
-            p = lane - (base + k * EDGE)
-            mid = jnp.where(same >= 0, same * CELLS + near - TS, -CELLS * 8)
-            src = jnp.where((p >= 1) & (p <= TS), jnp.maximum(mid + TS * p, -1), src)
-            src = jnp.where(p == 0, jnp.where(south >= 0, south * CELLS + CELLS - TS + near, -1), src)
-            src = jnp.where(p == TS + 1, jnp.where(north >= 0, north * CELLS + near, -1), src)
-    mine = slot_of(rows, source, jnp.int32(top))
-    theirs = slot_of(rows, target, jnp.int32(top))
-    both = (mine >= 0) & (theirs >= 0)
+    sides = [name for name in ("west", "east") if name in roles or "side" in roles]
+    if sides:
+        wanted = row + jnp.where(p == TS + 1, 1, 0) - jnp.where(p == 0, 1, 0)
+        slot = jnp.full((8, 128), -1, jnp.int32)
+        present = (p > 0) & (p <= TS)
+        for l in range(SLOTS):
+            slot = jnp.where(wanted == rows[source, l], l, slot)
+            present = present | (wanted == rows[target, l])
+        cell = jnp.where(p == 0, CELLS - TS, jnp.where(p == TS + 1, 0, TS * (p - 1))) + jnp.where(east, 0, TS - 1)
+        good = present & (row >= 0) & (wanted >= 0) & (slot >= 0)
+        from_west = target == (source + 1) % count if "west" in sides else False
+        from_east = target == (source + count - 1) % count if "east" in sides else False
+        good = good & ((jnp.logical_not(east) & from_west) | (east & from_east))
+        src = jnp.where(good, slot * CELLS + cell, src)
+
+    def top_slot(column):
+        found = jnp.int32(-1)
+        for l in range(SLOTS):
+            found = jnp.where(rows[column, l] == top, l, found)
+        return found
+
+    if sides and len(sides) == len(roles) and "side" not in roles or roles == ("side",):
+        return src
+    mine = top_slot(source)
     if "fold" in roles:
-        ok = both & (target == count - 1 - source)
-        c = lane - FOLD
-        last = jnp.where(ok, mine * CELLS + CELLS - 1, -CELLS * 8)
-        src = jnp.where((c >= 0) & (c < TS), jnp.maximum(last - c, -1), src)
-    through = both & (slot_of(rows, count - 1 - target, jnp.int32(top)) >= 0)
-    for role, base, near, here in (
-        ("corner_w", 0, 0, (count - source) % count),
-        ("corner_e", EAST, TS - 1, (2 * count - 2 - source) % count),
-    ):
-        if role not in roles:
-            continue
-        ok = through & (target == here)
-        spot = jnp.where(ok, base + theirs * EDGE + TS + 1, -1)
-        src = jnp.where(lane == spot, mine * CELLS + CELLS - TS + near, src)
+        good = (lane >= FOLD) & (lane < FOLD + TS) & (mine >= 0) & (target == count - 1 - source)
+        src = jnp.where(good, mine * CELLS + (CELLS - 1 + FOLD) - lane, src)
+    corners = [name for name in ("west", "east") if "corner" in roles or f"corner_{name}" in roles]
+    if corners:
+        good = (row == top) & (p == TS + 1) & (mine >= 0) & (top_slot(count - 1 - target) >= 0)
+        from_west = target == (count - source) % count if "west" in corners else False
+        from_east = target == (2 * count - 2 - source) % count if "east" in corners else False
+        good = good & ((jnp.logical_not(east) & from_west) | (east & from_east))
+        src = jnp.where(good, mine * CELLS + CELLS - TS + jnp.where(east, TS - 1, 0), src)
     return src
 
 
@@ -114,27 +118,16 @@
     return taps, halves, ref.at[at : at + 16]
 
 
-def pack_kernel(rows_hbm, fields_hbm, weights_hbm, bias_hbm, cot_hbm, *refs, count):
+def pack_kernel(rows_hbm, fields_hbm, *refs, count):
     n = len(halo_plans(count))
-    rows_out, fields_out, shared = refs[:3]
-    outs = refs[3 : 3 + n]
-    maps = refs[3 + n : 3 + 2 * n]
-    rows, bias, sem = refs[3 + 2 * n :]
-    own = weights_hbm.shape[1]
-    taps, halves, pieces = message_views(shared, own)
+    rows_out, fields_out = refs[:2]
+    outs = refs[2 : 2 + n]
+    maps = refs[2 + n : 2 + 2 * n]
+    rows, sem = refs[2 + 2 * n :]
     get_rows = pltpu.make_async_copy(rows_hbm, rows, sem.at[0])
     get_rows.start()
     get_fields = pltpu.make_async_copy(fields_hbm.at[0], fields_out, sem.at[1])
     get_fields.start()
-    get_bias = pltpu.make_async_copy(bias_hbm, bias, sem.at[2])
-    get_bias.start()
-    more = [pltpu.make_async_copy(weights_hbm.at[t], taps[t], sem.at[3 + t]) for t in range(9)]
-    for k in range(SLOTS):
-        for h in range(2):
-            source = cot_hbm.at[0, k, :, h * 128 : h * 128 + 128]
-            more.append(pltpu.make_async_copy(source, halves[k][h], sem.at[12 + 2 * k + h]))
-    for copy in more:
-        copy.start()
     get_rows.wait()
     position = lax.axis_index("tiles")
     plans = halo_plans(count)
@@ -146,14 +139,6 @@
     cells = jnp.concatenate([fields_out[k] for k in range(SLOTS)], axis=1)
     for out, hits in zip(outs, maps):
         out[...] = dot(cells, hits[...]).astype(BF16)
-    get_bias.wait()
-    line = jnp.concatenate([bias[...], jnp.zeros((1, 128 - own), F32)], axis=1)
-    high = line.astype(BF16).astype(F32)
-    middle = (line - high).astype(BF16).astype(F32)
-    low = line - high - middle
-    pieces[...] = jnp.concatenate([high, middle, low, jnp.zeros((13, 128), F32)], axis=0).astype(BF16)
-    for copy in more:
-        copy.wait()
     put_rows.wait()
 
 
@@ -170,8 +155,18 @@
     return full, at_top, above
 
 
-def window_kernel(rows, fields, shared, windows, spreads, kernel):
+def window_kernel(rows, fields, weights_hbm, bias_hbm, cot_hbm, windows, spreads, kernel, shared, bias, sem):
     own = kernel.shape[0] // 3
+    taps, halves, pieces = message_views(shared, own)
+    get_bias = pltpu.make_async_copy(bias_hbm, bias, sem.at[0])
+    get_bias.start()
+    more = [pltpu.make_async_copy(weights_hbm.at[t], taps[t], sem.at[1 + t]) for t in range(9)]
+    for k in range(SLOTS):
+        for h in range(2):
+            source = cot_hbm.at[0, k, :, h * 128 : h * 128 + 128]
+            more.append(pltpu.make_async_copy(source, halves[k][h], sem.at[10 + 2 * k + h]))
+    for copy in more:
+        copy.start()
     full, _, above = slot_flags(rows)
     column = iota((1, FRAME), 1) % TS
     lane128 = iota((1, 128), 1)
@@ -196,7 +191,14 @@
             spot = jnp.where(p == 0, FRAME - TS, TS * (p - 1)) + side * (TS - 1)
             hits = (p >= 0) & (p < EDGE) & (frame_lane == spot)
             spreads[side, k] = jnp.where(hits, 1.0, 0.0).astype(BF16)
-    taps, _, _ = message_views(shared, own)
+    get_bias.wait()
+    line = jnp.concatenate([bias[...], jnp.zeros((1, 128 - own), F32)], axis=1)
+    high = line.astype(BF16).astype(F32)
+    middle = (line - high).astype(BF16).astype(F32)
+    low = line - high - middle
+    pieces[...] = jnp.concatenate([high, middle, low, jnp.zeros((13, 128), F32)], axis=0).astype(BF16)
+    for copy in more:
+        copy.wait()
     for a in range(3):
         for b in range(3):
             kernel[a * own : (a + 1) * own, b * C : (b + 1) * C] = taps[3 * a + b][...]
@@ -392,18 +394,18 @@
     half_rows = -(-(9 * own + 1) // 32) * 16
     swap = [(0, 1), (1, 0)]
 
-    rows, tiles, shared, *packed = call(
+    pinned = [
+        pltpu.with_memory_space_constraint(x, pltpu.HBM)
+        for x in (tile_rows, fields, weights, bias.reshape(1, own), cotangent)
+    ]
+    rows, tiles, *packed = call(
         lambda *refs: pack_kernel(*refs, count=count),
-        [HBM] * 5,
-        [struct(tile_rows.shape, jnp.int32), struct((SLOTS, C, CELLS), BF16), struct((shared_rows, 128), BF16)]
+        [HBM] * 2,
+        [struct(tile_rows.shape, jnp.int32), struct((SLOTS, C, CELLS), BF16)]
         + [struct((C, 128), BF16)] * n
         + [struct((SLOTS * CELLS, 128), BF16)] * n,
-        [
-            pltpu.SMEM(tile_rows.shape, jnp.int32),
-            pltpu.VMEM((1, own), F32),
-            pltpu.SemaphoreType.DMA((12 + 2 * SLOTS,)),
-        ],
-    )(*(pltpu.with_memory_space_constraint(x, pltpu.HBM) for x in (tile_rows, fields, weights, bias.reshape(1, own), cotangent)))
+        [pltpu.SMEM(tile_rows.shape, jnp.int32), pltpu.SemaphoreType.DMA((2,))],
+    )(*pinned[:2])
     messages, maps = packed[:n], packed[n:]
     halos = []
     for (route, _), message in zip(plans, messages):
@@ -411,17 +413,19 @@
             halos.append(message)
         else:
             halos.append(lax.ppermute(message, "tiles", [(i, route(i)) for i in range(count)]))
-    others = [lax.ppermute(shared, "chan", [(i, (i + s) % chans) for i in range(chans)]) for s in range(1, chans)]
-
-    windows, spreads, kernel = call(
+
+    windows, spreads, kernel, shared = call(
         window_kernel,
-        [SMEM, VMEM, VMEM],
+        [SMEM, VMEM] + [HBM] * 3,
         [
             struct((SLOTS, 3 * C, FRAME), BF16),
             struct((2, SLOTS, 128, FRAME), BF16),
             struct((3 * own, 3 * C), BF16),
+            struct((shared_rows, 128), BF16),
         ],
-    )(rows, tiles, shared)
+        [pltpu.VMEM((1, own), F32), pltpu.SemaphoreType.DMA((10 + 2 * SLOTS,))],
+    )(rows, tiles, *pinned[2:])
+    others = [lax.ppermute(shared, "chan", [(i, (i + s) % chans) for i in range(chans)]) for s in range(1, chans)]
 
     windows, frames, result, keep, send = call(
         lambda *refs: forward_kernel(*refs, n_halos=n, half_rows=half_rows),
@@ -433,6 +437,7 @@
             struct((half_rows, 128), F32),
             struct((half_rows, 128), F32),
         ],
+        cost=pl.CostEstimate(flops=4 * 10**9, transcendentals=0, bytes_accessed=0),
     )(rows, tiles, shared, kernel, spreads, windows, *halos)
 
     send, others = lax.optimization_barrier((send, others))
@@ -452,20 +457,29 @@
         out_specs=[VMEM, VMEM, HBM],
     )(rows, shared, kernel, spreads, windows, frames, result, *others)
 
-    stride = 1
-    while stride < count:
-        other = lax.ppermute(rounded, "tiles", [(i, i ^ stride) for i in range(count)])
+    merged = None
+    routes = sum_routes(count)
+    for step, route in enumerate(routes):
+        pairs = [(i, route(i)) for i in range(count)]
+        if step == 1:
+            rounded, edges = lax.optimization_barrier((rounded, edges))
+        if count == 4 and step == 1:
+            both = lax.ppermute(jnp.concatenate([rounded, edges], axis=0), "tiles", pairs)
+            other, merged = both[:half_rows], both[half_rows:]
+        else:
+            other = lax.ppermute(rounded, "tiles", pairs)
         sums = rounded.astype(F32) + other.astype(F32)
         rounded = sums.astype(BF16)
-        if stride == 1:
-            rounded, edges = lax.optimization_barrier((rounded, edges))
-        stride *= 2
     grad_scale = 1.0 / math.sqrt(reps * fields.shape[0] * count * SLOTS * CELLS)
     sums = sums * grad_scale
-    returned = [
-        edges if route is None else lax.ppermute(edges, "tiles", [(route(i), i) for i in range(count)])
-        for route, _ in plans
-    ]
+    returned = []
+    for i, (route, _) in enumerate(plans):
+        if route is None:
+            returned.append(edges)
+        elif merged is not None and i == 0:
+            returned.append(merged)
+        else:
+            returned.append(lax.ppermute(edges, "tiles", [(route(j), j) for j in range(count)]))
     sums, returned = lax.optimization_barrier((sums, returned))
     grad_fields = call(
         finish_kernel,

time: 33.7 us -> 33.7 us (level)
  waiting for transfers between devices: 9.7 us -> 8.46 us
  Pallas kernels: 10.2 us -> 10.9 us
  starting transfers between devices: 12.8 us -> 13.4 us
    ppermute x1, waiting for transfers between devices: 0.01 us -> 2.46 us  [on_device(): lax.ppermute(shared, 'chan', [(i, (i + s) % chans) for i in range(chans)])]
    ppermute x3, waiting for transfers between devices: 3.04 us -> 0.6 us  [on_device(): lax.ppermute(message, 'tiles', [(i, route(i)) for i in range(count)])]
    ppermute x1, starting transfers between devices: 3 us -> 1.7 us  [on_device(): lax.ppermute(shared, 'chan', [(i, (i + s) % chans) for i in range(chans)])]
    ppermute x5 -> x4, waiting for transfers between devices: 4.93 us -> 3.67 us  [the longest x1 2.22 us: on_device(): lax.ppermute(jnp.concatenate([rounded, edges], axis=0), 'tiles', pairs)]
    ppermute x3, starting transfers between devices: 4.61 us -> 5.76 us  [on_device(): lax.ppermute(message, 'tiles', [(i, route(i)) for i in range(count)])]
    ppermute x5 -> x4, starting transfers between devices: 5.09 us -> 5.9 us  [the longest x1 3.22 us: on_device(): lax.ppermute(jnp.concatenate([rounded, edges], axis=0), 'tiles', pairs)]
    pallas_call x2, Pallas kernels: 2.62 us -> 3.3 us  [the longest x1 1.86 us: on_device(): call(window_kernel, [SMEM, VMEM] + [HBM] * 3, [struct((SLOTS, 3 * C, FRAM...]
  transfers between devices with their start and end apart: 11 -> 10, of which waited for: 7 -> 6; matrix products, arithmetic and copies ran while one was open for 0% -> 0% of each run, Pallas kernels for 23% -> 26%
where the time goes in v3:
time: 33.7 us; the launch traced here: 33.5 us
  starting transfers between devices  13.4 us (40%)
  Pallas kernels  10.9 us (32%)
  waiting for transfers between devices  8.46 us (25%)
  between operations  0.71 us (2%)
    ppermute x3, starting transfers between devices, on_device(): lax.ppermute(message, 'tiles', [(i, route(i)) for i in range(count)])  5.76 us
    pallas_call x1, Pallas kernels, on_device(): call(lambda *refs: backward_kernel(*refs, n_others=len(others)), [SMEM] +...  3.3 us
    ppermute x1, starting transfers between devices, on_device(): lax.ppermute(jnp.concatenate([rounded, edges], axis=0), 'tiles', pairs)  3.22 us
    pallas_call x1, Pallas kernels, on_device(): call(lambda *refs: forward_kernel(*refs, n_halos=n, half_rows=half_rows),...  2.52 us
    ppermute x1, waiting for transfers between devices, on_device(): lax.ppermute(shared, 'chan', [(i, (i + s) % chans) for i in range(chans)])  2.46 us
    ppermute x1, waiting for transfers between devices, on_device(): lax.ppermute(jnp.concatenate([rounded, edges], axis=0), 'tiles', pairs)  2.22 us
    pallas_call x1, Pallas kernels, on_device(): call(window_kernel, [SMEM, VMEM] + [HBM] * 3, [struct((SLOTS, 3 * C, FRAM...  1.86 us
    ppermute x1, starting transfers between devices, on_device(): lax.ppermute(shared, 'chan', [(i, (i + s) % chans) for i in range(chans)])  1.7 us
  transfers between devices with their start and end apart: 10, of which 6 were waited for; matrix products, arithmetic and copies ran while one was open for 0% of the time, Pallas kernels for 26%

profile of v3, /device:TPU:0, one launch (start us, length us, event | category | flops | bytes accessed | tf_op | source)
XLA Modules:
  0.0 33.5 jit_solution(3444679097620735236)
XLA Ops:
  0.6 1.4 %shard_map.84 = (s32[4,3]{1,0:T(4,128)S(1)}, bf16[3,128,256]{2,1,0:T(8,128)(2,1)S(1)}, bf16[128,128]{1,0:T(8,128)(2,1)S(1)}, bf16[128,128]{1,0:T(8,128)(2,1)S(1)...) custom-call(s32[4,3]{1,0:T(4,128)} %refs_0_.1, ...), custom_call_target="tpu_custom_call" | custom-call | tf_op jit(solution)/shard_map/pallas_call | solution.py:401
  2.1 5.1 %collective-permute-start = (bf16[128,128]{1,0:T(8,128)(2,1)S(1)}, bf16[128,128]{1,0:T(8,128)(2,1)S(1)}, u32[]{:S(2)}, u32[]{:S(2)}) collective-permute-start(bf16[128,128]{1,0:T(8,128)(2,1)S(1)} %get-tuple-element.45), channel_id=1, source_target_pairs={{0,12},{4,8},{8,4},{12,0},{1,13},{5,9},{9,5},{13,1},{2,14},{6,10},... | collective-permute-start | bytes 98312 | tf_op jit(solution)/shard_map/ppermute | solution.py:415
  7.2 0.6 %collective-permute-start.2 = (bf16[128,128]{1,0:T(8,128)(2,1)S(1)}, bf16[128,128]{1,0:T(8,128)(2,1)S(1)}, u32[]{:S(2)}, u32[]{:S(2)}) collective-permute-start(bf16[128,128]{1,0:T(8,128)(2,1)S(1)} %get-tuple-element.47), channel_id=1, source_target_pairs={{0,4},{4,0},{8,12},{12,8},{1,5},{5,1},{9,13},{13,9},{2,6},{6,2},{1... | collective-permute-start | bytes 98312 | tf_op jit(solution)/shard_map/ppermute | solution.py:415
  7.8 1.9 %shard_map.85 = (bf16[3,384,384]{2,1,0:T(8,128)(2,1)S(1)}, bf16[2,3,128,384]{3,2,1,0:T(8,128)(2,1)S(1)}, bf16[192,384]{1,0:T(8,128)(2,1)S(1)}, bf16[976,128]{1,0:T(8,128)(2,1)S(1)}) custom-call(s32[4,3]{1,0:T(4,128)S(1)} %get-tuple-element.39.rows.refs_0_, bf16[3,128,256]{2,1,0:T(8,128)(2,1)S(1)} %get-tuple-element.40.fields.refs_1_, ...), custom_call_target="tpu_custom_call" | custom-call | tf_op jit(solution)/shard_map/pallas_call | solution.py:417
  9.7 1.7 %collective-permute-start.3 = (bf16[976,128]{1,0:T(8,128)(2,1)S(1)}, bf16[976,128]{1,0:T(8,128)(2,1)S(1)}, u32[]{:S(2)}, u32[]{:S(2)}) collective-permute-start(bf16[976,128]{1,0:T(8,128)(2,1)S(1)} %get-tuple-element.41.refs_2_.refs_1_), channel_id=1, source_target_pairs={{0,2},{2,0},{1,3},{3,1},{4,6},{6,4},{5,7},{7,5},{8,10},{10,8},{9,1... | collective-permute-start | bytes 749576 | tf_op jit(solution)/shard_map/ppermute | solution.py:428
  11.4 0.0 collective-permute-done.refs_6_
  11.4 0.6 %collective-permute-done.1.refs_7_ = bf16[128,128]{1,0:T(8,128)(2,1)S(1)} collective-permute-done((bf16[128,128]{1,0:T(8,128)(2,1)S(1)}, bf16[128,128]{1,0:T(8,128)(2,1)S(1)}, u32[]{:S(2)}, u32[]{:S(2)}) %collective-permute-start.1) | collective-permute-done | bytes 32800 | tf_op jit(solution)/shard_map/ppermute | solution.py:415
  12.0 0.0 collective-permute-done.2.refs_8_
  12.0 2.5 %shard_map.86 = (bf16[3,384,384]{2,1,0:T(8,128)(2,1)S(1)}, bf16[3,192,384]{2,1,0:T(8,128)(2,1)S(1)}, bf16[3,64,256]{2,1,0:T(8,128)(2,1)S(1)}, f32[304,128]{1,0:T(8,128)S(1)}, f32[304,128]{1,0:T(8,128)S(1)}) custom-call(s32[4,3]{1,0:T(4,128)S(1)} %get-tuple-element.39.rows.refs_0_, bf16[3,128,256]{2,1,0:T(8,128)(2,1)S(1)} %get-tuple-element.40.fields.refs_1_, ...), custom_call_target="tpu_custom_call" | custom-call | flops 4000000000 | tf_op jit(solution)/shard_map/pallas_call | solution.py:430
  14.5 2.5 %collective-permute-done.3.refs_7_ = bf16[976,128]{1,0:T(8,128)(2,1)S(1)} collective-permute-done((bf16[976,128]{1,0:T(8,128)(2,1)S(1)}, bf16[976,128]{1,0:T(8,128)(2,1)S(1)}, u32[]{:S(2)}, u32[]{:S(2)}) %collective-permute-start.3) | collective-permute-done | bytes 249888 | tf_op jit(solution)/shard_map/ppermute | solution.py:428
  17.0 0.0 collective-permute-start.4
  17.0 1.4 %collective-permute-done.4 = f32[304,128]{1,0:T(8,128)S(1)} collective-permute-done((f32[304,128]{1,0:T(8,128)S(1)}, f32[304,128]{1,0:T(8,128)S(1)}, u32[]{:S(2)}, u32[]{:S(2)}) %collective-permute-start.4) | collective-permute-done | bytes 155680 | tf_op jit(solution)/shard_map/ppermute | solution.py:444
  18.4 1.5 %collective-permute-start.5 = (bf16[304,128]{1,0:T(8,128)(2,1)S(1)}, bf16[304,128]{1,0:T(8,128)(2,1)S(1)}, u32[]{:S(2)}, u32[]{:S(2)}) collective-permute-start(bf16[304,128]{1,0:T(8,128)(2,1)S(1)} %add_convert_fusion.1), channel_id=1, source_target_pairs={{0,4},{4,0},{8,12},{12,8},{1,5},{5,1},{9,13},{13,9},{2,6},{6,2},{1... | collective-permute-start | bytes 233480 | tf_op jit(solution)/shard_map/ppermute | solution.py:470
  19.9 3.3 %shard_map.87 = (f32[3,64,256]{2,1,0:T(8,128)S(1)}, bf16[64,128]{1,0:T(8,128)(2,1)S(1)}, bf16[1,3,64,256]{3,2,1,0:T(8,128)(2,1)}) custom-call(s32[4,3]{1,0:T(4,128)S(1)} %get-tuple-element.39.rows.refs_0_, bf16[976,128]{1,0:T(8,128)(2,1)S(1)} %get-tuple-element.41.refs_2_.refs_1_, bf16[192,384]{1,0:T(8,128)(2,1)S(1)} %get-tuple-element.42.refs_3_.refs_2_, ...), custom_call_target="tpu_custom_call" | custom-call | tf_op jit(solution)/shard_map/pallas_call | solution.py:448
  23.2 3.2 %collective-permute-start.6 = (bf16[368,128]{1,0:T(8,128)(2,1)S(1)}, bf16[368,128]{1,0:T(8,128)(2,1)S(1)}, u32[]{:S(2)}, u32[]{:S(2)}) collective-permute-start(bf16[368,128]{1,0:T(8,128)(2,1)S(1)} %pad_maximum_fusion), channel_id=1, source_target_pairs={{0,12},{4,8},{8,4},{12,0},{1,13},{5,9},{9,5},{13,1},{2,14},{6,10},... | collective-permute-start | bytes 282632 | tf_op jit(solution)/shard_map/ppermute | solution.py:467
  26.4 0.0 collective-permute-start.7
  26.5 1.2 %collective-permute-start.8 = (bf16[64,128]{1,0:T(8,128)(2,1)S(1)}, bf16[64,128]{1,0:T(8,128)(2,1)S(1)}, u32[]{:S(2)}, u32[]{:S(2)}) collective-permute-start(bf16[64,128]{1,0:T(8,128)(2,1)S(1)} %get-tuple-element.66.refs_3_), channel_id=1, source_target_pairs={{4,0},{0,4},{12,8},{8,12},{5,1},{1,5},{13,9},{9,13},{6,2},{2,6},{1... | collective-permute-start | bytes 49160 | tf_op jit(solution)/shard_map/ppermute | solution.py:482
  27.7 2.2 %collective-permute-done.6 = bf16[368,128]{1,0:T(8,128)(2,1)S(1)} collective-permute-done((bf16[368,128]{1,0:T(8,128)(2,1)S(1)}, bf16[368,128]{1,0:T(8,128)(2,1)S(1)}, u32[]{:S(2)}, u32[]{:S(2)}) %collective-permute-start.6) | collective-permute-done | bytes 94240 | tf_op jit(solution)/shard_map/ppermute | solution.py:467
  29.9 1.5 %collective-permute-done.7.refs_1_ = bf16[64,128]{1,0:T(8,128)(2,1)S(1)} collective-permute-done((bf16[64,128]{1,0:T(8,128)(2,1)S(1)}, bf16[64,128]{1,0:T(8,128)(2,1)S(1)}, u32[]{:S(2)}, u32[]{:S(2)}) %collective-permute-start.7) | collective-permute-done | bytes 16416 | tf_op jit(solution)/shard_map/ppermute | solution.py:482
  31.4 0.0 collective-permute-done.8.refs_2_
  31.4 0.0 collective-permute-start.9
  31.4 1.0 %shard_map.88 = bf16[1,3,64,256]{3,2,1,0:T(8,128)(2,1)} custom-call(f32[3,64,256]{2,1,0:T(8,128)S(1)} %get-tuple-element.58.base, bf16[64,128]{1,0:T(8,128)(2,1)S(1)} %slice.9.refs_0_, bf16[64,128]{1,0:T(8,128)(2,1)S(1)} %collective-permute-done.7.refs_1_, bf16[64,128]{1,0:T(8,128)(2,1)S(1)} %collective-permute-done.8.refs_2_, ...), custom_call_target="tpu_custom_call" | custom-call | tf_op jit(solution)/shard_map/pallas_call | solution.py:484
  32.4 0.3 %collective-permute-done.9.theirs = f32[304,128]{1,0:T(8,128)S(1)} collective-permute-done((f32[304,128]{1,0:T(8,128)S(1)}, f32[304,128]{1,0:T(8,128)S(1)}, u32[]{:S(2)}, u32[]{:S(2)}) %collective-permute-start.9) | collective-permute-done | bytes 155680 | tf_op jit(solution)/shard_map/ppermute | solution.py:493
  32.8 0.7 %shard_map.89 = (f32[9,64,128]{2,1,0:T(8,128)}, f32[1,64]{1,0:T(1,128)}) custom-call(f32[304,128]{1,0:T(8,128)S(1)} %add_multiply_fusion.mine, f32[304,128]{1,0:T(8,128)S(1)} %collective-permute-done.9.theirs), custom_call_target="tpu_custom_call" | custom-call | tf_op jit(solution)/shard_map/pallas_call | solution.py:489
  (7 shorter events, 0.1 us)
Async XLA Ops:
  2.1 9.3 %collective-permute-start = (bf16[128,128]{1,0:T(8,128)(2,1)S(1)}, bf16[128,128]{1,0:T(8,128)(2,1)S(1)}, u32[]{:S(2)}, u32[]{:S(2)}) collective-permute-start(bf16[128,128]{1,0:T(8,128)(2,1)S(1)} %get-tuple-element.45), channel_id=1, source_target_pairs={{0,12},{4,8},{8,4},{12,0},{1,13},{5,9},{9,5},{13,1},{2,14},{6,10},... | collective-permute-start | bytes 98312 | tf_op jit(solution)/shard_map/ppermute | solution.py:415
  7.2 4.8 %collective-permute-start.1 = (bf16[128,128]{1,0:T(8,128)(2,1)S(1)}, bf16[128,128]{1,0:T(8,128)(2,1)S(1)}, u32[]{:S(2)}, u32[]{:S(2)}) collective-permute-start(bf16[128,128]{1,0:T(8,128)(2,1)S(1)} %get-tuple-element.46), channel_id=1, source_target_pairs={{0,8},{4,12},{8,0},{12,4},{1,9},{5,13},{9,1},{13,5},{2,10},{6,14},... | collective-permute-start | bytes 98312 | tf_op jit(solution)/shard_map/ppermute | solution.py:415
  7.2 4.8 %collective-permute-start.2 = (bf16[128,128]{1,0:T(8,128)(2,1)S(1)}, bf16[128,128]{1,0:T(8,128)(2,1)S(1)}, u32[]{:S(2)}, u32[]{:S(2)}) collective-permute-start(bf16[128,128]{1,0:T(8,128)(2,1)S(1)} %get-tuple-element.47), channel_id=1, source_target_pairs={{0,4},{4,0},{8,12},{12,8},{1,5},{5,1},{9,13},{13,9},{2,6},{6,2},{1... | collective-permute-start | bytes 98312 | tf_op jit(solution)/shard_map/ppermute | solution.py:415
  9.7 7.3 %collective-permute-start.3 = (bf16[976,128]{1,0:T(8,128)(2,1)S(1)}, bf16[976,128]{1,0:T(8,128)(2,1)S(1)}, u32[]{:S(2)}, u32[]{:S(2)}) collective-permute-start(bf16[976,128]{1,0:T(8,128)(2,1)S(1)} %get-tuple-element.41.refs_2_.refs_1_), channel_id=1, source_target_pairs={{0,2},{2,0},{1,3},{3,1},{4,6},{6,4},{5,7},{7,5},{8,10},{10,8},{9,1... | collective-permute-start | bytes 749576 | tf_op jit(solution)/shard_map/ppermute | solution.py:428
  17.0 1.4 %collective-permute-start.4 = (f32[304,128]{1,0:T(8,128)S(1)}, f32[304,128]{1,0:T(8,128)S(1)}, u32[]{:S(2)}, u32[]{:S(2)}) collective-permute-start(f32[304,128]{1,0:T(8,128)S(1)} %get-tuple-element.53), channel_id=1, source_target_pairs={{0,1},{1,0},{2,3},{3,2},{4,5},{5,4},{6,7},{7,6},{8,9},{9,8},{10,11... | collective-permute-start | bytes 466952 | tf_op jit(solution)/shard_map/ppermute | solution.py:444
  18.4 4.8 %collective-permute-start.5 = (bf16[304,128]{1,0:T(8,128)(2,1)S(1)}, bf16[304,128]{1,0:T(8,128)(2,1)S(1)}, u32[]{:S(2)}, u32[]{:S(2)}) collective-permute-start(bf16[304,128]{1,0:T(8,128)(2,1)S(1)} %add_convert_fusion.1), channel_id=1, source_target_pairs={{0,4},{4,0},{8,12},{12,8},{1,5},{5,1},{9,13},{13,9},{2,6},{6,2},{1... | collective-permute-start | bytes 233480 | tf_op jit(solution)/shard_map/ppermute | solution.py:470
  23.2 6.7 %collective-permute-start.6 = (bf16[368,128]{1,0:T(8,128)(2,1)S(1)}, bf16[368,128]{1,0:T(8,128)(2,1)S(1)}, u32[]{:S(2)}, u32[]{:S(2)}) collective-permute-start(bf16[368,128]{1,0:T(8,128)(2,1)S(1)} %pad_maximum_fusion), channel_id=1, source_target_pairs={{0,12},{4,8},{8,4},{12,0},{1,13},{5,9},{9,5},{13,1},{2,14},{6,10},... | collective-permute-start | bytes 282632 | tf_op jit(solution)/shard_map/ppermute | solution.py:467
  26.4 4.9 %collective-permute-start.7 = (bf16[64,128]{1,0:T(8,128)(2,1)S(1)}, bf16[64,128]{1,0:T(8,128)(2,1)S(1)}, u32[]{:S(2)}, u32[]{:S(2)}) collective-permute-start(bf16[64,128]{1,0:T(8,128)(2,1)S(1)} %get-tuple-element.66.refs_3_), channel_id=1, source_target_pairs={{8,0},{12,4},{0,8},{4,12},{9,1},{13,5},{1,9},{5,13},{10,2},{14,6},... | collective-permute-start | bytes 49160 | tf_op jit(solution)/shard_map/ppermute | solution.py:482
  26.5 4.9 %collective-permute-start.8 = (bf16[64,128]{1,0:T(8,128)(2,1)S(1)}, bf16[64,128]{1,0:T(8,128)(2,1)S(1)}, u32[]{:S(2)}, u32[]{:S(2)}) collective-permute-start(bf16[64,128]{1,0:T(8,128)(2,1)S(1)} %get-tuple-element.66.refs_3_), channel_id=1, source_target_pairs={{4,0},{0,4},{12,8},{8,12},{5,1},{1,5},{13,9},{9,13},{6,2},{2,6},{1... | collective-permute-start | bytes 49160 | tf_op jit(solution)/shard_map/ppermute | solution.py:482
  31.4 1.4 %collective-permute-start.9 = (f32[304,128]{1,0:T(8,128)S(1)}, f32[304,128]{1,0:T(8,128)S(1)}, u32[]{:S(2)}, u32[]{:S(2)}) collective-permute-start(f32[304,128]{1,0:T(8,128)S(1)} %add_multiply_fusion.mine), channel_id=1, source_target_pairs={{0,1},{1,0},{2,3},{3,2},{4,5},{5,4},{6,7},{7,6},{8,9},{9,8},{10,11... | collective-permute-start | bytes 466952 | tf_op jit(solution)/shard_map/ppermute | solution.py:493

commit v4 on v3

--- a/solution.py
+++ b/solution.py
@@ -44,7 +44,7 @@
 
 def sum_routes(count):
     if count == 4:
-        return [lambda d: d ^ 1, lambda d: 3 - d]
+        return [lambda d: d ^ 2, lambda d: d ^ 1]
     return [lambda d, s=1 << i: d ^ s for i in range(count.bit_length() - 1)]
 
 
@@ -118,16 +118,27 @@
     return taps, halves, ref.at[at : at + 16]
 
 
-def pack_kernel(rows_hbm, fields_hbm, *refs, count):
+def pack_kernel(rows_hbm, fields_hbm, weights_hbm, bias_hbm, cot_hbm, *refs, count):
     n = len(halo_plans(count))
-    rows_out, fields_out = refs[:2]
-    outs = refs[2 : 2 + n]
-    maps = refs[2 + n : 2 + 2 * n]
-    rows, sem = refs[2 + 2 * n :]
+    rows_out, fields_out, shared = refs[:3]
+    outs = refs[3 : 3 + n]
+    maps = refs[3 + n : 3 + 2 * n]
+    rows, bias, sem = refs[3 + 2 * n :]
+    own = weights_hbm.shape[1]
+    taps, halves, pieces = message_views(shared, own)
     get_rows = pltpu.make_async_copy(rows_hbm, rows, sem.at[0])
     get_rows.start()
     get_fields = pltpu.make_async_copy(fields_hbm.at[0], fields_out, sem.at[1])
     get_fields.start()
+    get_bias = pltpu.make_async_copy(bias_hbm, bias, sem.at[2])
+    get_bias.start()
+    more = [pltpu.make_async_copy(weights_hbm.at[t], taps[t], sem.at[3 + t]) for t in range(9)]
+    for k in range(SLOTS):
+        for h in range(2):
+            source = cot_hbm.at[0, k, :, h * 128 : h * 128 + 128]
+            more.append(pltpu.make_async_copy(source, halves[k][h], sem.at[12 + 2 * k + h]))
+    for copy in more:
+        copy.start()
     get_rows.wait()
     position = lax.axis_index("tiles")
     plans = halo_plans(count)
@@ -135,10 +146,18 @@
         out[...] = halo_map(rows, count, position, plan)
     put_rows = pltpu.make_async_copy(rows, rows_out, sem.at[0])
     put_rows.start()
+    get_bias.wait()
+    line = jnp.concatenate([bias[...], jnp.zeros((1, 128 - own), F32)], axis=1)
+    high = line.astype(BF16).astype(F32)
+    middle = (line - high).astype(BF16).astype(F32)
+    low = line - high - middle
+    pieces[...] = jnp.concatenate([high, middle, low, jnp.zeros((13, 128), F32)], axis=0).astype(BF16)
     get_fields.wait()
     cells = jnp.concatenate([fields_out[k] for k in range(SLOTS)], axis=1)
     for out, hits in zip(outs, maps):
         out[...] = dot(cells, hits[...]).astype(BF16)
+    for copy in more:
+        copy.wait()
     put_rows.wait()
 
 
@@ -155,18 +174,9 @@
     return full, at_top, above
 
 
-def window_kernel(rows, fields, weights_hbm, bias_hbm, cot_hbm, windows, spreads, kernel, shared, bias, sem):
+def window_kernel(rows, fields, shared, windows, spreads, kernel):
     own = kernel.shape[0] // 3
-    taps, halves, pieces = message_views(shared, own)
-    get_bias = pltpu.make_async_copy(bias_hbm, bias, sem.at[0])
-    get_bias.start()
-    more = [pltpu.make_async_copy(weights_hbm.at[t], taps[t], sem.at[1 + t]) for t in range(9)]
-    for k in range(SLOTS):
-        for h in range(2):
-            source = cot_hbm.at[0, k, :, h * 128 : h * 128 + 128]
-            more.append(pltpu.make_async_copy(source, halves[k][h], sem.at[10 + 2 * k + h]))
-    for copy in more:
-        copy.start()
+    taps, _, _ = message_views(shared, own)
     full, _, above = slot_flags(rows)
     column = iota((1, FRAME), 1) % TS
     lane128 = iota((1, 128), 1)
@@ -191,14 +201,6 @@
             spot = jnp.where(p == 0, FRAME - TS, TS * (p - 1)) + side * (TS - 1)
             hits = (p >= 0) & (p < EDGE) & (frame_lane == spot)
             spreads[side, k] = jnp.where(hits, 1.0, 0.0).astype(BF16)
-    get_bias.wait()
-    line = jnp.concatenate([bias[...], jnp.zeros((1, 128 - own), F32)], axis=1)
-    high = line.astype(BF16).astype(F32)
-    middle = (line - high).astype(BF16).astype(F32)
-    low = line - high - middle
-    pieces[...] = jnp.concatenate([high, middle, low, jnp.zeros((13, 128), F32)], axis=0).astype(BF16)
-    for copy in more:
-        copy.wait()
     for a in range(3):
         for b in range(3):
             kernel[a * own : (a + 1) * own, b * C : (b + 1) * C] = taps[3 * a + b][...]
@@ -367,14 +369,13 @@
 HBM = pl.BlockSpec(memory_space=pltpu.HBM)
 
 
-def call(kernel, specs, outs, scratch=(), out_specs=None, cost=None):
+def call(kernel, specs, outs, scratch=(), out_specs=None):
     return pl.pallas_call(
         kernel,
         in_specs=specs,
         out_specs=out_specs or [VMEM] * len(outs),
         out_shape=outs,
         scratch_shapes=list(scratch),
-        cost_estimate=cost,
         compiler_params=pltpu.CompilerParams(vmem_limit_bytes=40 << 20),
     )
 
@@ -398,14 +399,22 @@
         pltpu.with_memory_space_constraint(x, pltpu.HBM)
         for x in (tile_rows, fields, weights, bias.reshape(1, own), cotangent)
     ]
-    rows, tiles, *packed = call(
+    rows, tiles, shared, *packed = call(
         lambda *refs: pack_kernel(*refs, count=count),
-        [HBM] * 2,
-        [struct(tile_rows.shape, jnp.int32), struct((SLOTS, C, CELLS), BF16)]
+        [HBM] * 5,
+        [
+            struct(tile_rows.shape, jnp.int32),
+            struct((SLOTS, C, CELLS), BF16),
+            struct((shared_rows, 128), BF16),
+        ]
         + [struct((C, 128), BF16)] * n
         + [struct((SLOTS * CELLS, 128), BF16)] * n,
-        [pltpu.SMEM(tile_rows.shape, jnp.int32), pltpu.SemaphoreType.DMA((2,))],
-    )(*pinned[:2])
+        [
+            pltpu.SMEM(tile_rows.shape, jnp.int32),
+            pltpu.VMEM((1, own), F32),
+            pltpu.SemaphoreType.DMA((12 + 2 * SLOTS,)),
+        ],
+    )(*pinned)
     messages, maps = packed[:n], packed[n:]
     halos = []
     for (route, _), message in zip(plans, messages):
@@ -414,17 +423,15 @@
         else:
             halos.append(lax.ppermute(message, "tiles", [(i, route(i)) for i in range(count)]))
 
-    windows, spreads, kernel, shared = call(
+    windows, spreads, kernel = call(
         window_kernel,
-        [SMEM, VMEM] + [HBM] * 3,
+        [SMEM] + [VMEM] * 2,
         [
             struct((SLOTS, 3 * C, FRAME), BF16),
             struct((2, SLOTS, 128, FRAME), BF16),
             struct((3 * own, 3 * C), BF16),
-            struct((shared_rows, 128), BF16),
         ],
-        [pltpu.VMEM((1, own), F32), pltpu.SemaphoreType.DMA((10 + 2 * SLOTS,))],
-    )(rows, tiles, *pinned[2:])
+    )(rows, tiles, shared)
     others = [lax.ppermute(shared, "chan", [(i, (i + s) % chans) for i in range(chans)]) for s in range(1, chans)]
 
     windows, frames, result, keep, send = call(
@@ -437,7 +444,6 @@
             struct((half_rows, 128), F32),
             struct((half_rows, 128), F32),
         ],
-        cost=pl.CostEstimate(flops=4 * 10**9, transcendentals=0, bytes_accessed=0),
     )(rows, tiles, shared, kernel, spreads, windows, *halos)
 
     send, others = lax.optimization_barrier((send, others))
@@ -476,7 +482,7 @@
     for i, (route, _) in enumerate(plans):
         if route is None:
             returned.append(edges)
-        elif merged is not None and i == 0:
+        elif merged is not None and i == 2:
             returned.append(merged)
         else:
             returned.append(lax.ppermute(edges, "tiles", [(route(j), j) for j in range(count)]))

time: 33.7 us -> 33.7 us (level)
  waiting for transfers between devices: 8.46 us -> 9.45 us
  Pallas kernels: 10.9 us -> 10.2 us
    ppermute x1, starting transfers between devices: 3.22 us -> 0.07 us  [on_device(): lax.ppermute(jnp.concatenate([rounded, edges], axis=0), 'tiles', pairs)]
    ppermute x1, waiting for transfers between devices: 2.46 us -> 0.01 us  [on_device(): lax.ppermute(shared, 'chan', [(i, (i + s) % chans) for i in range(chans)])]
    ppermute x3, waiting for transfers between devices: 0.6 us -> 3.05 us  [on_device(): lax.ppermute(message, 'tiles', [(i, route(i)) for i in range(count)])]
    ppermute x2, starting transfers between devices: 1.23 us -> 3.47 us  [on_device(): lax.ppermute(edges, 'tiles', [(route(j), j) for j in range(count)])]
    ppermute x3, starting transfers between devices: 5.76 us -> 4.39 us  [on_device(): lax.ppermute(message, 'tiles', [(i, route(i)) for i in range(count)])]
    ppermute x1, starting transfers between devices: 1.7 us -> 3 us  [on_device(): lax.ppermute(shared, 'chan', [(i, (i + s) % chans) for i in range(chans)])]
    ppermute x1, waiting for transfers between devices: 0.01 us -> 0.96 us  [on_device(): other = lax.ppermute(rounded, 'tiles', pairs)]
    ppermute x2, waiting for transfers between devices: 1.46 us -> 2.31 us  [on_device(): lax.ppermute(edges, 'tiles', [(route(j), j) for j in range(count)])]
  transfers between devices with their start and end apart: 10 -> 10, of which waited for: 6 -> 8; matrix products, arithmetic and copies ran while one was open for 0% -> 0% of each run, Pallas kernels for 26% -> 23%
where the time goes in v4:
time: 33.7 us; the launch traced here: 33.5 us
  starting transfers between devices  13.1 us (39%)
  Pallas kernels  10.2 us (30%)
  waiting for transfers between devices  9.45 us (28%)
  between operations  0.72 us (2%)
    ppermute x3, starting transfers between devices, on_device(): lax.ppermute(message, 'tiles', [(i, route(i)) for i in range(count)])  4.39 us
    ppermute x2, starting transfers between devices, on_device(): lax.ppermute(edges, 'tiles', [(route(j), j) for j in range(count)])  3.47 us
    pallas_call x1, Pallas kernels, on_device(): call(lambda *refs: backward_kernel(*refs, n_others=len(others)), [SMEM] +...  3.3 us
    ppermute x3, waiting for transfers between devices, on_device(): lax.ppermute(message, 'tiles', [(i, route(i)) for i in range(count)])  3.05 us
    ppermute x1, starting transfers between devices, on_device(): lax.ppermute(shared, 'chan', [(i, (i + s) % chans) for i in range(chans)])  3 us
    pallas_call x1, Pallas kernels, on_device(): call(lambda *refs: forward_kernel(*refs, n_halos=n, half_rows=half_rows),...  2.53 us
    ppermute x2, waiting for transfers between devices, on_device(): lax.ppermute(edges, 'tiles', [(route(j), j) for j in range(count)])  2.31 us
    ppermute x1, starting transfers between devices, on_device(): other = lax.ppermute(rounded, 'tiles', pairs)  2.09 us
  transfers between devices with their start and end apart: 10, of which 8 were waited for; matrix products, arithmetic and copies ran while one was open for 0% of the time, Pallas kernels for 23%

profile of v4, /device:TPU:0, one launch (start us, length us, event | category | flops | bytes accessed | tf_op | source)
XLA Modules:
  0.0 33.5 jit_solution(10051715279584094091)
XLA Ops:
  0.6 1.6 %shard_map.84 = (s32[4,3]{1,0:T(4,128)S(1)}, bf16[3,128,256]{2,1,0:T(8,128)(2,1)S(1)}, bf16[976,128]{1,0:T(8,128)(2,1)S(1)}, bf16[128,128]{1,0:T(8,128)(2,1)S(1)...) custom-call(s32[4,3]{1,0:T(4,128)} %refs_0_.1, ...), custom_call_target="tpu_custom_call" | custom-call | tf_op jit(solution)/shard_map/pallas_call | solution.py:402
  2.2 3.0 %collective-permute-start.3 = (bf16[976,128]{1,0:T(8,128)(2,1)S(1)}, bf16[976,128]{1,0:T(8,128)(2,1)S(1)}, u32[]{:S(2)}, u32[]{:S(2)}) collective-permute-start(bf16[976,128]{1,0:T(8,128)(2,1)S(1)} %get-tuple-element.40.shared.refs_2_.refs_1_), channel_id=1, source_target_pairs={{0,2},{2,0},{1,3},{3,1},{4,6},{6,4},{5,7},{7,5},{8,10},{10,8},{9,1... | collective-permute-start | bytes 749576 | tf_op jit(solution)/shard_map/ppermute | solution.py:435
  5.2 3.6 %collective-permute-start = (bf16[128,128]{1,0:T(8,128)(2,1)S(1)}, bf16[128,128]{1,0:T(8,128)(2,1)S(1)}, u32[]{:S(2)}, u32[]{:S(2)}) collective-permute-start(bf16[128,128]{1,0:T(8,128)(2,1)S(1)} %get-tuple-element.45), channel_id=1, source_target_pairs={{0,12},{4,8},{8,4},{12,0},{1,13},{5,9},{9,5},{13,1},{2,14},{6,10},... | collective-permute-start | bytes 98312 | tf_op jit(solution)/shard_map/ppermute | solution.py:424
  8.8 0.0 collective-permute-start.1
  8.8 0.8 %collective-permute-start.2 = (bf16[128,128]{1,0:T(8,128)(2,1)S(1)}, bf16[128,128]{1,0:T(8,128)(2,1)S(1)}, u32[]{:S(2)}, u32[]{:S(2)}) collective-permute-start(bf16[128,128]{1,0:T(8,128)(2,1)S(1)} %get-tuple-element.47), channel_id=1, source_target_pairs={{0,4},{4,0},{8,12},{12,8},{1,5},{5,1},{9,13},{13,9},{2,6},{6,2},{1... | collective-permute-start | bytes 98312 | tf_op jit(solution)/shard_map/ppermute | solution.py:424
  9.6 1.0 %shard_map.85 = (bf16[3,384,384]{2,1,0:T(8,128)(2,1)S(1)}, bf16[2,3,128,384]{3,2,1,0:T(8,128)(2,1)S(1)}, bf16[192,384]{1,0:T(8,128)(2,1)S(1)}) custom-call(s32[4,3]{1,0:T(4,128)S(1)} %get-tuple-element.39.rows.refs_0_, bf16[3,128,256]{2,1,0:T(8,128)(2,1)S(1)} %get-tuple-element.41.fields.refs_1_, bf16[976,128]{1,0:T(8,128)(2,1)S(1)} %get-tuple-element.40.shared.refs_2_.refs_1_), custom_call_target="tpu_custom_call" | custom-call | tf_op jit(solution)/shard_map/pallas_call | solution.py:426
  10.6 0.7 %collective-permute-done.refs_6_ = bf16[128,128]{1,0:T(8,128)(2,1)S(1)} collective-permute-done((bf16[128,128]{1,0:T(8,128)(2,1)S(1)}, bf16[128,128]{1,0:T(8,128)(2,1)S(1)}, u32[]{:S(2)}, u32[]{:S(2)}) %collective-permute-start) | collective-permute-done | bytes 32800 | tf_op jit(solution)/shard_map/ppermute | solution.py:424
  11.3 2.4 %collective-permute-done.1.refs_7_ = bf16[128,128]{1,0:T(8,128)(2,1)S(1)} collective-permute-done((bf16[128,128]{1,0:T(8,128)(2,1)S(1)}, bf16[128,128]{1,0:T(8,128)(2,1)S(1)}, u32[]{:S(2)}, u32[]{:S(2)}) %collective-permute-start.1) | collective-permute-done | bytes 32800 | tf_op jit(solution)/shard_map/ppermute | solution.py:424
  13.6 2.5 %shard_map.86 = (bf16[3,384,384]{2,1,0:T(8,128)(2,1)S(1)}, bf16[3,192,384]{2,1,0:T(8,128)(2,1)S(1)}, bf16[3,64,256]{2,1,0:T(8,128)(2,1)S(1)}, f32[304,128]{1,0:T(8,128)S(1)}, f32[304,128]{1,0:T(8,128)S(1)}) custom-call(s32[4,3]{1,0:T(4,128)S(1)} %get-tuple-element.39.rows.refs_0_, bf16[3,128,256]{2,1,0:T(8,128)(2,1)S(1)} %get-tuple-element.41.fields.refs_1_, ...), custom_call_target="tpu_custom_call" | custom-call | tf_op jit(solution)/shard_map/pallas_call | solution.py:437
  16.2 0.0 collective-permute-done.3.refs_7_
  16.2 0.1 collective-permute-start.4
  16.3 1.4 %collective-permute-done.4 = f32[304,128]{1,0:T(8,128)S(1)} collective-permute-done((f32[304,128]{1,0:T(8,128)S(1)}, f32[304,128]{1,0:T(8,128)S(1)}, u32[]{:S(2)}, u32[]{:S(2)}) %collective-permute-start.4) | collective-permute-done | bytes 155680 | tf_op jit(solution)/shard_map/ppermute | solution.py:450
  17.7 2.1 %collective-permute-start.5 = (bf16[304,128]{1,0:T(8,128)(2,1)S(1)}, bf16[304,128]{1,0:T(8,128)(2,1)S(1)}, u32[]{:S(2)}, u32[]{:S(2)}) collective-permute-start(bf16[304,128]{1,0:T(8,128)(2,1)S(1)} %add_convert_fusion.1), channel_id=1, source_target_pairs={{0,8},{4,12},{8,0},{12,4},{1,9},{5,13},{9,1},{13,5},{2,10},{6,14},... | collective-permute-start | bytes 233480 | tf_op jit(solution)/shard_map/ppermute | solution.py:476
  19.7 3.3 %shard_map.87 = (f32[3,64,256]{2,1,0:T(8,128)S(1)}, bf16[64,128]{1,0:T(8,128)(2,1)S(1)}, bf16[1,3,64,256]{3,2,1,0:T(8,128)(2,1)}) custom-call(s32[4,3]{1,0:T(4,128)S(1)} %get-tuple-element.39.rows.refs_0_, bf16[976,128]{1,0:T(8,128)(2,1)S(1)} %get-tuple-element.40.shared.refs_2_.refs_1_, bf16[192,384]{1,0:T(8,128)(2,1)S(1)} %get-tuple-element.42.refs_3_.refs_2_, ...), custom_call_target="tpu_custom_call" | custom-call | tf_op jit(solution)/shard_map/pallas_call | solution.py:454
  23.1 1.0 %collective-permute-done.5 = bf16[304,128]{1,0:T(8,128)(2,1)S(1)} collective-permute-done((bf16[304,128]{1,0:T(8,128)(2,1)S(1)}, bf16[304,128]{1,0:T(8,128)(2,1)S(1)}, u32[]{:S(2)}, u32[]{:S(2)}) %collective-permute-start.5) | collective-permute-done | bytes 77856 | tf_op jit(solution)/shard_map/ppermute | solution.py:476
  24.1 0.1 collective-permute-start.6
  24.1 2.6 %collective-permute-start.7 = (bf16[64,128]{1,0:T(8,128)(2,1)S(1)}, bf16[64,128]{1,0:T(8,128)(2,1)S(1)}, u32[]{:S(2)}, u32[]{:S(2)}) collective-permute-start(bf16[64,128]{1,0:T(8,128)(2,1)S(1)} %get-tuple-element.66.refs_3_), channel_id=1, source_target_pairs={{12,0},{8,4},{4,8},{0,12},{13,1},{9,5},{5,9},{1,13},{14,2},{10,6},... | collective-permute-start | bytes 49160 | tf_op jit(solution)/shard_map/ppermute | solution.py:488
  26.7 0.9 %collective-permute-start.8 = (bf16[64,128]{1,0:T(8,128)(2,1)S(1)}, bf16[64,128]{1,0:T(8,128)(2,1)S(1)}, u32[]{:S(2)}, u32[]{:S(2)}) collective-permute-start(bf16[64,128]{1,0:T(8,128)(2,1)S(1)} %get-tuple-element.66.refs_3_), channel_id=1, source_target_pairs={{8,0},{12,4},{0,8},{4,12},{9,1},{13,5},{1,9},{5,13},{10,2},{14,6},... | collective-permute-start | bytes 49160 | tf_op jit(solution)/shard_map/ppermute | solution.py:488
  27.6 1.4 %collective-permute-done.6 = bf16[368,128]{1,0:T(8,128)(2,1)S(1)} collective-permute-done((bf16[368,128]{1,0:T(8,128)(2,1)S(1)}, bf16[368,128]{1,0:T(8,128)(2,1)S(1)}, u32[]{:S(2)}, u32[]{:S(2)}) %collective-permute-start.6) | collective-permute-done | bytes 94240 | tf_op jit(solution)/shard_map/ppermute | solution.py:473
  29.1 0.7 %collective-permute-done.7.refs_0_ = bf16[64,128]{1,0:T(8,128)(2,1)S(1)} collective-permute-done((bf16[64,128]{1,0:T(8,128)(2,1)S(1)}, bf16[64,128]{1,0:T(8,128)(2,1)S(1)}, u32[]{:S(2)}, u32[]{:S(2)}) %collective-permute-start.7) | collective-permute-done | bytes 16416 | tf_op jit(solution)/shard_map/ppermute | solution.py:488
  29.8 1.6 %collective-permute-done.8.refs_1_ = bf16[64,128]{1,0:T(8,128)(2,1)S(1)} collective-permute-done((bf16[64,128]{1,0:T(8,128)(2,1)S(1)}, bf16[64,128]{1,0:T(8,128)(2,1)S(1)}, u32[]{:S(2)}, u32[]{:S(2)}) %collective-permute-start.8) | collective-permute-done | bytes 16416 | tf_op jit(solution)/shard_map/ppermute | solution.py:488
  31.4 1.0 %shard_map.88 = bf16[1,3,64,256]{3,2,1,0:T(8,128)(2,1)} custom-call(f32[3,64,256]{2,1,0:T(8,128)S(1)} %get-tuple-element.58.base, bf16[64,128]{1,0:T(8,128)(2,1)S(1)} %collective-permute-done.7.refs_0_, bf16[64,128]{1,0:T(8,128)(2,1)S(1)} %collective-permute-done.8.refs_1_, bf16[64,128]{1,0:T(8,128)(2,1)S(1)} %slice.9.refs_2_, ...), custom_call_target="tpu_custom_call" | custom-call | tf_op jit(solution)/shard_map/pallas_call | solution.py:490
  32.4 0.3 %collective-permute-done.9.theirs = f32[304,128]{1,0:T(8,128)S(1)} collective-permute-done((f32[304,128]{1,0:T(8,128)S(1)}, f32[304,128]{1,0:T(8,128)S(1)}, u32[]{:S(2)}, u32[]{:S(2)}) %collective-permute-start.9) | collective-permute-done | bytes 155680 | tf_op jit(solution)/shard_map/ppermute | solution.py:499
  32.8 0.7 %shard_map.89 = (f32[9,64,128]{2,1,0:T(8,128)}, f32[1,64]{1,0:T(1,128)}) custom-call(f32[304,128]{1,0:T(8,128)S(1)} %add_multiply_fusion.mine, f32[304,128]{1,0:T(8,128)S(1)} %collective-permute-done.9.theirs), custom_call_target="tpu_custom_call" | custom-call | tf_op jit(solution)/shard_map/pallas_call | solution.py:495
  (7 shorter events, 0.1 us)
Async XLA Ops:
  2.2 14.0 %collective-permute-start.3 = (bf16[976,128]{1,0:T(8,128)(2,1)S(1)}, bf16[976,128]{1,0:T(8,128)(2,1)S(1)}, u32[]{:S(2)}, u32[]{:S(2)}) collective-permute-start(bf16[976,128]{1,0:T(8,128)(2,1)S(1)} %get-tuple-element.40.shared.refs_2_.refs_1_), channel_id=1, source_target_pairs={{0,2},{2,0},{1,3},{3,1},{4,6},{6,4},{5,7},{7,5},{8,10},{10,8},{9,1... | collective-permute-start | bytes 749576 | tf_op jit(solution)/shard_map/ppermute | solution.py:435
  5.2 6.1 %collective-permute-start = (bf16[128,128]{1,0:T(8,128)(2,1)S(1)}, bf16[128,128]{1,0:T(8,128)(2,1)S(1)}, u32[]{:S(2)}, u32[]{:S(2)}) collective-permute-start(bf16[128,128]{1,0:T(8,128)(2,1)S(1)} %get-tuple-element.45), channel_id=1, source_target_pairs={{0,12},{4,8},{8,4},{12,0},{1,13},{5,9},{9,5},{13,1},{2,14},{6,10},... | collective-permute-start | bytes 98312 | tf_op jit(solution)/shard_map/ppermute | solution.py:424
  8.8 4.8 %collective-permute-start.1 = (bf16[128,128]{1,0:T(8,128)(2,1)S(1)}, bf16[128,128]{1,0:T(8,128)(2,1)S(1)}, u32[]{:S(2)}, u32[]{:S(2)}) collective-permute-start(bf16[128,128]{1,0:T(8,128)(2,1)S(1)} %get-tuple-element.46), channel_id=1, source_target_pairs={{0,8},{4,12},{8,0},{12,4},{1,9},{5,13},{9,1},{13,5},{2,10},{6,14},... | collective-permute-start | bytes 98312 | tf_op jit(solution)/shard_map/ppermute | solution.py:424
  8.8 4.8 %collective-permute-start.2 = (bf16[128,128]{1,0:T(8,128)(2,1)S(1)}, bf16[128,128]{1,0:T(8,128)(2,1)S(1)}, u32[]{:S(2)}, u32[]{:S(2)}) collective-permute-start(bf16[128,128]{1,0:T(8,128)(2,1)S(1)} %get-tuple-element.47), channel_id=1, source_target_pairs={{0,4},{4,0},{8,12},{12,8},{1,5},{5,1},{9,13},{13,9},{2,6},{6,2},{1... | collective-permute-start | bytes 98312 | tf_op jit(solution)/shard_map/ppermute | solution.py:424
  16.2 1.4 %collective-permute-start.4 = (f32[304,128]{1,0:T(8,128)S(1)}, f32[304,128]{1,0:T(8,128)S(1)}, u32[]{:S(2)}, u32[]{:S(2)}) collective-permute-start(f32[304,128]{1,0:T(8,128)S(1)} %get-tuple-element.53), channel_id=1, source_target_pairs={{0,1},{1,0},{2,3},{3,2},{4,5},{5,4},{6,7},{7,6},{8,9},{9,8},{10,11... | collective-permute-start | bytes 466952 | tf_op jit(solution)/shard_map/ppermute | solution.py:450
  17.7 6.4 %collective-permute-start.5 = (bf16[304,128]{1,0:T(8,128)(2,1)S(1)}, bf16[304,128]{1,0:T(8,128)(2,1)S(1)}, u32[]{:S(2)}, u32[]{:S(2)}) collective-permute-start(bf16[304,128]{1,0:T(8,128)(2,1)S(1)} %add_convert_fusion.1), channel_id=1, source_target_pairs={{0,8},{4,12},{8,0},{12,4},{1,9},{5,13},{9,1},{13,5},{2,10},{6,14},... | collective-permute-start | bytes 233480 | tf_op jit(solution)/shard_map/ppermute | solution.py:476
  24.1 5.0 %collective-permute-start.6 = (bf16[368,128]{1,0:T(8,128)(2,1)S(1)}, bf16[368,128]{1,0:T(8,128)(2,1)S(1)}, u32[]{:S(2)}, u32[]{:S(2)}) collective-permute-start(bf16[368,128]{1,0:T(8,128)(2,1)S(1)} %pad_maximum_fusion), channel_id=1, source_target_pairs={{0,4},{4,0},{8,12},{12,8},{1,5},{5,1},{9,13},{13,9},{2,6},{6,2},{1... | collective-permute-start | bytes 282632 | tf_op jit(solution)/shard_map/ppermute | solution.py:473
  24.1 5.7 %collective-permute-start.7 = (bf16[64,128]{1,0:T(8,128)(2,1)S(1)}, bf16[64,128]{1,0:T(8,128)(2,1)S(1)}, u32[]{:S(2)}, u32[]{:S(2)}) collective-permute-start(bf16[64,128]{1,0:T(8,128)(2,1)S(1)} %get-tuple-element.66.refs_3_), channel_id=1, source_target_pairs={{12,0},{8,4},{4,8},{0,12},{13,1},{9,5},{5,9},{1,13},{14,2},{10,6},... | collective-permute-start | bytes 49160 | tf_op jit(solution)/shard_map/ppermute | solution.py:488
  26.7 4.6 %collective-permute-start.8 = (bf16[64,128]{1,0:T(8,128)(2,1)S(1)}, bf16[64,128]{1,0:T(8,128)(2,1)S(1)}, u32[]{:S(2)}, u32[]{:S(2)}) collective-permute-start(bf16[64,128]{1,0:T(8,128)(2,1)S(1)} %get-tuple-element.66.refs_3_), channel_id=1, source_target_pairs={{8,0},{12,4},{0,8},{4,12},{9,1},{13,5},{1,9},{5,13},{10,2},{14,6},... | collective-permute-start | bytes 49160 | tf_op jit(solution)/shard_map/ppermute | solution.py:488
  31.4 1.4 %collective-permute-start.9 = (f32[304,128]{1,0:T(8,128)S(1)}, f32[304,128]{1,0:T(8,128)S(1)}, u32[]{:S(2)}, u32[]{:S(2)}) collective-permute-start(f32[304,128]{1,0:T(8,128)S(1)} %add_multiply_fusion.mine), channel_id=1, source_target_pairs={{0,1},{1,0},{2,3},{3,2},{4,5},{5,4},{6,7},{7,6},{8,9},{9,8},{10,11... | collective-permute-start | bytes 466952 | tf_op jit(solution)/shard_map/ppermute | solution.py:499

commit v5 on v4

--- a/solution.py
+++ b/solution.py
@@ -28,9 +28,9 @@
 def halo_plans(count):
     if count == 4:
         return [
+            (lambda d: d ^ 1, ("side",)),
             (lambda d: 3 - d, ("side", "fold")),
             (lambda d: d ^ 2, ("corner",)),
-            (lambda d: d ^ 1, ("side",)),
             (None, ("corner",)),
         ]
     return [
@@ -108,55 +108,50 @@
     return lax.dot_general(lhs, rhs, (dims, ((), ())), preferred_element_type=F32)
 
 
-def message_views(ref, own):
-    taps = [ref.at[t * own : (t + 1) * own] for t in range(9)]
-    base = 9 * own
-    halves = [
-        [ref.at[base + (2 * k + h) * own : base + (2 * k + h + 1) * own] for h in range(2)] for k in range(SLOTS)
+def pack_kernel(rows_hbm, fields_hbm, weights_hbm, bias_hbm, cot_hbm, *refs, count, chans, joined):
+    n = len(halo_plans(count))
+    rows_out, fields_out, weights_out, bias_out, cot_out = refs[:5]
+    outs = refs[5 : 5 + n]
+    maps = refs[5 + n : 5 + 2 * n]
+    shares = list(refs[5 + 2 * n : -2])
+    rows, sem = refs[-2:]
+    own = weights_hbm.shape[1]
+    moves = [
+        (rows_hbm, rows),
+        (fields_hbm.at[0], fields_out),
+        (weights_hbm, weights_out),
+        (bias_hbm, bias_out),
+        (cot_hbm.at[0], cot_out),
     ]
-    at = base + 2 * SLOTS * own
-    return taps, halves, ref.at[at : at + 16]
-
-
-def pack_kernel(rows_hbm, fields_hbm, weights_hbm, bias_hbm, cot_hbm, *refs, count):
-    n = len(halo_plans(count))
-    rows_out, fields_out, shared = refs[:3]
-    outs = refs[3 : 3 + n]
-    maps = refs[3 + n : 3 + 2 * n]
-    rows, bias, sem = refs[3 + 2 * n :]
-    own = weights_hbm.shape[1]
-    taps, halves, pieces = message_views(shared, own)
-    get_rows = pltpu.make_async_copy(rows_hbm, rows, sem.at[0])
-    get_rows.start()
-    get_fields = pltpu.make_async_copy(fields_hbm.at[0], fields_out, sem.at[1])
-    get_fields.start()
-    get_bias = pltpu.make_async_copy(bias_hbm, bias, sem.at[2])
-    get_bias.start()
-    more = [pltpu.make_async_copy(weights_hbm.at[t], taps[t], sem.at[3 + t]) for t in range(9)]
-    for k in range(SLOTS):
-        for h in range(2):
-            source = cot_hbm.at[0, k, :, h * 128 : h * 128 + 128]
-            more.append(pltpu.make_async_copy(source, halves[k][h], sem.at[12 + 2 * k + h]))
-    for copy in more:
+    copies = [pltpu.make_async_copy(src, dst, sem.at[i]) for i, (src, dst) in enumerate(moves)]
+    for copy in copies:
         copy.start()
-    get_rows.wait()
+    copies[0].wait()
     position = lax.axis_index("tiles")
     plans = halo_plans(count)
     for plan, out in zip(plans, maps):
         out[...] = halo_map(rows, count, position, plan)
     put_rows = pltpu.make_async_copy(rows, rows_out, sem.at[0])
     put_rows.start()
-    get_bias.wait()
-    line = jnp.concatenate([bias[...], jnp.zeros((1, 128 - own), F32)], axis=1)
-    high = line.astype(BF16).astype(F32)
-    middle = (line - high).astype(BF16).astype(F32)
-    low = line - high - middle
-    pieces[...] = jnp.concatenate([high, middle, low, jnp.zeros((13, 128), F32)], axis=0).astype(BF16)
-    get_fields.wait()
+    copies[1].wait()
     cells = jnp.concatenate([fields_out[k] for k in range(SLOTS)], axis=1)
     for out, hits in zip(outs, maps):
-        out[...] = dot(cells, hits[...]).astype(BF16)
-    for copy in more:
+        out[:C, :] = dot(cells, hits[...]).astype(BF16)
+    copies[2].wait()
+    if joined:
+        shares = [outs[0].at[C:, :]]
+    chan = lax.axis_index("chan")
+    each = 128 // own
+    place = iota((1, 128), 1) // own
+    for step, share in enumerate(shares):
+        start = (chan + step + 1) % chans * own
+        for block in range(-(-9 // each)):
+            packed = jnp.zeros((own, 128), F32)
+            for j in range(min(each, 9 - block * each)):
+                tap = pltpu.roll(weights_out[block * each + j].astype(F32), (j * own + 128 - start) % 128, 1)
+                packed = jnp.where(place == j, tap, packed)
+            share[block * own : (block + 1) * own, :] = packed.astype(BF16)
+    for copy in copies[3:]:
         copy.wait()
     put_rows.wait()
 
@@ -174,9 +169,8 @@
     return full, at_top, above
 
 
-def window_kernel(rows, fields, shared, windows, spreads, kernel):
-    own = kernel.shape[0] // 3
-    taps, _, _ = message_views(shared, own)
+def window_kernel(rows, fields, weights, windows, spreads, gathers, kernel, back_kernel, turned):
+    own = weights.shape[1]
     full, _, above = slot_flags(rows)
     column = iota((1, FRAME), 1) % TS
     lane128 = iota((1, 128), 1)
@@ -193,23 +187,28 @@
         windows[k, :C] = jnp.where(column == 0, 0.0, pltpu.roll(centre, 1, 1)).astype(BF16)
         windows[k, C : 2 * C] = centre.astype(BF16)
         windows[k, 2 * C :] = jnp.where(column == TS - 1, 0.0, pltpu.roll(centre, FRAME - 1, 1)).astype(BF16)
-    p_at = iota((128, FRAME), 0)
-    frame_lane = iota((128, FRAME), 1)
-    for side in range(2):
-        for k in range(SLOTS):
-            p = p_at - (side * EAST + k * EDGE)
-            spot = jnp.where(p == 0, FRAME - TS, TS * (p - 1)) + side * (TS - 1)
-            hits = (p >= 0) & (p < EDGE) & (frame_lane == spot)
-            spreads[side, k] = jnp.where(hits, 1.0, 0.0).astype(BF16)
-    for a in range(3):
-        for b in range(3):
-            kernel[a * own : (a + 1) * own, b * C : (b + 1) * C] = taps[3 * a + b][...]
-
-
-def column_of(pieces, own):
-    eye = iota((own, 128), 0) == iota((own, 128), 1)
-    parts = pieces[...].astype(F32)
-    line = parts[0:1] + parts[1:2] + parts[2:3]
+    for refs, shape, halo_dim in ((spreads, (128, FRAME), 0), (gathers, (FRAME, 128), 1)):
+        p_at = iota(shape, halo_dim)
+        frame_lane = iota(shape, 1 - halo_dim)
+        for side in range(2):
+            for k in range(SLOTS):
+                p = p_at - (side * EAST + k * EDGE)
+                spot = jnp.where(p == 0, FRAME - TS, TS * (p - 1)) + side * (TS - 1)
+                hits = (p >= 0) & (p < EDGE) & (frame_lane == spot)
+                refs[side, k] = jnp.where(hits, 1.0, 0.0).astype(BF16)
+    stack = jnp.concatenate(
+        [jnp.concatenate([weights[3 * a + b] for b in range(3)], axis=1) for a in range(3)], axis=0
+    )
+    kernel[...] = stack
+    turned[...] = jnp.transpose(stack.astype(F32))
+    start = pl.multiple_of(lax.axis_index("chan") * own, own)
+    for b in range(3):
+        back_kernel[b * own : (b + 1) * own, :] = turned[pl.ds(b * C + start, own), :].astype(BF16)
+
+
+def column_of(line):
+    own = line.shape[1]
+    eye = iota((own, own), 0) == iota((own, own), 1)
     return jnp.sum(jnp.where(eye, line, 0.0), axis=1, keepdims=True)
 
 
@@ -235,23 +234,18 @@
     return jnp.concatenate([pltpu.roll(wide, FRAME - TS, 1), wide, pltpu.roll(wide, TS, 1)], axis=0).astype(BF16)
 
 
-def upstream_of(halves, k, full):
-    return jnp.concatenate([halves[k][0][...], halves[k][1][...]], axis=1).astype(F32) * full[k]
-
-
-def forward_kernel(rows, fields, shared, kernel, spreads, windows, *refs, n_halos, half_rows):
+def forward_kernel(rows, fields, bias, cot, kernel, spreads, windows, *refs, n_halos, half_rows):
     halos = refs[:n_halos]
-    full_windows, frames, result, keep, send = refs[n_halos:]
+    frames, slopes_out, result, keep, send = refs[n_halos:]
     own = kernel.shape[0] // 3
     full, at_top, _ = slot_flags(rows)
     start = pl.multiple_of(lax.axis_index("chan") * own, own)
     rep = lax.axis_index("rep")
     lane128 = iota((1, 128), 1)
-    _, halves, pieces = message_views(shared, own)
-    bias_column = column_of(pieces, own)
-    halo = halos[0][...].astype(F32)
+    bias_column = column_of(bias[...])
+    halo = halos[0][:C, :].astype(F32)
     for ref in halos[1:]:
-        halo = halo + ref[...].astype(F32)
+        halo = halo + ref[:C, :].astype(F32)
     turned = pltpu.roll(halo, 128 - FOLD, 1)
     fold = jnp.where(lane128 < TS, turned, 0.0)
     fold_left = jnp.where((lane128 > 0) & (lane128 < TS), pltpu.roll(turned, 1, 1), 0.0)
@@ -267,11 +261,11 @@
         right = windows[k, 2 * C :] + (east + jnp.concatenate([rest, at_top[k] * fold_right], axis=1)).astype(BF16)
         centre = windows[k, C : 2 * C] + jnp.concatenate([rest, at_top[k] * fold], axis=1).astype(BF16)
         window = jnp.concatenate([left, centre, right], axis=0)
-        full_windows[k] = window
-        up = upstream_of(halves, k, full)
+        up = cot[k].astype(F32) * full[k]
         gelu, slopes = activation(kernel[...], window, bias_column, up)
         result[k] = (full[k] * (fields[k, pl.ds(start, own), :].astype(F32) + gelu)).astype(BF16)
         slope_sum = slope_sum + slopes
+        slopes_out[k * own : (k + 1) * own, :] = slopes.astype(BF16)
         frame = frame_of(slopes)
         frames[k] = frame
         grads = grads + dot(frame, window, ((1,), (1,)))
@@ -286,37 +280,38 @@
     send[...] = jnp.where(rep == 0, high, low)
 
 
-def backward_kernel(rows, shared, kernel, spreads, windows, frames, result, *refs, n_others):
-    others = refs[:n_others]
-    base, edges, result_out, turned, sem = refs[n_others:]
-    own = kernel.shape[0] // 3
+def backward_kernel(rows, cot, back_kernel, gathers, frames, result, *refs, joined):
+    base, edges, result_out, turned, sem = refs[-5:]
+    n = (len(refs) - 5) // 2
+    own = cot.shape[1]
     put = pltpu.make_async_copy(result, result_out.at[0], sem)
     put.start()
     full, at_top, above = slot_flags(rows)
-    start = pl.multiple_of(lax.axis_index("chan") * own, own)
     column = iota((1, FRAME), 1) % TS
     lane128 = iota((1, 128), 1)
-    kernels = [kernel[...]]
-    columns, ups = [], []
-    for ref in others:
-        taps, halves, pieces = message_views(ref, own)
-        kernels.append(
+    each = 128 // own
+    back_kernels = [back_kernel[...]]
+    for ref in refs[:n]:
+        taps = ref.at[C:, :] if joined else ref
+        for block in range(-(-9 // each)):
+            turned[block * 128 : (block + 1) * 128, :] = jnp.transpose(
+                taps[block * own : (block + 1) * own, :].astype(F32)
+            )
+        back_kernels.append(
             jnp.concatenate(
-                [jnp.concatenate([taps[3 * a + b][...] for b in range(3)], axis=1) for a in range(3)], axis=0
-            )
+                [
+                    jnp.concatenate([turned[t * own : (t + 1) * own, :] for t in (b, 3 + b, 6 + b)], axis=1)
+                    for b in range(3)
+                ],
+                axis=0,
+            ).astype(BF16)
         )
-        columns.append(column_of(pieces, own))
-        ups.append(halves)
-    turned[...] = jnp.transpose(jnp.concatenate(kernels, axis=0).astype(F32)).astype(BF16)
-    back_kernel = jnp.concatenate([turned[pl.ds(b * C + start, own), :] for b in range(3)], axis=0)
     edge_sum = jnp.zeros((own, 128), F32)
     pads = []
     for k in range(SLOTS):
-        stack = [frames[k]]
-        for other_kernel, bias_column, halves in zip(kernels[1:], columns, ups):
-            _, slopes = activation(other_kernel, windows[k], bias_column, upstream_of(halves, k, full))
-            stack.append(frame_of(slopes))
-        spread = dot(back_kernel, jnp.concatenate(stack, axis=0))
+        spread = dot(back_kernels[0], frames[k])
+        for other_kernel, slopes in zip(back_kernels[1:], refs[n : 2 * n]):
+            spread = spread + dot(other_kernel, frame_of(slopes[k * own : (k + 1) * own, :].astype(F32)))
         first, second, third = spread[:own], spread[own : 2 * own], spread[2 * own :]
         pad = (
             second
@@ -324,12 +319,11 @@
             + jnp.where(column > 0, pltpu.roll(third, 1, 1), 0.0)
         )
         pads.append(pad)
-        edge_sum = edge_sum + dot(first.astype(BF16), spreads[0, k], ((1,), (1,)))
-        edge_sum = edge_sum + dot(third.astype(BF16), spreads[1, k], ((1,), (1,)))
+        edge_sum = edge_sum + dot(first.astype(BF16), gathers[0, k])
+        edge_sum = edge_sum + dot(third.astype(BF16), gathers[1, k])
         crest = jnp.where(lane128 < TS, pad[:, CELLS:], 0.0) * at_top[k]
         edge_sum = edge_sum + pltpu.roll(crest, FOLD, 1)
     edges[...] = edge_sum.astype(BF16)
-    _, halves, _ = message_views(shared, own)
     for k in range(SLOTS):
         first = pads[k][:, :128]
         second = pads[k][:, 128:CELLS]
@@ -338,7 +332,7 @@
                 ends = pads[l][:, CELLS:]
                 first = first + jnp.where(lane128 < TS, ends, 0.0) * above[l][k]
                 second = second + jnp.where(lane128 >= 128 - TS, ends, 0.0) * above[k][l]
-        base[k] = upstream_of(halves, k, full) + jnp.concatenate([first, second], axis=1)
+        base[k] = cot[k].astype(F32) * full[k] + jnp.concatenate([first, second], axis=1)
     put.wait()
 
 
@@ -391,77 +385,85 @@
     reps = lax.axis_size("rep")
     plans = halo_plans(count)
     n = len(plans)
-    shared_rows = 9 * own + 2 * SLOTS * own + 16
     half_rows = -(-(9 * own + 1) // 32) * 16
     swap = [(0, 1), (1, 0)]
+    joined = count == 4 and chans == 2
+    share_rows = -(-9 // (128 // own)) * own
 
     pinned = [
         pltpu.with_memory_space_constraint(x, pltpu.HBM)
         for x in (tile_rows, fields, weights, bias.reshape(1, own), cotangent)
     ]
-    rows, tiles, shared, *packed = call(
-        lambda *refs: pack_kernel(*refs, count=count),
+    heights = [C + share_rows * (joined and i == 0) for i in range(n)]
+    rows, tiles, taps, bias_line, cot, *packed = call(
+        lambda *refs: pack_kernel(*refs, count=count, chans=chans, joined=joined),
         [HBM] * 5,
         [
             struct(tile_rows.shape, jnp.int32),
             struct((SLOTS, C, CELLS), BF16),
-            struct((shared_rows, 128), BF16),
+            struct((9, own, C), BF16),
+            struct((1, own), F32),
+            struct((SLOTS, own, CELLS), BF16),
         ]
-        + [struct((C, 128), BF16)] * n
-        + [struct((SLOTS * CELLS, 128), BF16)] * n,
-        [
-            pltpu.SMEM(tile_rows.shape, jnp.int32),
-            pltpu.VMEM((1, own), F32),
-            pltpu.SemaphoreType.DMA((12 + 2 * SLOTS,)),
-        ],
+        + [struct((height, 128), BF16) for height in heights]
+        + [struct((SLOTS * CELLS, 128), BF16)] * n
+        + [struct((share_rows, 128), BF16)] * (0 if joined else chans - 1),
+        [pltpu.SMEM(tile_rows.shape, jnp.int32), pltpu.SemaphoreType.DMA((5,))],
     )(*pinned)
-    messages, maps = packed[:n], packed[n:]
+    messages, maps, shares = packed[:n], packed[n : 2 * n], packed[2 * n :]
     halos = []
-    for (route, _), message in zip(plans, messages):
+    for i, ((route, _), message) in enumerate(zip(plans, messages)):
         if route is None:
             halos.append(message)
+        elif joined and i == 0:
+            pairs = [(2 * d + c, 2 * route(d) + 1 - c) for d in range(count) for c in range(2)]
+            halos.append(lax.ppermute(message, ("tiles", "chan"), pairs))
         else:
-            halos.append(lax.ppermute(message, "tiles", [(i, route(i)) for i in range(count)]))
-
-    windows, spreads, kernel = call(
+            halos.append(lax.ppermute(message, "tiles", [(d, route(d)) for d in range(count)]))
+    ring = [[(c, (c + s) % chans) for c in range(chans)] for s in range(1, chans)]
+    others = [halos[0]] if joined else [lax.ppermute(x, "chan", pairs) for x, pairs in zip(shares, ring)]
+
+    windows, spreads, gathers, kernel, back_kernel = call(
         window_kernel,
         [SMEM] + [VMEM] * 2,
         [
             struct((SLOTS, 3 * C, FRAME), BF16),
             struct((2, SLOTS, 128, FRAME), BF16),
+            struct((2, SLOTS, FRAME, 128), BF16),
             struct((3 * own, 3 * C), BF16),
+            struct((3 * own, 3 * own), BF16),
         ],
-    )(rows, tiles, shared)
-    others = [lax.ppermute(shared, "chan", [(i, (i + s) % chans) for i in range(chans)]) for s in range(1, chans)]
-
-    windows, frames, result, keep, send = call(
+        [pltpu.VMEM((3 * C, 3 * own), F32)],
+    )(rows, tiles, taps)
+
+    frames, slopes, result, keep, send = call(
         lambda *refs: forward_kernel(*refs, n_halos=n, half_rows=half_rows),
-        [SMEM] + [VMEM] * (5 + n),
+        [SMEM] + [VMEM] * (6 + n),
         [
-            struct((SLOTS, 3 * C, FRAME), BF16),
             struct((SLOTS, 3 * own, FRAME), BF16),
+            struct((SLOTS * own, CELLS), BF16),
             struct((SLOTS, own, CELLS), BF16),
             struct((half_rows, 128), F32),
             struct((half_rows, 128), F32),
         ],
-    )(rows, tiles, shared, kernel, spreads, windows, *halos)
-
-    send, others = lax.optimization_barrier((send, others))
+    )(rows, tiles, bias_line, cot, kernel, spreads, windows, *halos)
+
     sums = keep + lax.ppermute(send, "rep", swap)
     rounded = sums.astype(BF16)
     frames, rounded = lax.optimization_barrier((frames, rounded))
+    met = [lax.ppermute(slopes, "chan", pairs) for pairs in ring]
 
     base, edges, result = call(
-        lambda *refs: backward_kernel(*refs, n_others=len(others)),
-        [SMEM] + [VMEM] * (6 + len(others)),
+        lambda *refs: backward_kernel(*refs, joined=joined),
+        [SMEM] + [VMEM] * (5 + 2 * len(met)),
         [
             struct((SLOTS, own, CELLS), F32),
             struct((own, 128), BF16),
             struct((1, SLOTS, own, CELLS), BF16),
         ],
-        [pltpu.VMEM((3 * C, 3 * own * chans), BF16), pltpu.SemaphoreType.DMA],
+        [pltpu.VMEM((share_rows // own * 128, own), F32), pltpu.SemaphoreType.DMA],
         out_specs=[VMEM, VMEM, HBM],
-    )(rows, shared, kernel, spreads, windows, frames, result, *others)
+    )(rows, cot, back_kernel, gathers, frames, result, *others, *met)
 
     merged = None
     routes = sum_routes(count)
@@ -482,7 +484,7 @@
     for i, (route, _) in enumerate(plans):
         if route is None:
             returned.append(edges)
-        elif merged is not None and i == 2:
+        elif merged is not None and i == 0:
             returned.append(merged)
         else:
             returned.append(lax.ppermute(edges, "tiles", [(route(j), j) for j in range(count)]))

time: 33.7 us -> 34.5 us (1.024)
  waiting for transfers between devices: 9.45 us -> 12.9 us
  Pallas kernels: 10.2 us -> 8.79 us
  starting transfers between devices: 13.1 us -> 11.9 us
    ppermute x4, waiting for transfers between devices: 3.05 us -> 7.44 us  [the longest x2 3.77 us: on_device(): lax.ppermute(message, 'tiles', [(d, route(d)) for d in range(count)])]
    ppermute x1, starting transfers between devices: 2.09 us -> 0.15 us  [on_device(): other = lax.ppermute(rounded, 'tiles', pairs)]
    pallas_call x2, Pallas kernels: 4.89 us -> 3.22 us  [the longest x1 1.75 us: on_device(): call(lambda *refs: backward_kernel(*refs, joined=joined), [SMEM] + [VMEM]...]
    ppermute x2, starting transfers between devices: 3.47 us -> 4.37 us  [on_device(): lax.ppermute(edges, 'tiles', [(route(j), j) for j in range(count)])]
    ppermute x1, waiting for transfers between devices: 1.41 us -> 0.61 us  [on_device(): lax.ppermute(jnp.concatenate([rounded, edges], axis=0), 'tiles', pairs)]
    ppermute x1, waiting for transfers between devices: 1.37 us -> 0.77 us  [on_device(): sums = keep + lax.ppermute(send, 'rep', swap)]
    ppermute x1, waiting for transfers between devices: 0.96 us -> 1.33 us  [on_device(): other = lax.ppermute(rounded, 'tiles', pairs)]
  transfers between devices with their start and end apart: 10 -> 10, of which waited for: 8 -> 8; matrix products, arithmetic and copies ran while one was open for 0% -> 0% of each run, Pallas kernels for 23% -> 12%
where the time goes in v5:
time: 34.5 us; the launch traced here: 34.3 us
  waiting for transfers between devices  12.9 us (37%)
  starting transfers between devices  11.9 us (34%)
  Pallas kernels  8.79 us (25%)
  between operations  0.72 us (2%)
    ppermute x2, starting transfers between devices, on_device(): lax.ppermute(edges, 'tiles', [(route(j), j) for j in range(count)])  4.37 us
    ppermute x1, starting transfers between devices, on_device(): halos.append(lax.ppermute(message, ('tiles', 'chan'), pairs))  4.02 us
    ppermute x2, waiting for transfers between devices, on_device(): lax.ppermute(message, 'tiles', [(d, route(d)) for d in range(count)])  3.77 us
    ppermute x1, waiting for transfers between devices, on_device(): met = [lax.ppermute(slopes, 'chan', pairs) for pairs in ring]  3.67 us
    ppermute x2, starting transfers between devices, on_device(): lax.ppermute(message, 'tiles', [(d, route(d)) for d in range(count)])  2.59 us
    pallas_call x1, Pallas kernels, on_device(): call(lambda *refs: forward_kernel(*refs, n_halos=n, half_rows=half_rows),...  2.53 us
    ppermute x2, waiting for transfers between devices, on_device(): lax.ppermute(edges, 'tiles', [(route(j), j) for j in range(count)])  2.38 us
    pallas_call x1, Pallas kernels, on_device(): call(lambda *refs: backward_kernel(*refs, joined=joined), [SMEM] + [VMEM]...  1.75 us
  transfers between devices with their start and end apart: 10, of which 8 were waited for; matrix products, arithmetic and copies ran while one was open for 0% of the time, Pallas kernels for 12%

profile of v5, /device:TPU:0, one launch (start us, length us, event | category | flops | bytes accessed | tf_op | source)
XLA Modules:
  0.0 34.3 jit_solution(8538472115865977206)
XLA Ops:
  0.6 1.5 %shard_map.84 = (s32[4,3]{1,0:T(4,128)S(1)}, bf16[3,128,256]{2,1,0:T(8,128)(2,1)S(1)}, bf16[9,64,128]{2,1,0:T(8,128)(2,1)S(1)}, f32[1,64]{1,0:T(1,128)S(1)}, bf1...) custom-call(s32[4,3]{1,0:T(4,128)} %refs_0_.1, ...), custom_call_target="tpu_custom_call" | custom-call | tf_op jit(solution)/shard_map/pallas_call | solution.py:398
  2.1 4.0 %collective-permute-start = (bf16[448,128]{1,0:T(8,128)(2,1)S(1)}, bf16[448,128]{1,0:T(8,128)(2,1)S(1)}, u32[]{:S(2)}, u32[]{:S(2)}) collective-permute-start(bf16[448,128]{1,0:T(8,128)(2,1)S(1)} %get-tuple-element.51), channel_id=1, source_target_pairs={{0,6},{2,4},{4,2},{6,0},{8,14},{10,12},{12,10},{14,8},{1,7},{3,5},... | collective-permute-start | bytes 344072 | tf_op jit(solution)/shard_map/ppermute | solution.py:420
  6.1 2.5 %collective-permute-start.1 = (bf16[128,128]{1,0:T(8,128)(2,1)S(1)}, bf16[128,128]{1,0:T(8,128)(2,1)S(1)}, u32[]{:S(2)}, u32[]{:S(2)}) collective-permute-start(bf16[128,128]{1,0:T(8,128)(2,1)S(1)} %get-tuple-element.52), channel_id=1, source_target_pairs={{0,12},{4,8},{8,4},{12,0},{1,13},{5,9},{9,5},{13,1},{2,14},{6,10},... | collective-permute-start | bytes 98312 | tf_op jit(solution)/shard_map/ppermute | solution.py:422
  8.6 0.1 collective-permute-start.2
  8.7 1.3 %shard_map.85 = (bf16[3,384,384]{2,1,0:T(8,128)(2,1)S(1)}, bf16[2,3,128,384]{3,2,1,0:T(8,128)(2,1)S(1)}, bf16[2,3,384,128]{3,2,1,0:T(8,128)(2,1)S(1)}, bf16[192,384]{1,0:T(8,128)(2,1)S(1)}, bf16[192,192]{1,0:T(8,128)(2,1)S(1)}) custom-call(s32[4,3]{1,0:T(4,128)S(1)} %get-tuple-element.41.rows.refs_0_, ...), custom_call_target="tpu_custom_call" | custom-call | tf_op jit(solution)/shard_map/pallas_call | solution.py:426
  10.0 2.5 %collective-permute-done.1.refs_8_ = bf16[128,128]{1,0:T(8,128)(2,1)S(1)} collective-permute-done((bf16[128,128]{1,0:T(8,128)(2,1)S(1)}, bf16[128,128]{1,0:T(8,128)(2,1)S(1)}, u32[]{:S(2)}, u32[]{:S(2)}) %collective-permute-start.1) | collective-permute-done | bytes 32800 | tf_op jit(solution)/shard_map/ppermute | solution.py:422
  12.5 1.3 %collective-permute-done.2.refs_9_ = bf16[128,128]{1,0:T(8,128)(2,1)S(1)} collective-permute-done((bf16[128,128]{1,0:T(8,128)(2,1)S(1)}, bf16[128,128]{1,0:T(8,128)(2,1)S(1)}, u32[]{:S(2)}, u32[]{:S(2)}) %collective-permute-start.2) | collective-permute-done | bytes 32800 | tf_op jit(solution)/shard_map/ppermute | solution.py:422
  13.8 0.0 collective-permute-done.refs_7_.refs_6_
  13.8 2.5 %shard_map.86 = (bf16[3,192,384]{2,1,0:T(8,128)(2,1)S(1)}, bf16[192,256]{1,0:T(8,128)(2,1)S(1)}, bf16[3,64,256]{2,1,0:T(8,128)(2,1)S(1)}, f32[304,128]{1,0:T(8,128)S(1)}, f32[304,128]{1,0:T(8,128)S(1)}) custom-call(s32[4,3]{1,0:T(4,128)S(1)} %get-tuple-element.41.rows.refs_0_, bf16[3,128,256]{2,1,0:T(8,128)(2,1)S(1)} %get-tuple-element.43.fields.refs_1_, ...), custom_call_target="tpu_custom_call" | custom-call | tf_op jit(solution)/shard_map/pallas_call | solution.py:439
  16.3 0.1 collective-permute-start.3
  16.4 0.6 %collective-permute-start.4 = (bf16[192,256]{1,0:T(8,128)(2,1)S(1)}, bf16[192,256]{1,0:T(8,128)(2,1)S(1)}, u32[]{:S(2)}, u32[]{:S(2)}) collective-permute-start(bf16[192,256]{1,0:T(8,128)(2,1)S(1)} %get-tuple-element.60), channel_id=1, source_target_pairs={{0,2},{2,0},{1,3},{3,1},{4,6},{6,4},{5,7},{7,5},{8,10},{10,8},{9,1... | collective-permute-start | bytes 294920 | tf_op jit(solution)/shard_map/ppermute | solution.py:454
  17.0 0.8 %collective-permute-done.3 = f32[304,128]{1,0:T(8,128)S(1)} collective-permute-done((f32[304,128]{1,0:T(8,128)S(1)}, f32[304,128]{1,0:T(8,128)S(1)}, u32[]{:S(2)}, u32[]{:S(2)}) %collective-permute-start.3) | collective-permute-done | bytes 155680 | tf_op jit(solution)/shard_map/ppermute | solution.py:451
  17.8 0.1 collective-permute-start.5
  17.9 3.7 %collective-permute-done.4.refs_7_ = bf16[192,256]{1,0:T(8,128)(2,1)S(1)} collective-permute-done((bf16[192,256]{1,0:T(8,128)(2,1)S(1)}, bf16[192,256]{1,0:T(8,128)(2,1)S(1)}, u32[]{:S(2)}, u32[]{:S(2)}) %collective-permute-start.4) | collective-permute-done | bytes 98336 | tf_op jit(solution)/shard_map/ppermute | solution.py:454
  21.6 1.7 %shard_map.87 = (f32[3,64,256]{2,1,0:T(8,128)S(1)}, bf16[64,128]{1,0:T(8,128)(2,1)S(1)}, bf16[1,3,64,256]{3,2,1,0:T(8,128)(2,1)}) custom-call(s32[4,3]{1,0:T(4,128)S(1)} %get-tuple-element.41.rows.refs_0_, bf16[3,64,256]{2,1,0:T(8,128)(2,1)S(1)} %get-tuple-element.42.refs_3_.refs_1_, bf16[192,192]{1,0:T(8,128)(2,1)S(1)} %get-tuple-element.45.refs_2_, ...), custom_call_target="tpu_custom_call" | custom-call | tf_op jit(solution)/shard_map/pallas_call | solution.py:456
  23.3 1.3 %collective-permute-done.5 = bf16[304,128]{1,0:T(8,128)(2,1)S(1)} collective-permute-done((bf16[304,128]{1,0:T(8,128)(2,1)S(1)}, bf16[304,128]{1,0:T(8,128)(2,1)S(1)}, u32[]{:S(2)}, u32[]{:S(2)}) %collective-permute-start.5) | collective-permute-done | bytes 77856 | tf_op jit(solution)/shard_map/ppermute | solution.py:478
  24.7 0.1 collective-permute-start.6
  24.8 1.9 %collective-permute-start.8 = (bf16[64,128]{1,0:T(8,128)(2,1)S(1)}, bf16[64,128]{1,0:T(8,128)(2,1)S(1)}, u32[]{:S(2)}, u32[]{:S(2)}) collective-permute-start(bf16[64,128]{1,0:T(8,128)(2,1)S(1)} %get-tuple-element.70.refs_3_), channel_id=1, source_target_pairs={{8,0},{12,4},{0,8},{4,12},{9,1},{13,5},{1,9},{5,13},{10,2},{14,6},... | collective-permute-start | bytes 49160 | tf_op jit(solution)/shard_map/ppermute | solution.py:490
  26.7 2.5 %collective-permute-start.7 = (bf16[64,128]{1,0:T(8,128)(2,1)S(1)}, bf16[64,128]{1,0:T(8,128)(2,1)S(1)}, u32[]{:S(2)}, u32[]{:S(2)}) collective-permute-start(bf16[64,128]{1,0:T(8,128)(2,1)S(1)} %get-tuple-element.70.refs_3_), channel_id=1, source_target_pairs={{12,0},{8,4},{4,8},{0,12},{13,1},{9,5},{5,9},{1,13},{14,2},{10,6},... | collective-permute-start | bytes 49160 | tf_op jit(solution)/shard_map/ppermute | solution.py:490
  29.2 0.6 %collective-permute-done.6 = bf16[368,128]{1,0:T(8,128)(2,1)S(1)} collective-permute-done((bf16[368,128]{1,0:T(8,128)(2,1)S(1)}, bf16[368,128]{1,0:T(8,128)(2,1)S(1)}, u32[]{:S(2)}, u32[]{:S(2)}) %collective-permute-start.6) | collective-permute-done | bytes 94240 | tf_op jit(solution)/shard_map/ppermute | solution.py:475
  29.8 2.4 %collective-permute-done.7.refs_1_ = bf16[64,128]{1,0:T(8,128)(2,1)S(1)} collective-permute-done((bf16[64,128]{1,0:T(8,128)(2,1)S(1)}, bf16[64,128]{1,0:T(8,128)(2,1)S(1)}, u32[]{:S(2)}, u32[]{:S(2)}) %collective-permute-start.7) | collective-permute-done | bytes 16416 | tf_op jit(solution)/shard_map/ppermute | solution.py:490
  32.2 1.0 %shard_map.88 = bf16[1,3,64,256]{3,2,1,0:T(8,128)(2,1)} custom-call(f32[3,64,256]{2,1,0:T(8,128)S(1)} %get-tuple-element.62.base, bf16[64,128]{1,0:T(8,128)(2,1)S(1)} %slice.9.refs_0_, bf16[64,128]{1,0:T(8,128)(2,1)S(1)} %collective-permute-done.7.refs_1_, bf16[64,128]{1,0:T(8,128)(2,1)S(1)} %collective-permute-done.8.refs_2_, ...), custom_call_target="tpu_custom_call" | custom-call | tf_op jit(solution)/shard_map/pallas_call | solution.py:492
  33.2 0.3 %collective-permute-done.9.theirs = f32[304,128]{1,0:T(8,128)S(1)} collective-permute-done((f32[304,128]{1,0:T(8,128)S(1)}, f32[304,128]{1,0:T(8,128)S(1)}, u32[]{:S(2)}, u32[]{:S(2)}) %collective-permute-start.9) | collective-permute-done | bytes 155680 | tf_op jit(solution)/shard_map/ppermute | solution.py:501
  33.6 0.7 %shard_map.89 = (f32[9,64,128]{2,1,0:T(8,128)}, f32[1,64]{1,0:T(1,128)}) custom-call(f32[304,128]{1,0:T(8,128)S(1)} %add_multiply_fusion.mine, f32[304,128]{1,0:T(8,128)S(1)} %collective-permute-done.9.theirs), custom_call_target="tpu_custom_call" | custom-call | tf_op jit(solution)/shard_map/pallas_call | solution.py:497
  (7 shorter events, 0.1 us)
Async XLA Ops:
  2.1 11.7 %collective-permute-start = (bf16[448,128]{1,0:T(8,128)(2,1)S(1)}, bf16[448,128]{1,0:T(8,128)(2,1)S(1)}, u32[]{:S(2)}, u32[]{:S(2)}) collective-permute-start(bf16[448,128]{1,0:T(8,128)(2,1)S(1)} %get-tuple-element.51), channel_id=1, source_target_pairs={{0,6},{2,4},{4,2},{6,0},{8,14},{10,12},{12,10},{14,8},{1,7},{3,5},... | collective-permute-start | bytes 344072 | tf_op jit(solution)/shard_map/ppermute | solution.py:420
  6.1 6.4 %collective-permute-start.1 = (bf16[128,128]{1,0:T(8,128)(2,1)S(1)}, bf16[128,128]{1,0:T(8,128)(2,1)S(1)}, u32[]{:S(2)}, u32[]{:S(2)}) collective-permute-start(bf16[128,128]{1,0:T(8,128)(2,1)S(1)} %get-tuple-element.52), channel_id=1, source_target_pairs={{0,12},{4,8},{8,4},{12,0},{1,13},{5,9},{9,5},{13,1},{2,14},{6,10},... | collective-permute-start | bytes 98312 | tf_op jit(solution)/shard_map/ppermute | solution.py:422
  8.6 5.2 %collective-permute-start.2 = (bf16[128,128]{1,0:T(8,128)(2,1)S(1)}, bf16[128,128]{1,0:T(8,128)(2,1)S(1)}, u32[]{:S(2)}, u32[]{:S(2)}) collective-permute-start(bf16[128,128]{1,0:T(8,128)(2,1)S(1)} %get-tuple-element.53), channel_id=1, source_target_pairs={{0,8},{4,12},{8,0},{12,4},{1,9},{5,13},{9,1},{13,5},{2,10},{6,14},... | collective-permute-start | bytes 98312 | tf_op jit(solution)/shard_map/ppermute | solution.py:422
  16.3 1.4 %collective-permute-start.3 = (f32[304,128]{1,0:T(8,128)S(1)}, f32[304,128]{1,0:T(8,128)S(1)}, u32[]{:S(2)}, u32[]{:S(2)}) collective-permute-start(f32[304,128]{1,0:T(8,128)S(1)} %get-tuple-element.57), channel_id=1, source_target_pairs={{0,1},{1,0},{2,3},{3,2},{4,5},{5,4},{6,7},{7,6},{8,9},{9,8},{10,11... | collective-permute-start | bytes 466952 | tf_op jit(solution)/shard_map/ppermute | solution.py:451
  16.4 5.2 %collective-permute-start.4 = (bf16[192,256]{1,0:T(8,128)(2,1)S(1)}, bf16[192,256]{1,0:T(8,128)(2,1)S(1)}, u32[]{:S(2)}, u32[]{:S(2)}) collective-permute-start(bf16[192,256]{1,0:T(8,128)(2,1)S(1)} %get-tuple-element.60), channel_id=1, source_target_pairs={{0,2},{2,0},{1,3},{3,1},{4,6},{6,4},{5,7},{7,5},{8,10},{10,8},{9,1... | collective-permute-start | bytes 294920 | tf_op jit(solution)/shard_map/ppermute | solution.py:454
  17.8 6.9 %collective-permute-start.5 = (bf16[304,128]{1,0:T(8,128)(2,1)S(1)}, bf16[304,128]{1,0:T(8,128)(2,1)S(1)}, u32[]{:S(2)}, u32[]{:S(2)}) collective-permute-start(bf16[304,128]{1,0:T(8,128)(2,1)S(1)} %add_convert_fusion.1), channel_id=1, source_target_pairs={{0,8},{4,12},{8,0},{12,4},{1,9},{5,13},{9,1},{13,5},{2,10},{6,14},... | collective-permute-start | bytes 233480 | tf_op jit(solution)/shard_map/ppermute | solution.py:478
  24.7 5.1 %collective-permute-start.6 = (bf16[368,128]{1,0:T(8,128)(2,1)S(1)}, bf16[368,128]{1,0:T(8,128)(2,1)S(1)}, u32[]{:S(2)}, u32[]{:S(2)}) collective-permute-start(bf16[368,128]{1,0:T(8,128)(2,1)S(1)} %pad_maximum_fusion), channel_id=1, source_target_pairs={{0,4},{4,0},{8,12},{12,8},{1,5},{5,1},{9,13},{13,9},{2,6},{6,2},{1... | collective-permute-start | bytes 282632 | tf_op jit(solution)/shard_map/ppermute | solution.py:475
  24.8 5.0 %collective-permute-start.8 = (bf16[64,128]{1,0:T(8,128)(2,1)S(1)}, bf16[64,128]{1,0:T(8,128)(2,1)S(1)}, u32[]{:S(2)}, u32[]{:S(2)}) collective-permute-start(bf16[64,128]{1,0:T(8,128)(2,1)S(1)} %get-tuple-element.70.refs_3_), channel_id=1, source_target_pairs={{8,0},{12,4},{0,8},{4,12},{9,1},{13,5},{1,9},{5,13},{10,2},{14,6},... | collective-permute-start | bytes 49160 | tf_op jit(solution)/shard_map/ppermute | solution.py:490
  26.7 5.5 %collective-permute-start.7 = (bf16[64,128]{1,0:T(8,128)(2,1)S(1)}, bf16[64,128]{1,0:T(8,128)(2,1)S(1)}, u32[]{:S(2)}, u32[]{:S(2)}) collective-permute-start(bf16[64,128]{1,0:T(8,128)(2,1)S(1)} %get-tuple-element.70.refs_3_), channel_id=1, source_target_pairs={{12,0},{8,4},{4,8},{0,12},{13,1},{9,5},{5,9},{1,13},{14,2},{10,6},... | collective-permute-start | bytes 49160 | tf_op jit(solution)/shard_map/ppermute | solution.py:490
  32.2 1.4 %collective-permute-start.9 = (f32[304,128]{1,0:T(8,128)S(1)}, f32[304,128]{1,0:T(8,128)S(1)}, u32[]{:S(2)}, u32[]{:S(2)}) collective-permute-start(f32[304,128]{1,0:T(8,128)S(1)} %add_multiply_fusion.mine), channel_id=1, source_target_pairs={{0,1},{1,0},{2,3},{3,2},{4,5},{5,4},{6,7},{7,6},{8,9},{9,8},{10,11... | collective-permute-start | bytes 466952 | tf_op jit(solution)/shard_map/ppermute | solution.py:501

commit v6 on v4

--- a/solution.py
+++ b/solution.py
@@ -28,9 +28,9 @@
 def halo_plans(count):
     if count == 4:
         return [
+            (lambda d: d ^ 1, ("side",)),
             (lambda d: 3 - d, ("side", "fold")),
             (lambda d: d ^ 2, ("corner",)),
-            (lambda d: d ^ 1, ("side",)),
             (None, ("corner",)),
         ]
     return [
@@ -40,12 +40,6 @@
         (lambda d: (count - d) % count, ("corner_west",)),
         (lambda d: (2 * count - 2 - d) % count, ("corner_east",)),
     ]
-
-
-def sum_routes(count):
-    if count == 4:
-        return [lambda d: d ^ 2, lambda d: d ^ 1]
-    return [lambda d, s=1 << i: d ^ s for i in range(count.bit_length() - 1)]
 
 
 def halo_sources(rows, count, source, target, roles):
@@ -121,9 +115,11 @@
 def pack_kernel(rows_hbm, fields_hbm, weights_hbm, bias_hbm, cot_hbm, *refs, count):
     n = len(halo_plans(count))
     rows_out, fields_out, shared = refs[:3]
-    outs = refs[3 : 3 + n]
-    maps = refs[3 + n : 3 + 2 * n]
-    rows, bias, sem = refs[3 + 2 * n :]
+    maps = refs[3 : 3 + n]
+    outs = refs[3 + n : -3]
+    if count == 4:
+        outs = [outs[0].at[:C, :], outs[0].at[C:, :], *outs[1:]]
+    rows, bias, sem = refs[-3:]
     own = weights_hbm.shape[1]
     taps, halves, pieces = message_views(shared, own)
     get_rows = pltpu.make_async_copy(rows_hbm, rows, sem.at[0])
@@ -174,9 +170,21 @@
     return full, at_top, above
 
 
-def window_kernel(rows, fields, shared, windows, spreads, kernel):
+def turn(stack, turned):
+    own = stack.shape[0] // 3
+    start = pl.multiple_of(lax.axis_index("chan") * own, own)
+    turned[...] = jnp.transpose(stack.astype(F32))
+    return jnp.concatenate([turned[pl.ds(b * C + start, own), :] for b in range(3)], axis=0).astype(BF16)
+
+
+def stack_of(taps):
+    return jnp.concatenate(
+        [jnp.concatenate([taps[3 * a + b][...] for b in range(3)], axis=1) for a in range(3)], axis=0
+    )
+
+
+def window_kernel(rows, fields, shared, windows, spreads, gathers, kernel, back_kernel, turned):
     own = kernel.shape[0] // 3
-    taps, _, _ = message_views(shared, own)
     full, _, above = slot_flags(rows)
     column = iota((1, FRAME), 1) % TS
     lane128 = iota((1, 128), 1)
@@ -193,17 +201,18 @@
         windows[k, :C] = jnp.where(column == 0, 0.0, pltpu.roll(centre, 1, 1)).astype(BF16)
         windows[k, C : 2 * C] = centre.astype(BF16)
         windows[k, 2 * C :] = jnp.where(column == TS - 1, 0.0, pltpu.roll(centre, FRAME - 1, 1)).astype(BF16)
-    p_at = iota((128, FRAME), 0)
-    frame_lane = iota((128, FRAME), 1)
-    for side in range(2):
-        for k in range(SLOTS):
-            p = p_at - (side * EAST + k * EDGE)
-            spot = jnp.where(p == 0, FRAME - TS, TS * (p - 1)) + side * (TS - 1)
-            hits = (p >= 0) & (p < EDGE) & (frame_lane == spot)
-            spreads[side, k] = jnp.where(hits, 1.0, 0.0).astype(BF16)
-    for a in range(3):
-        for b in range(3):
-            kernel[a * own : (a + 1) * own, b * C : (b + 1) * C] = taps[3 * a + b][...]
+    for refs, shape, halo_dim in ((spreads, (128, FRAME), 0), (gathers, (FRAME, 128), 1)):
+        p_at = iota(shape, halo_dim)
+        frame_lane = iota(shape, 1 - halo_dim)
+        for side in range(2):
+            for k in range(SLOTS):
+                p = p_at - (side * EAST + k * EDGE)
+                spot = jnp.where(p == 0, FRAME - TS, TS * (p - 1)) + side * (TS - 1)
+                hits = (p >= 0) & (p < EDGE) & (frame_lane == spot)
+                refs[side, k] = jnp.where(hits, 1.0, 0.0).astype(BF16)
+    stack = stack_of(message_views(shared, own)[0])
+    kernel[...] = stack
+    back_kernel[...] = turn(stack, turned)
 
 
 def column_of(pieces, own):
@@ -286,37 +295,37 @@
     send[...] = jnp.where(rep == 0, high, low)
 
 
-def backward_kernel(rows, shared, kernel, spreads, windows, frames, result, *refs, n_others):
-    others = refs[:n_others]
-    base, edges, result_out, turned, sem = refs[n_others:]
-    own = kernel.shape[0] // 3
+def other_kernel(rows, windows, *refs):
+    n = (len(refs) - 1) // 3
+    turned = refs[-1]
+    full = slot_flags(rows)[0]
+    for ref, frames, back_kernel in zip(refs[:n], refs[n : 2 * n], refs[2 * n : 3 * n]):
+        own = back_kernel.shape[0] // 3
+        taps, halves, pieces = message_views(ref, own)
+        stack = stack_of(taps)
+        bias_column = column_of(pieces, own)
+        for k in range(SLOTS):
+            _, slopes = activation(stack, windows[k], bias_column, upstream_of(halves, k, full))
+            frames[k] = frame_of(slopes)
+        back_kernel[...] = turn(stack, turned)
+
+
+def backward_kernel(rows, shared, gathers, result, *refs):
+    base, edges, result_out, sem = refs[-4:]
+    n = (len(refs) - 4) // 2
+    frames, back_kernels = refs[:n], refs[n : 2 * n]
+    own = back_kernels[0].shape[0] // 3
     put = pltpu.make_async_copy(result, result_out.at[0], sem)
     put.start()
     full, at_top, above = slot_flags(rows)
-    start = pl.multiple_of(lax.axis_index("chan") * own, own)
     column = iota((1, FRAME), 1) % TS
     lane128 = iota((1, 128), 1)
-    kernels = [kernel[...]]
-    columns, ups = [], []
-    for ref in others:
-        taps, halves, pieces = message_views(ref, own)
-        kernels.append(
-            jnp.concatenate(
-                [jnp.concatenate([taps[3 * a + b][...] for b in range(3)], axis=1) for a in range(3)], axis=0
-            )
-        )
-        columns.append(column_of(pieces, own))
-        ups.append(halves)
-    turned[...] = jnp.transpose(jnp.concatenate(kernels, axis=0).astype(F32)).astype(BF16)
-    back_kernel = jnp.concatenate([turned[pl.ds(b * C + start, own), :] for b in range(3)], axis=0)
     edge_sum = jnp.zeros((own, 128), F32)
     pads = []
     for k in range(SLOTS):
-        stack = [frames[k]]
-        for other_kernel, bias_column, halves in zip(kernels[1:], columns, ups):
-            _, slopes = activation(other_kernel, windows[k], bias_column, upstream_of(halves, k, full))
-            stack.append(frame_of(slopes))
-        spread = dot(back_kernel, jnp.concatenate(stack, axis=0))
+        spread = dot(back_kernels[0][...], frames[0][k])
+        for frame, back_kernel in zip(frames[1:], back_kernels[1:]):
+            spread = spread + dot(back_kernel[...], frame[k])
         first, second, third = spread[:own], spread[own : 2 * own], spread[2 * own :]
         pad = (
             second
@@ -324,8 +333,8 @@
             + jnp.where(column > 0, pltpu.roll(third, 1, 1), 0.0)
         )
         pads.append(pad)
-        edge_sum = edge_sum + dot(first.astype(BF16), spreads[0, k], ((1,), (1,)))
-        edge_sum = edge_sum + dot(third.astype(BF16), spreads[1, k], ((1,), (1,)))
+        edge_sum = edge_sum + dot(first.astype(BF16), gathers[0, k])
+        edge_sum = edge_sum + dot(third.astype(BF16), gathers[1, k])
         crest = jnp.where(lane128 < TS, pad[:, CELLS:], 0.0) * at_top[k]
         edge_sum = edge_sum + pltpu.roll(crest, FOLD, 1)
     edges[...] = edge_sum.astype(BF16)
@@ -399,6 +408,7 @@
         pltpu.with_memory_space_constraint(x, pltpu.HBM)
         for x in (tile_rows, fields, weights, bias.reshape(1, own), cotangent)
     ]
+    heights = [2 * C, C, C] if count == 4 else [C] * n
     rows, tiles, shared, *packed = call(
         lambda *refs: pack_kernel(*refs, count=count),
         [HBM] * 5,
@@ -407,36 +417,42 @@
             struct((SLOTS, C, CELLS), BF16),
             struct((shared_rows, 128), BF16),
         ]
-        + [struct((C, 128), BF16)] * n
-        + [struct((SLOTS * CELLS, 128), BF16)] * n,
+        + [struct((SLOTS * CELLS, 128), BF16)] * n
+        + [struct((height, 128), BF16) for height in heights],
         [
             pltpu.SMEM(tile_rows.shape, jnp.int32),
             pltpu.VMEM((1, own), F32),
             pltpu.SemaphoreType.DMA((12 + 2 * SLOTS,)),
         ],
     )(*pinned)
-    messages, maps = packed[:n], packed[n:]
-    halos = []
-    for (route, _), message in zip(plans, messages):
-        if route is None:
-            halos.append(message)
-        else:
-            halos.append(lax.ppermute(message, "tiles", [(i, route(i)) for i in range(count)]))
-
-    windows, spreads, kernel = call(
+    maps, messages = packed[:n], packed[n:]
+
+    def move(x, route):
+        return lax.ppermute(x, "tiles", [(i, route(i)) for i in range(count)])
+
+    if count == 4:
+        near = move(messages[0], lambda d: d ^ 1)
+        halos = [near[:C], move(messages[1] + near[C:], lambda d: d ^ 2), messages[2]]
+    else:
+        halos = [move(message, route) for message, (route, _) in zip(messages, plans)]
+    others = [lax.ppermute(shared, "chan", [(i, (i + s) % chans) for i in range(chans)]) for s in range(1, chans)]
+
+    windows, spreads, gathers, kernel, back_kernel = call(
         window_kernel,
         [SMEM] + [VMEM] * 2,
         [
             struct((SLOTS, 3 * C, FRAME), BF16),
             struct((2, SLOTS, 128, FRAME), BF16),
+            struct((2, SLOTS, FRAME, 128), BF16),
             struct((3 * own, 3 * C), BF16),
+            struct((3 * own, 3 * own), BF16),
         ],
+        [pltpu.VMEM((3 * C, 3 * own), F32)],
     )(rows, tiles, shared)
-    others = [lax.ppermute(shared, "chan", [(i, (i + s) % chans) for i in range(chans)]) for s in range(1, chans)]
 
     windows, frames, result, keep, send = call(
-        lambda *refs: forward_kernel(*refs, n_halos=n, half_rows=half_rows),
-        [SMEM] + [VMEM] * (5 + n),
+        lambda *refs: forward_kernel(*refs, n_halos=len(halos), half_rows=half_rows),
+        [SMEM] + [VMEM] * (5 + len(halos)),
         [
             struct((SLOTS, 3 * C, FRAME), BF16),
             struct((SLOTS, 3 * own, FRAME), BF16),
@@ -448,45 +464,46 @@
 
     send, others = lax.optimization_barrier((send, others))
     sums = keep + lax.ppermute(send, "rep", swap)
+    other_frames = call(
+        other_kernel,
+        [SMEM, VMEM] + [VMEM] * len(others),
+        [struct((SLOTS, 3 * own, FRAME), BF16)] * len(others) + [struct((3 * own, 3 * own), BF16)] * len(others),
+        [pltpu.VMEM((3 * C, 3 * own), F32)],
+    )(rows, windows, *others)
+    other_frames, other_back = other_frames[: len(others)], other_frames[len(others) :]
     rounded = sums.astype(BF16)
-    frames, rounded = lax.optimization_barrier((frames, rounded))
+    frames, rounded, other_frames = lax.optimization_barrier((frames, rounded, other_frames))
 
     base, edges, result = call(
-        lambda *refs: backward_kernel(*refs, n_others=len(others)),
-        [SMEM] + [VMEM] * (6 + len(others)),
+        backward_kernel,
+        [SMEM] + [VMEM] * (5 + 2 * len(others)),
         [
             struct((SLOTS, own, CELLS), F32),
             struct((own, 128), BF16),
             struct((1, SLOTS, own, CELLS), BF16),
         ],
-        [pltpu.VMEM((3 * C, 3 * own * chans), BF16), pltpu.SemaphoreType.DMA],
+        [pltpu.SemaphoreType.DMA],
         out_specs=[VMEM, VMEM, HBM],
-    )(rows, shared, kernel, spreads, windows, frames, result, *others)
-
-    merged = None
-    routes = sum_routes(count)
-    for step, route in enumerate(routes):
-        pairs = [(i, route(i)) for i in range(count)]
-        if step == 1:
-            rounded, edges = lax.optimization_barrier((rounded, edges))
-        if count == 4 and step == 1:
-            both = lax.ppermute(jnp.concatenate([rounded, edges], axis=0), "tiles", pairs)
-            other, merged = both[:half_rows], both[half_rows:]
-        else:
-            other = lax.ppermute(rounded, "tiles", pairs)
-        sums = rounded.astype(F32) + other.astype(F32)
-        rounded = sums.astype(BF16)
+    )(rows, shared, gathers, result, frames, *other_frames, back_kernel, *other_back)
+
+    if count == 4:
+        across = move(edges, lambda d: d ^ 2)
+        other = move(rounded, lambda d: d ^ 2)
+        rounded = (rounded.astype(F32) + other.astype(F32)).astype(BF16)
+        rounded, across = lax.optimization_barrier((rounded, across))
+        both = move(jnp.concatenate([rounded, edges, across], axis=0), lambda d: d ^ 1)
+        sums = rounded.astype(F32) + both[:half_rows].astype(F32)
+        returned = [both[half_rows : half_rows + own], both[half_rows + own :], across, edges]
+    else:
+        for step in range(count.bit_length() - 1):
+            other = move(rounded, lambda d: d ^ (1 << step))
+            sums = rounded.astype(F32) + other.astype(F32)
+            rounded = sums.astype(BF16)
+        returned = [
+            lax.ppermute(edges, "tiles", [(route(j), j) for j in range(count)]) for route, _ in plans
+        ]
     grad_scale = 1.0 / math.sqrt(reps * fields.shape[0] * count * SLOTS * CELLS)
     sums = sums * grad_scale
-    returned = []
-    for i, (route, _) in enumerate(plans):
-        if route is None:
-            returned.append(edges)
-        elif merged is not None and i == 2:
-            returned.append(merged)
-        else:
-            returned.append(lax.ppermute(edges, "tiles", [(route(j), j) for j in range(count)]))
-    sums, returned = lax.optimization_barrier((sums, returned))
     grad_fields = call(
         finish_kernel,
         [VMEM] * (1 + 2 * n),

time: 33.7 us -> 33.1 us (0.982)
    ppermute x1, starting transfers between devices: 3 us -> 1.49 us  [on_device(): lax.ppermute(shared, 'chan', [(i, (i + s) % chans) for i in range(chans)])]
    ppermute x1, waiting for transfers between devices: 1.37 us -> 0.01 us  [on_device(): sums = keep + lax.ppermute(send, 'rep', swap)]
    ppermute x7 -> x5, waiting for transfers between devices: 7.73 us -> 8.91 us  [move(): return lax.ppermute(x, 'tiles', [(i, route(i)) for i in range(count)])]
    ppermute x7 -> x5, starting transfers between devices: 10 us -> 11.1 us  [move(): return lax.ppermute(x, 'tiles', [(i, route(i)) for i in range(count)])]
    pallas_call x2 -> x3, Pallas kernels: 5.83 us -> 5.49 us  [the longest x1 2.52 us: on_device(): call(lambda *refs: forward_kernel(*refs, n_halos=len(halos), half_rows=ha...]
  transfers between devices with their start and end apart: 10 -> 8, of which waited for: 8 -> 6; matrix products, arithmetic and copies ran while one was open for 0% -> 0% of each run, Pallas kernels for 23% -> 24%
where the time goes in v6:
time: 33.1 us; the launch traced here: 32.9 us
  starting transfers between devices  12.8 us (39%)
  Pallas kernels  10.1 us (31%)
  waiting for transfers between devices  9.24 us (28%)
  between operations  0.73 us (2%)
    ppermute x5, starting transfers between devices, move(): return lax.ppermute(x, 'tiles', [(i, route(i)) for i in range(count)])  11.1 us
    ppermute x5, waiting for transfers between devices, move(): return lax.ppermute(x, 'tiles', [(i, route(i)) for i in range(count)])  8.91 us
    pallas_call x1, Pallas kernels, on_device(): call(lambda *refs: forward_kernel(*refs, n_halos=len(halos), half_rows=ha...  2.52 us
    pallas_call x1, Pallas kernels, on_device(): call(backward_kernel, [SMEM] + [VMEM] * (5 + 2 * len(others)), [struct((S...  1.55 us
    pallas_call x1, Pallas kernels, on_device(): call(lambda *refs: pack_kernel(*refs, count=count), [HBM] * 5, [struct(ti...  1.55 us
    ppermute x1, starting transfers between devices, on_device(): lax.ppermute(shared, 'chan', [(i, (i + s) % chans) for i in range(chans)])  1.49 us
    pallas_call x1, Pallas kernels, on_device(): call(other_kernel, [SMEM, VMEM] + [VMEM] * len(others), [struct((SLOTS, 3...  1.42 us
    pallas_call x1, Pallas kernels, on_device(): call(window_kernel, [SMEM] + [VMEM] * 2, [struct((SLOTS, 3 * C, FRAME), B...  1.27 us
  transfers between devices with their start and end apart: 8, of which 6 were waited for; matrix products, arithmetic and copies ran while one was open for 0% of the time, Pallas kernels for 24%

profile of v6, /device:TPU:0, one launch (start us, length us, event | category | flops | bytes accessed | tf_op | source)
XLA Modules:
  0.0 32.9 jit_solution(4036273412998558471)
XLA Ops:
  0.6 1.5 %shard_map.84 = (s32[4,3]{1,0:T(4,128)S(1)}, bf16[3,128,256]{2,1,0:T(8,128)(2,1)S(1)}, bf16[976,128]{1,0:T(8,128)(2,1)S(1)}, bf16[768,128]{1,0:T(8,128)(2,1)S(1)...) custom-call(s32[4,3]{1,0:T(4,128)} %refs_0_.1, ...), custom_call_target="tpu_custom_call" | custom-call | tf_op jit(solution)/shard_map/pallas_call | solution.py:412
  2.2 3.1 %collective-permute-start = (bf16[256,128]{1,0:T(8,128)(2,1)S(1)}, bf16[256,128]{1,0:T(8,128)(2,1)S(1)}, u32[]{:S(2)}, u32[]{:S(2)}) collective-permute-start(bf16[256,128]{1,0:T(8,128)(2,1)S(1)} %get-tuple-element.45), channel_id=1, source_target_pairs={{0,4},{4,0},{8,12},{12,8},{1,5},{5,1},{9,13},{13,9},{2,6},{6,2},{1... | collective-permute-start | bytes 196616 | tf_op jit(solution)/shard_map/ppermute | solution.py:431
  5.3 1.5 %collective-permute-start.2 = (bf16[976,128]{1,0:T(8,128)(2,1)S(1)}, bf16[976,128]{1,0:T(8,128)(2,1)S(1)}, u32[]{:S(2)}, u32[]{:S(2)}) collective-permute-start(bf16[976,128]{1,0:T(8,128)(2,1)S(1)} %get-tuple-element.39.shared.refs_2_), channel_id=1, source_target_pairs={{0,2},{2,0},{1,3},{3,1},{4,6},{6,4},{5,7},{7,5},{8,10},{10,8},{9,1... | collective-permute-start | bytes 749576 | tf_op jit(solution)/shard_map/ppermute | solution.py:438
  6.8 0.8 %collective-permute-done = bf16[256,128]{1,0:T(8,128)(2,1)S(1)} collective-permute-done((bf16[256,128]{1,0:T(8,128)(2,1)S(1)}, bf16[256,128]{1,0:T(8,128)(2,1)S(1)}, u32[]{:S(2)}, u32[]{:S(2)}) %collective-permute-start) | collective-permute-done | bytes 65568 | tf_op jit(solution)/shard_map/ppermute | solution.py:431
  7.5 3.1 %collective-permute-start.1 = (bf16[128,128]{1,0:T(8,128)(2,1)S(1)}, bf16[128,128]{1,0:T(8,128)(2,1)S(1)}, u32[]{:S(2)}, u32[]{:S(2)}) collective-permute-start(bf16[128,128]{1,0:T(8,128)(2,1)S(1)} %get-tuple-element.74), channel_id=1, source_target_pairs={{0,8},{4,12},{8,0},{12,4},{1,9},{5,13},{9,1},{13,5},{2,10},{6,14},... | collective-permute-start | bytes 98312 | tf_op jit(solution)/shard_map/ppermute | solution.py:431
  10.6 1.3 %shard_map.85 = (bf16[3,384,384]{2,1,0:T(8,128)(2,1)S(1)}, bf16[2,3,128,384]{3,2,1,0:T(8,128)(2,1)S(1)}, bf16[2,3,384,128]{3,2,1,0:T(8,128)(2,1)S(1)}, bf16[192,384]{1,0:T(8,128)(2,1)S(1)}, bf16[192,192]{1,0:T(8,128)(2,1)S(1)}) custom-call(s32[4,3]{1,0:T(4,128)S(1)} %get-tuple-element.38.rows.refs_0_, ...), custom_call_target="tpu_custom_call" | custom-call | tf_op jit(solution)/shard_map/pallas_call | solution.py:440
  11.9 0.6 %collective-permute-done.1.refs_7_ = bf16[128,128]{1,0:T(8,128)(2,1)S(1)} collective-permute-done((bf16[128,128]{1,0:T(8,128)(2,1)S(1)}, bf16[128,128]{1,0:T(8,128)(2,1)S(1)}, u32[]{:S(2)}, u32[]{:S(2)}) %collective-permute-start.1) | collective-permute-done | bytes 32800 | tf_op jit(solution)/shard_map/ppermute | solution.py:431
  12.5 2.5 %shard_map.86 = (bf16[3,384,384]{2,1,0:T(8,128)(2,1)S(1)}, bf16[3,192,384]{2,1,0:T(8,128)(2,1)S(1)}, bf16[3,64,256]{2,1,0:T(8,128)(2,1)S(1)}, f32[304,128]{1,0:T(8,128)S(1)}, f32[304,128]{1,0:T(8,128)S(1)}) custom-call(s32[4,3]{1,0:T(4,128)S(1)} %get-tuple-element.38.rows.refs_0_, bf16[3,128,256]{2,1,0:T(8,128)(2,1)S(1)} %get-tuple-element.40.fields.refs_1_, ...), custom_call_target="tpu_custom_call" | custom-call | tf_op jit(solution)/shard_map/pallas_call | solution.py:453
  15.1 0.0 collective-permute-done.2.refs_0_
  15.1 0.1 collective-permute-start.3
  15.1 1.4 %shard_map.87 = (bf16[3,192,384]{2,1,0:T(8,128)(2,1)S(1)}, bf16[192,192]{1,0:T(8,128)(2,1)S(1)}) custom-call(s32[4,3]{1,0:T(4,128)S(1)} %get-tuple-element.38.rows.refs_0_, bf16[3,384,384]{2,1,0:T(8,128)(2,1)S(1)} %get-tuple-element.53.windows, bf16[976,128]{1,0:T(8,128)(2,1)S(1)} %collective-permute-done.2.refs_0_), custom_call_target="tpu_custom_call" | custom-call | tf_op jit(solution)/shard_map/pallas_call | solution.py:467
  16.6 0.0 collective-permute-done.3
  16.6 3.0 %collective-permute-start.4 = (bf16[304,128]{1,0:T(8,128)(2,1)S(1)}, bf16[304,128]{1,0:T(8,128)(2,1)S(1)}, u32[]{:S(2)}, u32[]{:S(2)}) collective-permute-start(bf16[304,128]{1,0:T(8,128)(2,1)S(1)} %add_convert_fusion.1), channel_id=1, source_target_pairs={{0,8},{4,12},{8,0},{12,4},{1,9},{5,13},{9,1},{13,5},{2,10},{6,14},... | collective-permute-start | bytes 233480 | tf_op jit(solution)/shard_map/ppermute | solution.py:431
  19.6 1.6 %shard_map.88 = (f32[3,64,256]{2,1,0:T(8,128)S(1)}, bf16[64,128]{1,0:T(8,128)(2,1)S(1)}, bf16[1,3,64,256]{3,2,1,0:T(8,128)(2,1)}) custom-call(s32[4,3]{1,0:T(4,128)S(1)} %get-tuple-element.38.rows.refs_0_, bf16[976,128]{1,0:T(8,128)(2,1)S(1)} %get-tuple-element.39.shared.refs_2_, bf16[2,3,384,128]{3,2,1,0:T(8,128)(2,1)S(1)} %get-tuple-element.41.gathers, ...), custom_call_target="tpu_custom_call" | custom-call | tf_op jit(solution)/shard_map/pallas_call | solution.py:477
  21.2 0.1 collective-permute-start.5
  21.2 3.0 %collective-permute-done.4 = bf16[304,128]{1,0:T(8,128)(2,1)S(1)} collective-permute-done((bf16[304,128]{1,0:T(8,128)(2,1)S(1)}, bf16[304,128]{1,0:T(8,128)(2,1)S(1)}, u32[]{:S(2)}, u32[]{:S(2)}) %collective-permute-start.4) | collective-permute-done | bytes 77856 | tf_op jit(solution)/shard_map/ppermute | solution.py:431
  24.3 1.6 %collective-permute-done.5.refs_2_ = bf16[64,128]{1,0:T(8,128)(2,1)S(1)} collective-permute-done((bf16[64,128]{1,0:T(8,128)(2,1)S(1)}, bf16[64,128]{1,0:T(8,128)(2,1)S(1)}, u32[]{:S(2)}, u32[]{:S(2)}) %collective-permute-start.5) | collective-permute-done | bytes 16416 | tf_op jit(solution)/shard_map/ppermute | solution.py:431
  25.9 1.9 %collective-permute-start.6 = (bf16[432,128]{1,0:T(8,128)(2,1)S(1)}, bf16[432,128]{1,0:T(8,128)(2,1)S(1)}, u32[]{:S(2)}, u32[]{:S(2)}) collective-permute-start(bf16[432,128]{1,0:T(8,128)(2,1)S(1)} %pad_maximum_fusion), channel_id=1, source_target_pairs={{0,4},{4,0},{8,12},{12,8},{1,5},{5,1},{9,13},{13,9},{2,6},{6,2},{1... | collective-permute-start | bytes 331784 | tf_op jit(solution)/shard_map/ppermute | solution.py:431
  27.7 3.0 %collective-permute-done.6 = bf16[432,128]{1,0:T(8,128)(2,1)S(1)} collective-permute-done((bf16[432,128]{1,0:T(8,128)(2,1)S(1)}, bf16[432,128]{1,0:T(8,128)(2,1)S(1)}, u32[]{:S(2)}, u32[]{:S(2)}) %collective-permute-start.6) | collective-permute-done | bytes 110624 | tf_op jit(solution)/shard_map/ppermute | solution.py:431
  30.7 0.1 collective-permute-start.7
  30.8 1.0 %shard_map.89 = bf16[1,3,64,256]{3,2,1,0:T(8,128)(2,1)} custom-call(f32[3,64,256]{2,1,0:T(8,128)S(1)} %get-tuple-element.61.base, bf16[64,128]{1,0:T(8,128)(2,1)S(1)} %get-tuple-element.73.refs_0_, bf16[64,128]{1,0:T(8,128)(2,1)S(1)} %get-tuple-element.72.refs_1_, bf16[64,128]{1,0:T(8,128)(2,1)S(1)} %collective-permute-done.5.refs_2_, ...), custom_call_target="tpu_custom_call" | custom-call | tf_op jit(solution)/shard_map/pallas_call | solution.py:507
  31.8 0.3 collective-permute-done.7.theirs
  32.2 0.7 %shard_map.90 = (f32[9,64,128]{2,1,0:T(8,128)}, f32[1,64]{1,0:T(1,128)}) custom-call(f32[304,128]{1,0:T(8,128)S(1)} %add_multiply_fusion.mine, f32[304,128]{1,0:T(8,128)S(1)} %collective-permute-done.7.theirs), custom_call_target="tpu_custom_call" | custom-call | tf_op jit(solution)/shard_map/pallas_call | solution.py:512
  (6 shorter events, 0.1 us)
Async XLA Ops:
  2.2 5.3 %collective-permute-start = (bf16[256,128]{1,0:T(8,128)(2,1)S(1)}, bf16[256,128]{1,0:T(8,128)(2,1)S(1)}, u32[]{:S(2)}, u32[]{:S(2)}) collective-permute-start(bf16[256,128]{1,0:T(8,128)(2,1)S(1)} %get-tuple-element.45), channel_id=1, source_target_pairs={{0,4},{4,0},{8,12},{12,8},{1,5},{5,1},{9,13},{13,9},{2,6},{6,2},{1... | collective-permute-start | bytes 196616 | tf_op jit(solution)/shard_map/ppermute | solution.py:431
  5.3 9.8 %collective-permute-start.2 = (bf16[976,128]{1,0:T(8,128)(2,1)S(1)}, bf16[976,128]{1,0:T(8,128)(2,1)S(1)}, u32[]{:S(2)}, u32[]{:S(2)}) collective-permute-start(bf16[976,128]{1,0:T(8,128)(2,1)S(1)} %get-tuple-element.39.shared.refs_2_), channel_id=1, source_target_pairs={{0,2},{2,0},{1,3},{3,1},{4,6},{6,4},{5,7},{7,5},{8,10},{10,8},{9,1... | collective-permute-start | bytes 749576 | tf_op jit(solution)/shard_map/ppermute | solution.py:438
  7.5 5.0 %collective-permute-start.1 = (bf16[128,128]{1,0:T(8,128)(2,1)S(1)}, bf16[128,128]{1,0:T(8,128)(2,1)S(1)}, u32[]{:S(2)}, u32[]{:S(2)}) collective-permute-start(bf16[128,128]{1,0:T(8,128)(2,1)S(1)} %get-tuple-element.74), channel_id=1, source_target_pairs={{0,8},{4,12},{8,0},{12,4},{1,9},{5,13},{9,1},{13,5},{2,10},{6,14},... | collective-permute-start | bytes 98312 | tf_op jit(solution)/shard_map/ppermute | solution.py:431
  15.1 1.5 %collective-permute-start.3 = (f32[304,128]{1,0:T(8,128)S(1)}, f32[304,128]{1,0:T(8,128)S(1)}, u32[]{:S(2)}, u32[]{:S(2)}) collective-permute-start(f32[304,128]{1,0:T(8,128)S(1)} %get-tuple-element.52), channel_id=1, source_target_pairs={{0,1},{1,0},{2,3},{3,2},{4,5},{5,4},{6,7},{7,6},{8,9},{9,8},{10,11... | collective-permute-start | bytes 466952 | tf_op jit(solution)/shard_map/ppermute | solution.py:466
  16.6 7.7 %collective-permute-start.4 = (bf16[304,128]{1,0:T(8,128)(2,1)S(1)}, bf16[304,128]{1,0:T(8,128)(2,1)S(1)}, u32[]{:S(2)}, u32[]{:S(2)}) collective-permute-start(bf16[304,128]{1,0:T(8,128)(2,1)S(1)} %add_convert_fusion.1), channel_id=1, source_target_pairs={{0,8},{4,12},{8,0},{12,4},{1,9},{5,13},{9,1},{13,5},{2,10},{6,14},... | collective-permute-start | bytes 233480 | tf_op jit(solution)/shard_map/ppermute | solution.py:431
  21.2 4.7 %collective-permute-start.5 = (bf16[64,128]{1,0:T(8,128)(2,1)S(1)}, bf16[64,128]{1,0:T(8,128)(2,1)S(1)}, u32[]{:S(2)}, u32[]{:S(2)}) collective-permute-start(bf16[64,128]{1,0:T(8,128)(2,1)S(1)} %get-tuple-element.63.refs_3_), channel_id=1, source_target_pairs={{0,8},{4,12},{8,0},{12,4},{1,9},{5,13},{9,1},{13,5},{2,10},{6,14},... | collective-permute-start | bytes 49160 | tf_op jit(solution)/shard_map/ppermute | solution.py:431
  25.9 4.8 %collective-permute-start.6 = (bf16[432,128]{1,0:T(8,128)(2,1)S(1)}, bf16[432,128]{1,0:T(8,128)(2,1)S(1)}, u32[]{:S(2)}, u32[]{:S(2)}) collective-permute-start(bf16[432,128]{1,0:T(8,128)(2,1)S(1)} %pad_maximum_fusion), channel_id=1, source_target_pairs={{0,4},{4,0},{8,12},{12,8},{1,5},{5,1},{9,13},{13,9},{2,6},{6,2},{1... | collective-permute-start | bytes 331784 | tf_op jit(solution)/shard_map/ppermute | solution.py:431
  30.7 1.4 %collective-permute-start.7 = (f32[304,128]{1,0:T(8,128)S(1)}, f32[304,128]{1,0:T(8,128)S(1)}, u32[]{:S(2)}, u32[]{:S(2)}) collective-permute-start(f32[304,128]{1,0:T(8,128)S(1)} %add_multiply_fusion.mine), channel_id=1, source_target_pairs={{0,1},{1,0},{2,3},{3,2},{4,5},{5,4},{6,7},{7,6},{8,9},{9,8},{10,11... | collective-permute-start | bytes 466952 | tf_op jit(solution)/shard_map/ppermute | solution.py:516

commit v7 on v6

--- a/solution.py
+++ b/solution.py
@@ -248,13 +248,21 @@
     return jnp.concatenate([halves[k][0][...], halves[k][1][...]], axis=1).astype(F32) * full[k]
 
 
-def forward_kernel(rows, fields, shared, kernel, spreads, windows, *refs, n_halos, half_rows):
+def half_of(count):
+    position = lax.axis_index("tiles")
+    rep = lax.axis_index("rep")
+    if count == 4:
+        return (rep + position + position // 2) % 2
+    return rep
+
+
+def forward_kernel(rows, fields, shared, kernel, spreads, windows, *refs, n_halos, half_rows, count):
     halos = refs[:n_halos]
     full_windows, frames, result, keep, send = refs[n_halos:]
     own = kernel.shape[0] // 3
     full, at_top, _ = slot_flags(rows)
     start = pl.multiple_of(lax.axis_index("chan") * own, own)
-    rep = lax.axis_index("rep")
+    half = half_of(count)
     lane128 = iota((1, 128), 1)
     _, halves, pieces = message_views(shared, own)
     bias_column = column_of(pieces, own)
@@ -291,8 +299,8 @@
     blocks.append(jnp.zeros((2 * half_rows - 9 * own - 1, 128), F32))
     sums = jnp.concatenate(blocks, axis=0)
     low, high = sums[:half_rows], sums[half_rows:]
-    keep[...] = jnp.where(rep == 0, low, high)
-    send[...] = jnp.where(rep == 0, high, low)
+    keep[...] = jnp.where(half == 0, low, high)
+    send[...] = jnp.where(half == 0, high, low)
 
 
 def other_kernel(rows, windows, *refs):
@@ -362,11 +370,11 @@
         out[0, k] = (base[k] + total[:, k * CELLS : (k + 1) * CELLS]).astype(BF16)
 
 
-def gather_kernel(mine, theirs, weights_out, bias_out):
-    rep = lax.axis_index("rep")
+def gather_kernel(mine, theirs, weights_out, bias_out, *, count):
+    half = half_of(count)
     own = weights_out.shape[1]
-    low = jnp.where(rep == 0, mine[...], theirs[...])
-    high = jnp.where(rep == 0, theirs[...], mine[...])
+    low = jnp.where(half == 0, mine[...], theirs[...])
+    high = jnp.where(half == 0, theirs[...], mine[...])
     sums = jnp.concatenate([low, high], axis=0)
     for t in range(9):
         weights_out[t] = sums[t * own : (t + 1) * own]
@@ -451,7 +459,7 @@
     )(rows, tiles, shared)
 
     windows, frames, result, keep, send = call(
-        lambda *refs: forward_kernel(*refs, n_halos=len(halos), half_rows=half_rows),
+        lambda *refs: forward_kernel(*refs, n_halos=len(halos), half_rows=half_rows, count=count),
         [SMEM] + [VMEM] * (5 + len(halos)),
         [
             struct((SLOTS, 3 * C, FRAME), BF16),
@@ -487,12 +495,18 @@
     )(rows, shared, gathers, result, frames, *other_frames, back_kernel, *other_back)
 
     if count == 4:
-        across = move(edges, lambda d: d ^ 2)
-        other = move(rounded, lambda d: d ^ 2)
+
+        def cross(x, route):
+            pairs = [(2 * d + r, 2 * route(d) + 1 - r) for d in range(count) for r in range(2)]
+            return lax.ppermute(x, ("tiles", "rep"), pairs)
+
+        across = cross(edges, lambda d: d ^ 2)
+        beside = lax.ppermute(edges, "rep", swap)
+        other = cross(rounded, lambda d: d ^ 2)
         rounded = (rounded.astype(F32) + other.astype(F32)).astype(BF16)
-        rounded, across = lax.optimization_barrier((rounded, across))
-        both = move(jnp.concatenate([rounded, edges, across], axis=0), lambda d: d ^ 1)
+        both = cross(jnp.concatenate([rounded, beside, across], axis=0), lambda d: d ^ 1)
         sums = rounded.astype(F32) + both[:half_rows].astype(F32)
+        across = lax.ppermute(across, "rep", swap)
         returned = [both[half_rows : half_rows + own], both[half_rows + own :], across, edges]
     else:
         for step in range(count.bit_length() - 1):
@@ -510,7 +524,7 @@
         [struct((1, SLOTS, own, CELLS), BF16)],
     )(base, *returned, *maps)[0]
     grad_weights, grad_bias = call(
-        gather_kernel,
+        lambda *refs: gather_kernel(*refs, count=count),
         [VMEM, VMEM],
         [struct((9, own, C), F32), struct((1, own), F32)],
     )(sums, lax.ppermute(sums, "rep", swap))

time: 33.1 us -> 33 us (level)
  waiting for transfers between devices: 9.24 us -> 8.57 us
  starting transfers between devices: 12.8 us -> 13.3 us
    ppermute x5 -> x2, waiting for transfers between devices: 8.91 us -> 1.37 us  [move(): return lax.ppermute(x, 'tiles', [(i, route(i)) for i in range(count)])]
    ppermute x0 -> x5, waiting for transfers between devices: none -> 7.12 us  [the longest x3 7.11 us: cross(): return lax.ppermute(x, ('tiles', 'rep'), pairs)]
    ppermute x0 -> x5, starting transfers between devices: none -> 5.22 us  [the longest x3 5.09 us: cross(): return lax.ppermute(x, ('tiles', 'rep'), pairs)]
    ppermute x5 -> x2, starting transfers between devices: 11.1 us -> 6.19 us  [move(): return lax.ppermute(x, 'tiles', [(i, route(i)) for i in range(count)])]
  transfers between devices with their start and end apart: 8 -> 10, of which waited for: 6 -> 6; matrix products, arithmetic and copies ran while one was open for 0% -> 0% of each run, Pallas kernels for 24% -> 24%
where the time goes in v7:
time: 33 us; the launch traced here: 32.8 us
  starting transfers between devices  13.3 us (40%)
  Pallas kernels  10.1 us (31%)
  waiting for transfers between devices  8.57 us (26%)
  between operations  0.73 us (2%)
    ppermute x3, waiting for transfers between devices, cross(): return lax.ppermute(x, ('tiles', 'rep'), pairs)  7.11 us
    ppermute x2, starting transfers between devices, move(): return lax.ppermute(x, 'tiles', [(i, route(i)) for i in range(count)])  6.19 us
    ppermute x3, starting transfers between devices, cross(): return lax.ppermute(x, ('tiles', 'rep'), pairs)  5.09 us
    pallas_call x1, Pallas kernels, on_device(): call(lambda *refs: forward_kernel(*refs, n_halos=len(halos), half_rows=ha...  2.52 us
    pallas_call x1, Pallas kernels, on_device(): call(backward_kernel, [SMEM] + [VMEM] * (5 + 2 * len(others)), [struct((S...  1.55 us
    pallas_call x1, Pallas kernels, on_device(): call(lambda *refs: pack_kernel(*refs, count=count), [HBM] * 5, [struct(ti...  1.55 us
    ppermute x1, starting transfers between devices, on_device(): lax.ppermute(shared, 'chan', [(i, (i + s) % chans) for i in range(chans)])  1.49 us
    pallas_call x1, Pallas kernels, on_device(): call(other_kernel, [SMEM, VMEM] + [VMEM] * len(others), [struct((SLOTS, 3...  1.42 us
  transfers between devices with their start and end apart: 10, of which 6 were waited for; matrix products, arithmetic and copies ran while one was open for 0% of the time, Pallas kernels for 24%

profile of v7, /device:TPU:0, one launch (start us, length us, event | category | flops | bytes accessed | tf_op | source)
XLA Modules:
  0.0 32.8 jit_solution(3996617466949718817)
XLA Ops:
  0.6 1.5 %shard_map.84 = (s32[4,3]{1,0:T(4,128)S(1)}, bf16[3,128,256]{2,1,0:T(8,128)(2,1)S(1)}, bf16[976,128]{1,0:T(8,128)(2,1)S(1)}, bf16[768,128]{1,0:T(8,128)(2,1)S(1)...) custom-call(s32[4,3]{1,0:T(4,128)} %refs_0_.1, ...), custom_call_target="tpu_custom_call" | custom-call | tf_op jit(solution)/shard_map/pallas_call | solution.py:420
  2.2 3.1 %collective-permute-start = (bf16[256,128]{1,0:T(8,128)(2,1)S(1)}, bf16[256,128]{1,0:T(8,128)(2,1)S(1)}, u32[]{:S(2)}, u32[]{:S(2)}) collective-permute-start(bf16[256,128]{1,0:T(8,128)(2,1)S(1)} %get-tuple-element.43), channel_id=1, source_target_pairs={{0,4},{4,0},{8,12},{12,8},{1,5},{5,1},{9,13},{13,9},{2,6},{6,2},{1... | collective-permute-start | bytes 196616 | tf_op jit(solution)/shard_map/ppermute | solution.py:439
  5.3 1.5 %collective-permute-start.2 = (bf16[976,128]{1,0:T(8,128)(2,1)S(1)}, bf16[976,128]{1,0:T(8,128)(2,1)S(1)}, u32[]{:S(2)}, u32[]{:S(2)}) collective-permute-start(bf16[976,128]{1,0:T(8,128)(2,1)S(1)} %get-tuple-element.37.shared.refs_2_), channel_id=1, source_target_pairs={{0,2},{2,0},{1,3},{3,1},{4,6},{6,4},{5,7},{7,5},{8,10},{10,8},{9,1... | collective-permute-start | bytes 749576 | tf_op jit(solution)/shard_map/ppermute | solution.py:446
  6.8 0.8 %collective-permute-done = bf16[256,128]{1,0:T(8,128)(2,1)S(1)} collective-permute-done((bf16[256,128]{1,0:T(8,128)(2,1)S(1)}, bf16[256,128]{1,0:T(8,128)(2,1)S(1)}, u32[]{:S(2)}, u32[]{:S(2)}) %collective-permute-start) | collective-permute-done | bytes 65568 | tf_op jit(solution)/shard_map/ppermute | solution.py:439
  7.5 3.1 %collective-permute-start.1 = (bf16[128,128]{1,0:T(8,128)(2,1)S(1)}, bf16[128,128]{1,0:T(8,128)(2,1)S(1)}, u32[]{:S(2)}, u32[]{:S(2)}) collective-permute-start(bf16[128,128]{1,0:T(8,128)(2,1)S(1)} %get-tuple-element.70), channel_id=1, source_target_pairs={{0,8},{4,12},{8,0},{12,4},{1,9},{5,13},{9,1},{13,5},{2,10},{6,14},... | collective-permute-start | bytes 98312 | tf_op jit(solution)/shard_map/ppermute | solution.py:439
  10.6 1.3 %shard_map.85 = (bf16[3,384,384]{2,1,0:T(8,128)(2,1)S(1)}, bf16[2,3,128,384]{3,2,1,0:T(8,128)(2,1)S(1)}, bf16[2,3,384,128]{3,2,1,0:T(8,128)(2,1)S(1)}, bf16[192,384]{1,0:T(8,128)(2,1)S(1)}, bf16[192,192]{1,0:T(8,128)(2,1)S(1)}) custom-call(s32[4,3]{1,0:T(4,128)S(1)} %get-tuple-element.36.rows.refs_0_, ...), custom_call_target="tpu_custom_call" | custom-call | tf_op jit(solution)/shard_map/pallas_call | solution.py:448
  11.9 0.6 %collective-permute-done.1.refs_7_ = bf16[128,128]{1,0:T(8,128)(2,1)S(1)} collective-permute-done((bf16[128,128]{1,0:T(8,128)(2,1)S(1)}, bf16[128,128]{1,0:T(8,128)(2,1)S(1)}, u32[]{:S(2)}, u32[]{:S(2)}) %collective-permute-start.1) | collective-permute-done | bytes 32800 | tf_op jit(solution)/shard_map/ppermute | solution.py:439
  12.5 2.5 %shard_map.86 = (bf16[3,384,384]{2,1,0:T(8,128)(2,1)S(1)}, bf16[3,192,384]{2,1,0:T(8,128)(2,1)S(1)}, bf16[3,64,256]{2,1,0:T(8,128)(2,1)S(1)}, f32[304,128]{1,0:T(8,128)S(1)}, f32[304,128]{1,0:T(8,128)S(1)}) custom-call(s32[4,3]{1,0:T(4,128)S(1)} %get-tuple-element.36.rows.refs_0_, bf16[3,128,256]{2,1,0:T(8,128)(2,1)S(1)} %get-tuple-element.38.fields.refs_1_, ...), custom_call_target="tpu_custom_call" | custom-call | tf_op jit(solution)/shard_map/pallas_call | solution.py:461
  15.1 0.0 collective-permute-done.2.refs_0_
  15.1 0.1 collective-permute-start.3
  15.1 1.4 %shard_map.87 = (bf16[3,192,384]{2,1,0:T(8,128)(2,1)S(1)}, bf16[192,192]{1,0:T(8,128)(2,1)S(1)}) custom-call(s32[4,3]{1,0:T(4,128)S(1)} %get-tuple-element.36.rows.refs_0_, bf16[3,384,384]{2,1,0:T(8,128)(2,1)S(1)} %get-tuple-element.51.windows, bf16[976,128]{1,0:T(8,128)(2,1)S(1)} %collective-permute-done.2.refs_0_), custom_call_target="tpu_custom_call" | custom-call | tf_op jit(solution)/shard_map/pallas_call | solution.py:475
  16.6 3.1 %collective-permute-start.4 = (bf16[304,128]{1,0:T(8,128)(2,1)S(1)}, bf16[304,128]{1,0:T(8,128)(2,1)S(1)}, u32[]{:S(2)}, u32[]{:S(2)}) collective-permute-start(bf16[304,128]{1,0:T(8,128)(2,1)S(1)} %add_convert_fusion.1), channel_id=1, source_target_pairs={{0,9},{1,8},{4,13},{5,12},{8,1},{9,0},{12,5},{13,4},{2,11},{3,10},... | collective-permute-start | bytes 233480 | tf_op jit(solution)/shard_map/ppermute | solution.py:501
  19.7 1.6 %shard_map.88 = (f32[3,64,256]{2,1,0:T(8,128)S(1)}, bf16[64,128]{1,0:T(8,128)(2,1)S(1)}, bf16[1,3,64,256]{3,2,1,0:T(8,128)(2,1)}) custom-call(s32[4,3]{1,0:T(4,128)S(1)} %get-tuple-element.36.rows.refs_0_, bf16[976,128]{1,0:T(8,128)(2,1)S(1)} %get-tuple-element.37.shared.refs_2_, bf16[2,3,384,128]{3,2,1,0:T(8,128)(2,1)S(1)} %get-tuple-element.39.gathers, ...), custom_call_target="tpu_custom_call" | custom-call | tf_op jit(solution)/shard_map/pallas_call | solution.py:485
  21.3 0.1 collective-permute-start.5
  21.3 0.1 collective-permute-start.6
  21.4 2.6 %collective-permute-done.4 = bf16[304,128]{1,0:T(8,128)(2,1)S(1)} collective-permute-done((bf16[304,128]{1,0:T(8,128)(2,1)S(1)}, bf16[304,128]{1,0:T(8,128)(2,1)S(1)}, u32[]{:S(2)}, u32[]{:S(2)}) %collective-permute-start.4) | collective-permute-done | bytes 77856 | tf_op jit(solution)/shard_map/ppermute | solution.py:501
  24.0 1.4 %collective-permute-done.6 = bf16[64,128]{1,0:T(8,128)(2,1)S(1)} collective-permute-done((bf16[64,128]{1,0:T(8,128)(2,1)S(1)}, bf16[64,128]{1,0:T(8,128)(2,1)S(1)}, u32[]{:S(2)}, u32[]{:S(2)}) %collective-permute-start.6) | collective-permute-done | bytes 16416 | tf_op jit(solution)/shard_map/ppermute | solution.py:501
  25.5 1.9 %collective-permute-start.7 = (bf16[432,128]{1,0:T(8,128)(2,1)S(1)}, bf16[432,128]{1,0:T(8,128)(2,1)S(1)}, u32[]{:S(2)}, u32[]{:S(2)}) collective-permute-start(bf16[432,128]{1,0:T(8,128)(2,1)S(1)} %pad_maximum_fusion), channel_id=1, source_target_pairs={{0,5},{1,4},{4,1},{5,0},{8,13},{9,12},{12,9},{13,8},{2,7},{3,6},{6... | collective-permute-start | bytes 331784 | tf_op jit(solution)/shard_map/ppermute | solution.py:501
  27.4 0.1 collective-permute-start.8
  27.5 3.1 %collective-permute-done.7 = bf16[432,128]{1,0:T(8,128)(2,1)S(1)} collective-permute-done((bf16[432,128]{1,0:T(8,128)(2,1)S(1)}, bf16[432,128]{1,0:T(8,128)(2,1)S(1)}, u32[]{:S(2)}, u32[]{:S(2)}) %collective-permute-start.7) | collective-permute-done | bytes 110624 | tf_op jit(solution)/shard_map/ppermute | solution.py:501
  30.6 0.3 %collective-permute-start.9 = (f32[304,128]{1,0:T(8,128)S(1)}, f32[304,128]{1,0:T(8,128)S(1)}, u32[]{:S(2)}, u32[]{:S(2)}) collective-permute-start(f32[304,128]{1,0:T(8,128)S(1)} %add_multiply_fusion.refs_0_), channel_id=1, source_target_pairs={{0,1},{1,0},{2,3},{3,2},{4,5},{5,4},{6,7},{7,6},{8,9},{9,8},{10,11... | collective-permute-start | bytes 466952 | tf_op jit(solution)/shard_map/ppermute | solution.py:530
  30.9 1.0 %shard_map.89 = bf16[1,3,64,256]{3,2,1,0:T(8,128)(2,1)} custom-call(f32[3,64,256]{2,1,0:T(8,128)S(1)} %get-tuple-element.59.base, bf16[64,128]{1,0:T(8,128)(2,1)S(1)} %get-tuple-element.69.refs_0_, bf16[64,128]{1,0:T(8,128)(2,1)S(1)} %get-tuple-element.68.refs_1_, bf16[64,128]{1,0:T(8,128)(2,1)S(1)} %collective-permute-done.8.refs_2_, ...), custom_call_target="tpu_custom_call" | custom-call | tf_op jit(solution)/shard_map/pallas_call | solution.py:521
  32.0 0.1 collective-permute-done.9.refs_1_
  32.0 0.7 %shard_map.90 = (f32[9,64,128]{2,1,0:T(8,128)}, f32[1,64]{1,0:T(1,128)}) custom-call(f32[304,128]{1,0:T(8,128)S(1)} %add_multiply_fusion.refs_0_, f32[304,128]{1,0:T(8,128)S(1)} %collective-permute-done.9.refs_1_), custom_call_target="tpu_custom_call" | custom-call | tf_op jit(solution)/shard_map/pallas_call | solution.py:526
  (9 shorter events, 0.1 us)
Async XLA Ops:
  2.2 5.3 %collective-permute-start = (bf16[256,128]{1,0:T(8,128)(2,1)S(1)}, bf16[256,128]{1,0:T(8,128)(2,1)S(1)}, u32[]{:S(2)}, u32[]{:S(2)}) collective-permute-start(bf16[256,128]{1,0:T(8,128)(2,1)S(1)} %get-tuple-element.43), channel_id=1, source_target_pairs={{0,4},{4,0},{8,12},{12,8},{1,5},{5,1},{9,13},{13,9},{2,6},{6,2},{1... | collective-permute-start | bytes 196616 | tf_op jit(solution)/shard_map/ppermute | solution.py:439
  5.3 9.8 %collective-permute-start.2 = (bf16[976,128]{1,0:T(8,128)(2,1)S(1)}, bf16[976,128]{1,0:T(8,128)(2,1)S(1)}, u32[]{:S(2)}, u32[]{:S(2)}) collective-permute-start(bf16[976,128]{1,0:T(8,128)(2,1)S(1)} %get-tuple-element.37.shared.refs_2_), channel_id=1, source_target_pairs={{0,2},{2,0},{1,3},{3,1},{4,6},{6,4},{5,7},{7,5},{8,10},{10,8},{9,1... | collective-permute-start | bytes 749576 | tf_op jit(solution)/shard_map/ppermute | solution.py:446
  7.5 5.0 %collective-permute-start.1 = (bf16[128,128]{1,0:T(8,128)(2,1)S(1)}, bf16[128,128]{1,0:T(8,128)(2,1)S(1)}, u32[]{:S(2)}, u32[]{:S(2)}) collective-permute-start(bf16[128,128]{1,0:T(8,128)(2,1)S(1)} %get-tuple-element.70), channel_id=1, source_target_pairs={{0,8},{4,12},{8,0},{12,4},{1,9},{5,13},{9,1},{13,5},{2,10},{6,14},... | collective-permute-start | bytes 98312 | tf_op jit(solution)/shard_map/ppermute | solution.py:439
  15.1 1.5 %collective-permute-start.3 = (f32[304,128]{1,0:T(8,128)S(1)}, f32[304,128]{1,0:T(8,128)S(1)}, u32[]{:S(2)}, u32[]{:S(2)}) collective-permute-start(f32[304,128]{1,0:T(8,128)S(1)} %get-tuple-element.50), channel_id=1, source_target_pairs={{0,1},{1,0},{2,3},{3,2},{4,5},{5,4},{6,7},{7,6},{8,9},{9,8},{10,11... | collective-permute-start | bytes 466952 | tf_op jit(solution)/shard_map/ppermute | solution.py:474
  16.6 7.4 %collective-permute-start.4 = (bf16[304,128]{1,0:T(8,128)(2,1)S(1)}, bf16[304,128]{1,0:T(8,128)(2,1)S(1)}, u32[]{:S(2)}, u32[]{:S(2)}) collective-permute-start(bf16[304,128]{1,0:T(8,128)(2,1)S(1)} %add_convert_fusion.1), channel_id=1, source_target_pairs={{0,9},{1,8},{4,13},{5,12},{8,1},{9,0},{12,5},{13,4},{2,11},{3,10},... | collective-permute-start | bytes 233480 | tf_op jit(solution)/shard_map/ppermute | solution.py:501
  21.3 2.8 %collective-permute-start.5 = (bf16[64,128]{1,0:T(8,128)(2,1)S(1)}, bf16[64,128]{1,0:T(8,128)(2,1)S(1)}, u32[]{:S(2)}, u32[]{:S(2)}) collective-permute-start(bf16[64,128]{1,0:T(8,128)(2,1)S(1)} %get-tuple-element.61.refs_3_), channel_id=1, source_target_pairs={{0,1},{1,0},{2,3},{3,2},{4,5},{5,4},{6,7},{7,6},{8,9},{9,8},{10,11... | collective-permute-start | bytes 49160 | tf_op jit(solution)/shard_map/ppermute | solution.py:504
  21.3 4.1 %collective-permute-start.6 = (bf16[64,128]{1,0:T(8,128)(2,1)S(1)}, bf16[64,128]{1,0:T(8,128)(2,1)S(1)}, u32[]{:S(2)}, u32[]{:S(2)}) collective-permute-start(bf16[64,128]{1,0:T(8,128)(2,1)S(1)} %get-tuple-element.61.refs_3_), channel_id=1, source_target_pairs={{0,9},{1,8},{4,13},{5,12},{8,1},{9,0},{12,5},{13,4},{2,11},{3,10},... | collective-permute-start | bytes 49160 | tf_op jit(solution)/shard_map/ppermute | solution.py:501
  25.5 5.1 %collective-permute-start.7 = (bf16[432,128]{1,0:T(8,128)(2,1)S(1)}, bf16[432,128]{1,0:T(8,128)(2,1)S(1)}, u32[]{:S(2)}, u32[]{:S(2)}) collective-permute-start(bf16[432,128]{1,0:T(8,128)(2,1)S(1)} %pad_maximum_fusion), channel_id=1, source_target_pairs={{0,5},{1,4},{4,1},{5,0},{8,13},{9,12},{12,9},{13,8},{2,7},{3,6},{6... | collective-permute-start | bytes 331784 | tf_op jit(solution)/shard_map/ppermute | solution.py:501
  27.4 3.5 %collective-permute-start.8 = (bf16[64,128]{1,0:T(8,128)(2,1)S(1)}, bf16[64,128]{1,0:T(8,128)(2,1)S(1)}, u32[]{:S(2)}, u32[]{:S(2)}) collective-permute-start(bf16[64,128]{1,0:T(8,128)(2,1)S(1)} %collective-permute-done.6), channel_id=1, source_target_pairs={{0,1},{1,0},{2,3},{3,2},{4,5},{5,4},{6,7},{7,6},{8,9},{9,8},{10,11... | collective-permute-start | bytes 49160 | tf_op jit(solution)/shard_map/ppermute | solution.py:509
  30.6 1.4 %collective-permute-start.9 = (f32[304,128]{1,0:T(8,128)S(1)}, f32[304,128]{1,0:T(8,128)S(1)}, u32[]{:S(2)}, u32[]{:S(2)}) collective-permute-start(f32[304,128]{1,0:T(8,128)S(1)} %add_multiply_fusion.refs_0_), channel_id=1, source_target_pairs={{0,1},{1,0},{2,3},{3,2},{4,5},{5,4},{6,7},{7,6},{8,9},{9,8},{10,11... | collective-permute-start | bytes 466952 | tf_op jit(solution)/shard_map/ppermute | solution.py:530

commit v8 on v7

--- a/solution.py
+++ b/solution.py
@@ -28,9 +28,9 @@
 def halo_plans(count):
     if count == 4:
         return [
-            (lambda d: d ^ 1, ("side",)),
             (lambda d: 3 - d, ("side", "fold")),
             (lambda d: d ^ 2, ("corner",)),
+            (lambda d: d ^ 1, ("side",)),
             (None, ("corner",)),
         ]
     return [
@@ -117,8 +117,6 @@
     rows_out, fields_out, shared = refs[:3]
     maps = refs[3 : 3 + n]
     outs = refs[3 + n : -3]
-    if count == 4:
-        outs = [outs[0].at[:C, :], outs[0].at[C:, :], *outs[1:]]
     rows, bias, sem = refs[-3:]
     own = weights_hbm.shape[1]
     taps, halves, pieces = message_views(shared, own)
@@ -386,13 +384,14 @@
 HBM = pl.BlockSpec(memory_space=pltpu.HBM)
 
 
-def call(kernel, specs, outs, scratch=(), out_specs=None):
+def call(kernel, specs, outs, scratch=(), out_specs=None, cost=None):
     return pl.pallas_call(
         kernel,
         in_specs=specs,
         out_specs=out_specs or [VMEM] * len(outs),
         out_shape=outs,
         scratch_shapes=list(scratch),
+        cost_estimate=cost,
         compiler_params=pltpu.CompilerParams(vmem_limit_bytes=40 << 20),
     )
 
@@ -416,7 +415,6 @@
         pltpu.with_memory_space_constraint(x, pltpu.HBM)
         for x in (tile_rows, fields, weights, bias.reshape(1, own), cotangent)
     ]
-    heights = [2 * C, C, C] if count == 4 else [C] * n
     rows, tiles, shared, *packed = call(
         lambda *refs: pack_kernel(*refs, count=count),
         [HBM] * 5,
@@ -426,7 +424,7 @@
             struct((shared_rows, 128), BF16),
         ]
         + [struct((SLOTS * CELLS, 128), BF16)] * n
-        + [struct((height, 128), BF16) for height in heights],
+        + [struct((C, 128), BF16)] * n,
         [
             pltpu.SMEM(tile_rows.shape, jnp.int32),
             pltpu.VMEM((1, own), F32),
@@ -438,11 +436,7 @@
     def move(x, route):
         return lax.ppermute(x, "tiles", [(i, route(i)) for i in range(count)])
 
-    if count == 4:
-        near = move(messages[0], lambda d: d ^ 1)
-        halos = [near[:C], move(messages[1] + near[C:], lambda d: d ^ 2), messages[2]]
-    else:
-        halos = [move(message, route) for message, (route, _) in zip(messages, plans)]
+    halos = [x if route is None else move(x, route) for x, (route, _) in zip(messages, plans)]
     others = [lax.ppermute(shared, "chan", [(i, (i + s) % chans) for i in range(chans)]) for s in range(1, chans)]
 
     windows, spreads, gathers, kernel, back_kernel = call(
@@ -468,6 +462,7 @@
             struct((half_rows, 128), F32),
             struct((half_rows, 128), F32),
         ],
+        cost=pl.CostEstimate(flops=4 * 10**9, transcendentals=0, bytes_accessed=0),
     )(rows, tiles, shared, kernel, spreads, windows, *halos)
 
     send, others = lax.optimization_barrier((send, others))
@@ -507,7 +502,7 @@
         both = cross(jnp.concatenate([rounded, beside, across], axis=0), lambda d: d ^ 1)
         sums = rounded.astype(F32) + both[:half_rows].astype(F32)
         across = lax.ppermute(across, "rep", swap)
-        returned = [both[half_rows : half_rows + own], both[half_rows + own :], across, edges]
+        returned = [both[half_rows + own :], across, both[half_rows : half_rows + own], edges]
     else:
         for step in range(count.bit_length() - 1):
             other = move(rounded, lambda d: d ^ (1 << step))

time: 33 us -> 32.3 us (0.979)
  waiting for transfers between devices: 8.57 us -> 8.18 us
    ppermute x3, waiting for transfers between devices: 7.11 us -> 6.14 us  [cross(): return lax.ppermute(x, ('tiles', 'rep'), pairs)]
    ppermute x1, waiting for transfers between devices: 0.01 us -> 0.53 us  [on_device(): lax.ppermute(shared, 'chan', [(i, (i + s) % chans) for i in range(chans)])]
    ppermute x2 -> x3, starting transfers between devices: 6.19 us -> 5.76 us  [move(): return lax.ppermute(x, 'tiles', [(i, route(i)) for i in range(count)])]
    ppermute x2 -> x3, waiting for transfers between devices: 1.37 us -> 1.25 us  [move(): return lax.ppermute(x, 'tiles', [(i, route(i)) for i in range(count)])]
  transfers between devices with their start and end apart: 10 -> 11, of which waited for: 6 -> 6; matrix products, arithmetic and copies ran while one was open for 0% -> 0% of each run, Pallas kernels for 24% -> 24%
where the time goes in v8:
time: 32.3 us; the launch traced here: 32.1 us
  starting transfers between devices  13 us (40%)
  Pallas kernels  10.1 us (31%)
  waiting for transfers between devices  8.18 us (25%)
  between operations  0.72 us (2%)
    ppermute x3, waiting for transfers between devices, cross(): return lax.ppermute(x, ('tiles', 'rep'), pairs)  6.14 us
    ppermute x3, starting transfers between devices, move(): return lax.ppermute(x, 'tiles', [(i, route(i)) for i in range(count)])  5.76 us
    ppermute x3, starting transfers between devices, cross(): return lax.ppermute(x, ('tiles', 'rep'), pairs)  5.08 us
    pallas_call x1, Pallas kernels, on_device(): call(lambda *refs: forward_kernel(*refs, n_halos=len(halos), half_rows=ha...  2.51 us
    ppermute x1, starting transfers between devices, on_device(): lax.ppermute(shared, 'chan', [(i, (i + s) % chans) for i in range(chans)])  1.63 us
    pallas_call x1, Pallas kernels, on_device(): call(lambda *refs: pack_kernel(*refs, count=count), [HBM] * 5, [struct(ti...  1.59 us
    pallas_call x1, Pallas kernels, on_device(): call(backward_kernel, [SMEM] + [VMEM] * (5 + 2 * len(others)), [struct((S...  1.55 us
    pallas_call x1, Pallas kernels, on_device(): call(other_kernel, [SMEM, VMEM] + [VMEM] * len(others), [struct((SLOTS, 3...  1.42 us
  transfers between devices with their start and end apart: 11, of which 6 were waited for; matrix products, arithmetic and copies ran while one was open for 0% of the time, Pallas kernels for 24%

profile of v8, /device:TPU:0, one launch (start us, length us, event | category | flops | bytes accessed | tf_op | source)
XLA Modules:
  0.0 32.1 jit_solution(3561466187855101081)
XLA Ops:
  0.6 1.6 %shard_map.84 = (s32[4,3]{1,0:T(4,128)S(1)}, bf16[3,128,256]{2,1,0:T(8,128)(2,1)S(1)}, bf16[976,128]{1,0:T(8,128)(2,1)S(1)}, bf16[768,128]{1,0:T(8,128)(2,1)S(1)...) custom-call(s32[4,3]{1,0:T(4,128)} %refs_0_.1, ...), custom_call_target="tpu_custom_call" | custom-call | tf_op jit(solution)/shard_map/pallas_call | solution.py:418
  2.2 5.1 %collective-permute-start = (bf16[128,128]{1,0:T(8,128)(2,1)S(1)}, bf16[128,128]{1,0:T(8,128)(2,1)S(1)}, u32[]{:S(2)}, u32[]{:S(2)}) collective-permute-start(bf16[128,128]{1,0:T(8,128)(2,1)S(1)} %get-tuple-element.44), channel_id=1, source_target_pairs={{0,12},{4,8},{8,4},{12,0},{1,13},{5,9},{9,5},{13,1},{2,14},{6,10},... | collective-permute-start | bytes 98312 | tf_op jit(solution)/shard_map/ppermute | solution.py:437
  7.3 0.0 collective-permute-start.1
  7.3 0.6 %collective-permute-start.2 = (bf16[128,128]{1,0:T(8,128)(2,1)S(1)}, bf16[128,128]{1,0:T(8,128)(2,1)S(1)}, u32[]{:S(2)}, u32[]{:S(2)}) collective-permute-start(bf16[128,128]{1,0:T(8,128)(2,1)S(1)} %get-tuple-element.46), channel_id=1, source_target_pairs={{0,4},{4,0},{8,12},{12,8},{1,5},{5,1},{9,13},{13,9},{2,6},{6,2},{1... | collective-permute-start | bytes 98312 | tf_op jit(solution)/shard_map/ppermute | solution.py:437
  8.0 1.6 %collective-permute-start.3 = (bf16[976,128]{1,0:T(8,128)(2,1)S(1)}, bf16[976,128]{1,0:T(8,128)(2,1)S(1)}, u32[]{:S(2)}, u32[]{:S(2)}) collective-permute-start(bf16[976,128]{1,0:T(8,128)(2,1)S(1)} %get-tuple-element.38.shared.refs_2_), channel_id=1, source_target_pairs={{0,2},{2,0},{1,3},{3,1},{4,6},{6,4},{5,7},{7,5},{8,10},{10,8},{9,1... | collective-permute-start | bytes 749576 | tf_op jit(solution)/shard_map/ppermute | solution.py:440
  9.6 1.3 %shard_map.85 = (bf16[3,384,384]{2,1,0:T(8,128)(2,1)S(1)}, bf16[2,3,128,384]{3,2,1,0:T(8,128)(2,1)S(1)}, bf16[2,3,384,128]{3,2,1,0:T(8,128)(2,1)S(1)}, bf16[192,384]{1,0:T(8,128)(2,1)S(1)}, bf16[192,192]{1,0:T(8,128)(2,1)S(1)}) custom-call(s32[4,3]{1,0:T(4,128)S(1)} %get-tuple-element.37.rows.refs_0_, ...), custom_call_target="tpu_custom_call" | custom-call | tf_op jit(solution)/shard_map/pallas_call | solution.py:442
  10.9 1.2 %collective-permute-done.1.refs_7_ = bf16[128,128]{1,0:T(8,128)(2,1)S(1)} collective-permute-done((bf16[128,128]{1,0:T(8,128)(2,1)S(1)}, bf16[128,128]{1,0:T(8,128)(2,1)S(1)}, u32[]{:S(2)}, u32[]{:S(2)}) %collective-permute-start.1) | collective-permute-done | bytes 32800 | tf_op jit(solution)/shard_map/ppermute | solution.py:437
  12.2 2.5 %shard_map.86 = (bf16[3,384,384]{2,1,0:T(8,128)(2,1)S(1)}, bf16[3,192,384]{2,1,0:T(8,128)(2,1)S(1)}, bf16[3,64,256]{2,1,0:T(8,128)(2,1)S(1)}, f32[304,128]{1,0:T(8,128)S(1)}, f32[304,128]{1,0:T(8,128)S(1)}) custom-call(s32[4,3]{1,0:T(4,128)S(1)} %get-tuple-element.37.rows.refs_0_, bf16[3,128,256]{2,1,0:T(8,128)(2,1)S(1)} %get-tuple-element.39.fields.refs_1_, ...), custom_call_target="tpu_custom_call" | custom-call | flops 4000000000 | tf_op jit(solution)/shard_map/pallas_call | solution.py:455
  14.7 0.5 %collective-permute-done.3.refs_0_ = bf16[976,128]{1,0:T(8,128)(2,1)S(1)} collective-permute-done((bf16[976,128]{1,0:T(8,128)(2,1)S(1)}, bf16[976,128]{1,0:T(8,128)(2,1)S(1)}, u32[]{:S(2)}, u32[]{:S(2)}) %collective-permute-start.3) | collective-permute-done | bytes 249888 | tf_op jit(solution)/shard_map/ppermute | solution.py:440
  15.2 1.4 %shard_map.87 = (bf16[3,192,384]{2,1,0:T(8,128)(2,1)S(1)}, bf16[192,192]{1,0:T(8,128)(2,1)S(1)}) custom-call(s32[4,3]{1,0:T(4,128)S(1)} %get-tuple-element.37.rows.refs_0_, bf16[3,384,384]{2,1,0:T(8,128)(2,1)S(1)} %get-tuple-element.53.windows, bf16[976,128]{1,0:T(8,128)(2,1)S(1)} %collective-permute-done.3.refs_0_), custom_call_target="tpu_custom_call" | custom-call | tf_op jit(solution)/shard_map/pallas_call | solution.py:470
  16.7 2.5 %collective-permute-start.5 = (bf16[304,128]{1,0:T(8,128)(2,1)S(1)}, bf16[304,128]{1,0:T(8,128)(2,1)S(1)}, u32[]{:S(2)}, u32[]{:S(2)}) collective-permute-start(bf16[304,128]{1,0:T(8,128)(2,1)S(1)} %add_convert_fusion.1), channel_id=1, source_target_pairs={{0,9},{1,8},{4,13},{5,12},{8,1},{9,0},{12,5},{13,4},{2,11},{3,10},... | collective-permute-start | bytes 233480 | tf_op jit(solution)/shard_map/ppermute | solution.py:496
  19.1 1.5 %shard_map.88 = (f32[3,64,256]{2,1,0:T(8,128)S(1)}, bf16[64,128]{1,0:T(8,128)(2,1)S(1)}, bf16[1,3,64,256]{3,2,1,0:T(8,128)(2,1)}) custom-call(s32[4,3]{1,0:T(4,128)S(1)} %get-tuple-element.37.rows.refs_0_, bf16[976,128]{1,0:T(8,128)(2,1)S(1)} %get-tuple-element.38.shared.refs_2_, bf16[2,3,384,128]{3,2,1,0:T(8,128)(2,1)S(1)} %get-tuple-element.40.gathers, ...), custom_call_target="tpu_custom_call" | custom-call | tf_op jit(solution)/shard_map/pallas_call | solution.py:480
  20.7 0.1 collective-permute-start.6
  20.8 0.8 %collective-permute-start.7 = (bf16[64,128]{1,0:T(8,128)(2,1)S(1)}, bf16[64,128]{1,0:T(8,128)(2,1)S(1)}, u32[]{:S(2)}, u32[]{:S(2)}) collective-permute-start(bf16[64,128]{1,0:T(8,128)(2,1)S(1)} %get-tuple-element.63.refs_3_), channel_id=1, source_target_pairs={{0,9},{1,8},{4,13},{5,12},{8,1},{9,0},{12,5},{13,4},{2,11},{3,10},... | collective-permute-start | bytes 49160 | tf_op jit(solution)/shard_map/ppermute | solution.py:496
  21.5 0.1 collective-permute-done.5
  21.7 0.2 collective-permute-done.6
  21.9 3.0 %collective-permute-done.7 = bf16[64,128]{1,0:T(8,128)(2,1)S(1)} collective-permute-done((bf16[64,128]{1,0:T(8,128)(2,1)S(1)}, bf16[64,128]{1,0:T(8,128)(2,1)S(1)}, u32[]{:S(2)}, u32[]{:S(2)}) %collective-permute-start.7) | collective-permute-done | bytes 16416 | tf_op jit(solution)/shard_map/ppermute | solution.py:496
  24.9 1.9 %collective-permute-start.8 = (bf16[432,128]{1,0:T(8,128)(2,1)S(1)}, bf16[432,128]{1,0:T(8,128)(2,1)S(1)}, u32[]{:S(2)}, u32[]{:S(2)}) collective-permute-start(bf16[432,128]{1,0:T(8,128)(2,1)S(1)} %pad_maximum_fusion), channel_id=1, source_target_pairs={{0,5},{1,4},{4,1},{5,0},{8,13},{9,12},{12,9},{13,8},{2,7},{3,6},{6... | collective-permute-start | bytes 331784 | tf_op jit(solution)/shard_map/ppermute | solution.py:496
  26.8 0.1 collective-permute-start.9
  26.8 3.0 %collective-permute-done.8 = bf16[432,128]{1,0:T(8,128)(2,1)S(1)} collective-permute-done((bf16[432,128]{1,0:T(8,128)(2,1)S(1)}, bf16[432,128]{1,0:T(8,128)(2,1)S(1)}, u32[]{:S(2)}, u32[]{:S(2)}) %collective-permute-start.8) | collective-permute-done | bytes 110624 | tf_op jit(solution)/shard_map/ppermute | solution.py:496
  29.9 0.4 %collective-permute-start.10 = (f32[304,128]{1,0:T(8,128)S(1)}, f32[304,128]{1,0:T(8,128)S(1)}, u32[]{:S(2)}, u32[]{:S(2)}) collective-permute-start(f32[304,128]{1,0:T(8,128)S(1)} %add_multiply_fusion.refs_0_), channel_id=1, source_target_pairs={{0,1},{1,0},{2,3},{3,2},{4,5},{5,4},{6,7},{7,6},{8,9},{9,8},{10,11... | collective-permute-start | bytes 466952 | tf_op jit(solution)/shard_map/ppermute | solution.py:525
  30.3 1.0 %shard_map.89 = bf16[1,3,64,256]{3,2,1,0:T(8,128)(2,1)} custom-call(f32[3,64,256]{2,1,0:T(8,128)S(1)} %get-tuple-element.61.base, bf16[64,128]{1,0:T(8,128)(2,1)S(1)} %get-tuple-element.71.refs_0_, bf16[64,128]{1,0:T(8,128)(2,1)S(1)} %collective-permute-done.9.refs_1_, bf16[64,128]{1,0:T(8,128)(2,1)S(1)} %get-tuple-element.70.refs_2_, ...), custom_call_target="tpu_custom_call" | custom-call | tf_op jit(solution)/shard_map/pallas_call | solution.py:516
  31.4 0.0 collective-permute-done.10.refs_1_
  31.4 0.7 %shard_map.90 = (f32[9,64,128]{2,1,0:T(8,128)}, f32[1,64]{1,0:T(1,128)}) custom-call(f32[304,128]{1,0:T(8,128)S(1)} %add_multiply_fusion.refs_0_, f32[304,128]{1,0:T(8,128)S(1)} %collective-permute-done.10.refs_1_), custom_call_target="tpu_custom_call" | custom-call | tf_op jit(solution)/shard_map/pallas_call | solution.py:521
  (10 shorter events, 0.1 us)
Async XLA Ops:
  2.2 8.7 %collective-permute-start = (bf16[128,128]{1,0:T(8,128)(2,1)S(1)}, bf16[128,128]{1,0:T(8,128)(2,1)S(1)}, u32[]{:S(2)}, u32[]{:S(2)}) collective-permute-start(bf16[128,128]{1,0:T(8,128)(2,1)S(1)} %get-tuple-element.44), channel_id=1, source_target_pairs={{0,12},{4,8},{8,4},{12,0},{1,13},{5,9},{9,5},{13,1},{2,14},{6,10},... | collective-permute-start | bytes 98312 | tf_op jit(solution)/shard_map/ppermute | solution.py:437
  7.3 4.8 %collective-permute-start.1 = (bf16[128,128]{1,0:T(8,128)(2,1)S(1)}, bf16[128,128]{1,0:T(8,128)(2,1)S(1)}, u32[]{:S(2)}, u32[]{:S(2)}) collective-permute-start(bf16[128,128]{1,0:T(8,128)(2,1)S(1)} %get-tuple-element.45), channel_id=1, source_target_pairs={{0,8},{4,12},{8,0},{12,4},{1,9},{5,13},{9,1},{13,5},{2,10},{6,14},... | collective-permute-start | bytes 98312 | tf_op jit(solution)/shard_map/ppermute | solution.py:437
  7.3 4.8 %collective-permute-start.2 = (bf16[128,128]{1,0:T(8,128)(2,1)S(1)}, bf16[128,128]{1,0:T(8,128)(2,1)S(1)}, u32[]{:S(2)}, u32[]{:S(2)}) collective-permute-start(bf16[128,128]{1,0:T(8,128)(2,1)S(1)} %get-tuple-element.46), channel_id=1, source_target_pairs={{0,4},{4,0},{8,12},{12,8},{1,5},{5,1},{9,13},{13,9},{2,6},{6,2},{1... | collective-permute-start | bytes 98312 | tf_op jit(solution)/shard_map/ppermute | solution.py:437
  8.0 7.2 %collective-permute-start.3 = (bf16[976,128]{1,0:T(8,128)(2,1)S(1)}, bf16[976,128]{1,0:T(8,128)(2,1)S(1)}, u32[]{:S(2)}, u32[]{:S(2)}) collective-permute-start(bf16[976,128]{1,0:T(8,128)(2,1)S(1)} %get-tuple-element.38.shared.refs_2_), channel_id=1, source_target_pairs={{0,2},{2,0},{1,3},{3,1},{4,6},{6,4},{5,7},{7,5},{8,10},{10,8},{9,1... | collective-permute-start | bytes 749576 | tf_op jit(solution)/shard_map/ppermute | solution.py:440
  15.2 1.4 %collective-permute-start.4 = (f32[304,128]{1,0:T(8,128)S(1)}, f32[304,128]{1,0:T(8,128)S(1)}, u32[]{:S(2)}, u32[]{:S(2)}) collective-permute-start(f32[304,128]{1,0:T(8,128)S(1)} %get-tuple-element.52), channel_id=1, source_target_pairs={{0,1},{1,0},{2,3},{3,2},{4,5},{5,4},{6,7},{7,6},{8,9},{9,8},{10,11... | collective-permute-start | bytes 466952 | tf_op jit(solution)/shard_map/ppermute | solution.py:469
  16.7 5.0 %collective-permute-start.5 = (bf16[304,128]{1,0:T(8,128)(2,1)S(1)}, bf16[304,128]{1,0:T(8,128)(2,1)S(1)}, u32[]{:S(2)}, u32[]{:S(2)}) collective-permute-start(bf16[304,128]{1,0:T(8,128)(2,1)S(1)} %add_convert_fusion.1), channel_id=1, source_target_pairs={{0,9},{1,8},{4,13},{5,12},{8,1},{9,0},{12,5},{13,4},{2,11},{3,10},... | collective-permute-start | bytes 233480 | tf_op jit(solution)/shard_map/ppermute | solution.py:496
  20.7 1.2 %collective-permute-start.6 = (bf16[64,128]{1,0:T(8,128)(2,1)S(1)}, bf16[64,128]{1,0:T(8,128)(2,1)S(1)}, u32[]{:S(2)}, u32[]{:S(2)}) collective-permute-start(bf16[64,128]{1,0:T(8,128)(2,1)S(1)} %get-tuple-element.63.refs_3_), channel_id=1, source_target_pairs={{0,1},{1,0},{2,3},{3,2},{4,5},{5,4},{6,7},{7,6},{8,9},{9,8},{10,11... | collective-permute-start | bytes 49160 | tf_op jit(solution)/shard_map/ppermute | solution.py:499
  20.8 4.1 %collective-permute-start.7 = (bf16[64,128]{1,0:T(8,128)(2,1)S(1)}, bf16[64,128]{1,0:T(8,128)(2,1)S(1)}, u32[]{:S(2)}, u32[]{:S(2)}) collective-permute-start(bf16[64,128]{1,0:T(8,128)(2,1)S(1)} %get-tuple-element.63.refs_3_), channel_id=1, source_target_pairs={{0,9},{1,8},{4,13},{5,12},{8,1},{9,0},{12,5},{13,4},{2,11},{3,10},... | collective-permute-start | bytes 49160 | tf_op jit(solution)/shard_map/ppermute | solution.py:496
  24.9 5.0 %collective-permute-start.8 = (bf16[432,128]{1,0:T(8,128)(2,1)S(1)}, bf16[432,128]{1,0:T(8,128)(2,1)S(1)}, u32[]{:S(2)}, u32[]{:S(2)}) collective-permute-start(bf16[432,128]{1,0:T(8,128)(2,1)S(1)} %pad_maximum_fusion), channel_id=1, source_target_pairs={{0,5},{1,4},{4,1},{5,0},{8,13},{9,12},{12,9},{13,8},{2,7},{3,6},{6... | collective-permute-start | bytes 331784 | tf_op jit(solution)/shard_map/ppermute | solution.py:496
  26.8 3.5 %collective-permute-start.9 = (bf16[64,128]{1,0:T(8,128)(2,1)S(1)}, bf16[64,128]{1,0:T(8,128)(2,1)S(1)}, u32[]{:S(2)}, u32[]{:S(2)}) collective-permute-start(bf16[64,128]{1,0:T(8,128)(2,1)S(1)} %collective-permute-done.7), channel_id=1, source_target_pairs={{0,1},{1,0},{2,3},{3,2},{4,5},{5,4},{6,7},{7,6},{8,9},{9,8},{10,11... | collective-permute-start | bytes 49160 | tf_op jit(solution)/shard_map/ppermute | solution.py:504
  29.9 1.4 %collective-permute-start.10 = (f32[304,128]{1,0:T(8,128)S(1)}, f32[304,128]{1,0:T(8,128)S(1)}, u32[]{:S(2)}, u32[]{:S(2)}) collective-permute-start(f32[304,128]{1,0:T(8,128)S(1)} %add_multiply_fusion.refs_0_), channel_id=1, source_target_pairs={{0,1},{1,0},{2,3},{3,2},{4,5},{5,4},{6,7},{7,6},{8,9},{9,8},{10,11... | collective-permute-start | bytes 466952 | tf_op jit(solution)/shard_map/ppermute | solution.py:525

commit v9 on v8

--- a/solution.py
+++ b/solution.py
@@ -465,8 +465,10 @@
         cost=pl.CostEstimate(flops=4 * 10**9, transcendentals=0, bytes_accessed=0),
     )(rows, tiles, shared, kernel, spreads, windows, *halos)
 
-    send, others = lax.optimization_barrier((send, others))
-    sums = keep + lax.ppermute(send, "rep", swap)
+    swapped, others = lax.optimization_barrier((lax.ppermute(send, "rep", swap), others))
+    sums = keep + swapped
+    rounded = sums.astype(BF16)
+    frames, rounded, others = lax.optimization_barrier((frames, rounded, others))
     other_frames = call(
         other_kernel,
         [SMEM, VMEM] + [VMEM] * len(others),
@@ -474,8 +476,6 @@
         [pltpu.VMEM((3 * C, 3 * own), F32)],
     )(rows, windows, *others)
     other_frames, other_back = other_frames[: len(others)], other_frames[len(others) :]
-    rounded = sums.astype(BF16)
-    frames, rounded, other_frames = lax.optimization_barrier((frames, rounded, other_frames))
 
     base, edges, result = call(
         backward_kernel,

time: 32.3 us -> 33 us (1.022)
  waiting for transfers between devices: 8.18 us -> 10 us
  starting transfers between devices: 13 us -> 11.9 us
    ppermute x3, starting transfers between devices: 5.08 us -> 3.36 us  [cross(): return lax.ppermute(x, ('tiles', 'rep'), pairs)]
    ppermute x1, waiting for transfers between devices: 0.01 us -> 1.37 us  [on_device(): lax.ppermute(send, 'rep', swap)]
    ppermute x3, waiting for transfers between devices: 6.14 us -> 7.19 us  [cross(): return lax.ppermute(x, ('tiles', 'rep'), pairs)]
    ppermute x1, waiting for transfers between devices: 0.53 us -> 0.01 us  [on_device(): lax.ppermute(shared, 'chan', [(i, (i + s) % chans) for i in range(chans)])]
    ppermute x1, starting transfers between devices: 0.07 us -> 0.42 us  [on_device(): beside = lax.ppermute(edges, 'rep', swap)]
    ppermute x1, starting transfers between devices: 0.06 us -> 0.4 us  [on_device(): across = lax.ppermute(across, 'rep', swap)]
where the time goes in v9:
time: 33 us; the launch traced here: 32.8 us
  starting transfers between devices  11.9 us (36%)
  Pallas kernels  10.1 us (31%)
  waiting for transfers between devices  10 us (30%)
  between operations  0.72 us (2%)
    ppermute x3, waiting for transfers between devices, cross(): return lax.ppermute(x, ('tiles', 'rep'), pairs)  7.19 us
    ppermute x3, starting transfers between devices, move(): return lax.ppermute(x, 'tiles', [(i, route(i)) for i in range(count)])  5.76 us
    ppermute x3, starting transfers between devices, cross(): return lax.ppermute(x, ('tiles', 'rep'), pairs)  3.36 us
    pallas_call x1, Pallas kernels, on_device(): call(lambda *refs: forward_kernel(*refs, n_halos=len(halos), half_rows=ha...  2.51 us
    ppermute x1, starting transfers between devices, on_device(): lax.ppermute(shared, 'chan', [(i, (i + s) % chans) for i in range(chans)])  1.63 us
    pallas_call x1, Pallas kernels, on_device(): call(lambda *refs: pack_kernel(*refs, count=count), [HBM] * 5, [struct(ti...  1.59 us
    pallas_call x1, Pallas kernels, on_device(): call(backward_kernel, [SMEM] + [VMEM] * (5 + 2 * len(others)), [struct((S...  1.56 us
    pallas_call x1, Pallas kernels, on_device(): call(other_kernel, [SMEM, VMEM] + [VMEM] * len(others), [struct((SLOTS, 3...  1.42 us
  transfers between devices with their start and end apart: 11, of which 6 were waited for; matrix products, arithmetic and copies ran while one was open for 0% of the time, Pallas kernels for 24%

profile of v9, /device:TPU:0, one launch (start us, length us, event | category | flops | bytes accessed | tf_op | source)
XLA Modules:
  0.0 32.8 jit_solution(17184391344915693608)
XLA Ops:
  0.6 1.6 %shard_map.84 = (s32[4,3]{1,0:T(4,128)S(1)}, bf16[3,128,256]{2,1,0:T(8,128)(2,1)S(1)}, bf16[976,128]{1,0:T(8,128)(2,1)S(1)}, bf16[768,128]{1,0:T(8,128)(2,1)S(1)...) custom-call(s32[4,3]{1,0:T(4,128)} %refs_0_.1, ...), custom_call_target="tpu_custom_call" | custom-call | tf_op jit(solution)/shard_map/pallas_call | solution.py:418
  2.2 5.1 %collective-permute-start = (bf16[128,128]{1,0:T(8,128)(2,1)S(1)}, bf16[128,128]{1,0:T(8,128)(2,1)S(1)}, u32[]{:S(2)}, u32[]{:S(2)}) collective-permute-start(bf16[128,128]{1,0:T(8,128)(2,1)S(1)} %get-tuple-element.44), channel_id=1, source_target_pairs={{0,12},{4,8},{8,4},{12,0},{1,13},{5,9},{9,5},{13,1},{2,14},{6,10},... | collective-permute-start | bytes 98312 | tf_op jit(solution)/shard_map/ppermute | solution.py:437
  7.3 0.6 %collective-permute-start.2 = (bf16[128,128]{1,0:T(8,128)(2,1)S(1)}, bf16[128,128]{1,0:T(8,128)(2,1)S(1)}, u32[]{:S(2)}, u32[]{:S(2)}) collective-permute-start(bf16[128,128]{1,0:T(8,128)(2,1)S(1)} %get-tuple-element.46), channel_id=1, source_target_pairs={{0,4},{4,0},{8,12},{12,8},{1,5},{5,1},{9,13},{13,9},{2,6},{6,2},{1... | collective-permute-start | bytes 98312 | tf_op jit(solution)/shard_map/ppermute | solution.py:437
  8.0 1.6 %collective-permute-start.4 = (bf16[976,128]{1,0:T(8,128)(2,1)S(1)}, bf16[976,128]{1,0:T(8,128)(2,1)S(1)}, u32[]{:S(2)}, u32[]{:S(2)}) collective-permute-start(bf16[976,128]{1,0:T(8,128)(2,1)S(1)} %get-tuple-element.38.shared.refs_2_), channel_id=1, source_target_pairs={{0,2},{2,0},{1,3},{3,1},{4,6},{6,4},{5,7},{7,5},{8,10},{10,8},{9,1... | collective-permute-start | bytes 749576 | tf_op jit(solution)/shard_map/ppermute | solution.py:440
  9.6 1.3 %shard_map.85 = (bf16[3,384,384]{2,1,0:T(8,128)(2,1)S(1)}, bf16[2,3,128,384]{3,2,1,0:T(8,128)(2,1)S(1)}, bf16[2,3,384,128]{3,2,1,0:T(8,128)(2,1)S(1)}, bf16[192,384]{1,0:T(8,128)(2,1)S(1)}, bf16[192,192]{1,0:T(8,128)(2,1)S(1)}) custom-call(s32[4,3]{1,0:T(4,128)S(1)} %get-tuple-element.37.rows.refs_0_, ...), custom_call_target="tpu_custom_call" | custom-call | tf_op jit(solution)/shard_map/pallas_call | solution.py:442
  10.9 0.0 collective-permute-done.refs_6_
  10.9 1.2 %collective-permute-done.1.refs_7_ = bf16[128,128]{1,0:T(8,128)(2,1)S(1)} collective-permute-done((bf16[128,128]{1,0:T(8,128)(2,1)S(1)}, bf16[128,128]{1,0:T(8,128)(2,1)S(1)}, u32[]{:S(2)}, u32[]{:S(2)}) %collective-permute-start.1) | collective-permute-done | bytes 32800 | tf_op jit(solution)/shard_map/ppermute | solution.py:437
  12.2 2.5 %shard_map.86 = (bf16[3,384,384]{2,1,0:T(8,128)(2,1)S(1)}, bf16[3,192,384]{2,1,0:T(8,128)(2,1)S(1)}, bf16[3,64,256]{2,1,0:T(8,128)(2,1)S(1)}, f32[304,128]{1,0:T(8,128)S(1)}, f32[304,128]{1,0:T(8,128)S(1)}) custom-call(s32[4,3]{1,0:T(4,128)S(1)} %get-tuple-element.37.rows.refs_0_, bf16[3,128,256]{2,1,0:T(8,128)(2,1)S(1)} %get-tuple-element.39.fields.refs_1_, ...), custom_call_target="tpu_custom_call" | custom-call | flops 4000000000 | tf_op jit(solution)/shard_map/pallas_call | solution.py:455
  14.7 0.1 collective-permute-start.3
  14.8 1.4 %collective-permute-done.3 = f32[304,128]{1,0:T(8,128)S(1)} collective-permute-done((f32[304,128]{1,0:T(8,128)S(1)}, f32[304,128]{1,0:T(8,128)S(1)}, u32[]{:S(2)}, u32[]{:S(2)}) %collective-permute-start.3) | collective-permute-done | bytes 155680 | tf_op jit(solution)/shard_map/ppermute | solution.py:468
  16.2 1.8 %collective-permute-start.5 = (bf16[304,128]{1,0:T(8,128)(2,1)S(1)}, bf16[304,128]{1,0:T(8,128)(2,1)S(1)}, u32[]{:S(2)}, u32[]{:S(2)}) collective-permute-start(bf16[304,128]{1,0:T(8,128)(2,1)S(1)} %add_convert_fusion.1), channel_id=1, source_target_pairs={{0,9},{1,8},{4,13},{5,12},{8,1},{9,0},{12,5},{13,4},{2,11},{3,10},... | collective-permute-start | bytes 233480 | tf_op jit(solution)/shard_map/ppermute | solution.py:496
  18.0 1.4 %shard_map.87 = (bf16[3,192,384]{2,1,0:T(8,128)(2,1)S(1)}, bf16[192,192]{1,0:T(8,128)(2,1)S(1)}) custom-call(s32[4,3]{1,0:T(4,128)S(1)} %get-tuple-element.37.rows.refs_0_, bf16[3,384,384]{2,1,0:T(8,128)(2,1)S(1)} %get-tuple-element.55.windows, bf16[976,128]{1,0:T(8,128)(2,1)S(1)} %collective-permute-done.4.refs_0_), custom_call_target="tpu_custom_call" | custom-call | tf_op jit(solution)/shard_map/pallas_call | solution.py:472
  19.4 1.6 %shard_map.88 = (f32[3,64,256]{2,1,0:T(8,128)S(1)}, bf16[64,128]{1,0:T(8,128)(2,1)S(1)}, bf16[1,3,64,256]{3,2,1,0:T(8,128)(2,1)}) custom-call(s32[4,3]{1,0:T(4,128)S(1)} %get-tuple-element.37.rows.refs_0_, bf16[976,128]{1,0:T(8,128)(2,1)S(1)} %get-tuple-element.38.shared.refs_2_, bf16[2,3,384,128]{3,2,1,0:T(8,128)(2,1)S(1)} %get-tuple-element.40.gathers, ...), custom_call_target="tpu_custom_call" | custom-call | tf_op jit(solution)/shard_map/pallas_call | solution.py:480
  21.0 0.4 %collective-permute-start.6 = (bf16[64,128]{1,0:T(8,128)(2,1)S(1)}, bf16[64,128]{1,0:T(8,128)(2,1)S(1)}, u32[]{:S(2)}, u32[]{:S(2)}) collective-permute-start(bf16[64,128]{1,0:T(8,128)(2,1)S(1)} %get-tuple-element.63.refs_3_), channel_id=1, source_target_pairs={{0,1},{1,0},{2,3},{3,2},{4,5},{5,4},{6,7},{7,6},{8,9},{9,8},{10,11... | collective-permute-start | bytes 49160 | tf_op jit(solution)/shard_map/ppermute | solution.py:499
  21.4 0.7 %collective-permute-start.7 = (bf16[64,128]{1,0:T(8,128)(2,1)S(1)}, bf16[64,128]{1,0:T(8,128)(2,1)S(1)}, u32[]{:S(2)}, u32[]{:S(2)}) collective-permute-start(bf16[64,128]{1,0:T(8,128)(2,1)S(1)} %get-tuple-element.63.refs_3_), channel_id=1, source_target_pairs={{0,9},{1,8},{4,13},{5,12},{8,1},{9,0},{12,5},{13,4},{2,11},{3,10},... | collective-permute-start | bytes 49160 | tf_op jit(solution)/shard_map/ppermute | solution.py:496
  22.1 1.3 %collective-permute-done.5 = bf16[304,128]{1,0:T(8,128)(2,1)S(1)} collective-permute-done((bf16[304,128]{1,0:T(8,128)(2,1)S(1)}, bf16[304,128]{1,0:T(8,128)(2,1)S(1)}, u32[]{:S(2)}, u32[]{:S(2)}) %collective-permute-start.5) | collective-permute-done | bytes 77856 | tf_op jit(solution)/shard_map/ppermute | solution.py:496
  23.4 2.1 %collective-permute-done.7 = bf16[64,128]{1,0:T(8,128)(2,1)S(1)} collective-permute-done((bf16[64,128]{1,0:T(8,128)(2,1)S(1)}, bf16[64,128]{1,0:T(8,128)(2,1)S(1)}, u32[]{:S(2)}, u32[]{:S(2)}) %collective-permute-start.7) | collective-permute-done | bytes 16416 | tf_op jit(solution)/shard_map/ppermute | solution.py:496
  25.5 0.9 %collective-permute-start.8 = (bf16[432,128]{1,0:T(8,128)(2,1)S(1)}, bf16[432,128]{1,0:T(8,128)(2,1)S(1)}, u32[]{:S(2)}, u32[]{:S(2)}) collective-permute-start(bf16[432,128]{1,0:T(8,128)(2,1)S(1)} %pad_maximum_fusion), channel_id=1, source_target_pairs={{0,5},{1,4},{4,1},{5,0},{8,13},{9,12},{12,9},{13,8},{2,7},{3,6},{6... | collective-permute-start | bytes 331784 | tf_op jit(solution)/shard_map/ppermute | solution.py:496
  26.4 0.4 %collective-permute-start.9 = (bf16[64,128]{1,0:T(8,128)(2,1)S(1)}, bf16[64,128]{1,0:T(8,128)(2,1)S(1)}, u32[]{:S(2)}, u32[]{:S(2)}) collective-permute-start(bf16[64,128]{1,0:T(8,128)(2,1)S(1)} %collective-permute-done.7), channel_id=1, source_target_pairs={{0,1},{1,0},{2,3},{3,2},{4,5},{5,4},{6,7},{7,6},{8,9},{9,8},{10,11... | collective-permute-start | bytes 49160 | tf_op jit(solution)/shard_map/ppermute | solution.py:504
  26.7 3.8 %collective-permute-done.8 = bf16[432,128]{1,0:T(8,128)(2,1)S(1)} collective-permute-done((bf16[432,128]{1,0:T(8,128)(2,1)S(1)}, bf16[432,128]{1,0:T(8,128)(2,1)S(1)}, u32[]{:S(2)}, u32[]{:S(2)}) %collective-permute-start.8) | collective-permute-done | bytes 110624 | tf_op jit(solution)/shard_map/ppermute | solution.py:496
  30.6 0.2 collective-permute-start.10
  30.8 1.0 %shard_map.89 = bf16[1,3,64,256]{3,2,1,0:T(8,128)(2,1)} custom-call(f32[3,64,256]{2,1,0:T(8,128)S(1)} %get-tuple-element.61.base, bf16[64,128]{1,0:T(8,128)(2,1)S(1)} %get-tuple-element.71.refs_0_, bf16[64,128]{1,0:T(8,128)(2,1)S(1)} %collective-permute-done.9.refs_1_, bf16[64,128]{1,0:T(8,128)(2,1)S(1)} %get-tuple-element.70.refs_2_, ...), custom_call_target="tpu_custom_call" | custom-call | tf_op jit(solution)/shard_map/pallas_call | solution.py:516
  31.9 0.2 collective-permute-done.10.refs_1_
  32.0 0.7 %shard_map.90 = (f32[9,64,128]{2,1,0:T(8,128)}, f32[1,64]{1,0:T(1,128)}) custom-call(f32[304,128]{1,0:T(8,128)S(1)} %add_multiply_fusion.refs_0_, f32[304,128]{1,0:T(8,128)S(1)} %collective-permute-done.10.refs_1_), custom_call_target="tpu_custom_call" | custom-call | tf_op jit(solution)/shard_map/pallas_call | solution.py:521
  (10 shorter events, 0.1 us)
Async XLA Ops:
  2.2 8.7 %collective-permute-start = (bf16[128,128]{1,0:T(8,128)(2,1)S(1)}, bf16[128,128]{1,0:T(8,128)(2,1)S(1)}, u32[]{:S(2)}, u32[]{:S(2)}) collective-permute-start(bf16[128,128]{1,0:T(8,128)(2,1)S(1)} %get-tuple-element.44), channel_id=1, source_target_pairs={{0,12},{4,8},{8,4},{12,0},{1,13},{5,9},{9,5},{13,1},{2,14},{6,10},... | collective-permute-start | bytes 98312 | tf_op jit(solution)/shard_map/ppermute | solution.py:437
  7.3 4.8 %collective-permute-start.1 = (bf16[128,128]{1,0:T(8,128)(2,1)S(1)}, bf16[128,128]{1,0:T(8,128)(2,1)S(1)}, u32[]{:S(2)}, u32[]{:S(2)}) collective-permute-start(bf16[128,128]{1,0:T(8,128)(2,1)S(1)} %get-tuple-element.45), channel_id=1, source_target_pairs={{0,8},{4,12},{8,0},{12,4},{1,9},{5,13},{9,1},{13,5},{2,10},{6,14},... | collective-permute-start | bytes 98312 | tf_op jit(solution)/shard_map/ppermute | solution.py:437
  7.3 4.8 %collective-permute-start.2 = (bf16[128,128]{1,0:T(8,128)(2,1)S(1)}, bf16[128,128]{1,0:T(8,128)(2,1)S(1)}, u32[]{:S(2)}, u32[]{:S(2)}) collective-permute-start(bf16[128,128]{1,0:T(8,128)(2,1)S(1)} %get-tuple-element.46), channel_id=1, source_target_pairs={{0,4},{4,0},{8,12},{12,8},{1,5},{5,1},{9,13},{13,9},{2,6},{6,2},{1... | collective-permute-start | bytes 98312 | tf_op jit(solution)/shard_map/ppermute | solution.py:437
  8.0 8.1 %collective-permute-start.4 = (bf16[976,128]{1,0:T(8,128)(2,1)S(1)}, bf16[976,128]{1,0:T(8,128)(2,1)S(1)}, u32[]{:S(2)}, u32[]{:S(2)}) collective-permute-start(bf16[976,128]{1,0:T(8,128)(2,1)S(1)} %get-tuple-element.38.shared.refs_2_), channel_id=1, source_target_pairs={{0,2},{2,0},{1,3},{3,1},{4,6},{6,4},{5,7},{7,5},{8,10},{10,8},{9,1... | collective-permute-start | bytes 749576 | tf_op jit(solution)/shard_map/ppermute | solution.py:440
  14.7 1.4 %collective-permute-start.3 = (f32[304,128]{1,0:T(8,128)S(1)}, f32[304,128]{1,0:T(8,128)S(1)}, u32[]{:S(2)}, u32[]{:S(2)}) collective-permute-start(f32[304,128]{1,0:T(8,128)S(1)} %get-tuple-element.51), channel_id=1, source_target_pairs={{0,1},{1,0},{2,3},{3,2},{4,5},{5,4},{6,7},{7,6},{8,9},{9,8},{10,11... | collective-permute-start | bytes 466952 | tf_op jit(solution)/shard_map/ppermute | solution.py:468
  16.2 7.2 %collective-permute-start.5 = (bf16[304,128]{1,0:T(8,128)(2,1)S(1)}, bf16[304,128]{1,0:T(8,128)(2,1)S(1)}, u32[]{:S(2)}, u32[]{:S(2)}) collective-permute-start(bf16[304,128]{1,0:T(8,128)(2,1)S(1)} %add_convert_fusion.1), channel_id=1, source_target_pairs={{0,9},{1,8},{4,13},{5,12},{8,1},{9,0},{12,5},{13,4},{2,11},{3,10},... | collective-permute-start | bytes 233480 | tf_op jit(solution)/shard_map/ppermute | solution.py:496
  21.0 2.4 %collective-permute-start.6 = (bf16[64,128]{1,0:T(8,128)(2,1)S(1)}, bf16[64,128]{1,0:T(8,128)(2,1)S(1)}, u32[]{:S(2)}, u32[]{:S(2)}) collective-permute-start(bf16[64,128]{1,0:T(8,128)(2,1)S(1)} %get-tuple-element.63.refs_3_), channel_id=1, source_target_pairs={{0,1},{1,0},{2,3},{3,2},{4,5},{5,4},{6,7},{7,6},{8,9},{9,8},{10,11... | collective-permute-start | bytes 49160 | tf_op jit(solution)/shard_map/ppermute | solution.py:499
  21.4 4.1 %collective-permute-start.7 = (bf16[64,128]{1,0:T(8,128)(2,1)S(1)}, bf16[64,128]{1,0:T(8,128)(2,1)S(1)}, u32[]{:S(2)}, u32[]{:S(2)}) collective-permute-start(bf16[64,128]{1,0:T(8,128)(2,1)S(1)} %get-tuple-element.63.refs_3_), channel_id=1, source_target_pairs={{0,9},{1,8},{4,13},{5,12},{8,1},{9,0},{12,5},{13,4},{2,11},{3,10},... | collective-permute-start | bytes 49160 | tf_op jit(solution)/shard_map/ppermute | solution.py:496
  25.5 5.1 %collective-permute-start.8 = (bf16[432,128]{1,0:T(8,128)(2,1)S(1)}, bf16[432,128]{1,0:T(8,128)(2,1)S(1)}, u32[]{:S(2)}, u32[]{:S(2)}) collective-permute-start(bf16[432,128]{1,0:T(8,128)(2,1)S(1)} %pad_maximum_fusion), channel_id=1, source_target_pairs={{0,5},{1,4},{4,1},{5,0},{8,13},{9,12},{12,9},{13,8},{2,7},{3,6},{6... | collective-permute-start | bytes 331784 | tf_op jit(solution)/shard_map/ppermute | solution.py:496
  26.4 4.5 %collective-permute-start.9 = (bf16[64,128]{1,0:T(8,128)(2,1)S(1)}, bf16[64,128]{1,0:T(8,128)(2,1)S(1)}, u32[]{:S(2)}, u32[]{:S(2)}) collective-permute-start(bf16[64,128]{1,0:T(8,128)(2,1)S(1)} %collective-permute-done.7), channel_id=1, source_target_pairs={{0,1},{1,0},{2,3},{3,2},{4,5},{5,4},{6,7},{7,6},{8,9},{9,8},{10,11... | collective-permute-start | bytes 49160 | tf_op jit(solution)/shard_map/ppermute | solution.py:504
  30.6 1.4 %collective-permute-start.10 = (f32[304,128]{1,0:T(8,128)S(1)}, f32[304,128]{1,0:T(8,128)S(1)}, u32[]{:S(2)}, u32[]{:S(2)}) collective-permute-start(f32[304,128]{1,0:T(8,128)S(1)} %add_multiply_fusion.refs_0_), channel_id=1, source_target_pairs={{0,1},{1,0},{2,3},{3,2},{4,5},{5,4},{6,7},{7,6},{8,9},{9,8},{10,11... | collective-permute-start | bytes 466952 | tf_op jit(solution)/shard_map/ppermute | solution.py:525

commit v10 on v8

--- a/solution.py
+++ b/solution.py
@@ -102,9 +102,12 @@
     return lax.dot_general(lhs, rhs, (dims, ((), ())), preferred_element_type=F32)
 
 
+PART = 5
+
+
 def message_views(ref, own):
-    taps = [ref.at[t * own : (t + 1) * own] for t in range(9)]
-    base = 9 * own
+    taps = [ref.at[t * own : (t + 1) * own] for t in range(PART)]
+    base = PART * own
     halves = [
         [ref.at[base + (2 * k + h) * own : base + (2 * k + h + 1) * own] for h in range(2)] for k in range(SLOTS)
     ]
@@ -114,9 +117,9 @@
 
 def pack_kernel(rows_hbm, fields_hbm, weights_hbm, bias_hbm, cot_hbm, *refs, count):
     n = len(halo_plans(count))
-    rows_out, fields_out, shared = refs[:3]
-    maps = refs[3 : 3 + n]
-    outs = refs[3 + n : -3]
+    rows_out, fields_out, shared, taps_out = refs[:4]
+    maps = refs[4 : 4 + n]
+    outs = refs[4 + n : -3]
     rows, bias, sem = refs[-3:]
     own = weights_hbm.shape[1]
     taps, halves, pieces = message_views(shared, own)
@@ -126,7 +129,9 @@
     get_fields.start()
     get_bias = pltpu.make_async_copy(bias_hbm, bias, sem.at[2])
     get_bias.start()
-    more = [pltpu.make_async_copy(weights_hbm.at[t], taps[t], sem.at[3 + t]) for t in range(9)]
+    first = lax.axis_index("rep") * (9 - PART)
+    more = [pltpu.make_async_copy(weights_hbm.at[first + t], taps[t], sem.at[3 + t]) for t in range(PART)]
+    more.append(pltpu.make_async_copy(weights_hbm, taps_out, sem.at[3 + PART]))
     for k in range(SLOTS):
         for h in range(2):
             source = cot_hbm.at[0, k, :, h * 128 : h * 128 + 128]
@@ -181,7 +186,7 @@
     )
 
 
-def window_kernel(rows, fields, shared, windows, spreads, gathers, kernel, back_kernel, turned):
+def window_kernel(rows, fields, taps, windows, spreads, gathers, kernel, back_kernel, turned):
     own = kernel.shape[0] // 3
     full, _, above = slot_flags(rows)
     column = iota((1, FRAME), 1) % TS
@@ -208,7 +213,7 @@
                 spot = jnp.where(p == 0, FRAME - TS, TS * (p - 1)) + side * (TS - 1)
                 hits = (p >= 0) & (p < EDGE) & (frame_lane == spot)
                 refs[side, k] = jnp.where(hits, 1.0, 0.0).astype(BF16)
-    stack = stack_of(message_views(shared, own)[0])
+    stack = stack_of([taps.at[t] for t in range(9)])
     kernel[...] = stack
     back_kernel[...] = turn(stack, turned)
 
@@ -302,12 +307,17 @@
 
 
 def other_kernel(rows, windows, *refs):
-    n = (len(refs) - 1) // 3
+    n = (len(refs) - 1) // 4
     turned = refs[-1]
     full = slot_flags(rows)[0]
-    for ref, frames, back_kernel in zip(refs[:n], refs[n : 2 * n], refs[2 * n : 3 * n]):
+    rep = lax.axis_index("rep")
+    for ref, swapped, frames, back_kernel in zip(*(refs[i * n : i * n + n] for i in range(4))):
         own = back_kernel.shape[0] // 3
-        taps, halves, pieces = message_views(ref, own)
+        part, halves, pieces = message_views(ref, own)
+        mine = [tap[...] for tap in part]
+        theirs = [swapped[t * own : (t + 1) * own, :] for t in range(PART)]
+        taps = [jnp.where(rep == 0, mine[t], theirs[t]) for t in range(PART)]
+        taps += [jnp.where(rep == 0, theirs[t], mine[t]) for t in range(2 * PART - 9, PART)]
         stack = stack_of(taps)
         bias_column = column_of(pieces, own)
         for k in range(SLOTS):
@@ -407,7 +417,7 @@
     reps = lax.axis_size("rep")
     plans = halo_plans(count)
     n = len(plans)
-    shared_rows = 9 * own + 2 * SLOTS * own + 16
+    shared_rows = PART * own + 2 * SLOTS * own + 16
     half_rows = -(-(9 * own + 1) // 32) * 16
     swap = [(0, 1), (1, 0)]
 
@@ -415,13 +425,14 @@
         pltpu.with_memory_space_constraint(x, pltpu.HBM)
         for x in (tile_rows, fields, weights, bias.reshape(1, own), cotangent)
     ]
-    rows, tiles, shared, *packed = call(
+    rows, tiles, shared, taps, *packed = call(
         lambda *refs: pack_kernel(*refs, count=count),
         [HBM] * 5,
         [
             struct(tile_rows.shape, jnp.int32),
             struct((SLOTS, C, CELLS), BF16),
             struct((shared_rows, 128), BF16),
+            struct((9, own, C), BF16),
         ]
         + [struct((SLOTS * CELLS, 128), BF16)] * n
         + [struct((C, 128), BF16)] * n,
@@ -450,7 +461,7 @@
             struct((3 * own, 3 * own), BF16),
         ],
         [pltpu.VMEM((3 * C, 3 * own), F32)],
-    )(rows, tiles, shared)
+    )(rows, tiles, taps)
 
     windows, frames, result, keep, send = call(
         lambda *refs: forward_kernel(*refs, n_halos=len(halos), half_rows=half_rows, count=count),
@@ -469,10 +480,10 @@
     sums = keep + lax.ppermute(send, "rep", swap)
     other_frames = call(
         other_kernel,
-        [SMEM, VMEM] + [VMEM] * len(others),
+        [SMEM, VMEM] + [VMEM] * (2 * len(others)),
         [struct((SLOTS, 3 * own, FRAME), BF16)] * len(others) + [struct((3 * own, 3 * own), BF16)] * len(others),
         [pltpu.VMEM((3 * C, 3 * own), F32)],
-    )(rows, windows, *others)
+    )(rows, windows, *others, *(lax.ppermute(x[: PART * own], "rep", swap) for x in others))
     other_frames, other_back = other_frames[: len(others)], other_frames[len(others) :]
     rounded = sums.astype(BF16)
     frames, rounded, other_frames = lax.optimization_barrier((frames, rounded, other_frames))

time: 32.3 us -> 32.9 us (1.019)
  waiting for transfers between devices: 8.18 us -> 8.95 us
    ppermute x3, starting transfers between devices: 5.08 us -> 3.8 us  [cross(): return lax.ppermute(x, ('tiles', 'rep'), pairs)]
    ppermute x0 -> x1, waiting for transfers between devices: none -> 0.98 us  [on_device(): lax.ppermute(x[:PART * own], 'rep', swap)]
    ppermute x3, waiting for transfers between devices: 6.14 us -> 6.71 us  [cross(): return lax.ppermute(x, ('tiles', 'rep'), pairs)]
    ppermute x1, waiting for transfers between devices: 0.53 us -> 0.01 us  [on_device(): lax.ppermute(shared, 'chan', [(i, (i + s) % chans) for i in range(chans)])]
    ppermute x0 -> x1, starting transfers between devices: none -> 0.49 us  [on_device(): lax.ppermute(x[:PART * own], 'rep', swap)]
  transfers between devices with their start and end apart: 11 -> 12, of which waited for: 6 -> 5; matrix products, arithmetic and copies ran while one was open for 0% -> 0% of each run, Pallas kernels for 24% -> 24%
where the time goes in v10:
time: 32.9 us; the launch traced here: 32.7 us
  starting transfers between devices  12.8 us (39%)
  Pallas kernels  10.1 us (31%)
  waiting for transfers between devices  8.95 us (27%)
  between operations  0.74 us (2%)
    ppermute x3, waiting for transfers between devices, cross(): return lax.ppermute(x, ('tiles', 'rep'), pairs)  6.71 us
    ppermute x3, starting transfers between devices, move(): return lax.ppermute(x, 'tiles', [(i, route(i)) for i in range(count)])  5.76 us
    ppermute x3, starting transfers between devices, cross(): return lax.ppermute(x, ('tiles', 'rep'), pairs)  3.8 us
    pallas_call x1, Pallas kernels, on_device(): call(lambda *refs: forward_kernel(*refs, n_halos=len(halos), half_rows=ha...  2.51 us
    ppermute x1, starting transfers between devices, on_device(): lax.ppermute(shared, 'chan', [(i, (i + s) % chans) for i in range(chans)])  1.63 us
    pallas_call x1, Pallas kernels, on_device(): call(backward_kernel, [SMEM] + [VMEM] * (5 + 2 * len(others)), [struct((S...  1.55 us
    pallas_call x1, Pallas kernels, on_device(): call(lambda *refs: pack_kernel(*refs, count=count), [HBM] * 5, [struct(ti...  1.54 us
    pallas_call x1, Pallas kernels, on_device(): call(other_kernel, [SMEM, VMEM] + [VMEM] * (2 * len(others)), [struct((SL...  1.41 us
  transfers between devices with their start and end apart: 12, of which 5 were waited for; matrix products, arithmetic and copies ran while one was open for 0% of the time, Pallas kernels for 24%

profile of v10, /device:TPU:0, one launch (start us, length us, event | category | flops | bytes accessed | tf_op | source)
XLA Modules:
  0.0 32.7 jit_solution(6277683228599206992)
XLA Ops:
  0.6 1.5 %shard_map.84 = (s32[4,3]{1,0:T(4,128)S(1)}, bf16[3,128,256]{2,1,0:T(8,128)(2,1)S(1)}, bf16[720,128]{1,0:T(8,128)(2,1)S(1)}, bf16[9,64,128]{2,1,0:T(8,128)(2,1)S...) custom-call(s32[4,3]{1,0:T(4,128)} %refs_0_.1, ...), custom_call_target="tpu_custom_call" | custom-call | tf_op jit(solution)/shard_map/pallas_call | solution.py:428
  2.2 5.1 %collective-permute-start = (bf16[128,128]{1,0:T(8,128)(2,1)S(1)}, bf16[128,128]{1,0:T(8,128)(2,1)S(1)}, u32[]{:S(2)}, u32[]{:S(2)}) collective-permute-start(bf16[128,128]{1,0:T(8,128)(2,1)S(1)} %get-tuple-element.46), channel_id=1, source_target_pairs={{0,12},{4,8},{8,4},{12,0},{1,13},{5,9},{9,5},{13,1},{2,14},{6,10},... | collective-permute-start | bytes 98312 | tf_op jit(solution)/shard_map/ppermute | solution.py:448
  7.3 0.0 collective-permute-start.1
  7.3 0.6 %collective-permute-start.2 = (bf16[128,128]{1,0:T(8,128)(2,1)S(1)}, bf16[128,128]{1,0:T(8,128)(2,1)S(1)}, u32[]{:S(2)}, u32[]{:S(2)}) collective-permute-start(bf16[128,128]{1,0:T(8,128)(2,1)S(1)} %get-tuple-element.48), channel_id=1, source_target_pairs={{0,4},{4,0},{8,12},{12,8},{1,5},{5,1},{9,13},{13,9},{2,6},{6,2},{1... | collective-permute-start | bytes 98312 | tf_op jit(solution)/shard_map/ppermute | solution.py:448
  7.9 1.6 %collective-permute-start.3 = (bf16[720,128]{1,0:T(8,128)(2,1)S(1)}, bf16[720,128]{1,0:T(8,128)(2,1)S(1)}, u32[]{:S(2)}, u32[]{:S(2)}) collective-permute-start(bf16[720,128]{1,0:T(8,128)(2,1)S(1)} %get-tuple-element.39.refs_2_.shared), channel_id=1, source_target_pairs={{0,2},{2,0},{1,3},{3,1},{4,6},{6,4},{5,7},{7,5},{8,10},{10,8},{9,1... | collective-permute-start | bytes 552968 | tf_op jit(solution)/shard_map/ppermute | solution.py:451
  9.6 1.3 %shard_map.85 = (bf16[3,384,384]{2,1,0:T(8,128)(2,1)S(1)}, bf16[2,3,128,384]{3,2,1,0:T(8,128)(2,1)S(1)}, bf16[2,3,384,128]{3,2,1,0:T(8,128)(2,1)S(1)}, bf16[192,384]{1,0:T(8,128)(2,1)S(1)}, bf16[192,192]{1,0:T(8,128)(2,1)S(1)}) custom-call(s32[4,3]{1,0:T(4,128)S(1)} %get-tuple-element.38.rows.refs_0_, ...), custom_call_target="tpu_custom_call" | custom-call | tf_op jit(solution)/shard_map/pallas_call | solution.py:453
  10.9 1.2 %collective-permute-done.1.refs_7_ = bf16[128,128]{1,0:T(8,128)(2,1)S(1)} collective-permute-done((bf16[128,128]{1,0:T(8,128)(2,1)S(1)}, bf16[128,128]{1,0:T(8,128)(2,1)S(1)}, u32[]{:S(2)}, u32[]{:S(2)}) %collective-permute-start.1) | collective-permute-done | bytes 32800 | tf_op jit(solution)/shard_map/ppermute | solution.py:448
  12.1 2.5 %shard_map.86 = (bf16[3,384,384]{2,1,0:T(8,128)(2,1)S(1)}, bf16[3,192,384]{2,1,0:T(8,128)(2,1)S(1)}, bf16[3,64,256]{2,1,0:T(8,128)(2,1)S(1)}, f32[304,128]{1,0:T(8,128)S(1)}, f32[304,128]{1,0:T(8,128)S(1)}) custom-call(s32[4,3]{1,0:T(4,128)S(1)} %get-tuple-element.38.rows.refs_0_, bf16[3,128,256]{2,1,0:T(8,128)(2,1)S(1)} %get-tuple-element.40.fields.refs_1_, ...), custom_call_target="tpu_custom_call" | custom-call | flops 4000000000 | tf_op jit(solution)/shard_map/pallas_call | solution.py:466
  14.6 0.1 collective-permute-start.4
  14.7 0.5 %collective-permute-start.5 = (bf16[320,128]{1,0:T(8,128)(2,1)S(1)}, bf16[320,128]{1,0:T(8,128)(2,1)S(1)}, u32[]{:S(2)}, u32[]{:S(2)}) collective-permute-start(bf16[320,128]{1,0:T(8,128)(2,1)S(1)} %slice.12), channel_id=1, source_target_pairs={{0,1},{1,0},{2,3},{3,2},{4,5},{5,4},{6,7},{7,6},{8,9},{9,8},{10,11... | collective-permute-start | bytes 245768 | tf_op jit(solution)/shard_map/ppermute | solution.py:486
  15.2 1.0 %collective-permute-done.5.refs_1_ = bf16[320,128]{1,0:T(8,128)(2,1)S(1)} collective-permute-done((bf16[320,128]{1,0:T(8,128)(2,1)S(1)}, bf16[320,128]{1,0:T(8,128)(2,1)S(1)}, u32[]{:S(2)}, u32[]{:S(2)}) %collective-permute-start.5) | collective-permute-done | bytes 81952 | tf_op jit(solution)/shard_map/ppermute | solution.py:486
  16.2 1.4 %shard_map.87 = (bf16[3,192,384]{2,1,0:T(8,128)(2,1)S(1)}, bf16[192,192]{1,0:T(8,128)(2,1)S(1)}) custom-call(s32[4,3]{1,0:T(4,128)S(1)} %get-tuple-element.38.rows.refs_0_, bf16[3,384,384]{2,1,0:T(8,128)(2,1)S(1)} %get-tuple-element.55.windows, bf16[720,128]{1,0:T(8,128)(2,1)S(1)} %collective-permute-done.3.refs_0_, ...), custom_call_target="tpu_custom_call" | custom-call | tf_op jit(solution)/shard_map/pallas_call | solution.py:481
  17.7 2.0 %collective-permute-start.6 = (bf16[304,128]{1,0:T(8,128)(2,1)S(1)}, bf16[304,128]{1,0:T(8,128)(2,1)S(1)}, u32[]{:S(2)}, u32[]{:S(2)}) collective-permute-start(bf16[304,128]{1,0:T(8,128)(2,1)S(1)} %add_convert_fusion.1), channel_id=1, source_target_pairs={{0,9},{1,8},{4,13},{5,12},{8,1},{9,0},{12,5},{13,4},{2,11},{3,10},... | collective-permute-start | bytes 233480 | tf_op jit(solution)/shard_map/ppermute | solution.py:507
  19.7 1.5 %shard_map.88 = (f32[3,64,256]{2,1,0:T(8,128)S(1)}, bf16[64,128]{1,0:T(8,128)(2,1)S(1)}, bf16[1,3,64,256]{3,2,1,0:T(8,128)(2,1)}) custom-call(s32[4,3]{1,0:T(4,128)S(1)} %get-tuple-element.38.rows.refs_0_, bf16[720,128]{1,0:T(8,128)(2,1)S(1)} %get-tuple-element.39.refs_2_.shared, bf16[2,3,384,128]{3,2,1,0:T(8,128)(2,1)S(1)} %get-tuple-element.42.gathers, ...), custom_call_target="tpu_custom_call" | custom-call | tf_op jit(solution)/shard_map/pallas_call | solution.py:491
  21.2 0.3 collective-permute-start.7
  21.5 0.8 %collective-permute-start.8 = (bf16[64,128]{1,0:T(8,128)(2,1)S(1)}, bf16[64,128]{1,0:T(8,128)(2,1)S(1)}, u32[]{:S(2)}, u32[]{:S(2)}) collective-permute-start(bf16[64,128]{1,0:T(8,128)(2,1)S(1)} %get-tuple-element.65.refs_3_), channel_id=1, source_target_pairs={{0,9},{1,8},{4,13},{5,12},{8,1},{9,0},{12,5},{13,4},{2,11},{3,10},... | collective-permute-start | bytes 49160 | tf_op jit(solution)/shard_map/ppermute | solution.py:507
  22.3 2.5 %collective-permute-done.6 = bf16[304,128]{1,0:T(8,128)(2,1)S(1)} collective-permute-done((bf16[304,128]{1,0:T(8,128)(2,1)S(1)}, bf16[304,128]{1,0:T(8,128)(2,1)S(1)}, u32[]{:S(2)}, u32[]{:S(2)}) %collective-permute-start.6) | collective-permute-done | bytes 77856 | tf_op jit(solution)/shard_map/ppermute | solution.py:507
  24.8 0.7 %collective-permute-done.8 = bf16[64,128]{1,0:T(8,128)(2,1)S(1)} collective-permute-done((bf16[64,128]{1,0:T(8,128)(2,1)S(1)}, bf16[64,128]{1,0:T(8,128)(2,1)S(1)}, u32[]{:S(2)}, u32[]{:S(2)}) %collective-permute-start.8) | collective-permute-done | bytes 16416 | tf_op jit(solution)/shard_map/ppermute | solution.py:507
  25.6 1.0 %collective-permute-start.9 = (bf16[432,128]{1,0:T(8,128)(2,1)S(1)}, bf16[432,128]{1,0:T(8,128)(2,1)S(1)}, u32[]{:S(2)}, u32[]{:S(2)}) collective-permute-start(bf16[432,128]{1,0:T(8,128)(2,1)S(1)} %pad_maximum_fusion), channel_id=1, source_target_pairs={{0,5},{1,4},{4,1},{5,0},{8,13},{9,12},{12,9},{13,8},{2,7},{3,6},{6... | collective-permute-start | bytes 331784 | tf_op jit(solution)/shard_map/ppermute | solution.py:507
  26.6 0.3 collective-permute-start.10
  26.9 3.5 %collective-permute-done.9 = bf16[432,128]{1,0:T(8,128)(2,1)S(1)} collective-permute-done((bf16[432,128]{1,0:T(8,128)(2,1)S(1)}, bf16[432,128]{1,0:T(8,128)(2,1)S(1)}, u32[]{:S(2)}, u32[]{:S(2)}) %collective-permute-start.9) | collective-permute-done | bytes 110624 | tf_op jit(solution)/shard_map/ppermute | solution.py:507
  30.4 0.5 %collective-permute-start.11 = (f32[304,128]{1,0:T(8,128)S(1)}, f32[304,128]{1,0:T(8,128)S(1)}, u32[]{:S(2)}, u32[]{:S(2)}) collective-permute-start(f32[304,128]{1,0:T(8,128)S(1)} %add_multiply_fusion.refs_0_), channel_id=1, source_target_pairs={{0,1},{1,0},{2,3},{3,2},{4,5},{5,4},{6,7},{7,6},{8,9},{9,8},{10,11... | collective-permute-start | bytes 466952 | tf_op jit(solution)/shard_map/ppermute | solution.py:536
  30.9 1.0 %shard_map.89 = bf16[1,3,64,256]{3,2,1,0:T(8,128)(2,1)} custom-call(f32[3,64,256]{2,1,0:T(8,128)S(1)} %get-tuple-element.63.base, bf16[64,128]{1,0:T(8,128)(2,1)S(1)} %get-tuple-element.73.refs_0_, bf16[64,128]{1,0:T(8,128)(2,1)S(1)} %collective-permute-done.10.refs_1_, bf16[64,128]{1,0:T(8,128)(2,1)S(1)} %get-tuple-element.72.refs_2_, ...), custom_call_target="tpu_custom_call" | custom-call | tf_op jit(solution)/shard_map/pallas_call | solution.py:527
  31.9 0.7 %shard_map.90 = (f32[9,64,128]{2,1,0:T(8,128)}, f32[1,64]{1,0:T(1,128)}) custom-call(f32[304,128]{1,0:T(8,128)S(1)} %add_multiply_fusion.refs_0_, f32[304,128]{1,0:T(8,128)S(1)} %collective-permute-done.11.refs_1_), custom_call_target="tpu_custom_call" | custom-call | tf_op jit(solution)/shard_map/pallas_call | solution.py:532
  (13 shorter events, 0.1 us)
Async XLA Ops:
  2.2 8.7 %collective-permute-start = (bf16[128,128]{1,0:T(8,128)(2,1)S(1)}, bf16[128,128]{1,0:T(8,128)(2,1)S(1)}, u32[]{:S(2)}, u32[]{:S(2)}) collective-permute-start(bf16[128,128]{1,0:T(8,128)(2,1)S(1)} %get-tuple-element.46), channel_id=1, source_target_pairs={{0,12},{4,8},{8,4},{12,0},{1,13},{5,9},{9,5},{13,1},{2,14},{6,10},... | collective-permute-start | bytes 98312 | tf_op jit(solution)/shard_map/ppermute | solution.py:448
  7.3 4.8 %collective-permute-start.1 = (bf16[128,128]{1,0:T(8,128)(2,1)S(1)}, bf16[128,128]{1,0:T(8,128)(2,1)S(1)}, u32[]{:S(2)}, u32[]{:S(2)}) collective-permute-start(bf16[128,128]{1,0:T(8,128)(2,1)S(1)} %get-tuple-element.47), channel_id=1, source_target_pairs={{0,8},{4,12},{8,0},{12,4},{1,9},{5,13},{9,1},{13,5},{2,10},{6,14},... | collective-permute-start | bytes 98312 | tf_op jit(solution)/shard_map/ppermute | solution.py:448
  7.3 4.8 %collective-permute-start.2 = (bf16[128,128]{1,0:T(8,128)(2,1)S(1)}, bf16[128,128]{1,0:T(8,128)(2,1)S(1)}, u32[]{:S(2)}, u32[]{:S(2)}) collective-permute-start(bf16[128,128]{1,0:T(8,128)(2,1)S(1)} %get-tuple-element.48), channel_id=1, source_target_pairs={{0,4},{4,0},{8,12},{12,8},{1,5},{5,1},{9,13},{13,9},{2,6},{6,2},{1... | collective-permute-start | bytes 98312 | tf_op jit(solution)/shard_map/ppermute | solution.py:448
  7.9 6.7 %collective-permute-start.3 = (bf16[720,128]{1,0:T(8,128)(2,1)S(1)}, bf16[720,128]{1,0:T(8,128)(2,1)S(1)}, u32[]{:S(2)}, u32[]{:S(2)}) collective-permute-start(bf16[720,128]{1,0:T(8,128)(2,1)S(1)} %get-tuple-element.39.refs_2_.shared), channel_id=1, source_target_pairs={{0,2},{2,0},{1,3},{3,1},{4,6},{6,4},{5,7},{7,5},{8,10},{10,8},{9,1... | collective-permute-start | bytes 552968 | tf_op jit(solution)/shard_map/ppermute | solution.py:451
  14.6 3.0 %collective-permute-start.4 = (f32[304,128]{1,0:T(8,128)S(1)}, f32[304,128]{1,0:T(8,128)S(1)}, u32[]{:S(2)}, u32[]{:S(2)}) collective-permute-start(f32[304,128]{1,0:T(8,128)S(1)} %get-tuple-element.54), channel_id=1, source_target_pairs={{0,1},{1,0},{2,3},{3,2},{4,5},{5,4},{6,7},{7,6},{8,9},{9,8},{10,11... | collective-permute-start | bytes 466952 | tf_op jit(solution)/shard_map/ppermute | solution.py:480
  14.7 1.5 %collective-permute-start.5 = (bf16[320,128]{1,0:T(8,128)(2,1)S(1)}, bf16[320,128]{1,0:T(8,128)(2,1)S(1)}, u32[]{:S(2)}, u32[]{:S(2)}) collective-permute-start(bf16[320,128]{1,0:T(8,128)(2,1)S(1)} %slice.12), channel_id=1, source_target_pairs={{0,1},{1,0},{2,3},{3,2},{4,5},{5,4},{6,7},{7,6},{8,9},{9,8},{10,11... | collective-permute-start | bytes 245768 | tf_op jit(solution)/shard_map/ppermute | solution.py:486
  17.7 7.1 %collective-permute-start.6 = (bf16[304,128]{1,0:T(8,128)(2,1)S(1)}, bf16[304,128]{1,0:T(8,128)(2,1)S(1)}, u32[]{:S(2)}, u32[]{:S(2)}) collective-permute-start(bf16[304,128]{1,0:T(8,128)(2,1)S(1)} %add_convert_fusion.1), channel_id=1, source_target_pairs={{0,9},{1,8},{4,13},{5,12},{8,1},{9,0},{12,5},{13,4},{2,11},{3,10},... | collective-permute-start | bytes 233480 | tf_op jit(solution)/shard_map/ppermute | solution.py:507
  21.2 3.6 %collective-permute-start.7 = (bf16[64,128]{1,0:T(8,128)(2,1)S(1)}, bf16[64,128]{1,0:T(8,128)(2,1)S(1)}, u32[]{:S(2)}, u32[]{:S(2)}) collective-permute-start(bf16[64,128]{1,0:T(8,128)(2,1)S(1)} %get-tuple-element.65.refs_3_), channel_id=1, source_target_pairs={{0,1},{1,0},{2,3},{3,2},{4,5},{5,4},{6,7},{7,6},{8,9},{9,8},{10,11... | collective-permute-start | bytes 49160 | tf_op jit(solution)/shard_map/ppermute | solution.py:510
  21.5 4.1 %collective-permute-start.8 = (bf16[64,128]{1,0:T(8,128)(2,1)S(1)}, bf16[64,128]{1,0:T(8,128)(2,1)S(1)}, u32[]{:S(2)}, u32[]{:S(2)}) collective-permute-start(bf16[64,128]{1,0:T(8,128)(2,1)S(1)} %get-tuple-element.65.refs_3_), channel_id=1, source_target_pairs={{0,9},{1,8},{4,13},{5,12},{8,1},{9,0},{12,5},{13,4},{2,11},{3,10},... | collective-permute-start | bytes 49160 | tf_op jit(solution)/shard_map/ppermute | solution.py:507
  25.6 4.8 %collective-permute-start.9 = (bf16[432,128]{1,0:T(8,128)(2,1)S(1)}, bf16[432,128]{1,0:T(8,128)(2,1)S(1)}, u32[]{:S(2)}, u32[]{:S(2)}) collective-permute-start(bf16[432,128]{1,0:T(8,128)(2,1)S(1)} %pad_maximum_fusion), channel_id=1, source_target_pairs={{0,5},{1,4},{4,1},{5,0},{8,13},{9,12},{12,9},{13,8},{2,7},{3,6},{6... | collective-permute-start | bytes 331784 | tf_op jit(solution)/shard_map/ppermute | solution.py:507
  26.6 4.3 %collective-permute-start.10 = (bf16[64,128]{1,0:T(8,128)(2,1)S(1)}, bf16[64,128]{1,0:T(8,128)(2,1)S(1)}, u32[]{:S(2)}, u32[]{:S(2)}) collective-permute-start(bf16[64,128]{1,0:T(8,128)(2,1)S(1)} %collective-permute-done.8), channel_id=1, source_target_pairs={{0,1},{1,0},{2,3},{3,2},{4,5},{5,4},{6,7},{7,6},{8,9},{9,8},{10,11... | collective-permute-start | bytes 49160 | tf_op jit(solution)/shard_map/ppermute | solution.py:515
  30.4 1.5 %collective-permute-start.11 = (f32[304,128]{1,0:T(8,128)S(1)}, f32[304,128]{1,0:T(8,128)S(1)}, u32[]{:S(2)}, u32[]{:S(2)}) collective-permute-start(f32[304,128]{1,0:T(8,128)S(1)} %add_multiply_fusion.refs_0_), channel_id=1, source_target_pairs={{0,1},{1,0},{2,3},{3,2},{4,5},{5,4},{6,7},{7,6},{8,9},{9,8},{10,11... | collective-permute-start | bytes 466952 | tf_op jit(solution)/shard_map/ppermute | solution.py:536

commit v11 on v9

--- a/solution.py
+++ b/solution.py
@@ -102,55 +102,34 @@
     return lax.dot_general(lhs, rhs, (dims, ((), ())), preferred_element_type=F32)
 
 
-def message_views(ref, own):
-    taps = [ref.at[t * own : (t + 1) * own] for t in range(9)]
-    base = 9 * own
-    halves = [
-        [ref.at[base + (2 * k + h) * own : base + (2 * k + h + 1) * own] for h in range(2)] for k in range(SLOTS)
-    ]
-    at = base + 2 * SLOTS * own
-    return taps, halves, ref.at[at : at + 16]
-
-
 def pack_kernel(rows_hbm, fields_hbm, weights_hbm, bias_hbm, cot_hbm, *refs, count):
     n = len(halo_plans(count))
-    rows_out, fields_out, shared = refs[:3]
-    maps = refs[3 : 3 + n]
-    outs = refs[3 + n : -3]
-    rows, bias, sem = refs[-3:]
-    own = weights_hbm.shape[1]
-    taps, halves, pieces = message_views(shared, own)
-    get_rows = pltpu.make_async_copy(rows_hbm, rows, sem.at[0])
-    get_rows.start()
-    get_fields = pltpu.make_async_copy(fields_hbm.at[0], fields_out, sem.at[1])
-    get_fields.start()
-    get_bias = pltpu.make_async_copy(bias_hbm, bias, sem.at[2])
-    get_bias.start()
-    more = [pltpu.make_async_copy(weights_hbm.at[t], taps[t], sem.at[3 + t]) for t in range(9)]
-    for k in range(SLOTS):
-        for h in range(2):
-            source = cot_hbm.at[0, k, :, h * 128 : h * 128 + 128]
-            more.append(pltpu.make_async_copy(source, halves[k][h], sem.at[12 + 2 * k + h]))
-    for copy in more:
+    rows_out, fields_out, weights_out, bias_out, cot_out = refs[:5]
+    maps = refs[5 : 5 + n]
+    outs = refs[5 + n : -2]
+    rows, sem = refs[-2:]
+    moves = [
+        (rows_hbm, rows),
+        (fields_hbm.at[0], fields_out),
+        (weights_hbm, weights_out),
+        (bias_hbm, bias_out),
+        (cot_hbm.at[0], cot_out),
+    ]
+    copies = [pltpu.make_async_copy(src, dst, sem.at[i]) for i, (src, dst) in enumerate(moves)]
+    for copy in copies:
         copy.start()
-    get_rows.wait()
+    copies[0].wait()
     position = lax.axis_index("tiles")
     plans = halo_plans(count)
     for plan, out in zip(plans, maps):
         out[...] = halo_map(rows, count, position, plan)
     put_rows = pltpu.make_async_copy(rows, rows_out, sem.at[0])
     put_rows.start()
-    get_bias.wait()
-    line = jnp.concatenate([bias[...], jnp.zeros((1, 128 - own), F32)], axis=1)
-    high = line.astype(BF16).astype(F32)
-    middle = (line - high).astype(BF16).astype(F32)
-    low = line - high - middle
-    pieces[...] = jnp.concatenate([high, middle, low, jnp.zeros((13, 128), F32)], axis=0).astype(BF16)
-    get_fields.wait()
+    copies[1].wait()
     cells = jnp.concatenate([fields_out[k] for k in range(SLOTS)], axis=1)
     for out, hits in zip(outs, maps):
         out[...] = dot(cells, hits[...]).astype(BF16)
-    for copy in more:
+    for copy in copies[2:]:
         copy.wait()
     put_rows.wait()
 
@@ -177,11 +156,11 @@
 
 def stack_of(taps):
     return jnp.concatenate(
-        [jnp.concatenate([taps[3 * a + b][...] for b in range(3)], axis=1) for a in range(3)], axis=0
+        [jnp.concatenate([taps[3 * a + b] for b in range(3)], axis=1) for a in range(3)], axis=0
     )
 
 
-def window_kernel(rows, fields, shared, windows, spreads, gathers, kernel, back_kernel, turned):
+def window_kernel(rows, fields, weights, windows, spreads, gathers, kernel, back_kernel, turned):
     own = kernel.shape[0] // 3
     full, _, above = slot_flags(rows)
     column = iota((1, FRAME), 1) % TS
@@ -208,15 +187,14 @@
                 spot = jnp.where(p == 0, FRAME - TS, TS * (p - 1)) + side * (TS - 1)
                 hits = (p >= 0) & (p < EDGE) & (frame_lane == spot)
                 refs[side, k] = jnp.where(hits, 1.0, 0.0).astype(BF16)
-    stack = stack_of(message_views(shared, own)[0])
+    stack = stack_of(weights)
     kernel[...] = stack
     back_kernel[...] = turn(stack, turned)
 
 
-def column_of(pieces, own):
-    eye = iota((own, 128), 0) == iota((own, 128), 1)
-    parts = pieces[...].astype(F32)
-    line = parts[0:1] + parts[1:2] + parts[2:3]
+def column_of(line):
+    own = line.shape[1]
+    eye = iota((own, own), 0) == iota((own, own), 1)
     return jnp.sum(jnp.where(eye, line, 0.0), axis=1, keepdims=True)
 
 
@@ -242,10 +220,6 @@
     return jnp.concatenate([pltpu.roll(wide, FRAME - TS, 1), wide, pltpu.roll(wide, TS, 1)], axis=0).astype(BF16)
 
 
-def upstream_of(halves, k, full):
-    return jnp.concatenate([halves[k][0][...], halves[k][1][...]], axis=1).astype(F32) * full[k]
-
-
 def half_of(count):
     position = lax.axis_index("tiles")
     rep = lax.axis_index("rep")
@@ -254,16 +228,15 @@
     return rep
 
 
-def forward_kernel(rows, fields, shared, kernel, spreads, windows, *refs, n_halos, half_rows, count):
+def forward_kernel(rows, fields, bias, cot, kernel, spreads, windows, *refs, n_halos, half_rows, count):
     halos = refs[:n_halos]
-    full_windows, frames, result, keep, send = refs[n_halos:]
+    frames, slopes_out, result, keep, send = refs[n_halos:]
     own = kernel.shape[0] // 3
     full, at_top, _ = slot_flags(rows)
     start = pl.multiple_of(lax.axis_index("chan") * own, own)
     half = half_of(count)
     lane128 = iota((1, 128), 1)
-    _, halves, pieces = message_views(shared, own)
-    bias_column = column_of(pieces, own)
+    bias_column = column_of(bias[...])
     halo = halos[0][...].astype(F32)
     for ref in halos[1:]:
         halo = halo + ref[...].astype(F32)
@@ -282,11 +255,11 @@
         right = windows[k, 2 * C :] + (east + jnp.concatenate([rest, at_top[k] * fold_right], axis=1)).astype(BF16)
         centre = windows[k, C : 2 * C] + jnp.concatenate([rest, at_top[k] * fold], axis=1).astype(BF16)
         window = jnp.concatenate([left, centre, right], axis=0)
-        full_windows[k] = window
-        up = upstream_of(halves, k, full)
+        up = cot[k].astype(F32) * full[k]
         gelu, slopes = activation(kernel[...], window, bias_column, up)
         result[k] = (full[k] * (fields[k, pl.ds(start, own), :].astype(F32) + gelu)).astype(BF16)
         slope_sum = slope_sum + slopes
+        slopes_out[k * own : (k + 1) * own, :] = slopes.astype(BF16)
         frame = frame_of(slopes)
         frames[k] = frame
         grads = grads + dot(frame, window, ((1,), (1,)))
@@ -301,25 +274,16 @@
     send[...] = jnp.where(half == 0, high, low)
 
 
-def other_kernel(rows, windows, *refs):
-    n = (len(refs) - 1) // 3
-    turned = refs[-1]
-    full = slot_flags(rows)[0]
-    for ref, frames, back_kernel in zip(refs[:n], refs[n : 2 * n], refs[2 * n : 3 * n]):
-        own = back_kernel.shape[0] // 3
-        taps, halves, pieces = message_views(ref, own)
-        stack = stack_of(taps)
-        bias_column = column_of(pieces, own)
-        for k in range(SLOTS):
-            _, slopes = activation(stack, windows[k], bias_column, upstream_of(halves, k, full))
-            frames[k] = frame_of(slopes)
-        back_kernel[...] = turn(stack, turned)
-
-
-def backward_kernel(rows, shared, gathers, result, *refs):
+def turn_kernel(*refs):
+    n = (len(refs) - 1) // 2
+    for ref, back_kernel in zip(refs[:n], refs[n : 2 * n]):
+        back_kernel[...] = turn(stack_of(ref), refs[-1])
+
+
+def backward_kernel(rows, cot, gathers, result, own_frames, *refs):
     base, edges, result_out, sem = refs[-4:]
-    n = (len(refs) - 4) // 2
-    frames, back_kernels = refs[:n], refs[n : 2 * n]
+    n = (len(refs) - 5) // 2
+    slopes, back_kernels = refs[:n], refs[n : 2 * n + 1]
     own = back_kernels[0].shape[0] // 3
     put = pltpu.make_async_copy(result, result_out.at[0], sem)
     put.start()
@@ -329,9 +293,10 @@
     edge_sum = jnp.zeros((own, 128), F32)
     pads = []
     for k in range(SLOTS):
-        spread = dot(back_kernels[0][...], frames[0][k])
-        for frame, back_kernel in zip(frames[1:], back_kernels[1:]):
-            spread = spread + dot(back_kernel[...], frame[k])
+        spread = dot(back_kernels[0][...], own_frames[k])
+        for other, back_kernel in zip(slopes, back_kernels[1:]):
+            frame = frame_of(other[k * own : (k + 1) * own, :].astype(F32))
+            spread = spread + dot(back_kernel[...], frame)
         first, second, third = spread[:own], spread[own : 2 * own], spread[2 * own :]
         pad = (
             second
@@ -344,7 +309,6 @@
         crest = jnp.where(lane128 < TS, pad[:, CELLS:], 0.0) * at_top[k]
         edge_sum = edge_sum + pltpu.roll(crest, FOLD, 1)
     edges[...] = edge_sum.astype(BF16)
-    _, halves, _ = message_views(shared, own)
     for k in range(SLOTS):
         first = pads[k][:, :128]
         second = pads[k][:, 128:CELLS]
@@ -353,7 +317,7 @@
                 ends = pads[l][:, CELLS:]
                 first = first + jnp.where(lane128 < TS, ends, 0.0) * above[l][k]
                 second = second + jnp.where(lane128 >= 128 - TS, ends, 0.0) * above[k][l]
-        base[k] = upstream_of(halves, k, full) + jnp.concatenate([first, second], axis=1)
+        base[k] = cot[k].astype(F32) * full[k] + jnp.concatenate([first, second], axis=1)
     put.wait()
 
 
@@ -407,7 +371,6 @@
     reps = lax.axis_size("rep")
     plans = halo_plans(count)
     n = len(plans)
-    shared_rows = 9 * own + 2 * SLOTS * own + 16
     half_rows = -(-(9 * own + 1) // 32) * 16
     swap = [(0, 1), (1, 0)]
 
@@ -415,21 +378,19 @@
         pltpu.with_memory_space_constraint(x, pltpu.HBM)
         for x in (tile_rows, fields, weights, bias.reshape(1, own), cotangent)
     ]
-    rows, tiles, shared, *packed = call(
+    rows, tiles, taps, bias_line, cot, *packed = call(
         lambda *refs: pack_kernel(*refs, count=count),
         [HBM] * 5,
         [
             struct(tile_rows.shape, jnp.int32),
             struct((SLOTS, C, CELLS), BF16),
-            struct((shared_rows, 128), BF16),
+            struct((9, own, C), BF16),
+            struct((1, own), F32),
+            struct((SLOTS, own, CELLS), BF16),
         ]
         + [struct((SLOTS * CELLS, 128), BF16)] * n
         + [struct((C, 128), BF16)] * n,
-        [
-            pltpu.SMEM(tile_rows.shape, jnp.int32),
-            pltpu.VMEM((1, own), F32),
-            pltpu.SemaphoreType.DMA((12 + 2 * SLOTS,)),
-        ],
+        [pltpu.SMEM(tile_rows.shape, jnp.int32), pltpu.SemaphoreType.DMA((5,))],
     )(*pinned)
     maps, messages = packed[:n], packed[n:]
 
@@ -437,7 +398,8 @@
         return lax.ppermute(x, "tiles", [(i, route(i)) for i in range(count)])
 
     halos = [x if route is None else move(x, route) for x, (route, _) in zip(messages, plans)]
-    others = [lax.ppermute(shared, "chan", [(i, (i + s) % chans) for i in range(chans)]) for s in range(1, chans)]
+    ring = [[(i, (i + s) % chans) for i in range(chans)] for s in range(1, chans)]
+    others = [lax.ppermute(taps, "chan", pairs) for pairs in ring]
 
     windows, spreads, gathers, kernel, back_kernel = call(
         window_kernel,
@@ -450,32 +412,32 @@
             struct((3 * own, 3 * own), BF16),
         ],
         [pltpu.VMEM((3 * C, 3 * own), F32)],
-    )(rows, tiles, shared)
-
-    windows, frames, result, keep, send = call(
+    )(rows, tiles, taps)
+
+    frames, slopes, result, keep, send = call(
         lambda *refs: forward_kernel(*refs, n_halos=len(halos), half_rows=half_rows, count=count),
-        [SMEM] + [VMEM] * (5 + len(halos)),
+        [SMEM] + [VMEM] * (6 + len(halos)),
         [
-            struct((SLOTS, 3 * C, FRAME), BF16),
             struct((SLOTS, 3 * own, FRAME), BF16),
+            struct((SLOTS * own, CELLS), BF16),
             struct((SLOTS, own, CELLS), BF16),
             struct((half_rows, 128), F32),
             struct((half_rows, 128), F32),
         ],
         cost=pl.CostEstimate(flops=4 * 10**9, transcendentals=0, bytes_accessed=0),
-    )(rows, tiles, shared, kernel, spreads, windows, *halos)
-
-    swapped, others = lax.optimization_barrier((lax.ppermute(send, "rep", swap), others))
-    sums = keep + swapped
+    )(rows, tiles, bias_line, cot, kernel, spreads, windows, *halos)
+
+    met = [lax.ppermute(slopes, "chan", pairs) for pairs in ring]
+    send, others = lax.optimization_barrier((send, others))
+    sums = keep + lax.ppermute(send, "rep", swap)
     rounded = sums.astype(BF16)
     frames, rounded, others = lax.optimization_barrier((frames, rounded, others))
-    other_frames = call(
-        other_kernel,
-        [SMEM, VMEM] + [VMEM] * len(others),
-        [struct((SLOTS, 3 * own, FRAME), BF16)] * len(others) + [struct((3 * own, 3 * own), BF16)] * len(others),
+    turned = call(
+        turn_kernel,
+        [VMEM] * len(others),
+        [struct((3 * own, 3 * own), BF16)] * len(others),
         [pltpu.VMEM((3 * C, 3 * own), F32)],
-    )(rows, windows, *others)
-    other_frames, other_back = other_frames[: len(others)], other_frames[len(others) :]
+    )(*others)
 
     base, edges, result = call(
         backward_kernel,
@@ -487,7 +449,7 @@
         ],
         [pltpu.SemaphoreType.DMA],
         out_specs=[VMEM, VMEM, HBM],
-    )(rows, shared, gathers, result, frames, *other_frames, back_kernel, *other_back)
+    )(rows, cot, gathers, result, frames, *met, back_kernel, *turned)
 
     if count == 4:
 
@@ -499,10 +461,10 @@
         beside = lax.ppermute(edges, "rep", swap)
         other = cross(rounded, lambda d: d ^ 2)
         rounded = (rounded.astype(F32) + other.astype(F32)).astype(BF16)
-        both = cross(jnp.concatenate([rounded, beside, across], axis=0), lambda d: d ^ 1)
-        sums = rounded.astype(F32) + both[:half_rows].astype(F32)
+        sums = rounded.astype(F32) + cross(rounded, lambda d: d ^ 1).astype(F32)
+        both = cross(jnp.concatenate([beside, across], axis=0), lambda d: d ^ 1)
         across = lax.ppermute(across, "rep", swap)
-        returned = [both[half_rows + own :], across, both[half_rows : half_rows + own], edges]
+        returned = [both[own:], across, both[:own], edges]
     else:
         for step in range(count.bit_length() - 1):
             other = move(rounded, lambda d: d ^ (1 << step))

time: 33 us -> 31.4 us (0.952)
  waiting for transfers between devices: 10 us -> 7.71 us
  starting transfers between devices: 11.9 us -> 13.9 us
  Pallas kernels: 10.1 us -> 8.83 us
    ppermute x3 -> x4, waiting for transfers between devices: 7.19 us -> 4.84 us  [cross(): return lax.ppermute(x, ('tiles', 'rep'), pairs)]
    ppermute x2 -> x3, starting transfers between devices: 1.71 us -> 3.26 us  [the longest x1 1.63 us: on_device(): others = [lax.ppermute(taps, 'chan', pairs) for pairs in ring]]
    pallas_call x1, Pallas kernels: 1.42 us -> 0.15 us  [on_device(): call(turn_kernel, [VMEM] * len(others), [struct((3 * own, 3 * own), BF16)...]
    ppermute x3 -> x4, starting transfers between devices: 3.36 us -> 3.81 us  [cross(): return lax.ppermute(x, ('tiles', 'rep'), pairs)]
    ppermute x1, starting transfers between devices: 0.42 us -> 0.85 us  [on_device(): beside = lax.ppermute(edges, 'rep', swap)]
    ppermute x2 -> x3, waiting for transfers between devices: 1.37 us -> 1.61 us  [the longest x1 1.61 us: on_device(): met = [lax.ppermute(slopes, 'chan', pairs) for pairs in ring]]
  transfers between devices with their start and end apart: 11 -> 13, of which waited for: 6 -> 5; matrix products, arithmetic and copies ran while one was open for 0% -> 0% of each run, Pallas kernels for 24% -> 21%
where the time goes in v11:
time: 31.4 us; the launch traced here: 31.3 us
  starting transfers between devices  13.9 us (44%)
  Pallas kernels  8.83 us (28%)
  waiting for transfers between devices  7.71 us (25%)
  between operations  0.73 us (2%)
    ppermute x3, starting transfers between devices, move(): return lax.ppermute(x, 'tiles', [(i, route(i)) for i in range(count)])  5.76 us
    ppermute x4, waiting for transfers between devices, cross(): return lax.ppermute(x, ('tiles', 'rep'), pairs)  4.84 us
    ppermute x4, starting transfers between devices, cross(): return lax.ppermute(x, ('tiles', 'rep'), pairs)  3.81 us
    pallas_call x1, Pallas kernels, on_device(): call(lambda *refs: forward_kernel(*refs, n_halos=len(halos), half_rows=ha...  2.52 us
    ppermute x1, starting transfers between devices, on_device(): others = [lax.ppermute(taps, 'chan', pairs) for pairs in ring]  1.63 us
    pallas_call x1, Pallas kernels, on_device(): call(backward_kernel, [SMEM] + [VMEM] * (5 + 2 * len(others)), [struct((S...  1.62 us
    ppermute x1, waiting for transfers between devices, on_device(): met = [lax.ppermute(slopes, 'chan', pairs) for pairs in ring]  1.61 us
    ppermute x1, starting transfers between devices, on_device(): met = [lax.ppermute(slopes, 'chan', pairs) for pairs in ring]  1.56 us
  transfers between devices with their start and end apart: 13, of which 5 were waited for; matrix products, arithmetic and copies ran while one was open for 0% of the time, Pallas kernels for 21%

profile of v11, /device:TPU:0, one launch (start us, length us, event | category | flops | bytes accessed | tf_op | source)
XLA Modules:
  0.0 31.3 jit_solution(4605944396019058509)
XLA Ops:
  0.6 1.5 %shard_map.84 = (s32[4,3]{1,0:T(4,128)S(1)}, bf16[3,128,256]{2,1,0:T(8,128)(2,1)S(1)}, bf16[9,64,128]{2,1,0:T(8,128)(2,1)S(1)}, f32[1,64]{1,0:T(1,128)S(1)}, bf1...) custom-call(s32[4,3]{1,0:T(4,128)} %refs_0_.1, ...), custom_call_target="tpu_custom_call" | custom-call | tf_op jit(solution)/shard_map/pallas_call | solution.py:381
  2.1 5.1 %collective-permute-start = (bf16[128,128]{1,0:T(8,128)(2,1)S(1)}, bf16[128,128]{1,0:T(8,128)(2,1)S(1)}, u32[]{:S(2)}, u32[]{:S(2)}) collective-permute-start(bf16[128,128]{1,0:T(8,128)(2,1)S(1)} %get-tuple-element.46), channel_id=1, source_target_pairs={{0,12},{4,8},{8,4},{12,0},{1,13},{5,9},{9,5},{13,1},{2,14},{6,10},... | collective-permute-start | bytes 98312 | tf_op jit(solution)/shard_map/ppermute | solution.py:398
  7.2 0.0 collective-permute-start.1
  7.2 0.6 %collective-permute-start.2 = (bf16[128,128]{1,0:T(8,128)(2,1)S(1)}, bf16[128,128]{1,0:T(8,128)(2,1)S(1)}, u32[]{:S(2)}, u32[]{:S(2)}) collective-permute-start(bf16[128,128]{1,0:T(8,128)(2,1)S(1)} %get-tuple-element.48), channel_id=1, source_target_pairs={{0,4},{4,0},{8,12},{12,8},{1,5},{5,1},{9,13},{13,9},{2,6},{6,2},{1... | collective-permute-start | bytes 98312 | tf_op jit(solution)/shard_map/ppermute | solution.py:398
  7.9 1.6 %collective-permute-start.3 = (bf16[9,64,128]{2,1,0:T(8,128)(2,1)S(1)}, bf16[9,64,128]{2,1,0:T(8,128)(2,1)S(1)}, u32[]{:S(2)}, u32[]{:S(2)}) collective-permute-start(bf16[9,64,128]{2,1,0:T(8,128)(2,1)S(1)} %get-tuple-element.40.weights), channel_id=1, source_target_pairs={{0,2},{2,0},{1,3},{3,1},{4,6},{6,4},{5,7},{7,5},{8,10},{10,8},{9,1... | collective-permute-start | bytes 442376 | tf_op jit(solution)/shard_map/ppermute | solution.py:402
  9.5 1.3 %shard_map.85 = (bf16[3,384,384]{2,1,0:T(8,128)(2,1)S(1)}, bf16[2,3,128,384]{3,2,1,0:T(8,128)(2,1)S(1)}, bf16[2,3,384,128]{3,2,1,0:T(8,128)(2,1)S(1)}, bf16[192,384]{1,0:T(8,128)(2,1)S(1)}, bf16[192,192]{1,0:T(8,128)(2,1)S(1)}) custom-call(s32[4,3]{1,0:T(4,128)S(1)} %get-tuple-element.37.rows.refs_0_, ...), custom_call_target="tpu_custom_call" | custom-call | tf_op jit(solution)/shard_map/pallas_call | solution.py:404
  10.8 1.2 %collective-permute-done.1.refs_8_ = bf16[128,128]{1,0:T(8,128)(2,1)S(1)} collective-permute-done((bf16[128,128]{1,0:T(8,128)(2,1)S(1)}, bf16[128,128]{1,0:T(8,128)(2,1)S(1)}, u32[]{:S(2)}, u32[]{:S(2)}) %collective-permute-start.1) | collective-permute-done | bytes 32800 | tf_op jit(solution)/shard_map/ppermute | solution.py:398
  12.0 2.5 %shard_map.86 = (bf16[3,192,384]{2,1,0:T(8,128)(2,1)S(1)}, bf16[192,256]{1,0:T(8,128)(2,1)S(1)}, bf16[3,64,256]{2,1,0:T(8,128)(2,1)S(1)}, f32[304,128]{1,0:T(8,128)S(1)}, f32[304,128]{1,0:T(8,128)S(1)}) custom-call(s32[4,3]{1,0:T(4,128)S(1)} %get-tuple-element.37.rows.refs_0_, bf16[3,128,256]{2,1,0:T(8,128)(2,1)S(1)} %get-tuple-element.39.fields.refs_1_, ...), custom_call_target="tpu_custom_call" | custom-call | flops 4000000000 | tf_op jit(solution)/shard_map/pallas_call | solution.py:417
  14.6 0.1 collective-permute-start.4
  14.7 1.6 %collective-permute-start.5 = (bf16[192,256]{1,0:T(8,128)(2,1)S(1)}, bf16[192,256]{1,0:T(8,128)(2,1)S(1)}, u32[]{:S(2)}, u32[]{:S(2)}) collective-permute-start(bf16[192,256]{1,0:T(8,128)(2,1)S(1)} %get-tuple-element.57), channel_id=1, source_target_pairs={{0,2},{2,0},{1,3},{3,1},{4,6},{6,4},{5,7},{7,5},{8,10},{10,8},{9,1... | collective-permute-start | bytes 294920 | tf_op jit(solution)/shard_map/ppermute | solution.py:430
  16.2 1.9 %collective-permute-start.10 = (bf16[304,128]{1,0:T(8,128)(2,1)S(1)}, bf16[304,128]{1,0:T(8,128)(2,1)S(1)}, u32[]{:S(2)}, u32[]{:S(2)}) collective-permute-start(bf16[304,128]{1,0:T(8,128)(2,1)S(1)} %add_convert_fusion.1), channel_id=1, source_target_pairs={{0,9},{1,8},{4,13},{5,12},{8,1},{9,0},{12,5},{13,4},{2,11},{3,10},... | collective-permute-start | bytes 233480 | tf_op jit(solution)/shard_map/ppermute | solution.py:458
  18.1 0.2 shard_map.87.refs_2_
  18.3 1.6 %collective-permute-done.5.refs_0_ = bf16[192,256]{1,0:T(8,128)(2,1)S(1)} collective-permute-done((bf16[192,256]{1,0:T(8,128)(2,1)S(1)}, bf16[192,256]{1,0:T(8,128)(2,1)S(1)}, u32[]{:S(2)}, u32[]{:S(2)}) %collective-permute-start.5) | collective-permute-done | bytes 98336 | tf_op jit(solution)/shard_map/ppermute | solution.py:430
  19.9 1.6 %shard_map.88 = (f32[3,64,256]{2,1,0:T(8,128)S(1)}, bf16[64,128]{1,0:T(8,128)(2,1)S(1)}, bf16[1,3,64,256]{3,2,1,0:T(8,128)(2,1)}) custom-call(s32[4,3]{1,0:T(4,128)S(1)} %get-tuple-element.37.rows.refs_0_, bf16[3,64,256]{2,1,0:T(8,128)(2,1)S(1)} %get-tuple-element.38.refs_3_.cot, bf16[2,3,384,128]{3,2,1,0:T(8,128)(2,1)S(1)} %get-tuple-element.41.gathers, ...), custom_call_target="tpu_custom_call" | custom-call | tf_op jit(solution)/shard_map/pallas_call | solution.py:442
  21.5 1.4 %collective-permute-start.7 = (bf16[64,128]{1,0:T(8,128)(2,1)S(1)}, bf16[64,128]{1,0:T(8,128)(2,1)S(1)}, u32[]{:S(2)}, u32[]{:S(2)}) collective-permute-start(bf16[64,128]{1,0:T(8,128)(2,1)S(1)} %get-tuple-element.62.refs_3_), channel_id=1, source_target_pairs={{0,9},{1,8},{4,13},{5,12},{8,1},{9,0},{12,5},{13,4},{2,11},{3,10},... | collective-permute-start | bytes 49160 | tf_op jit(solution)/shard_map/ppermute | solution.py:458
  22.9 0.8 %collective-permute-start.6 = (bf16[64,128]{1,0:T(8,128)(2,1)S(1)}, bf16[64,128]{1,0:T(8,128)(2,1)S(1)}, u32[]{:S(2)}, u32[]{:S(2)}) collective-permute-start(bf16[64,128]{1,0:T(8,128)(2,1)S(1)} %get-tuple-element.62.refs_3_), channel_id=1, source_target_pairs={{0,1},{1,0},{2,3},{3,2},{4,5},{5,4},{6,7},{7,6},{8,9},{9,8},{10,11... | collective-permute-start | bytes 49160 | tf_op jit(solution)/shard_map/ppermute | solution.py:461
  23.7 0.6 %collective-permute-start.11 = (bf16[304,128]{1,0:T(8,128)(2,1)S(1)}, bf16[304,128]{1,0:T(8,128)(2,1)S(1)}, u32[]{:S(2)}, u32[]{:S(2)}) collective-permute-start(bf16[304,128]{1,0:T(8,128)(2,1)S(1)} %add_convert_fusion), channel_id=1, source_target_pairs={{0,5},{1,4},{4,1},{5,0},{8,13},{9,12},{12,9},{13,8},{2,7},{3,6},{6... | collective-permute-start | bytes 233480 | tf_op jit(solution)/shard_map/ppermute | solution.py:458
  24.3 1.5 %collective-permute-done.7 = bf16[64,128]{1,0:T(8,128)(2,1)S(1)} collective-permute-done((bf16[64,128]{1,0:T(8,128)(2,1)S(1)}, bf16[64,128]{1,0:T(8,128)(2,1)S(1)}, u32[]{:S(2)}, u32[]{:S(2)}) %collective-permute-start.7) | collective-permute-done | bytes 16416 | tf_op jit(solution)/shard_map/ppermute | solution.py:458
  25.8 0.1 collective-permute-start.9
  25.9 2.4 %collective-permute-done.11 = bf16[304,128]{1,0:T(8,128)(2,1)S(1)} collective-permute-done((bf16[304,128]{1,0:T(8,128)(2,1)S(1)}, bf16[304,128]{1,0:T(8,128)(2,1)S(1)}, u32[]{:S(2)}, u32[]{:S(2)}) %collective-permute-start.11) | collective-permute-done | bytes 77856 | tf_op jit(solution)/shard_map/ppermute | solution.py:458
  28.3 0.2 collective-permute-start.12
  28.5 1.0 %collective-permute-done.8 = bf16[128,128]{1,0:T(8,128)(2,1)S(1)} collective-permute-done((bf16[128,128]{1,0:T(8,128)(2,1)S(1)}, bf16[128,128]{1,0:T(8,128)(2,1)S(1)}, u32[]{:S(2)}, u32[]{:S(2)}) %collective-permute-start.8) | collective-permute-done | bytes 32800 | tf_op jit(solution)/shard_map/ppermute | solution.py:458
  29.5 1.0 %shard_map.89 = bf16[1,3,64,256]{3,2,1,0:T(8,128)(2,1)} custom-call(f32[3,64,256]{2,1,0:T(8,128)S(1)} %get-tuple-element.61.base, bf16[64,128]{1,0:T(8,128)(2,1)S(1)} %get-tuple-element.71.refs_0_, bf16[64,128]{1,0:T(8,128)(2,1)S(1)} %collective-permute-done.9.refs_1_, bf16[64,128]{1,0:T(8,128)(2,1)S(1)} %get-tuple-element.70.refs_2_, ...), custom_call_target="tpu_custom_call" | custom-call | tf_op jit(solution)/shard_map/pallas_call | solution.py:478
  30.5 0.7 %shard_map.90 = (f32[9,64,128]{2,1,0:T(8,128)}, f32[1,64]{1,0:T(1,128)}) custom-call(f32[304,128]{1,0:T(8,128)S(1)} %add_multiply_fusion.refs_0_, f32[304,128]{1,0:T(8,128)S(1)} %collective-permute-done.12.refs_1_), custom_call_target="tpu_custom_call" | custom-call | tf_op jit(solution)/shard_map/pallas_call | solution.py:483
  (14 shorter events, 0.1 us)
Async XLA Ops:
  2.1 8.7 %collective-permute-start = (bf16[128,128]{1,0:T(8,128)(2,1)S(1)}, bf16[128,128]{1,0:T(8,128)(2,1)S(1)}, u32[]{:S(2)}, u32[]{:S(2)}) collective-permute-start(bf16[128,128]{1,0:T(8,128)(2,1)S(1)} %get-tuple-element.46), channel_id=1, source_target_pairs={{0,12},{4,8},{8,4},{12,0},{1,13},{5,9},{9,5},{13,1},{2,14},{6,10},... | collective-permute-start | bytes 98312 | tf_op jit(solution)/shard_map/ppermute | solution.py:398
  7.2 4.8 %collective-permute-start.1 = (bf16[128,128]{1,0:T(8,128)(2,1)S(1)}, bf16[128,128]{1,0:T(8,128)(2,1)S(1)}, u32[]{:S(2)}, u32[]{:S(2)}) collective-permute-start(bf16[128,128]{1,0:T(8,128)(2,1)S(1)} %get-tuple-element.47), channel_id=1, source_target_pairs={{0,8},{4,12},{8,0},{12,4},{1,9},{5,13},{9,1},{13,5},{2,10},{6,14},... | collective-permute-start | bytes 98312 | tf_op jit(solution)/shard_map/ppermute | solution.py:398
  7.2 4.8 %collective-permute-start.2 = (bf16[128,128]{1,0:T(8,128)(2,1)S(1)}, bf16[128,128]{1,0:T(8,128)(2,1)S(1)}, u32[]{:S(2)}, u32[]{:S(2)}) collective-permute-start(bf16[128,128]{1,0:T(8,128)(2,1)S(1)} %get-tuple-element.48), channel_id=1, source_target_pairs={{0,4},{4,0},{8,12},{12,8},{1,5},{5,1},{9,13},{13,9},{2,6},{6,2},{1... | collective-permute-start | bytes 98312 | tf_op jit(solution)/shard_map/ppermute | solution.py:398
  7.9 6.7 %collective-permute-start.3 = (bf16[9,64,128]{2,1,0:T(8,128)(2,1)S(1)}, bf16[9,64,128]{2,1,0:T(8,128)(2,1)S(1)}, u32[]{:S(2)}, u32[]{:S(2)}) collective-permute-start(bf16[9,64,128]{2,1,0:T(8,128)(2,1)S(1)} %get-tuple-element.40.weights), channel_id=1, source_target_pairs={{0,2},{2,0},{1,3},{3,1},{4,6},{6,4},{5,7},{7,5},{8,10},{10,8},{9,1... | collective-permute-start | bytes 442376 | tf_op jit(solution)/shard_map/ppermute | solution.py:402
  14.6 1.6 %collective-permute-start.4 = (f32[304,128]{1,0:T(8,128)S(1)}, f32[304,128]{1,0:T(8,128)S(1)}, u32[]{:S(2)}, u32[]{:S(2)}) collective-permute-start(f32[304,128]{1,0:T(8,128)S(1)} %get-tuple-element.54), channel_id=1, source_target_pairs={{0,1},{1,0},{2,3},{3,2},{4,5},{5,4},{6,7},{7,6},{8,9},{9,8},{10,11... | collective-permute-start | bytes 466952 | tf_op jit(solution)/shard_map/ppermute | solution.py:432
  14.7 5.2 %collective-permute-start.5 = (bf16[192,256]{1,0:T(8,128)(2,1)S(1)}, bf16[192,256]{1,0:T(8,128)(2,1)S(1)}, u32[]{:S(2)}, u32[]{:S(2)}) collective-permute-start(bf16[192,256]{1,0:T(8,128)(2,1)S(1)} %get-tuple-element.57), channel_id=1, source_target_pairs={{0,2},{2,0},{1,3},{3,1},{4,6},{6,4},{5,7},{7,5},{8,10},{10,8},{9,1... | collective-permute-start | bytes 294920 | tf_op jit(solution)/shard_map/ppermute | solution.py:430
  16.2 7.5 %collective-permute-start.10 = (bf16[304,128]{1,0:T(8,128)(2,1)S(1)}, bf16[304,128]{1,0:T(8,128)(2,1)S(1)}, u32[]{:S(2)}, u32[]{:S(2)}) collective-permute-start(bf16[304,128]{1,0:T(8,128)(2,1)S(1)} %add_convert_fusion.1), channel_id=1, source_target_pairs={{0,9},{1,8},{4,13},{5,12},{8,1},{9,0},{12,5},{13,4},{2,11},{3,10},... | collective-permute-start | bytes 233480 | tf_op jit(solution)/shard_map/ppermute | solution.py:458
  21.5 4.3 %collective-permute-start.7 = (bf16[64,128]{1,0:T(8,128)(2,1)S(1)}, bf16[64,128]{1,0:T(8,128)(2,1)S(1)}, u32[]{:S(2)}, u32[]{:S(2)}) collective-permute-start(bf16[64,128]{1,0:T(8,128)(2,1)S(1)} %get-tuple-element.62.refs_3_), channel_id=1, source_target_pairs={{0,9},{1,8},{4,13},{5,12},{8,1},{9,0},{12,5},{13,4},{2,11},{3,10},... | collective-permute-start | bytes 49160 | tf_op jit(solution)/shard_map/ppermute | solution.py:458
  22.9 3.0 %collective-permute-start.6 = (bf16[64,128]{1,0:T(8,128)(2,1)S(1)}, bf16[64,128]{1,0:T(8,128)(2,1)S(1)}, u32[]{:S(2)}, u32[]{:S(2)}) collective-permute-start(bf16[64,128]{1,0:T(8,128)(2,1)S(1)} %get-tuple-element.62.refs_3_), channel_id=1, source_target_pairs={{0,1},{1,0},{2,3},{3,2},{4,5},{5,4},{6,7},{7,6},{8,9},{9,8},{10,11... | collective-permute-start | bytes 49160 | tf_op jit(solution)/shard_map/ppermute | solution.py:461
  23.7 4.5 %collective-permute-start.11 = (bf16[304,128]{1,0:T(8,128)(2,1)S(1)}, bf16[304,128]{1,0:T(8,128)(2,1)S(1)}, u32[]{:S(2)}, u32[]{:S(2)}) collective-permute-start(bf16[304,128]{1,0:T(8,128)(2,1)S(1)} %add_convert_fusion), channel_id=1, source_target_pairs={{0,5},{1,4},{4,1},{5,0},{8,13},{9,12},{12,9},{13,8},{2,7},{3,6},{6... | collective-permute-start | bytes 233480 | tf_op jit(solution)/shard_map/ppermute | solution.py:458
  25.8 3.6 %collective-permute-start.8 = (bf16[128,128]{1,0:T(8,128)(2,1)S(1)}, bf16[128,128]{1,0:T(8,128)(2,1)S(1)}, u32[]{:S(2)}, u32[]{:S(2)}) collective-permute-start(bf16[128,128]{1,0:T(8,128)(2,1)S(1)} %pad_maximum_fusion), channel_id=1, source_target_pairs={{0,5},{1,4},{4,1},{5,0},{8,13},{9,12},{12,9},{13,8},{2,7},{3,6},{6... | collective-permute-start | bytes 98312 | tf_op jit(solution)/shard_map/ppermute | solution.py:458
  25.8 3.6 %collective-permute-start.9 = (bf16[64,128]{1,0:T(8,128)(2,1)S(1)}, bf16[64,128]{1,0:T(8,128)(2,1)S(1)}, u32[]{:S(2)}, u32[]{:S(2)}) collective-permute-start(bf16[64,128]{1,0:T(8,128)(2,1)S(1)} %collective-permute-done.7), channel_id=1, source_target_pairs={{0,1},{1,0},{2,3},{3,2},{4,5},{5,4},{6,7},{7,6},{8,9},{9,8},{10,11... | collective-permute-start | bytes 49160 | tf_op jit(solution)/shard_map/ppermute | solution.py:466
  28.3 2.2 %collective-permute-start.12 = (f32[304,128]{1,0:T(8,128)S(1)}, f32[304,128]{1,0:T(8,128)S(1)}, u32[]{:S(2)}, u32[]{:S(2)}) collective-permute-start(f32[304,128]{1,0:T(8,128)S(1)} %add_multiply_fusion.refs_0_), channel_id=1, source_target_pairs={{0,1},{1,0},{2,3},{3,2},{4,5},{5,4},{6,7},{7,6},{8,9},{9,8},{10,11... | collective-permute-start | bytes 466952 | tf_op jit(solution)/shard_map/ppermute | solution.py:487

commit v12 on v11

--- a/solution.py
+++ b/solution.py
@@ -245,7 +245,7 @@
     fold_left = jnp.where((lane128 > 0) & (lane128 < TS), pltpu.roll(turned, 1, 1), 0.0)
     fold_right = jnp.where(lane128 < TS - 1, pltpu.roll(turned, 127, 1), 0.0)
     halo = halo.astype(BF16)
-    grads = jnp.zeros((3 * own, 3 * C), F32)
+    slope_frames, full_windows = [], []
     slope_sum = jnp.zeros((own, CELLS), F32)
     for k in range(SLOTS):
         west = dot(halo, spreads[0, k])
@@ -262,7 +262,9 @@
         slopes_out[k * own : (k + 1) * own, :] = slopes.astype(BF16)
         frame = frame_of(slopes)
         frames[k] = frame
-        grads = grads + dot(frame, window, ((1,), (1,)))
+        slope_frames.append(frame)
+        full_windows.append(window)
+    grads = dot(jnp.concatenate(slope_frames, axis=1), jnp.concatenate(full_windows, axis=1), ((1,), (1,)))
     blocks = [grads[a * own : (a + 1) * own, b * C : (b + 1) * C] for a in range(3) for b in range(3)]
     eye = iota((own, 128), 0) == iota((own, 128), 1)
     bias_line = jnp.sum(jnp.where(eye, jnp.sum(slope_sum, axis=1, keepdims=True), 0.0), axis=0, keepdims=True)

time: 31.4 us -> 30.6 us (0.975)
  waiting for transfers between devices: 7.71 us -> 6.93 us
  starting transfers between devices: 13.9 us -> 14.5 us
  Pallas kernels: 8.83 us -> 8.27 us
    ppermute x4, waiting for transfers between devices: 4.84 us -> 4.06 us  [cross(): return lax.ppermute(x, ('tiles', 'rep'), pairs)]
    pallas_call x1, Pallas kernels: 2.52 us -> 1.97 us  [on_device(): call(lambda *refs: forward_kernel(*refs, n_halos=len(halos), half_rows=ha...]
    ppermute x4, starting transfers between devices: 3.81 us -> 4.33 us  [cross(): return lax.ppermute(x, ('tiles', 'rep'), pairs)]
  transfers between devices with their start and end apart: 13 -> 13, of which waited for: 5 -> 5; matrix products, arithmetic and copies ran while one was open for 0% -> 0% of each run, Pallas kernels for 21% -> 20%
where the time goes in v12:
time: 30.6 us; the launch traced here: 30.4 us
  starting transfers between devices  14.5 us (47%)
  Pallas kernels  8.27 us (27%)
  waiting for transfers between devices  6.93 us (23%)
  between operations  0.72 us (2%)
    ppermute x3, starting transfers between devices, move(): return lax.ppermute(x, 'tiles', [(i, route(i)) for i in range(count)])  5.76 us
    ppermute x4, starting transfers between devices, cross(): return lax.ppermute(x, ('tiles', 'rep'), pairs)  4.33 us
    ppermute x4, waiting for transfers between devices, cross(): return lax.ppermute(x, ('tiles', 'rep'), pairs)  4.06 us
    pallas_call x1, Pallas kernels, on_device(): call(lambda *refs: forward_kernel(*refs, n_halos=len(halos), half_rows=ha...  1.97 us
    ppermute x1, starting transfers between devices, on_device(): others = [lax.ppermute(taps, 'chan', pairs) for pairs in ring]  1.63 us
    pallas_call x1, Pallas kernels, on_device(): call(backward_kernel, [SMEM] + [VMEM] * (5 + 2 * len(others)), [struct((S...  1.61 us
    ppermute x1, waiting for transfers between devices, on_device(): met = [lax.ppermute(slopes, 'chan', pairs) for pairs in ring]  1.61 us
    ppermute x1, starting transfers between devices, on_device(): met = [lax.ppermute(slopes, 'chan', pairs) for pairs in ring]  1.55 us
  transfers between devices with their start and end apart: 13, of which 5 were waited for; matrix products, arithmetic and copies ran while one was open for 0% of the time, Pallas kernels for 20%

profile of v12, /device:TPU:0, one launch (start us, length us, event | category | flops | bytes accessed | tf_op | source)
XLA Modules:
  0.0 30.4 jit_solution(9277854186310113218)
XLA Ops:
  0.6 1.5 %shard_map.84 = (s32[4,3]{1,0:T(4,128)S(1)}, bf16[3,128,256]{2,1,0:T(8,128)(2,1)S(1)}, bf16[9,64,128]{2,1,0:T(8,128)(2,1)S(1)}, f32[1,64]{1,0:T(1,128)S(1)}, bf1...) custom-call(s32[4,3]{1,0:T(4,128)} %refs_0_.1, ...), custom_call_target="tpu_custom_call" | custom-call | tf_op jit(solution)/shard_map/pallas_call | solution.py:383
  2.1 5.1 %collective-permute-start = (bf16[128,128]{1,0:T(8,128)(2,1)S(1)}, bf16[128,128]{1,0:T(8,128)(2,1)S(1)}, u32[]{:S(2)}, u32[]{:S(2)}) collective-permute-start(bf16[128,128]{1,0:T(8,128)(2,1)S(1)} %get-tuple-element.46), channel_id=1, source_target_pairs={{0,12},{4,8},{8,4},{12,0},{1,13},{5,9},{9,5},{13,1},{2,14},{6,10},... | collective-permute-start | bytes 98312 | tf_op jit(solution)/shard_map/ppermute | solution.py:400
  7.2 0.6 %collective-permute-start.2 = (bf16[128,128]{1,0:T(8,128)(2,1)S(1)}, bf16[128,128]{1,0:T(8,128)(2,1)S(1)}, u32[]{:S(2)}, u32[]{:S(2)}) collective-permute-start(bf16[128,128]{1,0:T(8,128)(2,1)S(1)} %get-tuple-element.48), channel_id=1, source_target_pairs={{0,4},{4,0},{8,12},{12,8},{1,5},{5,1},{9,13},{13,9},{2,6},{6,2},{1... | collective-permute-start | bytes 98312 | tf_op jit(solution)/shard_map/ppermute | solution.py:400
  7.9 1.6 %collective-permute-start.3 = (bf16[9,64,128]{2,1,0:T(8,128)(2,1)S(1)}, bf16[9,64,128]{2,1,0:T(8,128)(2,1)S(1)}, u32[]{:S(2)}, u32[]{:S(2)}) collective-permute-start(bf16[9,64,128]{2,1,0:T(8,128)(2,1)S(1)} %get-tuple-element.40.weights), channel_id=1, source_target_pairs={{0,2},{2,0},{1,3},{3,1},{4,6},{6,4},{5,7},{7,5},{8,10},{10,8},{9,1... | collective-permute-start | bytes 442376 | tf_op jit(solution)/shard_map/ppermute | solution.py:404
  9.5 1.3 %shard_map.85 = (bf16[3,384,384]{2,1,0:T(8,128)(2,1)S(1)}, bf16[2,3,128,384]{3,2,1,0:T(8,128)(2,1)S(1)}, bf16[2,3,384,128]{3,2,1,0:T(8,128)(2,1)S(1)}, bf16[192,384]{1,0:T(8,128)(2,1)S(1)}, bf16[192,192]{1,0:T(8,128)(2,1)S(1)}) custom-call(s32[4,3]{1,0:T(4,128)S(1)} %get-tuple-element.37.rows.refs_0_, ...), custom_call_target="tpu_custom_call" | custom-call | tf_op jit(solution)/shard_map/pallas_call | solution.py:406
  10.8 1.2 %collective-permute-done.1.refs_8_ = bf16[128,128]{1,0:T(8,128)(2,1)S(1)} collective-permute-done((bf16[128,128]{1,0:T(8,128)(2,1)S(1)}, bf16[128,128]{1,0:T(8,128)(2,1)S(1)}, u32[]{:S(2)}, u32[]{:S(2)}) %collective-permute-start.1) | collective-permute-done | bytes 32800 | tf_op jit(solution)/shard_map/ppermute | solution.py:400
  12.0 2.0 %shard_map.86 = (bf16[3,192,384]{2,1,0:T(8,128)(2,1)S(1)}, bf16[192,256]{1,0:T(8,128)(2,1)S(1)}, bf16[3,64,256]{2,1,0:T(8,128)(2,1)S(1)}, f32[304,128]{1,0:T(8,128)S(1)}, f32[304,128]{1,0:T(8,128)S(1)}) custom-call(s32[4,3]{1,0:T(4,128)S(1)} %get-tuple-element.37.rows.refs_0_, bf16[3,128,256]{2,1,0:T(8,128)(2,1)S(1)} %get-tuple-element.39.fields.refs_1_, ...), custom_call_target="tpu_custom_call" | custom-call | flops 4000000000 | tf_op jit(solution)/shard_map/pallas_call | solution.py:419
  14.0 0.1 collective-permute-start.4
  14.1 1.6 %collective-permute-start.5 = (bf16[192,256]{1,0:T(8,128)(2,1)S(1)}, bf16[192,256]{1,0:T(8,128)(2,1)S(1)}, u32[]{:S(2)}, u32[]{:S(2)}) collective-permute-start(bf16[192,256]{1,0:T(8,128)(2,1)S(1)} %get-tuple-element.57), channel_id=1, source_target_pairs={{0,2},{2,0},{1,3},{3,1},{4,6},{6,4},{5,7},{7,5},{8,10},{10,8},{9,1... | collective-permute-start | bytes 294920 | tf_op jit(solution)/shard_map/ppermute | solution.py:432
  15.7 1.9 %collective-permute-start.10 = (bf16[304,128]{1,0:T(8,128)(2,1)S(1)}, bf16[304,128]{1,0:T(8,128)(2,1)S(1)}, u32[]{:S(2)}, u32[]{:S(2)}) collective-permute-start(bf16[304,128]{1,0:T(8,128)(2,1)S(1)} %add_convert_fusion.1), channel_id=1, source_target_pairs={{0,9},{1,8},{4,13},{5,12},{8,1},{9,0},{12,5},{13,4},{2,11},{3,10},... | collective-permute-start | bytes 233480 | tf_op jit(solution)/shard_map/ppermute | solution.py:460
  17.6 0.2 shard_map.87.refs_2_
  17.7 1.6 %collective-permute-done.5.refs_0_ = bf16[192,256]{1,0:T(8,128)(2,1)S(1)} collective-permute-done((bf16[192,256]{1,0:T(8,128)(2,1)S(1)}, bf16[192,256]{1,0:T(8,128)(2,1)S(1)}, u32[]{:S(2)}, u32[]{:S(2)}) %collective-permute-start.5) | collective-permute-done | bytes 98336 | tf_op jit(solution)/shard_map/ppermute | solution.py:432
  19.3 1.6 %shard_map.88 = (f32[3,64,256]{2,1,0:T(8,128)S(1)}, bf16[64,128]{1,0:T(8,128)(2,1)S(1)}, bf16[1,3,64,256]{3,2,1,0:T(8,128)(2,1)}) custom-call(s32[4,3]{1,0:T(4,128)S(1)} %get-tuple-element.37.rows.refs_0_, bf16[3,64,256]{2,1,0:T(8,128)(2,1)S(1)} %get-tuple-element.38.refs_3_.cot, bf16[2,3,384,128]{3,2,1,0:T(8,128)(2,1)S(1)} %get-tuple-element.41.gathers, ...), custom_call_target="tpu_custom_call" | custom-call | tf_op jit(solution)/shard_map/pallas_call | solution.py:444
  20.9 1.4 %collective-permute-start.7 = (bf16[64,128]{1,0:T(8,128)(2,1)S(1)}, bf16[64,128]{1,0:T(8,128)(2,1)S(1)}, u32[]{:S(2)}, u32[]{:S(2)}) collective-permute-start(bf16[64,128]{1,0:T(8,128)(2,1)S(1)} %get-tuple-element.62.refs_3_), channel_id=1, source_target_pairs={{0,9},{1,8},{4,13},{5,12},{8,1},{9,0},{12,5},{13,4},{2,11},{3,10},... | collective-permute-start | bytes 49160 | tf_op jit(solution)/shard_map/ppermute | solution.py:460
  22.3 0.9 %collective-permute-start.6 = (bf16[64,128]{1,0:T(8,128)(2,1)S(1)}, bf16[64,128]{1,0:T(8,128)(2,1)S(1)}, u32[]{:S(2)}, u32[]{:S(2)}) collective-permute-start(bf16[64,128]{1,0:T(8,128)(2,1)S(1)} %get-tuple-element.62.refs_3_), channel_id=1, source_target_pairs={{0,1},{1,0},{2,3},{3,2},{4,5},{5,4},{6,7},{7,6},{8,9},{9,8},{10,11... | collective-permute-start | bytes 49160 | tf_op jit(solution)/shard_map/ppermute | solution.py:463
  23.2 0.9 %collective-permute-start.11 = (bf16[304,128]{1,0:T(8,128)(2,1)S(1)}, bf16[304,128]{1,0:T(8,128)(2,1)S(1)}, u32[]{:S(2)}, u32[]{:S(2)}) collective-permute-start(bf16[304,128]{1,0:T(8,128)(2,1)S(1)} %add_convert_fusion), channel_id=1, source_target_pairs={{0,5},{1,4},{4,1},{5,0},{8,13},{9,12},{12,9},{13,8},{2,7},{3,6},{6... | collective-permute-start | bytes 233480 | tf_op jit(solution)/shard_map/ppermute | solution.py:460
  24.0 1.1 %collective-permute-done.7 = bf16[64,128]{1,0:T(8,128)(2,1)S(1)} collective-permute-done((bf16[64,128]{1,0:T(8,128)(2,1)S(1)}, bf16[64,128]{1,0:T(8,128)(2,1)S(1)}, u32[]{:S(2)}, u32[]{:S(2)}) %collective-permute-start.7) | collective-permute-done | bytes 16416 | tf_op jit(solution)/shard_map/ppermute | solution.py:460
  25.2 0.3 collective-permute-start.8
  25.4 0.1 collective-permute-start.9
  25.5 2.2 %collective-permute-done.11 = bf16[304,128]{1,0:T(8,128)(2,1)S(1)} collective-permute-done((bf16[304,128]{1,0:T(8,128)(2,1)S(1)}, bf16[304,128]{1,0:T(8,128)(2,1)S(1)}, u32[]{:S(2)}, u32[]{:S(2)}) %collective-permute-start.11) | collective-permute-done | bytes 77856 | tf_op jit(solution)/shard_map/ppermute | solution.py:460
  27.7 0.2 collective-permute-start.12
  27.9 0.7 %collective-permute-done.8 = bf16[128,128]{1,0:T(8,128)(2,1)S(1)} collective-permute-done((bf16[128,128]{1,0:T(8,128)(2,1)S(1)}, bf16[128,128]{1,0:T(8,128)(2,1)S(1)}, u32[]{:S(2)}, u32[]{:S(2)}) %collective-permute-start.8) | collective-permute-done | bytes 32800 | tf_op jit(solution)/shard_map/ppermute | solution.py:460
  28.7 1.0 %shard_map.89 = bf16[1,3,64,256]{3,2,1,0:T(8,128)(2,1)} custom-call(f32[3,64,256]{2,1,0:T(8,128)S(1)} %get-tuple-element.61.base, bf16[64,128]{1,0:T(8,128)(2,1)S(1)} %get-tuple-element.71.refs_0_, bf16[64,128]{1,0:T(8,128)(2,1)S(1)} %collective-permute-done.9.refs_1_, bf16[64,128]{1,0:T(8,128)(2,1)S(1)} %get-tuple-element.70.refs_2_, ...), custom_call_target="tpu_custom_call" | custom-call | tf_op jit(solution)/shard_map/pallas_call | solution.py:480
  29.7 0.7 %shard_map.90 = (f32[9,64,128]{2,1,0:T(8,128)}, f32[1,64]{1,0:T(1,128)}) custom-call(f32[304,128]{1,0:T(8,128)S(1)} %add_multiply_fusion.refs_0_, f32[304,128]{1,0:T(8,128)S(1)} %collective-permute-done.12.refs_1_), custom_call_target="tpu_custom_call" | custom-call | tf_op jit(solution)/shard_map/pallas_call | solution.py:485
  (14 shorter events, 0.1 us)
Async XLA Ops:
  2.1 8.7 %collective-permute-start = (bf16[128,128]{1,0:T(8,128)(2,1)S(1)}, bf16[128,128]{1,0:T(8,128)(2,1)S(1)}, u32[]{:S(2)}, u32[]{:S(2)}) collective-permute-start(bf16[128,128]{1,0:T(8,128)(2,1)S(1)} %get-tuple-element.46), channel_id=1, source_target_pairs={{0,12},{4,8},{8,4},{12,0},{1,13},{5,9},{9,5},{13,1},{2,14},{6,10},... | collective-permute-start | bytes 98312 | tf_op jit(solution)/shard_map/ppermute | solution.py:400
  7.2 4.8 %collective-permute-start.1 = (bf16[128,128]{1,0:T(8,128)(2,1)S(1)}, bf16[128,128]{1,0:T(8,128)(2,1)S(1)}, u32[]{:S(2)}, u32[]{:S(2)}) collective-permute-start(bf16[128,128]{1,0:T(8,128)(2,1)S(1)} %get-tuple-element.47), channel_id=1, source_target_pairs={{0,8},{4,12},{8,0},{12,4},{1,9},{5,13},{9,1},{13,5},{2,10},{6,14},... | collective-permute-start | bytes 98312 | tf_op jit(solution)/shard_map/ppermute | solution.py:400
  7.2 4.8 %collective-permute-start.2 = (bf16[128,128]{1,0:T(8,128)(2,1)S(1)}, bf16[128,128]{1,0:T(8,128)(2,1)S(1)}, u32[]{:S(2)}, u32[]{:S(2)}) collective-permute-start(bf16[128,128]{1,0:T(8,128)(2,1)S(1)} %get-tuple-element.48), channel_id=1, source_target_pairs={{0,4},{4,0},{8,12},{12,8},{1,5},{5,1},{9,13},{13,9},{2,6},{6,2},{1... | collective-permute-start | bytes 98312 | tf_op jit(solution)/shard_map/ppermute | solution.py:400
  7.9 6.2 %collective-permute-start.3 = (bf16[9,64,128]{2,1,0:T(8,128)(2,1)S(1)}, bf16[9,64,128]{2,1,0:T(8,128)(2,1)S(1)}, u32[]{:S(2)}, u32[]{:S(2)}) collective-permute-start(bf16[9,64,128]{2,1,0:T(8,128)(2,1)S(1)} %get-tuple-element.40.weights), channel_id=1, source_target_pairs={{0,2},{2,0},{1,3},{3,1},{4,6},{6,4},{5,7},{7,5},{8,10},{10,8},{9,1... | collective-permute-start | bytes 442376 | tf_op jit(solution)/shard_map/ppermute | solution.py:404
  14.0 1.6 %collective-permute-start.4 = (f32[304,128]{1,0:T(8,128)S(1)}, f32[304,128]{1,0:T(8,128)S(1)}, u32[]{:S(2)}, u32[]{:S(2)}) collective-permute-start(f32[304,128]{1,0:T(8,128)S(1)} %get-tuple-element.54), channel_id=1, source_target_pairs={{0,1},{1,0},{2,3},{3,2},{4,5},{5,4},{6,7},{7,6},{8,9},{9,8},{10,11... | collective-permute-start | bytes 466952 | tf_op jit(solution)/shard_map/ppermute | solution.py:434
  14.1 5.2 %collective-permute-start.5 = (bf16[192,256]{1,0:T(8,128)(2,1)S(1)}, bf16[192,256]{1,0:T(8,128)(2,1)S(1)}, u32[]{:S(2)}, u32[]{:S(2)}) collective-permute-start(bf16[192,256]{1,0:T(8,128)(2,1)S(1)} %get-tuple-element.57), channel_id=1, source_target_pairs={{0,2},{2,0},{1,3},{3,1},{4,6},{6,4},{5,7},{7,5},{8,10},{10,8},{9,1... | collective-permute-start | bytes 294920 | tf_op jit(solution)/shard_map/ppermute | solution.py:432
  15.7 7.5 %collective-permute-start.10 = (bf16[304,128]{1,0:T(8,128)(2,1)S(1)}, bf16[304,128]{1,0:T(8,128)(2,1)S(1)}, u32[]{:S(2)}, u32[]{:S(2)}) collective-permute-start(bf16[304,128]{1,0:T(8,128)(2,1)S(1)} %add_convert_fusion.1), channel_id=1, source_target_pairs={{0,9},{1,8},{4,13},{5,12},{8,1},{9,0},{12,5},{13,4},{2,11},{3,10},... | collective-permute-start | bytes 233480 | tf_op jit(solution)/shard_map/ppermute | solution.py:460
  20.9 4.2 %collective-permute-start.7 = (bf16[64,128]{1,0:T(8,128)(2,1)S(1)}, bf16[64,128]{1,0:T(8,128)(2,1)S(1)}, u32[]{:S(2)}, u32[]{:S(2)}) collective-permute-start(bf16[64,128]{1,0:T(8,128)(2,1)S(1)} %get-tuple-element.62.refs_3_), channel_id=1, source_target_pairs={{0,9},{1,8},{4,13},{5,12},{8,1},{9,0},{12,5},{13,4},{2,11},{3,10},... | collective-permute-start | bytes 49160 | tf_op jit(solution)/shard_map/ppermute | solution.py:460
  22.3 2.9 %collective-permute-start.6 = (bf16[64,128]{1,0:T(8,128)(2,1)S(1)}, bf16[64,128]{1,0:T(8,128)(2,1)S(1)}, u32[]{:S(2)}, u32[]{:S(2)}) collective-permute-start(bf16[64,128]{1,0:T(8,128)(2,1)S(1)} %get-tuple-element.62.refs_3_), channel_id=1, source_target_pairs={{0,1},{1,0},{2,3},{3,2},{4,5},{5,4},{6,7},{7,6},{8,9},{9,8},{10,11... | collective-permute-start | bytes 49160 | tf_op jit(solution)/shard_map/ppermute | solution.py:463
  23.2 4.5 %collective-permute-start.11 = (bf16[304,128]{1,0:T(8,128)(2,1)S(1)}, bf16[304,128]{1,0:T(8,128)(2,1)S(1)}, u32[]{:S(2)}, u32[]{:S(2)}) collective-permute-start(bf16[304,128]{1,0:T(8,128)(2,1)S(1)} %add_convert_fusion), channel_id=1, source_target_pairs={{0,5},{1,4},{4,1},{5,0},{8,13},{9,12},{12,9},{13,8},{2,7},{3,6},{6... | collective-permute-start | bytes 233480 | tf_op jit(solution)/shard_map/ppermute | solution.py:460
  25.2 3.5 %collective-permute-start.8 = (bf16[128,128]{1,0:T(8,128)(2,1)S(1)}, bf16[128,128]{1,0:T(8,128)(2,1)S(1)}, u32[]{:S(2)}, u32[]{:S(2)}) collective-permute-start(bf16[128,128]{1,0:T(8,128)(2,1)S(1)} %pad_maximum_fusion), channel_id=1, source_target_pairs={{0,5},{1,4},{4,1},{5,0},{8,13},{9,12},{12,9},{13,8},{2,7},{3,6},{6... | collective-permute-start | bytes 98312 | tf_op jit(solution)/shard_map/ppermute | solution.py:460
  25.4 3.2 %collective-permute-start.9 = (bf16[64,128]{1,0:T(8,128)(2,1)S(1)}, bf16[64,128]{1,0:T(8,128)(2,1)S(1)}, u32[]{:S(2)}, u32[]{:S(2)}) collective-permute-start(bf16[64,128]{1,0:T(8,128)(2,1)S(1)} %collective-permute-done.7), channel_id=1, source_target_pairs={{0,1},{1,0},{2,3},{3,2},{4,5},{5,4},{6,7},{7,6},{8,9},{9,8},{10,11... | collective-permute-start | bytes 49160 | tf_op jit(solution)/shard_map/ppermute | solution.py:468
  27.7 2.0 %collective-permute-start.12 = (f32[304,128]{1,0:T(8,128)S(1)}, f32[304,128]{1,0:T(8,128)S(1)}, u32[]{:S(2)}, u32[]{:S(2)}) collective-permute-start(f32[304,128]{1,0:T(8,128)S(1)} %add_multiply_fusion.refs_0_), channel_id=1, source_target_pairs={{0,1},{1,0},{2,3},{3,2},{4,5},{5,4},{6,7},{7,6},{8,9},{9,8},{10,11... | collective-permute-start | bytes 466952 | tf_op jit(solution)/shard_map/ppermute | solution.py:489

commit v13 on v12

--- a/solution.py
+++ b/solution.py
@@ -293,7 +293,7 @@
     column = iota((1, FRAME), 1) % TS
     lane128 = iota((1, 128), 1)
     edge_sum = jnp.zeros((own, 128), F32)
-    pads = []
+    pads, rims, places = [], [], []
     for k in range(SLOTS):
         spread = dot(back_kernels[0][...], own_frames[k])
         for other, back_kernel in zip(slopes, back_kernels[1:]):
@@ -306,10 +306,11 @@
             + jnp.where(column > 0, pltpu.roll(third, 1, 1), 0.0)
         )
         pads.append(pad)
-        edge_sum = edge_sum + dot(first.astype(BF16), gathers[0, k])
-        edge_sum = edge_sum + dot(third.astype(BF16), gathers[1, k])
+        rims += [first.astype(BF16), third.astype(BF16)]
+        places += [gathers[0, k], gathers[1, k]]
         crest = jnp.where(lane128 < TS, pad[:, CELLS:], 0.0) * at_top[k]
         edge_sum = edge_sum + pltpu.roll(crest, FOLD, 1)
+    edge_sum = edge_sum + dot(jnp.concatenate(rims, axis=1), jnp.concatenate(places, axis=0))
     edges[...] = edge_sum.astype(BF16)
     for k in range(SLOTS):
         first = pads[k][:, :128]
@@ -326,10 +327,8 @@
 def finish_kernel(base, *refs):
     out = refs[-1]
     n = len(refs) // 2
-    total = None
-    for received, hits in zip(refs[:n], refs[n:]):
-        part = dot(received[...], hits[...], ((1,), (1,)))
-        total = part if total is None else total + part
+    parts = jnp.concatenate([ref[...] for ref in refs[:n]], axis=1)
+    total = dot(parts, jnp.concatenate([ref[...] for ref in refs[n : 2 * n]], axis=1), ((1,), (1,)))
     for k in range(SLOTS):
         out[0, k] = (base[k] + total[:, k * CELLS : (k + 1) * CELLS]).astype(BF16)
 

time: 30.6 us -> 30.7 us (level)
  no operation moved by 1% of the time
where the time goes in v13:
time: 30.7 us; the launch traced here: 30.6 us
  starting transfers between devices  14.5 us (47%)
  Pallas kernels  8.4 us (27%)
  waiting for transfers between devices  6.93 us (23%)
  between operations  0.72 us (2%)
    ppermute x3, starting transfers between devices, move(): return lax.ppermute(x, 'tiles', [(i, route(i)) for i in range(count)])  5.76 us
    ppermute x4, starting transfers between devices, cross(): return lax.ppermute(x, ('tiles', 'rep'), pairs)  4.33 us
    ppermute x4, waiting for transfers between devices, cross(): return lax.ppermute(x, ('tiles', 'rep'), pairs)  4.06 us
    pallas_call x1, Pallas kernels, on_device(): call(lambda *refs: forward_kernel(*refs, n_halos=len(halos), half_rows=ha...  1.97 us
    pallas_call x1, Pallas kernels, on_device(): call(backward_kernel, [SMEM] + [VMEM] * (5 + 2 * len(others)), [struct((S...  1.77 us
    ppermute x1, starting transfers between devices, on_device(): others = [lax.ppermute(taps, 'chan', pairs) for pairs in ring]  1.63 us
    ppermute x1, waiting for transfers between devices, on_device(): met = [lax.ppermute(slopes, 'chan', pairs) for pairs in ring]  1.61 us
    ppermute x1, starting transfers between devices, on_device(): met = [lax.ppermute(slopes, 'chan', pairs) for pairs in ring]  1.55 us
  transfers between devices with their start and end apart: 13, of which 5 were waited for; matrix products, arithmetic and copies ran while one was open for 0% of the time, Pallas kernels for 20%

profile of v13, /device:TPU:0, one launch (start us, length us, event | category | flops | bytes accessed | tf_op | source)
XLA Modules:
  0.0 30.6 jit_solution(13782322745921682385)
XLA Ops:
  0.6 1.5 %shard_map.84 = (s32[4,3]{1,0:T(4,128)S(1)}, bf16[3,128,256]{2,1,0:T(8,128)(2,1)S(1)}, bf16[9,64,128]{2,1,0:T(8,128)(2,1)S(1)}, f32[1,64]{1,0:T(1,128)S(1)}, bf1...) custom-call(s32[4,3]{1,0:T(4,128)} %refs_0_.1, ...), custom_call_target="tpu_custom_call" | custom-call | tf_op jit(solution)/shard_map/pallas_call | solution.py:382
  2.1 5.1 %collective-permute-start = (bf16[128,128]{1,0:T(8,128)(2,1)S(1)}, bf16[128,128]{1,0:T(8,128)(2,1)S(1)}, u32[]{:S(2)}, u32[]{:S(2)}) collective-permute-start(bf16[128,128]{1,0:T(8,128)(2,1)S(1)} %get-tuple-element.46), channel_id=1, source_target_pairs={{0,12},{4,8},{8,4},{12,0},{1,13},{5,9},{9,5},{13,1},{2,14},{6,10},... | collective-permute-start | bytes 98312 | tf_op jit(solution)/shard_map/ppermute | solution.py:399
  7.2 0.6 %collective-permute-start.2 = (bf16[128,128]{1,0:T(8,128)(2,1)S(1)}, bf16[128,128]{1,0:T(8,128)(2,1)S(1)}, u32[]{:S(2)}, u32[]{:S(2)}) collective-permute-start(bf16[128,128]{1,0:T(8,128)(2,1)S(1)} %get-tuple-element.48), channel_id=1, source_target_pairs={{0,4},{4,0},{8,12},{12,8},{1,5},{5,1},{9,13},{13,9},{2,6},{6,2},{1... | collective-permute-start | bytes 98312 | tf_op jit(solution)/shard_map/ppermute | solution.py:399
  7.9 1.6 %collective-permute-start.3 = (bf16[9,64,128]{2,1,0:T(8,128)(2,1)S(1)}, bf16[9,64,128]{2,1,0:T(8,128)(2,1)S(1)}, u32[]{:S(2)}, u32[]{:S(2)}) collective-permute-start(bf16[9,64,128]{2,1,0:T(8,128)(2,1)S(1)} %get-tuple-element.40.weights), channel_id=1, source_target_pairs={{0,2},{2,0},{1,3},{3,1},{4,6},{6,4},{5,7},{7,5},{8,10},{10,8},{9,1... | collective-permute-start | bytes 442376 | tf_op jit(solution)/shard_map/ppermute | solution.py:403
  9.5 1.3 %shard_map.85 = (bf16[3,384,384]{2,1,0:T(8,128)(2,1)S(1)}, bf16[2,3,128,384]{3,2,1,0:T(8,128)(2,1)S(1)}, bf16[2,3,384,128]{3,2,1,0:T(8,128)(2,1)S(1)}, bf16[192,384]{1,0:T(8,128)(2,1)S(1)}, bf16[192,192]{1,0:T(8,128)(2,1)S(1)}) custom-call(s32[4,3]{1,0:T(4,128)S(1)} %get-tuple-element.37.rows.refs_0_, ...), custom_call_target="tpu_custom_call" | custom-call | tf_op jit(solution)/shard_map/pallas_call | solution.py:405
  10.8 1.2 %collective-permute-done.1.refs_8_ = bf16[128,128]{1,0:T(8,128)(2,1)S(1)} collective-permute-done((bf16[128,128]{1,0:T(8,128)(2,1)S(1)}, bf16[128,128]{1,0:T(8,128)(2,1)S(1)}, u32[]{:S(2)}, u32[]{:S(2)}) %collective-permute-start.1) | collective-permute-done | bytes 32800 | tf_op jit(solution)/shard_map/ppermute | solution.py:399
  12.0 2.0 %shard_map.86 = (bf16[3,192,384]{2,1,0:T(8,128)(2,1)S(1)}, bf16[192,256]{1,0:T(8,128)(2,1)S(1)}, bf16[3,64,256]{2,1,0:T(8,128)(2,1)S(1)}, f32[304,128]{1,0:T(8,128)S(1)}, f32[304,128]{1,0:T(8,128)S(1)}) custom-call(s32[4,3]{1,0:T(4,128)S(1)} %get-tuple-element.37.rows.refs_0_, bf16[3,128,256]{2,1,0:T(8,128)(2,1)S(1)} %get-tuple-element.39.fields.refs_1_, ...), custom_call_target="tpu_custom_call" | custom-call | flops 4000000000 | tf_op jit(solution)/shard_map/pallas_call | solution.py:418
  14.0 0.1 collective-permute-start.4
  14.1 1.6 %collective-permute-start.5 = (bf16[192,256]{1,0:T(8,128)(2,1)S(1)}, bf16[192,256]{1,0:T(8,128)(2,1)S(1)}, u32[]{:S(2)}, u32[]{:S(2)}) collective-permute-start(bf16[192,256]{1,0:T(8,128)(2,1)S(1)} %get-tuple-element.57), channel_id=1, source_target_pairs={{0,2},{2,0},{1,3},{3,1},{4,6},{6,4},{5,7},{7,5},{8,10},{10,8},{9,1... | collective-permute-start | bytes 294920 | tf_op jit(solution)/shard_map/ppermute | solution.py:431
  15.7 1.9 %collective-permute-start.10 = (bf16[304,128]{1,0:T(8,128)(2,1)S(1)}, bf16[304,128]{1,0:T(8,128)(2,1)S(1)}, u32[]{:S(2)}, u32[]{:S(2)}) collective-permute-start(bf16[304,128]{1,0:T(8,128)(2,1)S(1)} %add_convert_fusion.1), channel_id=1, source_target_pairs={{0,9},{1,8},{4,13},{5,12},{8,1},{9,0},{12,5},{13,4},{2,11},{3,10},... | collective-permute-start | bytes 233480 | tf_op jit(solution)/shard_map/ppermute | solution.py:459
  17.6 0.2 shard_map.87.refs_2_
  17.7 1.6 %collective-permute-done.5.refs_0_ = bf16[192,256]{1,0:T(8,128)(2,1)S(1)} collective-permute-done((bf16[192,256]{1,0:T(8,128)(2,1)S(1)}, bf16[192,256]{1,0:T(8,128)(2,1)S(1)}, u32[]{:S(2)}, u32[]{:S(2)}) %collective-permute-start.5) | collective-permute-done | bytes 98336 | tf_op jit(solution)/shard_map/ppermute | solution.py:431
  19.3 1.8 %shard_map.88 = (f32[3,64,256]{2,1,0:T(8,128)S(1)}, bf16[64,128]{1,0:T(8,128)(2,1)S(1)}, bf16[1,3,64,256]{3,2,1,0:T(8,128)(2,1)}) custom-call(s32[4,3]{1,0:T(4,128)S(1)} %get-tuple-element.37.rows.refs_0_, bf16[3,64,256]{2,1,0:T(8,128)(2,1)S(1)} %get-tuple-element.38.refs_3_.cot, bf16[2,3,384,128]{3,2,1,0:T(8,128)(2,1)S(1)} %get-tuple-element.41.gathers, ...), custom_call_target="tpu_custom_call" | custom-call | tf_op jit(solution)/shard_map/pallas_call | solution.py:443
  21.1 1.3 %collective-permute-start.7 = (bf16[64,128]{1,0:T(8,128)(2,1)S(1)}, bf16[64,128]{1,0:T(8,128)(2,1)S(1)}, u32[]{:S(2)}, u32[]{:S(2)}) collective-permute-start(bf16[64,128]{1,0:T(8,128)(2,1)S(1)} %get-tuple-element.62.refs_3_), channel_id=1, source_target_pairs={{0,9},{1,8},{4,13},{5,12},{8,1},{9,0},{12,5},{13,4},{2,11},{3,10},... | collective-permute-start | bytes 49160 | tf_op jit(solution)/shard_map/ppermute | solution.py:459
  22.5 0.9 %collective-permute-start.6 = (bf16[64,128]{1,0:T(8,128)(2,1)S(1)}, bf16[64,128]{1,0:T(8,128)(2,1)S(1)}, u32[]{:S(2)}, u32[]{:S(2)}) collective-permute-start(bf16[64,128]{1,0:T(8,128)(2,1)S(1)} %get-tuple-element.62.refs_3_), channel_id=1, source_target_pairs={{0,1},{1,0},{2,3},{3,2},{4,5},{5,4},{6,7},{7,6},{8,9},{9,8},{10,11... | collective-permute-start | bytes 49160 | tf_op jit(solution)/shard_map/ppermute | solution.py:462
  23.3 0.9 %collective-permute-start.11 = (bf16[304,128]{1,0:T(8,128)(2,1)S(1)}, bf16[304,128]{1,0:T(8,128)(2,1)S(1)}, u32[]{:S(2)}, u32[]{:S(2)}) collective-permute-start(bf16[304,128]{1,0:T(8,128)(2,1)S(1)} %add_convert_fusion), channel_id=1, source_target_pairs={{0,5},{1,4},{4,1},{5,0},{8,13},{9,12},{12,9},{13,8},{2,7},{3,6},{6... | collective-permute-start | bytes 233480 | tf_op jit(solution)/shard_map/ppermute | solution.py:459
  24.2 1.1 %collective-permute-done.7 = bf16[64,128]{1,0:T(8,128)(2,1)S(1)} collective-permute-done((bf16[64,128]{1,0:T(8,128)(2,1)S(1)}, bf16[64,128]{1,0:T(8,128)(2,1)S(1)}, u32[]{:S(2)}, u32[]{:S(2)}) %collective-permute-start.7) | collective-permute-done | bytes 16416 | tf_op jit(solution)/shard_map/ppermute | solution.py:459
  25.3 0.3 collective-permute-start.8
  25.6 0.1 collective-permute-start.9
  25.7 2.2 %collective-permute-done.11 = bf16[304,128]{1,0:T(8,128)(2,1)S(1)} collective-permute-done((bf16[304,128]{1,0:T(8,128)(2,1)S(1)}, bf16[304,128]{1,0:T(8,128)(2,1)S(1)}, u32[]{:S(2)}, u32[]{:S(2)}) %collective-permute-start.11) | collective-permute-done | bytes 77856 | tf_op jit(solution)/shard_map/ppermute | solution.py:459
  27.9 0.2 collective-permute-start.12
  28.1 0.7 %collective-permute-done.8 = bf16[128,128]{1,0:T(8,128)(2,1)S(1)} collective-permute-done((bf16[128,128]{1,0:T(8,128)(2,1)S(1)}, bf16[128,128]{1,0:T(8,128)(2,1)S(1)}, u32[]{:S(2)}, u32[]{:S(2)}) %collective-permute-start.8) | collective-permute-done | bytes 32800 | tf_op jit(solution)/shard_map/ppermute | solution.py:459
  28.8 1.0 %shard_map.89 = bf16[1,3,64,256]{3,2,1,0:T(8,128)(2,1)} custom-call(f32[3,64,256]{2,1,0:T(8,128)S(1)} %get-tuple-element.61.base, bf16[64,128]{1,0:T(8,128)(2,1)S(1)} %get-tuple-element.71.refs_0_, bf16[64,128]{1,0:T(8,128)(2,1)S(1)} %collective-permute-done.9.refs_1_, bf16[64,128]{1,0:T(8,128)(2,1)S(1)} %get-tuple-element.70.refs_2_, ...), custom_call_target="tpu_custom_call" | custom-call | tf_op jit(solution)/shard_map/pallas_call | solution.py:479
  29.8 0.7 %shard_map.90 = (f32[9,64,128]{2,1,0:T(8,128)}, f32[1,64]{1,0:T(1,128)}) custom-call(f32[304,128]{1,0:T(8,128)S(1)} %add_multiply_fusion.refs_0_, f32[304,128]{1,0:T(8,128)S(1)} %collective-permute-done.12.refs_1_), custom_call_target="tpu_custom_call" | custom-call | tf_op jit(solution)/shard_map/pallas_call | solution.py:484
  (14 shorter events, 0.1 us)
Async XLA Ops:
  2.1 8.7 %collective-permute-start = (bf16[128,128]{1,0:T(8,128)(2,1)S(1)}, bf16[128,128]{1,0:T(8,128)(2,1)S(1)}, u32[]{:S(2)}, u32[]{:S(2)}) collective-permute-start(bf16[128,128]{1,0:T(8,128)(2,1)S(1)} %get-tuple-element.46), channel_id=1, source_target_pairs={{0,12},{4,8},{8,4},{12,0},{1,13},{5,9},{9,5},{13,1},{2,14},{6,10},... | collective-permute-start | bytes 98312 | tf_op jit(solution)/shard_map/ppermute | solution.py:399
  7.2 4.8 %collective-permute-start.1 = (bf16[128,128]{1,0:T(8,128)(2,1)S(1)}, bf16[128,128]{1,0:T(8,128)(2,1)S(1)}, u32[]{:S(2)}, u32[]{:S(2)}) collective-permute-start(bf16[128,128]{1,0:T(8,128)(2,1)S(1)} %get-tuple-element.47), channel_id=1, source_target_pairs={{0,8},{4,12},{8,0},{12,4},{1,9},{5,13},{9,1},{13,5},{2,10},{6,14},... | collective-permute-start | bytes 98312 | tf_op jit(solution)/shard_map/ppermute | solution.py:399
  7.2 4.8 %collective-permute-start.2 = (bf16[128,128]{1,0:T(8,128)(2,1)S(1)}, bf16[128,128]{1,0:T(8,128)(2,1)S(1)}, u32[]{:S(2)}, u32[]{:S(2)}) collective-permute-start(bf16[128,128]{1,0:T(8,128)(2,1)S(1)} %get-tuple-element.48), channel_id=1, source_target_pairs={{0,4},{4,0},{8,12},{12,8},{1,5},{5,1},{9,13},{13,9},{2,6},{6,2},{1... | collective-permute-start | bytes 98312 | tf_op jit(solution)/shard_map/ppermute | solution.py:399
  7.9 6.2 %collective-permute-start.3 = (bf16[9,64,128]{2,1,0:T(8,128)(2,1)S(1)}, bf16[9,64,128]{2,1,0:T(8,128)(2,1)S(1)}, u32[]{:S(2)}, u32[]{:S(2)}) collective-permute-start(bf16[9,64,128]{2,1,0:T(8,128)(2,1)S(1)} %get-tuple-element.40.weights), channel_id=1, source_target_pairs={{0,2},{2,0},{1,3},{3,1},{4,6},{6,4},{5,7},{7,5},{8,10},{10,8},{9,1... | collective-permute-start | bytes 442376 | tf_op jit(solution)/shard_map/ppermute | solution.py:403
  14.0 1.6 %collective-permute-start.4 = (f32[304,128]{1,0:T(8,128)S(1)}, f32[304,128]{1,0:T(8,128)S(1)}, u32[]{:S(2)}, u32[]{:S(2)}) collective-permute-start(f32[304,128]{1,0:T(8,128)S(1)} %get-tuple-element.54), channel_id=1, source_target_pairs={{0,1},{1,0},{2,3},{3,2},{4,5},{5,4},{6,7},{7,6},{8,9},{9,8},{10,11... | collective-permute-start | bytes 466952 | tf_op jit(solution)/shard_map/ppermute | solution.py:433
  14.1 5.2 %collective-permute-start.5 = (bf16[192,256]{1,0:T(8,128)(2,1)S(1)}, bf16[192,256]{1,0:T(8,128)(2,1)S(1)}, u32[]{:S(2)}, u32[]{:S(2)}) collective-permute-start(bf16[192,256]{1,0:T(8,128)(2,1)S(1)} %get-tuple-element.57), channel_id=1, source_target_pairs={{0,2},{2,0},{1,3},{3,1},{4,6},{6,4},{5,7},{7,5},{8,10},{10,8},{9,1... | collective-permute-start | bytes 294920 | tf_op jit(solution)/shard_map/ppermute | solution.py:431
  15.7 7.6 %collective-permute-start.10 = (bf16[304,128]{1,0:T(8,128)(2,1)S(1)}, bf16[304,128]{1,0:T(8,128)(2,1)S(1)}, u32[]{:S(2)}, u32[]{:S(2)}) collective-permute-start(bf16[304,128]{1,0:T(8,128)(2,1)S(1)} %add_convert_fusion.1), channel_id=1, source_target_pairs={{0,9},{1,8},{4,13},{5,12},{8,1},{9,0},{12,5},{13,4},{2,11},{3,10},... | collective-permute-start | bytes 233480 | tf_op jit(solution)/shard_map/ppermute | solution.py:459
  21.1 4.2 %collective-permute-start.7 = (bf16[64,128]{1,0:T(8,128)(2,1)S(1)}, bf16[64,128]{1,0:T(8,128)(2,1)S(1)}, u32[]{:S(2)}, u32[]{:S(2)}) collective-permute-start(bf16[64,128]{1,0:T(8,128)(2,1)S(1)} %get-tuple-element.62.refs_3_), channel_id=1, source_target_pairs={{0,9},{1,8},{4,13},{5,12},{8,1},{9,0},{12,5},{13,4},{2,11},{3,10},... | collective-permute-start | bytes 49160 | tf_op jit(solution)/shard_map/ppermute | solution.py:459
  22.5 2.9 %collective-permute-start.6 = (bf16[64,128]{1,0:T(8,128)(2,1)S(1)}, bf16[64,128]{1,0:T(8,128)(2,1)S(1)}, u32[]{:S(2)}, u32[]{:S(2)}) collective-permute-start(bf16[64,128]{1,0:T(8,128)(2,1)S(1)} %get-tuple-element.62.refs_3_), channel_id=1, source_target_pairs={{0,1},{1,0},{2,3},{3,2},{4,5},{5,4},{6,7},{7,6},{8,9},{9,8},{10,11... | collective-permute-start | bytes 49160 | tf_op jit(solution)/shard_map/ppermute | solution.py:462
  23.3 4.5 %collective-permute-start.11 = (bf16[304,128]{1,0:T(8,128)(2,1)S(1)}, bf16[304,128]{1,0:T(8,128)(2,1)S(1)}, u32[]{:S(2)}, u32[]{:S(2)}) collective-permute-start(bf16[304,128]{1,0:T(8,128)(2,1)S(1)} %add_convert_fusion), channel_id=1, source_target_pairs={{0,5},{1,4},{4,1},{5,0},{8,13},{9,12},{12,9},{13,8},{2,7},{3,6},{6... | collective-permute-start | bytes 233480 | tf_op jit(solution)/shard_map/ppermute | solution.py:459
  25.3 3.5 %collective-permute-start.8 = (bf16[128,128]{1,0:T(8,128)(2,1)S(1)}, bf16[128,128]{1,0:T(8,128)(2,1)S(1)}, u32[]{:S(2)}, u32[]{:S(2)}) collective-permute-start(bf16[128,128]{1,0:T(8,128)(2,1)S(1)} %pad_maximum_fusion), channel_id=1, source_target_pairs={{0,5},{1,4},{4,1},{5,0},{8,13},{9,12},{12,9},{13,8},{2,7},{3,6},{6... | collective-permute-start | bytes 98312 | tf_op jit(solution)/shard_map/ppermute | solution.py:459
  25.6 3.3 %collective-permute-start.9 = (bf16[64,128]{1,0:T(8,128)(2,1)S(1)}, bf16[64,128]{1,0:T(8,128)(2,1)S(1)}, u32[]{:S(2)}, u32[]{:S(2)}) collective-permute-start(bf16[64,128]{1,0:T(8,128)(2,1)S(1)} %collective-permute-done.7), channel_id=1, source_target_pairs={{0,1},{1,0},{2,3},{3,2},{4,5},{5,4},{6,7},{7,6},{8,9},{9,8},{10,11... | collective-permute-start | bytes 49160 | tf_op jit(solution)/shard_map/ppermute | solution.py:467
  27.9 1.9 %collective-permute-start.12 = (f32[304,128]{1,0:T(8,128)S(1)}, f32[304,128]{1,0:T(8,128)S(1)}, u32[]{:S(2)}, u32[]{:S(2)}) collective-permute-start(f32[304,128]{1,0:T(8,128)S(1)} %add_multiply_fusion.refs_0_), channel_id=1, source_target_pairs={{0,1},{1,0},{2,3},{3,2},{4,5},{5,4},{6,7},{7,6},{8,9},{9,8},{10,11... | collective-permute-start | bytes 466952 | tf_op jit(solution)/shard_map/ppermute | solution.py:488
